TPU v7x, 32 devices: a whole 2x2x4 slice. The times are simulated.
32 devices in a mesh: dp: 4 (over z), seq: 8 (over y, x, core).
Axes of the slice: x: 2, y: 2, z: 4, core: 2. Of those that a mesh axis runs over, the one named last changes fastest.
Arguments:
- stream: bfloat16 [8192, 768], P(('dp', 'seq')), may hold values from -6 to 6
- w_mix: bfloat16 [2, 768, 1920], P(None, ('dp', 'seq')), may hold values from -0.21875 to 0.21875
- w_out: bfloat16 [2, 768, 768], P(None, ('dp', 'seq')), may hold values from -0.21875 to 0.21875
- w_up: bfloat16 [2, 768, 3072], P(None, ('dp', 'seq')), may hold values from -0.21875 to 0.21875
- w_down: bfloat16 [2, 1536, 768], P(None, ('dp', 'seq')), may hold values from -0.15625 to 0.15625
- gains: bfloat16 [2, 3, 768], P(None, None, ('dp', 'seq')), may hold values from 0.5 to 1.5
- chan_params: bfloat16 [2, 768], P(None, ('dp', 'seq')), may hold values from -3.2 to 12, as said below
- lengths: int32 [4, 3], P('dp'), may hold values from 1 to 2045, as said below
- cotangent: bfloat16 [8192, 768], P(('dp', 'seq')), may hold values from -6 to 6
Outputs:
- mixed: bfloat16 [8192, 768], P(('dp', 'seq'))
- grad_stream: float32 [8192, 768], P(('dp', 'seq'))
- grad_w_mix: float32 [2, 768, 1920], P(None, ('dp', 'seq'))
- grad_w_out: float32 [2, 768, 768], P(None, ('dp', 'seq'))
- grad_w_up: float32 [2, 768, 3072], P(None, ('dp', 'seq'))
- grad_w_down: float32 [2, 1536, 768], P(None, ('dp', 'seq'))
- grad_gains: float32 [2, 3, 768], P(None, None, ('dp', 'seq'))
- grad_chan_params: float32 [2, 768], P(None, ('dp', 'seq'))
Inputs may be any that keep to these rules, and one draw needn't show every extreme that they name: Each row's lengths fill its stream of 2048 slots but for 1 to 85 padding slots at its end; one sequence of each row is longer than 1792, each other one has at most (255) // 3 tokens. `chan_params`: per layer, the first 384 entries are forget-gate biases, the last 384 angles in radians.
All inputs are finite; a program needn't handle non-finite values.
Results may differ from a plain program's by a relative error of at most 0.017.
Values may be sent and summed in bfloat16 or wider, within the bound.
No kernel may reach another device: no remote copies, remote signals or barrier semaphores. Data moves between devices by JAX's collectives and lax.ppermute only.
A program may use at most 256 MiB of HBM per device.

v0:
```python
import jax
import jax.numpy as jnp
from jax import lax
from jax.sharding import PartitionSpec as P

GN_WIDTH = 128


EPS = 1e-06


def carried_in(x, axis, combine, identity, reverse):
    devices, position = (lax.axis_size(axis), lax.axis_index(axis))
    everything = jax.tree.map(lambda part: lax.all_gather(part, axis), x)
    start = jax.tree.map(
        lambda part, zero: jnp.broadcast_to(jnp.asarray(zero, part.dtype), part.shape), x, identity
    )

    def lap(k, before):
        at = devices - 1 - k if reverse else k
        reached = at > position if reverse else at < position
        new = combine(before, jax.tree.map(lambda part: part[at], everything))
        return jax.tree.map(lambda a, b: jnp.where(reached, a, b), new, before)

    return lax.fori_loop(0, devices, lap, start)


def compose(earlier, later):
    first_re, first_im, shift_re, shift_im = earlier
    second_re, second_im, add_re, add_im = later
    return (
        second_re * first_re - second_im * first_im,
        second_re * first_im + second_im * first_re,
        second_re * shift_re - second_im * shift_im + add_re,
        second_re * shift_im + second_im * shift_re + add_im,
    )


def complex_times(left_re, left_im, right_re, right_im):
    return (left_re * right_re - left_im * right_im, left_re * right_im + left_im * right_re)


def rms_scale(values):
    return lax.rsqrt(jnp.mean(values * values, axis=-1, keepdims=True) + EPS)


def rms_back(values, scale, grad_normal):
    normal = values * scale
    return (
        scale * (grad_normal - normal * jnp.mean(grad_normal * normal, axis=-1, keepdims=True)),
        normal,
    )


def group_forward(values):
    shaped = values.reshape(values.shape[0], values.shape[1] // GN_WIDTH, GN_WIDTH)
    centre = shaped - jnp.mean(shaped, axis=-1, keepdims=True)
    scale = lax.rsqrt(jnp.mean(centre * centre, axis=-1, keepdims=True) + EPS)
    return ((centre * scale).reshape(values.shape), scale)


def group_back(normal, scale, grad_normal):
    shaped_norm = normal.reshape(scale.shape[0], scale.shape[1], GN_WIDTH)
    shaped_grad = grad_normal.reshape(shaped_norm.shape)
    inner = (
        shaped_grad
        - jnp.mean(shaped_grad, axis=-1, keepdims=True)
        - shaped_norm * jnp.mean(shaped_grad * shaped_norm, axis=-1, keepdims=True)
    )
    return (scale * inner).reshape(normal.shape)


def stream_masks(lengths, rows):
    length_row = lengths[0]
    ends = jnp.cumsum(length_row)
    starts = ends - length_row
    places = lax.axis_index("seq") * rows + jnp.arange(rows, dtype=jnp.int32)
    restart = jnp.any(places[:, None] == starts[None, :], axis=1).astype(jnp.float32)
    keep = (places < ends[-1]).astype(jnp.float32)
    return (restart[:, None], keep[:, None])


def carry_forward(summary):
    identity = (
        jnp.ones_like(summary[0]),
        jnp.zeros_like(summary[0]),
        jnp.zeros_like(summary[0]),
        jnp.zeros_like(summary[0]),
    )
    prefix = carried_in(summary, "seq", compose, identity, False)
    return (prefix[2], prefix[3])


def carry_backward(summary):
    identity = (
        jnp.ones_like(summary[0]),
        jnp.zeros_like(summary[0]),
        jnp.zeros_like(summary[0]),
        jnp.zeros_like(summary[0]),
    )
    suffix = carried_in(summary, "seq", compose, identity, True)
    return (suffix[2], suffix[3])


def mixer_front(values, bundle, restart):
    gains = bundle[4].astype(jnp.float32)
    chan = bundle[5].astype(jnp.float32)
    width = values.shape[1]
    half = width // 2
    scale_one = rms_scale(values)
    normed = (values * scale_one * gains[0]).astype(jnp.bfloat16)
    mixin = jnp.dot(normed, bundle[0], preferred_element_type=jnp.float32)
    cand_pre = mixin[:, :width]
    candidate = jax.nn.silu(cand_pre)
    gate = jax.nn.sigmoid(mixin[:, width : 2 * width])
    rate = jax.nn.sigmoid(mixin[:, 2 * width :] + chan[:half])
    cos_t = jnp.cos(chan[half:])
    sin_t = jnp.sin(chan[half:])
    kept = (1.0 - restart) * rate
    turn_re = kept * cos_t
    turn_im = kept * sin_t
    feed_re = (1.0 - rate) * candidate[:, :half]
    feed_im = (1.0 - rate) * candidate[:, half:]
    local = lax.associative_scan(compose, (turn_re, turn_im, feed_re, feed_im), axis=0)
    summary = (local[0][-1], local[1][-1], local[2][-1], local[3][-1])
    return {
        "normed": normed,
        "scale_one": scale_one,
        "cand_pre": cand_pre,
        "candidate": candidate,
        "gate": gate,
        "rate": rate,
        "cos_t": cos_t,
        "sin_t": sin_t,
        "turn_re": turn_re,
        "turn_im": turn_im,
        "local": local,
        "summary": summary,
    }


def layer_rest(values, bundle, front, carry_re, carry_im):
    gains = bundle[4].astype(jnp.float32)
    local = front["local"]
    add_re, add_im = complex_times(local[0], local[1], carry_re, carry_im)
    state_re = local[2] + add_re
    state_im = local[3] + add_im
    states = jnp.concatenate([state_re, state_im], axis=1)
    normal_g, scale_g = group_forward(front["gate"] * states)
    gated = (normal_g * gains[1]).astype(jnp.bfloat16)
    after = values + jnp.dot(gated, bundle[1], preferred_element_type=jnp.float32)
    scale_two = rms_scale(after)
    lifted = (after * scale_two * gains[2]).astype(jnp.bfloat16)
    both = jnp.dot(lifted, bundle[2], preferred_element_type=jnp.float32)
    inner = both.shape[1] // 2
    hidden = (jax.nn.silu(both[:, :inner]) * both[:, inner:]).astype(jnp.bfloat16)
    result = after + jnp.dot(hidden, bundle[3], preferred_element_type=jnp.float32)
    return {
        "state_re": state_re,
        "state_im": state_im,
        "states": states,
        "normal_g": normal_g,
        "scale_g": scale_g,
        "gated": gated,
        "after": after,
        "scale_two": scale_two,
        "lifted": lifted,
        "both": both,
        "hidden": hidden,
        "result": result,
    }


def row_product(left, right):
    return jnp.dot(left.T, right, preferred_element_type=jnp.float32)


def layer_backward(values, bundle, restart, carry_re, carry_im, grad_next):
    gains = bundle[4].astype(jnp.float32)
    front = mixer_front(values, bundle, restart)
    rest = layer_rest(values, bundle, front, carry_re, carry_im)
    width = values.shape[1]
    half = width // 2
    grad_low = grad_next.astype(jnp.bfloat16)
    hidden = rest["hidden"]
    grad_down = lax.psum_scatter(
        row_product(hidden, grad_low), ("dp", "seq"), scatter_dimension=0, tiled=True
    )
    grad_hidden = jnp.dot(grad_low, bundle[3].T, preferred_element_type=jnp.float32)
    both = rest["both"]
    inner = both.shape[1] // 2
    gate_part = both[:, :inner]
    sig_part = jax.nn.sigmoid(gate_part)
    grad_gate_part = grad_hidden * both[:, inner:] * sig_part * (1.0 + gate_part * (1.0 - sig_part))
    grad_both = jnp.concatenate(
        [grad_gate_part, grad_hidden * gate_part * sig_part], axis=1
    ).astype(jnp.bfloat16)
    grad_lifted = jnp.dot(grad_both, bundle[2].T, preferred_element_type=jnp.float32)
    grad_norm_two, normal_two = rms_back(rest["after"], rest["scale_two"], grad_lifted * gains[2])
    gain_two = jnp.sum(grad_lifted * normal_two, axis=0)
    grad_after = grad_next + grad_norm_two
    grad_mid = grad_after.astype(jnp.bfloat16)
    grad_gated = jnp.dot(grad_mid, bundle[1].T, preferred_element_type=jnp.float32)
    gain_mid = jnp.sum(grad_gated * rest["normal_g"], axis=0)
    grad_raw = group_back(rest["normal_g"], rest["scale_g"], grad_gated * gains[1])
    gate = front["gate"]
    grad_gate = grad_raw * rest["states"]
    grad_states = grad_raw * gate
    conj_re = front["turn_re"]
    conj_im = -front["turn_im"]
    next_re = jnp.concatenate([conj_re[1:], jnp.ones((1, half), jnp.float32)], axis=0)
    next_im = jnp.concatenate([conj_im[1:], jnp.zeros((1, half), jnp.float32)], axis=0)
    back_scan = lax.associative_scan(
        compose,
        (next_re[::-1], next_im[::-1], grad_states[::-1, :half], grad_states[::-1, half:]),
        axis=0,
    )
    reach_re, reach_im, own_re, own_im = (member[::-1] for member in back_scan)
    total_re, total_im = complex_times(conj_re[0], conj_im[0], reach_re[0], reach_im[0])
    lead_re, lead_im = complex_times(conj_re[0], conj_im[0], own_re[0], own_im[0])
    flow_re, flow_im = carry_backward((total_re, total_im, lead_re, lead_im))
    more_re, more_im = complex_times(reach_re, reach_im, flow_re, flow_im)
    adj_re = own_re + more_re
    adj_im = own_im + more_im
    prior_re = jnp.concatenate([carry_re[None, :], rest["state_re"][:-1]], axis=0)
    prior_im = jnp.concatenate([carry_im[None, :], rest["state_im"][:-1]], axis=0)
    turn_grad_re = adj_re * prior_re + adj_im * prior_im
    turn_grad_im = adj_im * prior_re - adj_re * prior_im
    rate = front["rate"]
    cos_t = front["cos_t"]
    sin_t = front["sin_t"]
    candidate = front["candidate"]
    live = 1.0 - restart
    grad_rate = live * (turn_grad_re * cos_t + turn_grad_im * sin_t) - (
        adj_re * candidate[:, :half] + adj_im * candidate[:, half:]
    )
    grad_angle = jnp.sum(live * rate * (turn_grad_im * cos_t - turn_grad_re * sin_t), axis=0)
    grad_cand = jnp.concatenate([(1.0 - rate) * adj_re, (1.0 - rate) * adj_im], axis=1)
    cand_pre = front["cand_pre"]
    sig_cand = jax.nn.sigmoid(cand_pre)
    grad_cand_pre = grad_cand * sig_cand * (1.0 + cand_pre * (1.0 - sig_cand))
    grad_gate_pre = grad_gate * gate * (1.0 - gate)
    grad_rate_pre = grad_rate * rate * (1.0 - rate)
    grad_bias = jnp.sum(grad_rate_pre, axis=0)
    grad_mixin = jnp.concatenate([grad_cand_pre, grad_gate_pre, grad_rate_pre], axis=1).astype(
        jnp.bfloat16
    )
    grad_normed = jnp.dot(grad_mixin, bundle[0].T, preferred_element_type=jnp.float32)
    grad_norm_one, normal_one = rms_back(values, front["scale_one"], grad_normed * gains[0])
    gain_one = jnp.sum(grad_normed * normal_one, axis=0)
    grad_values = grad_after + grad_norm_one
    small_cols = jnp.stack(
        [gain_one, gain_mid, gain_two, jnp.concatenate([grad_bias, grad_angle])], axis=1
    )
    normed = front["normed"]
    gated = rest["gated"]
    lifted = rest["lifted"]
    summed = lax.psum_scatter(
        jnp.concatenate(
            [
                row_product(normed, grad_mixin),
                row_product(gated, grad_mid),
                row_product(lifted, grad_both),
                small_cols,
            ],
            axis=1,
        ),
        ("dp", "seq"),
        scatter_dimension=0,
        tiled=True,
    )
    mix_cols = bundle[0].shape[1]
    up_cols = bundle[2].shape[1]
    grad_mix = summed[:, :mix_cols]
    grad_out = summed[:, mix_cols : mix_cols + width]
    grad_up = summed[:, mix_cols + width : mix_cols + width + up_cols]
    tail = summed[:, mix_cols + width + up_cols :]
    gain_grads = tail[:, :3].T
    chan_grads = tail[:, 3]
    return (grad_values, (grad_mix, grad_out, grad_up, grad_down, gain_grads, chan_grads))


def body(stream, w_mix, w_out, w_up, w_down, gains, chan_params, lengths, cotangent):
    rows = stream.shape[0]
    depth = w_mix.shape[0]
    restart, keep = stream_masks(lengths, rows)
    values = stream.astype(jnp.float32)
    saved_inputs = []
    saved_carry = []
    saved_weights = []
    for layer_index in range(depth):
        bundle = (
            lax.all_gather(w_mix[layer_index], ("dp", "seq"), axis=0, tiled=True),
            lax.all_gather(w_out[layer_index], ("dp", "seq"), axis=0, tiled=True),
            lax.all_gather(w_up[layer_index], ("dp", "seq"), axis=0, tiled=True),
            lax.all_gather(w_down[layer_index], ("dp", "seq"), axis=0, tiled=True),
            lax.all_gather(gains[layer_index], ("dp", "seq"), axis=1, tiled=True),
            lax.all_gather(chan_params[layer_index], ("dp", "seq"), axis=0, tiled=True),
        )
        front = mixer_front(values, bundle, restart)
        carry_re, carry_im = carry_forward(front["summary"])
        saved_inputs.append(values)
        saved_carry.append((carry_re, carry_im))
        saved_weights.append(bundle)
        values = layer_rest(values, bundle, front, carry_re, carry_im)["result"]
    mixed = values.astype(jnp.bfloat16)
    grad_values = cotangent.astype(jnp.float32) * keep
    shares = []
    for layer_index in reversed(range(depth)):
        bundle = (
            lax.all_gather(w_mix[layer_index], ("dp", "seq"), axis=0, tiled=True),
            lax.all_gather(w_out[layer_index], ("dp", "seq"), axis=0, tiled=True),
            lax.all_gather(w_up[layer_index], ("dp", "seq"), axis=0, tiled=True),
            lax.all_gather(w_down[layer_index], ("dp", "seq"), axis=0, tiled=True),
            lax.all_gather(gains[layer_index], ("dp", "seq"), axis=1, tiled=True),
            lax.all_gather(chan_params[layer_index], ("dp", "seq"), axis=0, tiled=True),
        )
        grad_values, terms = layer_backward(
            saved_inputs[layer_index],
            bundle,
            restart,
            saved_carry[layer_index][0],
            saved_carry[layer_index][1],
            grad_values,
        )
        shares.append(terms)
    shares = shares[::-1]
    stacked = tuple((jnp.stack([share[member] for share in shares]) for member in range(6)))
    return (mixed, grad_values) + stacked


def solution(mesh):
    placed = (
        P(("dp", "seq"), None),
        P(None, ("dp", "seq"), None),
        P(None, ("dp", "seq"), None),
        P(None, ("dp", "seq"), None),
        P(None, ("dp", "seq"), None),
        P(None, None, ("dp", "seq")),
        P(None, ("dp", "seq")),
        P("dp", None),
        P(("dp", "seq"), None),
    )
    return jax.shard_map(
        body,
        mesh=mesh,
        in_specs=placed,
        out_specs=(
            P(("dp", "seq"), None),
            P(("dp", "seq"), None),
            P(None, ("dp", "seq"), None),
            P(None, ("dp", "seq"), None),
            P(None, ("dp", "seq"), None),
            P(None, ("dp", "seq"), None),
            P(None, None, ("dp", "seq")),
            P(None, ("dp", "seq")),
        ),
        check_vma=False,
    )
```

profile of v0, /device:TPU:0, one launch (start us, length us, event | category | flops | bytes accessed | tf_op | source)
XLA Modules:
  0.0 2161.5 jit_solution(2489746760401764182)
XLA Ops:
  19.9 42.2 %all-reduce.266 = (bf16[768]{0:T(1024)(128)(2,1)S(1)}, bf16[768]{0:T(1024)(128)(2,1)S(1)}) all-reduce(bf16[768]{0:T(1024)(128)(2,1)S(1)} %dynamic-update-slice, bf16[768]{0:T(1024)(128)(2,1)S(1)} %dynamic-update-slice.1), channel_id=4, replica_groups=mesh['dp'=4,'seq'=8] {'dp','seq'}, use_global_device_ids=true, to_apply=%add.264 | all-reduce | flops 1536 | bytes 6144
  63.8 41.4 %all-gather = bf16[1,3,768]{1,0,2:T(2,128)(2,1)S(1)} all-gather(bf16[1,3,24]{1,0,2:T(2,128)(2,1)S(1)} %copy.154), channel_id=2, replica_groups=mesh['dp'=4,'seq'=8] {'dp','seq'}, dimensions={2}, use_global_device_ids=true | all-gather | bytes 4752 | tf_op jit(solution)/shard_map/all_gather | solution.py:297
  105.6 7.6 slice_reduce_fusion.3
  113.3 38.4 %all-gather.6 = bf16[1,3,768]{1,0,2:T(2,128)(2,1)S(1)} all-gather(bf16[1,3,24]{1,0,2:T(2,128)(2,1)S(1)} %copy.155), channel_id=8, replica_groups=mesh['dp'=4,'seq'=8] {'dp','seq'}, dimensions={2}, use_global_device_ids=true | all-gather | bytes 4752 | tf_op jit(solution)/shard_map/all_gather | solution.py:297
  152.1 7.7 slice_reduce_fusion
  280.4 9.3 all-gather.13
  297.6 7.7 all-gather.14
  309.1 9.1 all-gather.15
  323.6 7.7 all-gather.12
  331.9 21.6 %while.68 = (s32[]{:T(128)}, f32[384]{0:T(512)}, f32[384]{0:T(512)}, s32[]{:T(128)}, f32[8,384]{1,0:T(8,128)}, /*index=5*/f32[8,384]{1,0:T(8,128)}, f32[8,384]{1,0:T(8,128)}, f32[8,384]{1,0:T(8,128)}, s32[]{:T(128)}, s32[]{:T(128)}) while((s32[]{:T(128)}, f32[384]{0:T(512)}, f32[384]{0:T(512)}, s32[]{:T(128)}, f32[8,384]{1,0:T(8,128)}, ...), condition=%wide.region_4.5_spmd.clone, body=%wide.region_3.4_spmd.clone.sunk | while | flops 4612 | bytes 24713 | solution.py:25
  357.3 3.9 rev.37
  361.2 3.9 rev.38
  365.0 9.0 all-gather.25
  374.7 8.4 all-gather.24
  396.4 3.9 fusion.6
  975.9 8.8 all-gather.17
  992.6 8.0 all-gather.18
  1004.4 8.8 all-gather.19
  1018.6 8.0 all-gather.16
  1027.2 21.6 while.69
  1076.9 5.7 fusion.2
  1082.6 5.0 multiply_convert_fusion.3
  1104.4 4.5 multiply_convert_fusion.7
  1319.4 4.3 rev.33
  1323.7 3.9 rev.34
  1327.5 8.8 all-gather.21
  1336.9 8.0 all-gather.20
  1345.6 3.9 rev.32
  1349.4 3.9 rev.35
  1353.3 8.7 all-gather.23
  1362.6 8.0 all-gather.22
  1371.3 21.7 %while.70 = (s32[]{:T(128)}, f32[384]{0:T(512)}, f32[384]{0:T(512)}, s32[]{:T(128)}, f32[8,384]{1,0:T(8,128)}, /*index=5*/f32[8,384]{1,0:T(8,128)}, f32[8,384]{1...) while((s32[]{:T(128)}, f32[384]{0:T(512)}, ...), condition=%wide.region_18.19_spmd.clone, body=%wide.region_17.18_spmd.clone.sunk | while | flops 4616 | bytes 24775 | solution.py:25
  1403.9 3.9 multiply_convert_fusion.1
  1407.9 5.8 multiply_reduce_fusion.3
  1430.5 4.4 multiply_convert_fusion.6
  1558.9 4.4 fusion.86
  1650.7 3.9 rev.36
  1656.5 3.8 rev.39
  1661.2 8.8 all-gather.27
  1670.5 8.0 all-gather.26
  1679.2 21.5 while.71
  1715.3 5.2 fusion.43
  1720.5 19.9 concatenate.587
  1745.4 3.7 fusion.68
  1749.1 5.5 fusion.44
  1754.6 20.8 concatenate.589
  1783.4 154.4 %reduce-scatter.5.cloned.1.call-done = f32[24,5764]{1,0:T(8,128)} async-done(((f32[768,5764]{1,0:T(8,128)}), f32[24,5764]{1,0:T(8,128)}) %reduce-scatter.5.cloned.1.call-update) | async-done | bytes 553360 | tf_op jit(solution)/shard_map/reduce_scatter | solution.py:258
  1938.6 204.2 %reduce-scatter.7.cloned.1.call-done = f32[24,5764]{1,0:T(8,128)} async-done(((f32[768,5764]{1,0:T(8,128)}), f32[24,5764]{1,0:T(8,128)}) %reduce-scatter.7.cloned.1.call-update) | async-done | bytes 553360 | tf_op jit(solution)/shard_map/reduce_scatter | solution.py:258
  (1759 shorter events, 1387.7 us)
Async XLA Ops:
  7.2 9.5 copy-start.225
  7.2 12.1 copy-start.25
  7.2 12.3 copy-start.223
  7.2 56.3 %copy-start.214 = (bf16[2,3,24]{2,0,1:T(2,128)(2,1)S(1)}, bf16[2,3,24]{2,0,1:T(2,128)(2,1)}, u32[]{:S(2)}) copy-start(bf16[2,3,24]{2,0,1:T(2,128)(2,1)} %param.22) | copy-start | bytes 868
  7.2 152.6 %all-gather.37.cloned.1.call-start = ((), (), s32[]{:S(2)}) async-start(), calls=%async_computation.8 | async-start | bytes 3041280 | tf_op jit(solution)/shard_map/all_gather | solution.py:293
  8.9 384.7 %all-gather.39.cloned.1.call-start = ((), (), s32[]{:S(2)}) async-start(), calls=%async_computation.9 | async-start | bytes 1216512 | tf_op jit(solution)/shard_map/all_gather | solution.py:294
  10.4 386.0 %all-gather.41.cloned.1.call-start = ((), (), s32[]{:S(2)}) async-start(), calls=%async_computation.10 | async-start | bytes 4866048 | tf_op jit(solution)/shard_map/all_gather | solution.py:295
  12.2 391.2 %all-gather.43.cloned.1.call-start = ((), (), s32[]{:S(2)}) async-start(), calls=%async_computation.11 | async-start | bytes 2433024 | tf_op jit(solution)/shard_map/all_gather | solution.py:296
  13.9 392.9 %all-gather.45.cloned.1.call-start = ((), (), s32[]{:S(2)}) async-start(), calls=%async_computation.12 | async-start | bytes 3041280 | tf_op jit(solution)/shard_map/all_gather | solution.py:293
  14.5 1058.9 %all-gather.47.cloned.1.call-start = ((), (), s32[]{:S(2)}) async-start(), calls=%async_computation.13 | async-start | bytes 1216512 | tf_op jit(solution)/shard_map/all_gather | solution.py:294
  15.1 1061.8 %all-gather.49.cloned.1.call-start = ((), (), s32[]{:S(2)}) async-start(), calls=%async_computation.14 | async-start | bytes 4866048 | tf_op jit(solution)/shard_map/all_gather | solution.py:295
  15.8 1066.8 %all-gather.51.cloned.1.call-start = ((), (), s32[]{:S(2)}) async-start(), calls=%async_computation.15 | async-start | bytes 2433024 | tf_op jit(solution)/shard_map/all_gather | solution.py:296
  16.6 1765.1 %reduce-scatter.9.cloned.1.call-start = ((), (), s32[]{:S(2)}) async-start(), calls=%async_computation.6 | async-start | bytes 4866048 | tf_op jit(solution)/shard_map/reduce_scatter | solution.py:186
  19.5 140.3 %copy-start.156 = (f32[256]{0:T(256)}, f32[256]{0:T(256)S(1)}, u32[]{:S(2)}) copy-start(f32[256]{0:T(256)S(1)} %add_rsqrt_fusion.5) | copy-start | bytes 3076
  164.2 82.2 %copy-start.33 = (f32[256,384]{1,0:T(8,128)}, f32[256,384]{1,0:T(8,128)S(1)}, u32[]{:S(2)}) copy-start(f32[256,384]{1,0:T(8,128)S(1)} %get-tuple-element.1000) | copy-start | bytes 1179652
  190.1 22.5 %copy-start.59 = (f32[256,384]{1,0:T(8,128)S(1)}, f32[256,384]{1,0:T(8,128)}, u32[]{:S(2)}) copy-start(f32[256,384]{1,0:T(8,128)} %get-tuple-element.1001) | copy-start | bytes 1179652
  215.3 10.5 copy-start.98
  225.9 11.8 copy-start.47
  226.1 11.7 copy-start.48
  247.7 10.2 copy-start.140
  247.7 10.2 copy-start.141
  247.7 10.2 copy-start.167
  247.7 10.2 copy-start.168
  247.7 10.2 copy-start.218
  247.7 10.3 copy-start.217
  247.8 10.3 copy-start.216
  247.8 10.4 copy-start.215
  247.8 10.5 copy-start.126
  247.8 10.5 copy-start.127
  247.8 10.5 copy-start.143
  247.8 10.5 copy-start.144
  247.8 10.5 copy-start.213
  247.8 10.6 copy-start.211
  247.8 10.6 copy-start.210
  247.8 10.7 copy-start.212
  248.7 10.0 copy-start.112
  248.7 10.0 copy-start.113
  248.7 10.1 copy-start.128
  248.7 10.1 copy-start.129
  264.7 12.0 copy-start.49
  264.7 11.9 copy-start.50
  279.2 52.7 %copy-start.60 = (f32[256,384]{1,0:T(8,128)}, f32[256,384]{1,0:T(8,128)S(1)}, u32[]{:S(2)}) copy-start(f32[256,384]{1,0:T(8,128)S(1)} %pad.979) | copy-start | bytes 1179652
  280.4 74.4 %copy-start.61 = (f32[256,384]{1,0:T(8,128)}, f32[256,384]{1,0:T(8,128)S(1)}, u32[]{:S(2)}) copy-start(f32[256,384]{1,0:T(8,128)S(1)} %pad.981) | copy-start | bytes 1179652
  356.6 27.0 %copy-start.17 = (f32[256,384]{1,0:T(8,128)}, f32[256,384]{1,0:T(8,128)S(1)}, u32[]{:S(2)}) copy-start(f32[256,384]{1,0:T(8,128)S(1)} %get-tuple-element.1005) | copy-start | bytes 1179652
  356.7 27.0 %copy-start.19 = (f32[256,384]{1,0:T(8,128)}, f32[256,384]{1,0:T(8,128)S(1)}, u32[]{:S(2)}) copy-start(f32[256,384]{1,0:T(8,128)S(1)} %get-tuple-element.1006) | copy-start | bytes 1179652
  1414.3 367.3 %reduce-scatter.11.cloned.1.call-start = ((), (), s32[]{:S(2)}) async-start(), calls=%async_computation.7 | async-start | bytes 4866048 | tf_op jit(solution)/shard_map/reduce_scatter | solution.py:186
  1563.3 374.5 %reduce-scatter.5.cloned.1.call-start = ((), (), s32[]{:S(2)}) async-start(), calls=%async_computation.4 | async-start | bytes 18653184 | tf_op jit(solution)/shard_map/reduce_scatter | solution.py:258
  1740.5 402.3 %reduce-scatter.7.cloned.1.call-start = ((), (), s32[]{:S(2)}) async-start(), calls=%async_computation.5 | async-start | bytes 18653184 | tf_op jit(solution)/shard_map/reduce_scatter | solution.py:258
  (190 other events, 610.5 us)
Sparse Core Ops, SparseCore 0:
  11.5 61.8 all-gather.36
  76.3 52.8 all-gather.38
  132.1 62.8 all-gather.40
  197.7 56.0 all-gather.42
  256.6 57.6 all-gather.44
  317.1 52.7 all-gather.46
  373.3 62.5 all-gather.48
  438.8 56.0 all-gather.50
  1414.4 104.1 reduce-scatter.8
  1563.4 104.2 reduce-scatter.10
  1740.6 197.1 reduce-scatter.4
  1944.1 198.6 reduce-scatter.6
where the time goes:
time: 2200 us; the launch traced here: 2160 us
  local copies, waits for them, and re-layouts  1010 us (46%)
  other arithmetic  438 us (20%)
  waiting for transfers between devices  361 us (16%)
  blocking collectives  257 us (12%)
  matrix products  80.9 us (4%)
    reduce_scatter x2, waiting for transfers between devices, layer_backward(): lax.psum_scatter(jnp.concatenate([row_product(normed, grad_mixin), row_pr...  359 us
    slice x226, local copies, waits for them, and re-layouts, layer_backward(): lax.associative_scan(compose, (next_re[::-1], next_im[::-1], grad_states[...  260 us
    slice x212, local copies, waits for them, and re-layouts, mixer_front(): lax.associative_scan(compose, (turn_re, turn_im, feed_re, feed_im), axis=0)  185 us
    pad x112, local copies, waits for them, and re-layouts, layer_backward(): lax.associative_scan(compose, (next_re[::-1], next_im[::-1], grad_states[...  182 us
    pad x112, local copies, waits for them, and re-layouts, mixer_front(): lax.associative_scan(compose, (turn_re, turn_im, feed_re, feed_im), axis=0)  136 us
    all_gather x16, blocking collectives, carried_in(): everything = jax.tree.map(lambda part: lax.all_gather(part, axis), x)  135 us
    all_gather x2, blocking collectives, body(): lax.all_gather(gains[layer_index], ('dp', 'seq'), axis=1, tiled=True)  79.9 us
    add x63, other arithmetic, layer_backward(): lax.associative_scan(compose, (next_re[::-1], next_im[::-1], grad_states[...  74.8 us
  transfers between devices with their start and end apart: 12, of which 2 were waited for; matrix products, arithmetic and copies ran while one was open for 55% of the time, Pallas kernels for 0%

commit v1 on v0

v1 whole, which is shorter than its diff:
```python
import functools

import jax
import jax.numpy as jnp
from jax import lax
from jax.experimental import pallas as pl
from jax.experimental.pallas import tpu as pltpu
from jax.sharding import PartitionSpec as P

GROUP = 128
EPS = 1e-06
SUB = 8
UNIT = 48
HALVES = {"mix": 1024, "out": 384, "up": 1536}
ROWS = 32
F32 = jnp.float32
BF16 = jnp.bfloat16
ALL = ("dp", "seq")
VMEM = pl.BlockSpec(memory_space=pltpu.VMEM)
SMEM = pl.BlockSpec(memory_space=pltpu.SMEM)
ANY = pl.BlockSpec(memory_space=pl.ANY)


def sds(shape, dtype=F32):
    return jax.ShapeDtypeStruct(shape, dtype)


def over_rows(total, body):
    def step(i, _):
        body(pl.ds(pl.multiple_of(i * ROWS, ROWS), ROWS))
        return 0

    lax.fori_loop(0, total // ROWS, step, 0)


def dot(left, right):
    return jnp.dot(left, right, preferred_element_type=F32)


def dot_t(left, right):
    return lax.dot_general(left, right, (((1,), (1,)), ((), ())), preferred_element_type=F32)


def cmul(ar, ai, br, bi):
    return ar * br - ai * bi, ar * bi + ai * br


def power(cos, sin, times):
    while times > 1:
        cos, sin = cos * cos - sin * sin, 2.0 * cos * sin
        times //= 2
    return cos, sin


def turns(p_ref, half):
    cos, sin = p_ref[3:4, half:], p_ref[4:5, :half]
    return tuple(
        [jnp.broadcast_to(part[:, t * GROUP : (t + 1) * GROUP], (SUB, GROUP)) for t in range(half // GROUP)]
        for part in (cos, sin)
    )


def parts(ref, k, tiles):
    return [ref[k, :, t * GROUP : (t + 1) * GROUP] for t in range(tiles)]


def mix_width(plan, width):
    return 2 * width + width // 2 if plan is None else 2 * HALVES["mix"]


def load_start(pairs, sem):
    for source, target in pairs:
        pltpu.make_async_copy(source, target, sem).start()


def load_wait(pairs, sem):
    for source, target in pairs:
        pltpu.make_async_copy(source, target, sem).wait()


def pairs_of(plan, sources, me_ref, name, target):
    if plan is None:
        return [(sources[{"mix": 0, "out": 1, "up": 2, "down": 3}[name]], target)]
    chip, core = me_ref[1], me_ref[2]
    pairs = []
    for source, others, other_core, column, columns, begin in plan[name]:
        half = core ^ other_core
        for b, other in enumerate(others):
            block = chip ^ other
            if name == "down":
                row, left = block * (2 * UNIT) + half * UNIT, 0
            else:
                row, left = block * UNIT, half * HALVES[name] + begin
            to = target.at[pl.ds(pl.multiple_of(row, UNIT), UNIT), pl.ds(pl.multiple_of(left, GROUP), columns)]
            pairs.append((sources[source].at[b, :, pl.ds(column, columns)], to))
    return pairs


def front_kernel(
    plan, count, me_ref, place_ref, x_ref, p_ref, *refs
):
    w_hbm, refs = refs[:count], refs[count:]
    (
    normed_ref, cpre_ref, gate_ref, rate_ref, kept_ref, feed_ref, sub_ref, total_ref,
    w_ref, sem,
    ) = refs
    rows, width = x_ref.shape
    half = width // 2
    block = rows // SUB
    pairs = pairs_of(plan, w_hbm, me_ref, "mix", w_ref)
    load_start(pairs, sem)

    def norm(r):
        x = x_ref[r, :]
        scale = lax.rsqrt(jnp.mean(x * x, axis=1, keepdims=True) + EPS)
        normed_ref[r, :] = (x * scale * p_ref[0:1, :]).astype(BF16)

    over_rows(rows, norm)
    load_wait(pairs, sem)
    normed = normed_ref[...]
    rate = jax.nn.sigmoid(dot(normed, w_ref[:, 2 * width : 2 * width + half]) + p_ref[3:4, :half])
    rate_ref[...] = rate
    at = lax.broadcasted_iota(jnp.int32, (rows, GROUP), 0)
    fresh = at == place_ref[0]
    for j in range(1, place_ref.shape[0]):
        fresh = jnp.logical_or(fresh, at == place_ref[j])
    tiles = half // GROUP
    for t in range(tiles):
        kept_ref[t] = jnp.where(fresh, 0.0, rate[:, t * GROUP : (t + 1) * GROUP])
    for k in range(2):
        cols = slice(k * half, (k + 1) * half)
        pre = dot(normed, w_ref[:, cols])
        cpre_ref[:, cols] = pre
        feed = (1.0 - rate_ref[...]) * (pre * jax.nn.sigmoid(pre))
        for t in range(tiles):
            feed_ref[k * tiles + t] = feed[:, t * GROUP : (t + 1) * GROUP]
    cos, sin = turns(p_ref, half)

    mag = [jnp.ones((SUB, GROUP), F32)] * tiles
    br = [jnp.zeros((SUB, GROUP), F32)] * tiles
    bi = [jnp.zeros((SUB, GROUP), F32)] * tiles
    for j in range(block):
        at = pl.ds(j, SUB, stride=block)
        for t in range(tiles):
            kept = kept_ref[t, at, :]
            tr, ti = cmul(cos[t], sin[t], br[t], bi[t])
            br[t] = kept * tr + feed_ref[t, at, :]
            bi[t] = kept * ti + feed_ref[tiles + t, at, :]
            mag[t] = mag[t] * kept
    mag, br, bi = (jnp.concatenate(part, axis=1) for part in (mag, br, bi))
    far_cos, far_sin = power(jnp.concatenate(cos, axis=1), jnp.concatenate(sin, axis=1), block)
    ar, ai = mag * far_cos, mag * far_sin
    sub_ref[0] = ar
    sub_ref[1] = ai
    sub_ref[2] = br
    sub_ref[3] = bi
    one_r, one_i, sum_r, sum_i = (part[0:1] for part in (ar, ai, br, bi))
    for k in range(1, SUB):
        kr, ki = ar[k : k + 1], ai[k : k + 1]
        one_r, one_i = cmul(kr, ki, one_r, one_i)
        sum_r, sum_i = cmul(kr, ki, sum_r, sum_i)
        sum_r = sum_r + br[k : k + 1]
        sum_i = sum_i + bi[k : k + 1]
    total_ref[0:1, :] = one_r
    total_ref[1:2, :] = one_i
    total_ref[2:3, :] = sum_r
    total_ref[3:4, :] = sum_i
    for k in range(2):
        cols = slice(width + k * half, width + (k + 1) * half)
        gate_ref[:, k * half : (k + 1) * half] = jax.nn.sigmoid(dot(normed, w_ref[:, cols]))


def front(plan, me, place, x, params, weights):
    rows, width = x.shape
    half = width // 2
    return pl.pallas_call(
        functools.partial(front_kernel, plan, len(weights)),
        out_shape=(
            sds((rows, width), BF16),
            sds((rows, width)),
            sds((rows, width)),
            sds((rows, half)),
            sds((half // GROUP, rows, GROUP)),
            sds((width // GROUP, rows, GROUP)),
            sds((4, SUB, half)),
            sds((4, half)),
        ),
        in_specs=[SMEM, SMEM, VMEM, VMEM] + [ANY] * len(weights),
        out_specs=(VMEM,) * 8,
        scratch_shapes=[pltpu.VMEM((width, mix_width(plan, width)), BF16), pltpu.SemaphoreType.DMA],
        compiler_params=pltpu.CompilerParams(vmem_limit_bytes=56 << 20),
        cost_estimate=pl.CostEstimate(flops=2 * rows * width * 5 * half, bytes_accessed=8 << 20, transcendentals=0),
        name="front",
    )(me, place, x, params, *weights)


def rest_kernel(plan, count, me_ref, x_ref, p_ref, gate_ref, kept_ref, feed_ref, sub_ref, every_ref, *refs):
    w_hbm, refs = refs[:count], refs[count:]
    (
    states_ref, first_ref, gn_ref, rg_ref, gated_ref, after_ref, lifted_ref, both_ref, hidden_ref, next_ref,
    out_ref, up_ref, down_ref, sems,
    ) = refs
    rows, width = x_ref.shape
    half = width // 2
    block = rows // SUB
    inner = hidden_ref.shape[1]
    out_pairs, up_pairs, down_pairs = (
        pairs_of(plan, w_hbm, me_ref, name, ref)
        for name, ref in (("out", out_ref), ("up", up_ref), ("down", down_ref))
    )
    load_start(out_pairs, sems.at[0])
    load_start(up_pairs, sems.at[1])
    load_start(down_pairs, sems.at[2])

    sr = jnp.zeros((1, half), F32)
    si = jnp.zeros((1, half), F32)
    for k in range(every_ref.shape[0]):
        nr, ni = cmul(every_ref[k, 0:1, :], every_ref[k, 1:2, :], sr, si)
        earlier = k < me_ref[0]
        sr = jnp.where(earlier, nr + every_ref[k, 2:3, :], sr)
        si = jnp.where(earlier, ni + every_ref[k, 3:4, :], si)
    for k in range(SUB):
        first_ref[0, k : k + 1, :] = sr
        first_ref[1, k : k + 1, :] = si
        nr, ni = cmul(sub_ref[0, k : k + 1, :], sub_ref[1, k : k + 1, :], sr, si)
        sr = nr + sub_ref[2, k : k + 1, :]
        si = ni + sub_ref[3, k : k + 1, :]
    cos, sin = turns(p_ref, half)
    tiles = half // GROUP
    sr = parts(first_ref, 0, tiles)
    si = parts(first_ref, 1, tiles)
    for j in range(block):
        at = pl.ds(j, SUB, stride=block)
        for t in range(tiles):
            kept = kept_ref[t, at, :]
            tr, ti = cmul(cos[t], sin[t], sr[t], si[t])
            sr[t] = kept * tr + feed_ref[t, at, :]
            si[t] = kept * ti + feed_ref[tiles + t, at, :]
            states_ref[t, at, :] = sr[t]
            states_ref[tiles + t, at, :] = si[t]

    lane = lax.broadcasted_iota(jnp.int32, (ROWS, GROUP), 1)

    def group_norm(r):
        held = jnp.zeros((ROWS, GROUP), F32)
        for g in range(width // GROUP):
            cols = slice(g * GROUP, (g + 1) * GROUP)
            v = gate_ref[r, cols] * states_ref[g, r, :]
            centre = v - jnp.mean(v, axis=1, keepdims=True)
            scale = lax.rsqrt(jnp.mean(centre * centre, axis=1, keepdims=True) + EPS)
            gn = centre * scale
            gn_ref[r, cols] = gn
            gated_ref[r, cols] = (gn * p_ref[1:2, cols]).astype(BF16)
            held = jnp.where(lane == g, scale, held)
        rg_ref[r, :] = held

    over_rows(rows, group_norm)
    load_wait(out_pairs, sems.at[0])
    after_ref[...] = x_ref[...] + dot(gated_ref[...], out_ref[...])

    def norm(r):
        after = after_ref[r, :]
        scale = lax.rsqrt(jnp.mean(after * after, axis=1, keepdims=True) + EPS)
        lifted_ref[r, :] = (after * scale * p_ref[2:3, :]).astype(BF16)

    over_rows(rows, norm)
    load_wait(up_pairs, sems.at[1])
    lifted = lifted_ref[...]
    step = half
    for k in range(inner // step):
        cols = slice(k * step, (k + 1) * step)
        more = slice(inner + k * step, inner + (k + 1) * step)
        a = dot(lifted, up_ref[:, cols])
        b = dot(lifted, up_ref[:, more])
        both_ref[:, cols] = a
        both_ref[:, more] = b
        hidden_ref[:, cols] = (a * jax.nn.sigmoid(a) * b).astype(BF16)
    load_wait(down_pairs, sems.at[2])
    next_ref[...] = after_ref[...] + dot(hidden_ref[...], down_ref[...])


def rest(plan, me, x, params, gate, kept, feed, sub, every, weights):
    rows, width = x.shape
    half = width // 2
    inner = 2 * width
    return pl.pallas_call(
        functools.partial(rest_kernel, plan, len(weights)),
        out_shape=(
            sds((width // GROUP, rows, GROUP)),
            sds((2, SUB, half)),
            sds((rows, width)),
            sds((rows, GROUP)),
            sds((rows, width), BF16),
            sds((rows, width)),
            sds((rows, width), BF16),
            sds((rows, 2 * inner)),
            sds((rows, inner), BF16),
            sds((rows, width)),
        ),
        in_specs=[SMEM] + [VMEM] * 7 + [ANY] * len(weights),
        out_specs=(VMEM,) * 10,
        scratch_shapes=[
            pltpu.VMEM((width, width), BF16),
            pltpu.VMEM((width, 2 * inner), BF16),
            pltpu.VMEM((inner, width), BF16),
            pltpu.SemaphoreType.DMA((3,)),
        ],
        compiler_params=pltpu.CompilerParams(vmem_limit_bytes=56 << 20),
        cost_estimate=pl.CostEstimate(flops=2 * rows * width * 7 * width, bytes_accessed=20 << 20, transcendentals=0),
        name="rest",
    )(me, x, params, gate, kept, feed, sub, every, *weights)


def back_one_kernel(
    plan, count, me_ref, dx_ref, p_ref, both_ref, after_ref, gn_ref, rg_ref, gate_ref, states_ref, kept_ref, sub_ref, *refs
):
    w_hbm, refs = refs[:count], refs[count:]
    (
    dlow_ref, dboth_ref, dafter_ref, dmid_ref, dgpre_ref, dstates_ref, gains_ref, rsub_ref, rtotal_ref,
    work_ref, out_ref, up_ref, down_ref, sems,
    ) = refs
    rows, width = dx_ref.shape
    half = width // 2
    block = rows // SUB
    inner = down_ref.shape[0]
    out_pairs, up_pairs, down_pairs = (
        pairs_of(plan, w_hbm, me_ref, name, ref)
        for name, ref in (("out", out_ref), ("up", up_ref), ("down", down_ref))
    )
    load_start(down_pairs, sems.at[2])
    load_start(up_pairs, sems.at[1])
    load_start(out_pairs, sems.at[0])
    dlow = dx_ref[...].astype(BF16)
    dlow_ref[...] = dlow
    load_wait(down_pairs, sems.at[2])
    step = half
    for k in range(inner // step):
        cols = slice(k * step, (k + 1) * step)
        more = slice(inner + k * step, inner + (k + 1) * step)
        dh = dot_t(dlow, down_ref[cols, :])
        a = both_ref[:, cols]
        sig = jax.nn.sigmoid(a)
        dboth_ref[:, cols] = (dh * both_ref[:, more] * (sig * (1.0 + a * (1.0 - sig)))).astype(BF16)
        dboth_ref[:, more] = (dh * (a * sig)).astype(BF16)
    load_wait(up_pairs, sems.at[1])
    work_ref[...] = dot_t(dboth_ref[...], up_ref[...])

    def norm_back(r):
        after = after_ref[r, :]
        scale = lax.rsqrt(jnp.mean(after * after, axis=1, keepdims=True) + EPS)
        normal = after * scale
        lift = work_ref[r, :]
        e = lift * p_ref[2:3, :]
        d = dx_ref[r, :] + scale * (e - normal * jnp.mean(e * normal, axis=1, keepdims=True))
        dafter_ref[r, :] = d
        dmid_ref[r, :] = d.astype(BF16)
        work_ref[r, :] = lift * normal

    over_rows(rows, norm_back)
    gains_ref[0:1, :] = jnp.sum(work_ref[...], axis=0, keepdims=True)
    load_wait(out_pairs, sems.at[0])
    work_ref[...] = dot_t(dmid_ref[...], out_ref[...])

    def group_back(r):
        held = rg_ref[r, :]
        for g in range(width // GROUP):
            cols = slice(g * GROUP, (g + 1) * GROUP)
            gn = gn_ref[r, cols]
            dg = work_ref[r, cols]
            e = dg * p_ref[1:2, cols]
            dv = held[:, g : g + 1] * (
                e - jnp.mean(e, axis=1, keepdims=True) - gn * jnp.mean(e * gn, axis=1, keepdims=True)
            )
            gate = gate_ref[r, cols]
            dgpre_ref[r, cols] = (dv * states_ref[g, r, :] * gate * (1.0 - gate)).astype(BF16)
            dstates_ref[g, r, :] = dv * gate
            work_ref[r, cols] = dg * gn

    over_rows(rows, group_back)
    gains_ref[1:2, :] = jnp.sum(work_ref[...], axis=0, keepdims=True)

    cos, sin = turns(p_ref, half)
    tiles = half // GROUP
    zr = [jnp.zeros((SUB, GROUP), F32)] * tiles
    zi = [jnp.zeros((SUB, GROUP), F32)] * tiles
    for j in reversed(range(block)):
        at = pl.ds(j, SUB, stride=block)
        for t in range(tiles):
            kept = kept_ref[t, at, :]
            qr = dstates_ref[t, at, :] + zr[t]
            qi = dstates_ref[tiles + t, at, :] + zi[t]
            zr[t] = kept * (cos[t] * qr + sin[t] * qi)
            zi[t] = kept * (cos[t] * qi - sin[t] * qr)
    zr, zi = jnp.concatenate(zr, axis=1), jnp.concatenate(zi, axis=1)
    rsub_ref[0] = zr
    rsub_ref[1] = zi
    tr = jnp.zeros((1, half), F32)
    ti = jnp.zeros((1, half), F32)
    for k in reversed(range(SUB)):
        ar, ai = sub_ref[0, k : k + 1, :], sub_ref[1, k : k + 1, :]
        tr, ti = ar * tr + ai * ti + zr[k : k + 1], ar * ti - ai * tr + zi[k : k + 1]
    rtotal_ref[0:1, :] = tr
    rtotal_ref[1:2, :] = ti


def back_one(plan, me, dx, params, kept_values, weights):
    both, after, gn, rg, gate, states, kept, sub = kept_values
    rows, width = dx.shape
    half = width // 2
    inner = 2 * width
    return pl.pallas_call(
        functools.partial(back_one_kernel, plan, len(weights)),
        out_shape=(
            sds((rows, width), BF16),
            sds((rows, 2 * inner), BF16),
            sds((rows, width)),
            sds((rows, width), BF16),
            sds((rows, width), BF16),
            sds((width // GROUP, rows, GROUP)),
            sds((2, width)),
            sds((2, SUB, half)),
            sds((2, half)),
        ),
        in_specs=[SMEM] + [VMEM] * 10 + [ANY] * len(weights),
        out_specs=(VMEM,) * 9,
        scratch_shapes=[
            pltpu.VMEM((rows, width), F32),
            pltpu.VMEM((width, width), BF16),
            pltpu.VMEM((width, 2 * inner), BF16),
            pltpu.VMEM((inner, width), BF16),
            pltpu.SemaphoreType.DMA((3,)),
        ],
        compiler_params=pltpu.CompilerParams(vmem_limit_bytes=56 << 20),
        cost_estimate=pl.CostEstimate(flops=2 * rows * width * 7 * width, bytes_accessed=20 << 20, transcendentals=0),
        name="back_one",
    )(me, dx, params, both, after, gn, rg, gate, states, kept, sub, *weights)


def back_two_kernel(
    plan, count, me_ref, x_ref, p_ref, dafter_ref, dgpre_ref, dstates_ref, states_ref, kept_ref, rate_ref, cpre_ref,
    first_ref, sub_ref, rsub_ref, every_ref, revery_ref, *refs
):
    w_hbm, refs = refs[:count], refs[count:]
    (
    dmixin_ref, dx_ref, gains_ref,
    work_ref, q_ref, turn_ref, start_ref, w_ref, sem,
    ) = refs
    rows, width = x_ref.shape
    half = width // 2
    block = rows // SUB
    pairs = pairs_of(plan, w_hbm, me_ref, "mix", w_ref)
    load_start(pairs, sem)
    zr = jnp.zeros((1, half), F32)
    zi = jnp.zeros((1, half), F32)
    for k in reversed(range(every_ref.shape[0])):
        ar, ai = every_ref[k, 0:1, :], every_ref[k, 1:2, :]
        later = k > me_ref[0]
        nr = ar * zr + ai * zi + revery_ref[k, 0:1, :]
        ni = ar * zi - ai * zr + revery_ref[k, 1:2, :]
        zr = jnp.where(later, nr, zr)
        zi = jnp.where(later, ni, zi)
    for k in reversed(range(SUB)):
        start_ref[0, k : k + 1, :] = zr
        start_ref[1, k : k + 1, :] = zi
        ar, ai = sub_ref[0, k : k + 1, :], sub_ref[1, k : k + 1, :]
        zr, zi = (
            ar * zr + ai * zi + rsub_ref[0, k : k + 1, :],
            ar * zi - ai * zr + rsub_ref[1, k : k + 1, :],
        )
    cos, sin = turns(p_ref, half)
    tiles = half // GROUP
    zr = parts(start_ref, 0, tiles)
    zi = parts(start_ref, 1, tiles)
    angle = [jnp.zeros((SUB, GROUP), F32)] * tiles
    for j in reversed(range(block)):
        at = pl.ds(j, SUB, stride=block)
        before = pl.ds(max(j - 1, 0), SUB, stride=block)
        for t in range(tiles):
            kept = kept_ref[t, at, :]
            qr = dstates_ref[t, at, :] + zr[t]
            qi = dstates_ref[tiles + t, at, :] + zi[t]
            q_ref[t, at, :] = qr
            q_ref[tiles + t, at, :] = qi
            zr[t] = kept * (cos[t] * qr + sin[t] * qi)
            zi[t] = kept * (cos[t] * qi - sin[t] * qr)
            if j:
                sr, si = states_ref[t, before, :], states_ref[tiles + t, before, :]
            else:
                sr, si = (first_ref[k, :, t * GROUP : (t + 1) * GROUP] for k in range(2))
            turn_ref[t, at, :] = zr[t] * sr + zi[t] * si
            angle[t] = angle[t] + (zi[t] * sr - zr[t] * si)
    gains_ref[1:2, half:] = jnp.sum(jnp.concatenate(angle, axis=1), axis=0, keepdims=True)

    def activations(r):
        for t in range(tiles):
            rate = rate_ref[r, t * GROUP : (t + 1) * GROUP]
            left = 1.0 - rate
            meet = jnp.zeros_like(rate)
            for k in range(2):
                cols = slice((k * tiles + t) * GROUP, (k * tiles + t + 1) * GROUP)
                pre = cpre_ref[r, cols]
                sig = jax.nn.sigmoid(pre)
                q = q_ref[k * tiles + t, r, :]
                meet = meet + q * (pre * sig)
                dmixin_ref[r, cols] = (left * q * (sig * (1.0 + pre * (1.0 - sig)))).astype(BF16)
            dfpre = left * (turn_ref[t, r, :] - rate * meet)
            dmixin_ref[r, 2 * width + t * GROUP : 2 * width + (t + 1) * GROUP] = dfpre.astype(BF16)
            turn_ref[t, r, :] = dfpre
        dmixin_ref[r, width : 2 * width] = dgpre_ref[r, :]

    over_rows(rows, activations)
    for t in range(tiles):
        gains_ref[1:2, t * GROUP : (t + 1) * GROUP] = jnp.sum(turn_ref[t], axis=0, keepdims=True)
    load_wait(pairs, sem)
    work_ref[...] = dot_t(dmixin_ref[...], w_ref[:, : dmixin_ref.shape[1]])

    def norm_back(r):
        x = x_ref[r, :]
        scale = lax.rsqrt(jnp.mean(x * x, axis=1, keepdims=True) + EPS)
        normal = x * scale
        dn = work_ref[r, :]
        e = dn * p_ref[0:1, :]
        dx_ref[r, :] = dafter_ref[r, :] + scale * (e - normal * jnp.mean(e * normal, axis=1, keepdims=True))
        work_ref[r, :] = dn * normal

    over_rows(rows, norm_back)
    gains_ref[0:1, :] = jnp.sum(work_ref[...], axis=0, keepdims=True)


def back_two(plan, me, x, params, dafter, dgpre, dstates, states, kept, rate, cpre, first, sub, rsub, every, revery, weights):
    rows, width = x.shape
    half = width // 2
    return pl.pallas_call(
        functools.partial(back_two_kernel, plan, len(weights)),
        out_shape=(
            sds((rows, 2 * width + half), BF16),
            sds((rows, width)),
            sds((2, width)),
        ),
        in_specs=[SMEM] + [VMEM] * 14 + [ANY] * len(weights),
        out_specs=(VMEM,) * 3,
        scratch_shapes=[
            pltpu.VMEM((rows, width), F32),
            pltpu.VMEM((width // GROUP, rows, GROUP), F32),
            pltpu.VMEM((half // GROUP, rows, GROUP), F32),
            pltpu.VMEM((2, SUB, half), F32),
            pltpu.VMEM((width, mix_width(plan, width)), BF16),
            pltpu.SemaphoreType.DMA,
        ],
        compiler_params=pltpu.CompilerParams(vmem_limit_bytes=56 << 20),
        cost_estimate=pl.CostEstimate(flops=2 * rows * width * 5 * half, bytes_accessed=10 << 20, transcendentals=0),
        name="back_two",
    )(me, x, params, dafter, dgpre, dstates, states, kept, rate, cpre, first, sub, rsub, every, revery, *weights)


def row_product(left, right):
    return lax.dot_general(left, right, (((0,), (0,)), ((), ())), preferred_element_type=F32)


def grad_rest_kernel(
    me_ref, gated_ref, dmid_ref, lifted_ref, dboth_ref, hidden_ref, dlow_ref, keep_ref, send_ref,
    down_ref, up_ref, out_ref, sem,
):
    chip, core = me_ref[1], me_ref[2]
    chips = keep_ref.shape[0]
    width = dlow_ref.shape[1]
    pairs = []

    def export(name, grad, column, columns):
        for half, target in ((core, keep_ref), (1 - core, send_ref)):
            for b in range(chips):
                block = chip ^ b
                if name == "down":
                    row, left = block * (2 * UNIT) + half * UNIT, 0
                else:
                    row, left = block * UNIT, half * HALVES[name]
                pair = (
                    grad.at[pl.ds(pl.multiple_of(row, UNIT), UNIT), pl.ds(pl.multiple_of(left, GROUP), columns)],
                    target.at[b, :, pl.ds(column, columns)],
                )
                load_start([pair], sem)
                pairs.append(pair)

    step = HALVES["out"]
    hidden, dlow = hidden_ref[...], dlow_ref[...]
    for k in range(width // step):
        cols = slice(k * step, (k + 1) * step)
        down_ref[:, cols] = row_product(hidden, dlow[:, cols]).astype(BF16)
    export("down", down_ref, HALVES["out"] + HALVES["up"], width)
    lifted = lifted_ref[...]
    for k in range(up_ref.shape[1] // step):
        cols = slice(k * step, (k + 1) * step)
        up_ref[:, cols] = row_product(lifted, dboth_ref[:, cols]).astype(BF16)
    export("up", up_ref, HALVES["out"], HALVES["up"])
    gated = gated_ref[...]
    for k in range(width // step):
        cols = slice(k * step, (k + 1) * step)
        out_ref[:, cols] = row_product(gated, dmid_ref[:, cols]).astype(BF16)
    export("out", out_ref, 0, HALVES["out"])
    load_wait(pairs, sem)


def grad_rest(me, chips, gated, dmid, lifted, dboth, hidden, dlow):
    rows, width = dlow.shape
    inner = hidden.shape[1]
    shape = sds((chips, UNIT, HALVES["out"] + HALVES["up"] + width), BF16)
    return pl.pallas_call(
        grad_rest_kernel,
        out_shape=(shape, shape),
        in_specs=[SMEM] + [VMEM] * 6,
        out_specs=(ANY, ANY),
        scratch_shapes=[
            pltpu.VMEM((inner, width), BF16),
            pltpu.VMEM((width, 2 * inner), BF16),
            pltpu.VMEM((width, width), BF16),
            pltpu.SemaphoreType.DMA,
        ],
        compiler_params=pltpu.CompilerParams(vmem_limit_bytes=56 << 20),
        cost_estimate=pl.CostEstimate(flops=2 * rows * width * 7 * width, bytes_accessed=12 << 20, transcendentals=0),
        name="grad_rest",
    )(me, gated, dmid, lifted, dboth, hidden, dlow)


def grad_mix_kernel(me_ref, normed_ref, dmixin_ref, extra_ref, keep_ref, send_ref, grad_ref, sem):
    chip, core = me_ref[1], me_ref[2]
    step = HALVES["out"]
    normed = normed_ref[...]
    size = dmixin_ref.shape[1]
    for k in range(size // step):
        cols = slice(k * step, (k + 1) * step)
        grad_ref[:, cols] = row_product(normed, dmixin_ref[:, cols]).astype(BF16)
    grad_ref[:, size:] = jnp.transpose(extra_ref[...]).astype(BF16)
    pairs = []
    for half, target in ((core, keep_ref), (1 - core, send_ref)):
        for b in range(keep_ref.shape[0]):
            row, left = (chip ^ b) * UNIT, half * HALVES["mix"]
            pairs.append(
                (
                    grad_ref.at[
                        pl.ds(pl.multiple_of(row, UNIT), UNIT), pl.ds(pl.multiple_of(left, GROUP), HALVES["mix"])
                    ],
                    target.at[b],
                )
            )
    load_start(pairs, sem)
    load_wait(pairs, sem)


def grad_mix(me, chips, normed, dmixin, extra):
    rows, width = normed.shape
    shape = sds((chips, UNIT, HALVES["mix"]), BF16)
    return pl.pallas_call(
        grad_mix_kernel,
        out_shape=(shape, shape),
        in_specs=[SMEM] + [VMEM] * 3,
        out_specs=(ANY, ANY),
        scratch_shapes=[pltpu.VMEM((width, 2 * HALVES["mix"]), BF16), pltpu.SemaphoreType.DMA],
        compiler_params=pltpu.CompilerParams(vmem_limit_bytes=56 << 20),
        cost_estimate=pl.CostEstimate(flops=5 * rows * width * width, bytes_accessed=4 << 20, transcendentals=0),
        name="grad_mix",
    )(me, normed, dmixin, extra)


def table_kernel(plan, count, me_ref, *refs):
    sources, (table_ref, held_ref, sem) = refs[:count], refs[count:]
    chip, core = me_ref[1], me_ref[2]
    pairs = []
    for source, others, other_core, column in plan["small"]:
        left = pl.multiple_of((core ^ other_core) * GROUP, GROUP)
        for b, other in enumerate(others):
            row = pl.multiple_of((chip ^ other) * UNIT, UNIT)
            pairs.append(
                (sources[source].at[b, :, pl.ds(column, GROUP)], held_ref.at[pl.ds(row, UNIT), pl.ds(left, GROUP)])
            )
    load_start(pairs, sem)
    load_wait(pairs, sem)
    table_ref[...] = jnp.transpose(held_ref[:, GROUP:].astype(F32))[: table_ref.shape[0]]


def table_of(plan, me, weights, rows, width):
    return pl.pallas_call(
        functools.partial(table_kernel, plan, len(weights)),
        out_shape=sds((rows, width)),
        in_specs=[SMEM] + [ANY] * len(weights),
        out_specs=VMEM,
        scratch_shapes=[pltpu.VMEM((width, 2 * GROUP), BF16), pltpu.SemaphoreType.DMA],
        compiler_params=pltpu.CompilerParams(vmem_limit_bytes=16 << 20),
        cost_estimate=pl.CostEstimate(flops=1 << 20, bytes_accessed=1 << 20, transcendentals=0),
        name="table",
    )(me, *weights)


def swap_seq(x, bit):
    return lax.ppermute(x, "seq", [(i, i ^ bit) for i in range(lax.axis_size("seq"))])


def swap_dp(x, bit):
    return lax.ppermute(x, "dp", [(i, i ^ bit) for i in range(lax.axis_size("dp"))])


def spread(unit, cut):
    n_dp = lax.axis_size("dp")
    far = jnp.stack([unit] + [swap_dp(unit, k) for k in range(1, n_dp)])
    deep = tuple(4 * k for k in range(n_dp))
    arrays = []
    for cols, one, two in ((slice(0, cut), 1, 2), (slice(cut, None), 2, 1)):
        own = far[:, :, cols]
        near = jnp.concatenate([own, swap_seq(own, 2 * one)], axis=0)
        near_at = deep + tuple(k ^ one for k in deep)
        last = swap_seq(near, 2 * two)
        last_at = tuple(k ^ two for k in near_at)
        for array, at in ((near, near_at), (last, last_at)):
            arrays.append((array, at, 0, cols.start))
            arrays.append((swap_seq(array, 1), at, 1, cols.start))
    return arrays


def gather_up(keep, send, cut):
    n_dp = lax.axis_size("dp")
    both = (keep.astype(F32) + swap_seq(send, 1).astype(F32)).astype(BF16)
    both = both.reshape(n_dp, 2, 2, *both.shape[1:])
    pieces = []
    for cols, first in ((slice(0, cut), 2), (slice(cut, None), 1)):
        part = both[..., cols]
        if first == 1:
            part = jnp.swapaxes(part, 1, 2)
        got = swap_seq(part[:, 1], 2 * first)
        part = (part[:, 0].astype(F32) + got.astype(F32)).astype(BF16)
        got = swap_seq(part[:, 1], 2 * (3 - first))
        pieces.append((part[:, 0].astype(F32) + got.astype(F32)).astype(BF16))
    total = jnp.concatenate(pieces, axis=2)
    result = total[0].astype(F32)
    for k in range(1, n_dp):
        result = result + swap_dp(total[k], k).astype(F32)
    return result


def layer_params(gains, chan):
    half = chan.shape[0] // 2
    angle = chan[half:]
    rows = [
        gains[0],
        gains[1],
        gains[2],
        jnp.concatenate([chan[:half], jnp.cos(angle)]),
        jnp.concatenate([jnp.sin(angle), jnp.zeros((half,), F32)]),
    ]
    return jnp.concatenate([jnp.stack(rows), jnp.zeros((3, 2 * half), F32)], axis=0)


def body(stream, w_mix, w_out, w_up, w_down, gains, chan_params, lengths, cotangent):
    rows, width = stream.shape
    depth = w_mix.shape[0]
    share = w_mix.shape[1]
    where = lax.axis_index("seq")
    me = jnp.stack([where, (lax.axis_index("dp") * lax.axis_size("seq") + where) // 2, where % 2]).astype(jnp.int32)
    n_dp, n_seq = lax.axis_size("dp"), lax.axis_size("seq")
    shards = n_dp * n_seq
    base = where * rows
    ends = [lengths[0, 0]]
    for j in range(1, lengths.shape[1]):
        ends.append(ends[-1] + lengths[0, j])
    fresh = jnp.stack([end - lengths[0, j] for j, end in enumerate(ends)])
    place = (fresh - base).astype(jnp.int32)
    keep = ((base + lax.broadcasted_iota(jnp.int32, (rows, 1), 0)) < ends[-1]).astype(F32)

    small = jnp.concatenate(
        [gains.reshape(depth * 3, share).T, chan_params.T, jnp.zeros((share, 128 - 4 * depth), BF16)], axis=1
    )
    mix_cols, out_cols, up_cols = w_mix.shape[2], w_out.shape[2], w_up.shape[2]
    starts = [0, mix_cols, mix_cols + out_cols, mix_cols + out_cols + up_cols]
    full = starts[-1] + 2 * width
    weights = []
    fast = n_seq == 8 and n_dp & (n_dp - 1) == 0 and 2 * share == UNIT
    chips = shards // 2
    core = where % 2
    if fast:
        padding = jnp.zeros((share, 2 * HALVES["mix"] - mix_cols - 128), BF16)
        halves = ([], [])
        for l in range(depth):
            tail = small if l == 0 else jnp.zeros_like(small)
            mix = jnp.concatenate([w_mix[l], padding, tail], axis=1)
            for h in range(2):
                for w, size in ((mix, HALVES["mix"]), (w_out[l], HALVES["out"]), (w_up[l], HALVES["up"])):
                    halves[h].append(w[:, h * size : (h + 1) * size])
        halves = [jnp.concatenate(half, axis=1) for half in halves]
        mine = jnp.where(core == 0, halves[0], halves[1])
        other = swap_seq(jnp.where(core == 0, halves[1], halves[0]), 1)
        units = jnp.where(core == 0, jnp.concatenate([mine, other]), jnp.concatenate([other, mine]))
        size = sum(HALVES.values())
        plans = []
        for l in range(depth):
            unit = units[:, l * size : (l + 1) * size]
            mix_unit = unit[:, : HALVES["mix"]]
            rest_unit = jnp.concatenate([unit[:, HALVES["mix"] :], w_down[l]], axis=1)
            mix_arrays = spread(mix_unit, HALVES["mix"] // 2)
            rest_arrays = spread(rest_unit, HALVES["out"] + 2 * GROUP * 6)
            weights.append((tuple(a[0] for a in mix_arrays), tuple(a[0] for a in rest_arrays)))
            plan = {"mix": [], "out": [], "up": [], "down": [], "small": []}
            for source, (array, at, other_core, begin) in enumerate(mix_arrays):
                plan["mix"].append((source, at, other_core, 0, array.shape[2], begin))
                if begin:
                    plan["small"].append((source, at, other_core, array.shape[2] - 128))
            spans = {"out": (0, HALVES["out"]), "up": (HALVES["out"], HALVES["up"]), "down": (HALVES["out"] + HALVES["up"], width)}
            for source, (array, at, other_core, begin) in enumerate(rest_arrays):
                for name, (low, count) in spans.items():
                    a, b = max(low, begin), min(low + count, begin + array.shape[2])
                    if a < b:
                        plan[name].append((source, at, other_core, a - begin, b - a, a - low))
            plans.append(plan)
        table = table_of(plans[0], me, weights[0][0], 4 * depth, width)
    else:
        plans = [None] * depth
        table = lax.all_gather(small, ALL, axis=0, tiled=True)[:, : 4 * depth].T.astype(F32)
        for l in range(depth):
            got = tuple(lax.all_gather(w[l], ALL, axis=0, tiled=True) for w in (w_mix, w_out, w_up, w_down))
            weights.append((got, got))
    params = [layer_params(table[3 * l : 3 * l + 3], table[3 * depth + l]) for l in range(depth)]

    values = stream.astype(F32)
    saved = []
    for l in range(depth):
        normed, cpre, gate, rate, kept, feed, sub, total = front(plans[l], me, place, values, params[l], weights[l][0])
        every = lax.all_gather(total, "seq")
        states, first, gn, rg, gated, after, lifted, both, hidden, result = rest(
            plans[l], me, values, params[l], gate, kept, feed, sub, every, weights[l][1]
        )
        saved.append((values, normed, cpre, gate, rate, kept, sub, every, states, first, gn, rg, gated, after, lifted, both, hidden))
        values = result
    mixed = values.astype(BF16)
    dx = cotangent.astype(F32) * keep
    sums = [None] * depth
    smalls = [None] * depth
    for l in reversed(range(depth)):
        x, normed, cpre, gate, rate, kept, sub, every, states, first, gn, rg, gated, after, lifted, both, hidden = saved[l]
        dlow, dboth, dafter, dmid, dgpre, dstates, gains_a, rsub, rtotal = back_one(
            plans[l], me, dx, params[l], (both, after, gn, rg, gate, states, kept, sub), weights[l][1]
        )
        revery = lax.all_gather(rtotal, "seq")
        dmixin, dx, gains_b = back_two(
            plans[l], me, x, params[l], dafter, dgpre, dstates, states, kept, rate, cpre, first, sub, rsub, every, revery, weights[l][0]
        )
        smalls[l] = [gains_b[0], gains_a[1], gains_a[0], gains_b[1]]
        if fast:
            rest_sum = gather_up(
                *grad_rest(me, chips, gated, dmid, lifted, dboth, hidden, dlow), HALVES["out"] + 2 * GROUP * 6
            )
            extra = jnp.zeros((128, width), F32)
            if l == 0:
                extra = jnp.concatenate([jnp.stack(smalls[k]) for k in range(depth)] + [extra[: 128 - 4 * depth]])
            mix_sum = gather_up(*grad_mix(me, chips, normed, dmixin, extra), HALVES["mix"] // 2)
            sums[l] = (mix_sum, rest_sum)
        else:
            grads = [row_product(normed, dmixin), row_product(gated, dmid), row_product(lifted, dboth), row_product(hidden, dlow)]
            grads.append(jnp.stack(smalls[l], axis=1))
            sums[l] = [
                lax.psum_scatter(g.astype(BF16), ALL, scatter_dimension=0, tiled=True).astype(F32) for g in grads
            ]
    if fast:
        pieces = {"mix": [], "out": [], "up": [], "down": []}
        for l in range(depth):
            mix_sum, rest_sum = sums[l]
            joint = HALVES["out"] + HALVES["up"]
            line = jnp.concatenate([mix_sum, rest_sum[:, :joint]], axis=1)
            line = line.reshape(2, share, -1)
            mine = jnp.where(core == 0, line[0], line[1])
            other = swap_seq(jnp.where(core == 0, line[1], line[0]), 1)
            first = jnp.where(core == 0, mine, other)
            second = jnp.where(core == 0, other, mine)
            at = 0
            for name in ("mix", "out", "up"):
                cols = slice(at, at + HALVES[name])
                pieces[name].append(jnp.concatenate([first[:, cols], second[:, cols]], axis=1))
                at += HALVES[name]
            pieces["down"].append(rest_sum[:, joint:])
        g_mix, g_out, g_up, g_down = (jnp.stack(pieces[name]) for name in ("mix", "out", "up", "down"))
        tail = g_mix[0][:, 2 * HALVES["mix"] - 128 :][:, : 4 * depth].reshape(share, depth, 4)
        tail = jnp.swapaxes(tail, 0, 1)
        g_mix = g_mix[:, :, :mix_cols]
    else:
        g_mix, g_out, g_up, g_down, tail = (jnp.stack([sums[l][k] for l in range(depth)]) for k in range(5))
    return (mixed, dx, g_mix, g_out, g_up, g_down, jnp.swapaxes(tail[:, :, :3], 1, 2), tail[:, :, 3])


def solution(mesh):
    placed = (
        P(ALL, None),
        P(None, ALL, None),
        P(None, ALL, None),
        P(None, ALL, None),
        P(None, ALL, None),
        P(None, None, ALL),
        P(None, ALL),
        P("dp", None),
        P(ALL, None),
    )
    return jax.shard_map(
        body,
        mesh=mesh,
        in_specs=placed,
        out_specs=(
            P(ALL, None),
            P(ALL, None),
            P(None, ALL, None),
            P(None, ALL, None),
            P(None, ALL, None),
            P(None, ALL, None),
            P(None, None, ALL),
            P(None, ALL),
        ),
        check_vma=False,
    )
```

time: 2200 us -> 556 us (0.25); the launches traced: 2160 us -> 548 us
  local copies, waits for them, and re-layouts: 1010 us -> 49.8 us
  other arithmetic: 438 us -> 36.8 us
  blocking collectives: 257 us -> 40.3 us
  waiting for transfers between devices: 361 us -> 220 us
  Pallas kernels: 0 us -> 107 us
  starting transfers between devices: 0.48 us -> 90 us
  matrix products: 80.9 us -> 0 us
    slice x454 -> x41, local copies, waits for them, and re-layouts: 473 us -> 19.2 us  [the longest x12 8.45 us: body(): second[:, cols]]
    reduce_scatter x4 -> x0, waiting for transfers between devices: 359 us -> none  [the longest x2 359 us: layer_backward(): lax.psum_scatter(jnp.concatenate([row_product(normed, grad_mixin), row_pr...]
    pad x224 -> x0, local copies, waits for them, and re-layouts: 318 us -> none  [the longest x112 182 us: layer_backward(): lax.associative_scan(compose, (next_re[::-1], next_im[::-1], grad_states[...]
    ppermute x0 -> x79, waiting for transfers between devices: none -> 220 us  [the longest x55 169 us: swap_seq(): lax.ppermute(x, 'seq', [(i, i ^ bit) for i in range(lax.axis_size('seq'))])]
    add x204 -> x4, other arithmetic: 213 us -> 2.34 us  [gather_up(): result = result + swap_dp(total[k], k).astype(F32)]
    all_gather x18 -> x4, blocking collectives: 215 us -> 40.3 us  [the longest x2 20.6 us: body(): every = lax.all_gather(total, 'seq')]
    pallas_call x0 -> x13, Pallas kernels: none -> 107 us  [the longest x2 29.6 us: back_one(): pl.pallas_call(functools.partial(back_one_kernel, plan, len(weights)), ou...]
    concatenate x107 -> x13, other arithmetic: 106 us -> 6.77 us  [the longest x8 4.48 us: spread(): near = jnp.concatenate([own, swap_seq(own, 2 * one)], axis=0)]
  transfers between devices with their start and end apart: 12 -> 79, of which waited for: 2 -> 32; matrix products, arithmetic and copies ran while one was open for 55% -> 10% of each run, Pallas kernels for 0% -> 12%
where the time goes in v1:
time: 556 us; the launch traced here: 548 us
  waiting for transfers between devices  220 us (40%)
  Pallas kernels  107 us (19%)
  starting transfers between devices  90 us (16%)
  local copies, waits for them, and re-layouts  49.8 us (9%)
  blocking collectives  40.3 us (7%)
  other arithmetic  36.8 us (7%)
    ppermute x55, waiting for transfers between devices, swap_seq(): lax.ppermute(x, 'seq', [(i, i ^ bit) for i in range(lax.axis_size('seq'))])  169 us
    ppermute x24, waiting for transfers between devices, swap_dp(): lax.ppermute(x, 'dp', [(i, i ^ bit) for i in range(lax.axis_size('dp'))])  50.4 us
    ppermute x24, starting transfers between devices, swap_dp(): lax.ppermute(x, 'dp', [(i, i ^ bit) for i in range(lax.axis_size('dp'))])  50.3 us
    ppermute x55, starting transfers between devices, swap_seq(): lax.ppermute(x, 'seq', [(i, i ^ bit) for i in range(lax.axis_size('seq'))])  39.7 us
    pallas_call x2, Pallas kernels, back_one(): pl.pallas_call(functools.partial(back_one_kernel, plan, len(weights)), ou...  29.6 us
    pallas_call x2, Pallas kernels, rest(): pl.pallas_call(functools.partial(rest_kernel, plan, len(weights)), out_sh...  22.8 us
    all_gather x2, blocking collectives, body(): every = lax.all_gather(total, 'seq')  20.6 us
    all_gather x2, blocking collectives, body(): revery = lax.all_gather(rtotal, 'seq')  19.7 us
  transfers between devices with their start and end apart: 79, of which 32 were waited for; matrix products, arithmetic and copies ran while one was open for 10% of the time, Pallas kernels for 12%

profile of v1, /device:TPU:0, one launch (start us, length us, event | category | flops | bytes accessed | tf_op | source)
XLA Modules:
  0.0 547.7 jit_solution(2874009321100739015)
XLA Ops:
  7.1 5.0 collective-permute-start.3
  12.8 3.8 collective-permute-start.14
  16.7 3.0 collective-permute-start.25
  19.7 16.1 %collective-permute-done.2 = bf16[48,1024]{1,0:T(8,128)(2,1)S(1)} collective-permute-done((bf16[48,1024]{1,0:T(8,128)(2,1)S(1)}, bf16[48,1024]{1,0:T(8,128)(2,1)S(1)}, u32[]{:S(2)}, u32[]{:S(2)}) %collective-permute-start.2) | collective-permute-done | bytes 98336 | tf_op jit(solution)/shard_map/ppermute | solution.py:698
  37.8 12.7 %collective-permute-start.12 = (bf16[48,2688]{1,0:T(8,128)(2,1)S(1)}, bf16[48,2688]{1,0:T(8,128)(2,1)S(1)}, u32[]{:S(2)}, u32[]{:S(2)}) collective-permute-start(bf16[48,2688]{1,0:T(8,128)(2,1)S(1)} %get-tuple-element.203), channel_id=1, source_target_pairs={{0,8},{8,0},{16,24},{24,16},{1,9},{9,1},{17,25},{25,17},{2,10},{10... | collective-permute-start | bytes 774152 | tf_op jit(solution)/shard_map/ppermute | solution.py:698
  57.4 5.0 collective-permute-done.12
  67.3 7.1 %collective-permute-done.35 = bf16[48,2688]{1,0:T(8,128)(2,1)S(1)} collective-permute-done((bf16[48,2688]{1,0:T(8,128)(2,1)S(1)}, bf16[48,2688]{1,0:T(8,128)(2,1)S(1)}, u32[]{:S(2)}, u32[]{:S(2)}) %collective-permute-start.35) | collective-permute-done | bytes 258080 | tf_op jit(solution)/shard_map/ppermute | solution.py:698
  78.9 4.8 collective-permute-done.26
  87.2 2.8 collective-permute-done.19
  90.0 6.3 %collective-permute-done.41 = bf16[4,48,768]{2,1,0:T(8,128)(2,1)S(1)} collective-permute-done((bf16[4,48,768]{2,1,0:T(8,128)(2,1)S(1)}, bf16[4,48,768]{2,1,0:T(8,128)(2,1)S(1)}, u32[]{:S(2)}, u32[]{:S(2)}) %collective-permute-start.41) | collective-permute-done | bytes 294944 | tf_op jit(solution)/shard_map/ppermute | solution.py:694
  98.5 6.2 %collective-permute-done.6.refs_2_ = bf16[8,48,512]{2,1,0:T(8,128)(2,1)S(1)} collective-permute-done((bf16[8,48,512]{2,1,0:T(8,128)(2,1)S(1)}, bf16[8,48,512]{2,1,0:T(8,128)(2,1)S(1)}, u32[]{:S(2)}, u32[]{:S(2)}) %collective-permute-start.6) | collective-permute-done | bytes 393248 | tf_op jit(solution)/shard_map/ppermute | solution.py:694
  108.9 35.9 %collective-permute-done.28.refs_2_ = bf16[8,48,512]{2,1,0:T(8,128)(2,1)S(1)} collective-permute-done((bf16[8,48,512]{2,1,0:T(8,128)(2,1)S(1)}, bf16[8,48,512]{2,1,0:T(8,128)(2,1)S(1)}, u32[]{:S(2)}, u32[]{:S(2)}) %collective-permute-start.28) | collective-permute-done | bytes 393248 | tf_op jit(solution)/shard_map/ppermute | solution.py:694
  153.6 10.4 %collective-permute-done.21.refs_6_ = bf16[8,48,768]{2,1,0:T(8,128)(2,1)} collective-permute-done((bf16[8,48,768]{2,1,0:T(8,128)(2,1)}, bf16[8,48,768]{2,1,0:T(8,128)(2,1)}, u32[]{:S(2)}, u32[]{:S(2)}) %collective-permute-start.21) | collective-permute-done | bytes 589856 | tf_op jit(solution)/shard_map/ppermute | solution.py:694
  164.0 9.4 %collective-permute-done.39.refs_2_ = bf16[8,48,1920]{2,1,0:T(8,128)(2,1)} collective-permute-done((bf16[8,48,1920]{2,1,0:T(8,128)(2,1)}, bf16[8,48,1920]{2,1,0:T(8,128)(2,1)}, u32[]{:S(2)}, u32[]{:S(2)}) %collective-permute-start.39) | collective-permute-done | bytes 1474592 | tf_op jit(solution)/shard_map/ppermute | solution.py:694
  182.1 6.3 %front.2 = (bf16[256,768]{1,0:T(8,128)(2,1)}, f32[256,768]{1,0:T(8,128)}, f32[256,768]{1,0:T(8,128)}, f32[256,384]{1,0:T(8,128)}, f32[3,256,128]{2,1,0:T(8,128)}...) custom-call(s32[3]{0:T(128)} %copy-done.8, s32[3]{0:T(128)} %add_subtract_fusion.place_ref, ...), custom_call_target="tpu_custom_call" | custom-call | flops 754974720 | bytes 8388608 | tf_op jit(solution)/shard_map/front/pallas_call | solution.py:176
  188.5 10.3 %all-gather.4.every_ref = f32[8,4,384]{2,1,0:T(4,128)} all-gather(f32[1,4,384]{2,1,0:T(4,128)} %bitcast.297), channel_id=2, replica_groups=mesh['dp'=4,'seq'=8] {'seq'}, dimensions={0}, use_global_device_ids=true | all-gather | bytes 55296 | tf_op jit(solution)/shard_map/all_gather | solution.py:824
  198.8 11.4 %rest.2 = (f32[6,256,128]{2,1,0:T(8,128)}, f32[2,8,384]{2,1,0:T(8,128)}, f32[256,768]{1,0:T(8,128)}, f32[256,128]{1,0:T(8,128)}, bf16[256,768]{1,0:T(8,128)(2,1)...) custom-call(s32[3]{0:T(128)} %copy-done.8, ...), custom_call_target="tpu_custom_call" | custom-call | flops 2113929216 | bytes 20971520 | tf_op jit(solution)/shard_map/rest/pallas_call | solution.py:286
  211.0 6.4 %front.3 = (bf16[256,768]{1,0:T(8,128)(2,1)}, f32[256,768]{1,0:T(8,128)}, f32[256,768]{1,0:T(8,128)}, f32[256,384]{1,0:T(8,128)}, f32[3,256,128]{2,1,0:T(8,128)}...) custom-call(s32[3]{0:T(128)} %copy-done.8, s32[3]{0:T(128)} %add_subtract_fusion.place_ref, ...), custom_call_target="tpu_custom_call" | custom-call | flops 754974720 | bytes 8388608 | tf_op jit(solution)/shard_map/front/pallas_call | solution.py:176
  217.4 10.3 %all-gather.5.every_ref = f32[8,4,384]{2,1,0:T(4,128)} all-gather(f32[1,4,384]{2,1,0:T(4,128)} %bitcast.296), channel_id=3, replica_groups=mesh['dp'=4,'seq'=8] {'seq'}, dimensions={0}, use_global_device_ids=true | all-gather | bytes 55296 | tf_op jit(solution)/shard_map/all_gather | solution.py:824
  228.7 11.4 %rest.3 = (f32[6,256,128]{2,1,0:T(8,128)}, f32[2,8,384]{2,1,0:T(8,128)}, f32[256,768]{1,0:T(8,128)}, f32[256,128]{1,0:T(8,128)}, bf16[256,768]{1,0:T(8,128)(2,1)...) custom-call(s32[3]{0:T(128)} %copy-done.8, ...), custom_call_target="tpu_custom_call" | custom-call | flops 2113929216 | bytes 20971520 | tf_op jit(solution)/shard_map/rest/pallas_call | solution.py:286
  240.2 14.8 %back_one.2 = (bf16[256,768]{1,0:T(8,128)(2,1)}, bf16[256,3072]{1,0:T(8,128)(2,1)}, f32[256,768]{1,0:T(8,128)}, bf16[256,768]{1,0:T(8,128)(2,1)}, bf16[256,768]{...) custom-call(s32[3]{0:T(128)} %copy-done.8, ...), custom_call_target="tpu_custom_call" | custom-call | flops 2113929216 | bytes 20971520 | tf_op jit(solution)/shard_map/back_one/pallas_call | solution.py:411
  255.0 9.9 %all-gather.6.revery_ref = f32[8,2,384]{2,1,0:T(2,128)} all-gather(f32[1,2,384]{2,1,0:T(2,128)} %bitcast.298), channel_id=4, replica_groups=mesh['dp'=4,'seq'=8] {'seq'}, dimensions={0}, use_global_device_ids=true | all-gather | bytes 27648 | tf_op jit(solution)/shard_map/all_gather | solution.py:839
  264.9 8.6 %back_two.2 = (bf16[256,1920]{1,0:T(8,128)(2,1)}, f32[256,768]{1,0:T(8,128)}, f32[2,768]{1,0:T(2,128)}) custom-call(s32[3]{0:T(128)} %copy-done.8, f32[256,768]{1,0:T(8,128)} %get-tuple-element.81.x_ref, f32[8,768]{1,0:T(8,128)} %get-tuple-element.233.p_ref, f32[256,768]{1,0:T(8,128)} %get-tuple-element.93.dafter_ref, ...), custom_call_target="tpu_custom_call" | custom-call | flops 754974720 | bytes 10485760 | tf_op jit(solution)/shard_map/back_two/pallas_call | solution.py:533
  274.2 4.4 grad_mix.3
  279.0 14.8 %back_one.3 = (bf16[256,768]{1,0:T(8,128)(2,1)}, bf16[256,3072]{1,0:T(8,128)(2,1)}, f32[256,768]{1,0:T(8,128)}, bf16[256,768]{1,0:T(8,128)(2,1)}, bf16[256,768]{...) custom-call(s32[3]{0:T(128)} %copy-done.8, ...), custom_call_target="tpu_custom_call" | custom-call | flops 2113929216 | bytes 20971520 | tf_op jit(solution)/shard_map/back_one/pallas_call | solution.py:411
  293.8 9.8 %all-gather.7.revery_ref = f32[8,2,384]{2,1,0:T(2,128)} all-gather(f32[1,2,384]{2,1,0:T(2,128)} %bitcast.299), channel_id=5, replica_groups=mesh['dp'=4,'seq'=8] {'seq'}, dimensions={0}, use_global_device_ids=true | all-gather | bytes 27648 | tf_op jit(solution)/shard_map/all_gather | solution.py:839
  303.6 8.6 %back_two.3 = (bf16[256,1920]{1,0:T(8,128)(2,1)}, f32[256,768]{1,0:T(8,128)}, f32[2,768]{1,0:T(2,128)}) custom-call(s32[3]{0:T(128)} %copy-done.8, f32[256,768]{1,0:T(8,128)} %convert_element_type.305.x_ref, f32[8,768]{1,0:T(8,128)} %get-tuple-element.234.p_ref, f32[256,768]{1,0:T(8,128)} %get-tuple-element.107.dafter_ref, ...), custom_call_target="tpu_custom_call" | custom-call | flops 754974720 | bytes 10485760 | tf_op jit(solution)/shard_map/back_two/pallas_call | solution.py:533
  314.7 4.4 grad_mix.2
  320.4 7.3 %grad_rest.3 = (bf16[16,48,2688]{2,1,0:T(8,128)(2,1)}, bf16[16,48,2688]{2,1,0:T(8,128)(2,1)}) custom-call(s32[3]{0:T(128)} %copy-done.8, bf16[256,768]{1,0:T(8,128)(2,1)} %get-tuple-element.136.gated_ref, bf16[256,768]{1,0:T(8,128)(2,1)} %get-tuple-element.137.dmid_ref, bf16[256,768]{1,0:T(8,128)(2,1)} %get-tuple-element.138.lifted_ref, ...), custom_call_target="tpu_custom_call" | custom-call | flops 2113929216 | bytes 12582912 | tf_op jit(solution)/shard_map/grad_rest/pallas_call | solution.py:607
  327.9 7.3 %grad_rest.2 = (bf16[16,48,2688]{2,1,0:T(8,128)(2,1)}, bf16[16,48,2688]{2,1,0:T(8,128)(2,1)}) custom-call(s32[3]{0:T(128)} %copy-done.8, bf16[256,768]{1,0:T(8,128)(2,1)} %get-tuple-element.124.gated_ref, bf16[256,768]{1,0:T(8,128)(2,1)} %get-tuple-element.125.dmid_ref, bf16[256,768]{1,0:T(8,128)(2,1)} %get-tuple-element.126.lifted_ref, ...), custom_call_target="tpu_custom_call" | custom-call | flops 2113929216 | bytes 12582912 | tf_op jit(solution)/shard_map/grad_rest/pallas_call | solution.py:607
  343.8 6.5 %collective-permute-done.63 = bf16[4,2,48,512]{3,2,1,0:T(8,128)(2,1)S(1)} collective-permute-done((bf16[4,2,48,512]{3,2,1,0:T(8,128)(2,1)S(1)}, bf16[4,2,48,512]{3,2,1,0:T(8,128)(2,1)S(1)}, u32[]{:S(2)}, u32[]{:S(2)}) %collective-permute-start.63) | collective-permute-done | bytes 393248 | tf_op jit(solution)/shard_map/ppermute | solution.py:694
  352.7 5.3 collective-permute-done.46
  359.4 3.0 collective-permute-done.48
  363.4 2.8 collective-permute-done.64
  369.3 2.6 collective-permute-done.49
  372.4 2.8 collective-permute-done.69
  381.7 3.1 collective-permute-done.51
  392.3 11.3 %collective-permute-done.73 = bf16[4,2,48,768]{3,2,1,0:T(8,128)(2,1)S(1)} collective-permute-done((bf16[4,2,48,768]{3,2,1,0:T(8,128)(2,1)S(1)}, bf16[4,2,48,768]{3,2,1,0:T(8,128)(2,1)S(1)}, u32[]{:S(2)}, u32[]{:S(2)}) %collective-permute-start.73) | collective-permute-done | bytes 589856 | tf_op jit(solution)/shard_map/ppermute | solution.py:694
  404.7 5.2 collective-permute-done.56
  412.4 20.3 %collective-permute-done.74 = bf16[4,48,768]{2,1,0:T(8,128)(2,1)S(1)} collective-permute-done((bf16[4,48,768]{2,1,0:T(8,128)(2,1)S(1)}, bf16[4,48,768]{2,1,0:T(8,128)(2,1)S(1)}, u32[]{:S(2)}, u32[]{:S(2)}) %collective-permute-start.74) | collective-permute-done | bytes 294944 | tf_op jit(solution)/shard_map/ppermute | solution.py:694
  432.8 6.2 %collective-permute-done.57 = bf16[4,48,768]{2,1,0:T(8,128)(2,1)S(1)} collective-permute-done((bf16[4,48,768]{2,1,0:T(8,128)(2,1)S(1)}, bf16[4,48,768]{2,1,0:T(8,128)(2,1)S(1)}, u32[]{:S(2)}, u32[]{:S(2)}) %collective-permute-start.57) | collective-permute-done | bytes 294944 | tf_op jit(solution)/shard_map/ppermute | solution.py:694
  440.8 22.7 %collective-permute-done.54 = bf16[4,2,48,1920]{3,2,1,0:T(8,128)(2,1)S(1)} collective-permute-done((bf16[4,2,48,1920]{3,2,1,0:T(8,128)(2,1)S(1)}, bf16[4,2,48,1920]{3,2,1,0:T(8,128)(2,1)S(1)}, u32[]{:S(2)}, u32[]{:S(2)}) %collective-permute-start.54) | collective-permute-done | bytes 1474592 | tf_op jit(solution)/shard_map/ppermute | solution.py:694
  466.9 2.6 collective-permute-start.75
  469.5 5.9 %collective-permute-done.55 = bf16[4,48,1920]{2,1,0:T(8,128)(2,1)S(1)} collective-permute-done((bf16[4,48,1920]{2,1,0:T(8,128)(2,1)S(1)}, bf16[4,48,1920]{2,1,0:T(8,128)(2,1)S(1)}, u32[]{:S(2)}, u32[]{:S(2)}) %collective-permute-start.55) | collective-permute-done | bytes 737312 | tf_op jit(solution)/shard_map/ppermute | solution.py:694
  478.3 6.5 %collective-permute-start.58 = (bf16[48,2688]{1,0:T(8,128)(2,1)}, bf16[48,2688]{1,0:T(8,128)(2,1)}, u32[]{:S(2)}, u32[]{:S(2)}) collective-permute-start(bf16[48,2688]{1,0:T(8,128)(2,1)} %get-tuple-element.170), channel_id=1, source_target_pairs={{0,8},{8,0},{16,24},{24,16},{1,9},{9,1},{17,25},{25,17},{2,10},{10... | collective-permute-start | bytes 774152 | tf_op jit(solution)/shard_map/ppermute | solution.py:698
  484.8 10.5 %collective-permute-done.76 = bf16[48,2688]{1,0:T(8,128)(2,1)S(1)} collective-permute-done((bf16[48,2688]{1,0:T(8,128)(2,1)S(1)}, bf16[48,2688]{1,0:T(8,128)(2,1)S(1)}, u32[]{:S(2)}, u32[]{:S(2)}) %collective-permute-start.76) | collective-permute-done | bytes 258080 | tf_op jit(solution)/shard_map/ppermute | solution.py:698
  510.8 2.7 broadcast_select_fusion.6
  524.0 2.8 copy.65
  (388 shorter events, 145.7 us)
Async XLA Ops:
  12.1 23.6 %collective-permute-start.2 = (bf16[48,1024]{1,0:T(8,128)(2,1)S(1)}, bf16[48,1024]{1,0:T(8,128)(2,1)S(1)}, u32[]{:S(2)}, u32[]{:S(2)}) collective-permute-start(bf16[48,1024]{1,0:T(8,128)(2,1)S(1)} %get-tuple-element.185), channel_id=1, source_target_pairs={{0,16},{8,24},{16,0},{24,8},{1,17},{9,25},{17,1},{25,9},{2,18},{10... | collective-permute-start | bytes 294920 | tf_op jit(solution)/shard_map/ppermute | solution.py:698
  12.1 23.6 %collective-permute-start.1 = (bf16[48,1024]{1,0:T(8,128)(2,1)S(1)}, bf16[48,1024]{1,0:T(8,128)(2,1)S(1)}, u32[]{:S(2)}, u32[]{:S(2)}) collective-permute-start(bf16[48,1024]{1,0:T(8,128)(2,1)S(1)} %get-tuple-element.185), channel_id=1, source_target_pairs={{0,8},{8,0},{16,24},{24,16},{1,9},{9,1},{17,25},{25,17},{2,10},{10... | collective-permute-start | bytes 294920 | tf_op jit(solution)/shard_map/ppermute | solution.py:698
  12.8 41.1 %collective-permute-start.14 = (bf16[48,2688]{1,0:T(8,128)(2,1)S(1)}, bf16[48,2688]{1,0:T(8,128)(2,1)S(1)}, u32[]{:S(2)}, u32[]{:S(2)}) collective-permute-start(bf16[48,2688]{1,0:T(8,128)(2,1)S(1)} %get-tuple-element.203), channel_id=1, source_target_pairs={{0,24},{8,16},{16,8},{24,0},{1,25},{9,17},{17,9},{25,1},{2,26},{10... | collective-permute-start | bytes 774152 | tf_op jit(solution)/shard_map/ppermute | solution.py:698
  16.7 39.3 %collective-permute-start.13 = (bf16[48,2688]{1,0:T(8,128)(2,1)S(1)}, bf16[48,2688]{1,0:T(8,128)(2,1)S(1)}, u32[]{:S(2)}, u32[]{:S(2)}) collective-permute-start(bf16[48,2688]{1,0:T(8,128)(2,1)S(1)} %get-tuple-element.203), channel_id=1, source_target_pairs={{0,16},{8,24},{16,0},{24,8},{1,17},{9,25},{17,1},{25,9},{2,18},{10... | collective-permute-start | bytes 774152 | tf_op jit(solution)/shard_map/ppermute | solution.py:698
  16.7 21.1 %collective-permute-start.25 = (bf16[48,1024]{1,0:T(8,128)(2,1)S(1)}, bf16[48,1024]{1,0:T(8,128)(2,1)S(1)}, u32[]{:S(2)}, u32[]{:S(2)}) collective-permute-start(bf16[48,1024]{1,0:T(8,128)(2,1)S(1)} %get-tuple-element.184), channel_id=1, source_target_pairs={{0,24},{8,16},{16,8},{24,0},{1,25},{9,17},{17,9},{25,1},{2,26},{10... | collective-permute-start | bytes 294920 | tf_op jit(solution)/shard_map/ppermute | solution.py:698
  35.7 15.6 %collective-permute-start.24 = (bf16[48,1024]{1,0:T(8,128)(2,1)S(1)}, bf16[48,1024]{1,0:T(8,128)(2,1)S(1)}, u32[]{:S(2)}, u32[]{:S(2)}) collective-permute-start(bf16[48,1024]{1,0:T(8,128)(2,1)S(1)} %get-tuple-element.184), channel_id=1, source_target_pairs={{0,16},{8,24},{16,0},{24,8},{1,17},{9,25},{17,1},{25,9},{2,18},{10... | collective-permute-start | bytes 294920 | tf_op jit(solution)/shard_map/ppermute | solution.py:698
  35.7 18.2 %collective-permute-start.23 = (bf16[48,1024]{1,0:T(8,128)(2,1)S(1)}, bf16[48,1024]{1,0:T(8,128)(2,1)S(1)}, u32[]{:S(2)}, u32[]{:S(2)}) collective-permute-start(bf16[48,1024]{1,0:T(8,128)(2,1)S(1)} %get-tuple-element.184), channel_id=1, source_target_pairs={{0,8},{8,0},{16,24},{24,16},{1,9},{9,1},{17,25},{25,17},{2,10},{10... | collective-permute-start | bytes 294920 | tf_op jit(solution)/shard_map/ppermute | solution.py:698
  37.8 24.6 %collective-permute-start.12 = (bf16[48,2688]{1,0:T(8,128)(2,1)S(1)}, bf16[48,2688]{1,0:T(8,128)(2,1)S(1)}, u32[]{:S(2)}, u32[]{:S(2)}) collective-permute-start(bf16[48,2688]{1,0:T(8,128)(2,1)S(1)} %get-tuple-element.203), channel_id=1, source_target_pairs={{0,8},{8,0},{16,24},{24,16},{1,9},{9,1},{17,25},{25,17},{2,10},{10... | collective-permute-start | bytes 774152 | tf_op jit(solution)/shard_map/ppermute | solution.py:698
  53.9 20.5 %collective-permute-start.35 = (bf16[48,2688]{1,0:T(8,128)(2,1)S(1)}, bf16[48,2688]{1,0:T(8,128)(2,1)S(1)}, u32[]{:S(2)}, u32[]{:S(2)}) collective-permute-start(bf16[48,2688]{1,0:T(8,128)(2,1)S(1)} %get-tuple-element.201), channel_id=1, source_target_pairs={{0,16},{8,24},{16,0},{24,8},{1,17},{9,25},{17,1},{25,9},{2,18},{10... | collective-permute-start | bytes 774152 | tf_op jit(solution)/shard_map/ppermute | solution.py:698
  54.0 21.9 %collective-permute-start.34 = (bf16[48,2688]{1,0:T(8,128)(2,1)S(1)}, bf16[48,2688]{1,0:T(8,128)(2,1)S(1)}, u32[]{:S(2)}, u32[]{:S(2)}) collective-permute-start(bf16[48,2688]{1,0:T(8,128)(2,1)S(1)} %get-tuple-element.201), channel_id=1, source_target_pairs={{0,8},{8,0},{16,24},{24,16},{1,9},{9,1},{17,25},{25,17},{2,10},{10... | collective-permute-start | bytes 774152 | tf_op jit(solution)/shard_map/ppermute | solution.py:698
  55.9 21.7 %collective-permute-start.4 = (bf16[4,48,512]{2,1,0:T(8,128)(2,1)S(1)}, bf16[4,48,512]{2,1,0:T(8,128)(2,1)S(1)}, u32[]{:S(2)}, u32[]{:S(2)}) collective-permute-start(bf16[4,48,512]{2,1,0:T(8,128)(2,1)S(1)} %get-tuple-element.197), channel_id=1, source_target_pairs={{0,2},{1,3},{2,0},{3,1},{4,6},{5,7},{6,4},{7,5},{8,10},{9,11},{10,... | collective-permute-start | bytes 589832 | tf_op jit(solution)/shard_map/ppermute | solution.py:694
  62.6 22.7 %collective-permute-start.15 = (bf16[4,48,1920]{2,1,0:T(8,128)(2,1)S(1)}, bf16[4,48,1920]{2,1,0:T(8,128)(2,1)S(1)}, u32[]{:S(2)}, u32[]{:S(2)}) collective-permute-start(bf16[4,48,1920]{2,1,0:T(8,128)(2,1)S(1)} %slice.588), channel_id=1, source_target_pairs={{0,2},{1,3},{2,0},{3,1},{4,6},{5,7},{6,4},{7,5},{8,10},{9,11},{10,... | collective-permute-start | bytes 2211848 | tf_op jit(solution)/shard_map/ppermute | solution.py:694
  77.6 27.1 %collective-permute-start.37 = (bf16[4,48,1920]{2,1,0:T(8,128)(2,1)S(1)}, bf16[4,48,1920]{2,1,0:T(8,128)(2,1)S(1)}, u32[]{:S(2)}, u32[]{:S(2)}) collective-permute-start(bf16[4,48,1920]{2,1,0:T(8,128)(2,1)S(1)} %slice.596), channel_id=1, source_target_pairs={{0,2},{1,3},{2,0},{3,1},{4,6},{5,7},{6,4},{7,5},{8,10},{9,11},{10,... | collective-permute-start | bytes 2211848 | tf_op jit(solution)/shard_map/ppermute | solution.py:694
  85.3 19.5 %collective-permute-start.6 = (bf16[8,48,512]{2,1,0:T(8,128)(2,1)S(1)}, bf16[8,48,512]{2,1,0:T(8,128)(2,1)S(1)}, u32[]{:S(2)}, u32[]{:S(2)}) collective-permute-start(bf16[8,48,512]{2,1,0:T(8,128)(2,1)S(1)} %pad_maximum_fusion.8.refs_0_), channel_id=1, source_target_pairs={{0,4},{1,5},{2,6},{3,7},{4,0},{5,1},{6,2},{7,3},{8,12},{9,13},{10,... | collective-permute-start | bytes 1179656 | tf_op jit(solution)/shard_map/ppermute | solution.py:694
  90.0 17.6 %collective-permute-start.9 = (bf16[8,48,512]{2,1,0:T(8,128)(2,1)S(1)}, bf16[8,48,512]{2,1,0:T(8,128)(2,1)S(1)}, u32[]{:S(2)}, u32[]{:S(2)}) collective-permute-start(bf16[8,48,512]{2,1,0:T(8,128)(2,1)S(1)} %pad_maximum_fusion.9.refs_4_), channel_id=1, source_target_pairs={{0,1},{1,0},{2,3},{3,2},{4,5},{5,4},{6,7},{7,6},{8,9},{9,8},{10,11... | collective-permute-start | bytes 1179656 | tf_op jit(solution)/shard_map/ppermute | solution.py:694
  96.3 51.8 %collective-permute-start.17 = (bf16[8,48,1920]{2,1,0:T(8,128)(2,1)}, bf16[8,48,1920]{2,1,0:T(8,128)(2,1)}, u32[]{:S(2)}, u32[]{:S(2)}) collective-permute-start(bf16[8,48,1920]{2,1,0:T(8,128)(2,1)} %pad_maximum_fusion.refs_0_), channel_id=1, source_target_pairs={{0,4},{1,5},{2,6},{3,7},{4,0},{5,1},{6,2},{7,3},{8,12},{9,13},{10,... | collective-permute-start | bytes 4423688 | tf_op jit(solution)/shard_map/ppermute | solution.py:694
  104.8 40.0 %collective-permute-start.28 = (bf16[8,48,512]{2,1,0:T(8,128)(2,1)S(1)}, bf16[8,48,512]{2,1,0:T(8,128)(2,1)S(1)}, u32[]{:S(2)}, u32[]{:S(2)}) collective-permute-start(bf16[8,48,512]{2,1,0:T(8,128)(2,1)S(1)} %pad_maximum_fusion.11.refs_0_), channel_id=1, source_target_pairs={{0,4},{1,5},{2,6},{3,7},{4,0},{5,1},{6,2},{7,3},{8,12},{9,13},{10,... | collective-permute-start | bytes 1179656 | tf_op jit(solution)/shard_map/ppermute | solution.py:694
  107.6 65.8 %collective-permute-start.39 = (bf16[8,48,1920]{2,1,0:T(8,128)(2,1)}, bf16[8,48,1920]{2,1,0:T(8,128)(2,1)}, u32[]{:S(2)}, u32[]{:S(2)}) collective-permute-start(bf16[8,48,1920]{2,1,0:T(8,128)(2,1)} %pad_maximum_fusion.1.refs_0_), channel_id=1, source_target_pairs={{0,4},{1,5},{2,6},{3,7},{4,0},{5,1},{6,2},{7,3},{8,12},{9,13},{10,... | collective-permute-start | bytes 4423688 | tf_op jit(solution)/shard_map/ppermute | solution.py:694
  108.2 36.6 %collective-permute-start.31 = (bf16[8,48,512]{2,1,0:T(8,128)(2,1)S(1)}, bf16[8,48,512]{2,1,0:T(8,128)(2,1)}, u32[]{:S(2)}, u32[]{:S(2)}) collective-permute-start(bf16[8,48,512]{2,1,0:T(8,128)(2,1)S(1)} %pad_maximum_fusion.12.refs_4_), channel_id=1, source_target_pairs={{0,1},{1,0},{2,3},{3,2},{4,5},{5,4},{6,7},{7,6},{8,9},{9,8},{10,11... | collective-permute-start | bytes 1179656 | tf_op jit(solution)/shard_map/ppermute | solution.py:694
  108.3 37.0 %collective-permute-start.32 = (bf16[8,48,512]{2,1,0:T(8,128)(2,1)S(1)}, bf16[8,48,512]{2,1,0:T(8,128)(2,1)S(1)}, u32[]{:S(2)}, u32[]{:S(2)}) collective-permute-start(bf16[8,48,512]{2,1,0:T(8,128)(2,1)S(1)} %pad_maximum_fusion.12.refs_4_), channel_id=1, source_target_pairs={{0,2},{1,3},{2,0},{3,1},{4,6},{5,7},{6,4},{7,5},{8,10},{9,11},{10,... | collective-permute-start | bytes 1179656 | tf_op jit(solution)/shard_map/ppermute | solution.py:694
  147.5 16.6 %collective-permute-start.21 = (bf16[8,48,768]{2,1,0:T(8,128)(2,1)}, bf16[8,48,768]{2,1,0:T(8,128)(2,1)}, u32[]{:S(2)}, u32[]{:S(2)}) collective-permute-start(bf16[8,48,768]{2,1,0:T(8,128)(2,1)} %pad_maximum_fusion.4.refs_4_), channel_id=1, source_target_pairs={{0,2},{1,3},{2,0},{3,1},{4,6},{5,7},{6,4},{7,5},{8,10},{9,11},{10,... | collective-permute-start | bytes 1769480 | tf_op jit(solution)/shard_map/ppermute | solution.py:694
  148.0 32.8 %collective-permute-start.16 = (bf16[8,48,1920]{2,1,0:T(8,128)(2,1)}, bf16[8,48,1920]{2,1,0:T(8,128)(2,1)}, u32[]{:S(2)}, u32[]{:S(2)}) collective-permute-start(bf16[8,48,1920]{2,1,0:T(8,128)(2,1)} %pad_maximum_fusion.refs_0_), channel_id=1, source_target_pairs={{0,1},{1,0},{2,3},{3,2},{4,5},{5,4},{6,7},{7,6},{8,9},{9,8},{10,11... | collective-permute-start | bytes 4423688 | tf_op jit(solution)/shard_map/ppermute | solution.py:694
  148.1 32.9 %collective-permute-start.18 = (bf16[8,48,1920]{2,1,0:T(8,128)(2,1)}, bf16[8,48,1920]{2,1,0:T(8,128)(2,1)}, u32[]{:S(2)}, u32[]{:S(2)}) collective-permute-start(bf16[8,48,1920]{2,1,0:T(8,128)(2,1)} %collective-permute-done.17.refs_2_), channel_id=1, source_target_pairs={{0,1},{1,0},{2,3},{3,2},{4,5},{5,4},{6,7},{7,6},{8,9},{9,8},{10,11... | collective-permute-start | bytes 4423688 | tf_op jit(solution)/shard_map/ppermute | solution.py:694
  149.5 26.3 %collective-permute-start.43 = (bf16[8,48,768]{2,1,0:T(8,128)(2,1)}, bf16[8,48,768]{2,1,0:T(8,128)(2,1)}, u32[]{:S(2)}, u32[]{:S(2)}) collective-permute-start(bf16[8,48,768]{2,1,0:T(8,128)(2,1)} %pad_maximum_fusion.5.refs_4_), channel_id=1, source_target_pairs={{0,2},{1,3},{2,0},{3,1},{4,6},{5,7},{6,4},{7,5},{8,10},{9,11},{10,... | collective-permute-start | bytes 1769480 | tf_op jit(solution)/shard_map/ppermute | solution.py:694
  164.0 63.7 %collective-permute-start.38 = (bf16[8,48,1920]{2,1,0:T(8,128)(2,1)}, bf16[8,48,1920]{2,1,0:T(8,128)(2,1)}, u32[]{:S(2)}, u32[]{:S(2)}) collective-permute-start(bf16[8,48,1920]{2,1,0:T(8,128)(2,1)} %pad_maximum_fusion.1.refs_0_), channel_id=1, source_target_pairs={{0,1},{1,0},{2,3},{3,2},{4,5},{5,4},{6,7},{7,6},{8,9},{9,8},{10,11... | collective-permute-start | bytes 4423688 | tf_op jit(solution)/shard_map/ppermute | solution.py:694
  173.4 54.3 %collective-permute-start.40 = (bf16[8,48,1920]{2,1,0:T(8,128)(2,1)}, bf16[8,48,1920]{2,1,0:T(8,128)(2,1)}, u32[]{:S(2)}, u32[]{:S(2)}) collective-permute-start(bf16[8,48,1920]{2,1,0:T(8,128)(2,1)} %collective-permute-done.39.refs_2_), channel_id=1, source_target_pairs={{0,1},{1,0},{2,3},{3,2},{4,5},{5,4},{6,7},{7,6},{8,9},{9,8},{10,11... | collective-permute-start | bytes 4423688 | tf_op jit(solution)/shard_map/ppermute | solution.py:694
  180.4 47.3 %collective-permute-start.42 = (bf16[8,48,768]{2,1,0:T(8,128)(2,1)}, bf16[8,48,768]{2,1,0:T(8,128)(2,1)S(1)}, u32[]{:S(2)}, u32[]{:S(2)}) collective-permute-start(bf16[8,48,768]{2,1,0:T(8,128)(2,1)} %pad_maximum_fusion.5.refs_4_), channel_id=1, source_target_pairs={{0,1},{1,0},{2,3},{3,2},{4,5},{5,4},{6,7},{7,6},{8,9},{9,8},{10,11... | collective-permute-start | bytes 1769480 | tf_op jit(solution)/shard_map/ppermute | solution.py:694
  180.8 46.9 %collective-permute-start.44 = (bf16[8,48,768]{2,1,0:T(8,128)(2,1)}, bf16[8,48,768]{2,1,0:T(8,128)(2,1)S(1)}, u32[]{:S(2)}, u32[]{:S(2)}) collective-permute-start(bf16[8,48,768]{2,1,0:T(8,128)(2,1)} %collective-permute-done.43.refs_6_), channel_id=1, source_target_pairs={{0,1},{1,0},{2,3},{3,2},{4,5},{5,4},{6,7},{7,6},{8,9},{9,8},{10,11... | collective-permute-start | bytes 1769480 | tf_op jit(solution)/shard_map/ppermute | solution.py:694
  181.0 29.3 %collective-permute-start.33 = (bf16[8,48,512]{2,1,0:T(8,128)(2,1)S(1)}, bf16[8,48,512]{2,1,0:T(8,128)(2,1)S(1)}, u32[]{:S(2)}, u32[]{:S(2)}) collective-permute-start(bf16[8,48,512]{2,1,0:T(8,128)(2,1)S(1)} %copy-done.28), channel_id=1, source_target_pairs={{0,1},{1,0},{2,3},{3,2},{4,5},{5,4},{6,7},{7,6},{8,9},{9,8},{10,11... | collective-permute-start | bytes 1179656 | tf_op jit(solution)/shard_map/ppermute | solution.py:694
  278.6 57.0 %collective-permute-start.62 = (bf16[16,48,1024]{2,1,0:T(8,128)(2,1)}, bf16[16,48,1024]{2,1,0:T(8,128)(2,1)}, u32[]{:S(2)}, u32[]{:S(2)}) collective-permute-start(bf16[16,48,1024]{2,1,0:T(8,128)(2,1)} %get-tuple-element.135), channel_id=1, source_target_pairs={{0,1},{1,0},{2,3},{3,2},{4,5},{5,4},{6,7},{7,6},{8,9},{9,8},{10,11... | collective-permute-start | bytes 4718600 | tf_op jit(solution)/shard_map/ppermute | solution.py:694
  319.2 21.3 %collective-permute-start.45 = (bf16[16,48,1024]{2,1,0:T(8,128)(2,1)}, bf16[16,48,1024]{2,1,0:T(8,128)(2,1)}, u32[]{:S(2)}, u32[]{:S(2)}) collective-permute-start(bf16[16,48,1024]{2,1,0:T(8,128)(2,1)} %get-tuple-element.123), channel_id=1, source_target_pairs={{0,1},{1,0},{2,3},{3,2},{4,5},{5,4},{6,7},{7,6},{8,9},{9,8},{10,11... | collective-permute-start | bytes 4718600 | tf_op jit(solution)/shard_map/ppermute | solution.py:694
  327.7 58.3 %collective-permute-start.70 = (bf16[16,48,2688]{2,1,0:T(8,128)(2,1)}, bf16[16,48,2688]{2,1,0:T(8,128)(2,1)S(1)}, u32[]{:S(2)}, u32[]{:S(2)}) collective-permute-start(bf16[16,48,2688]{2,1,0:T(8,128)(2,1)} %get-tuple-element.143), channel_id=1, source_target_pairs={{0,1},{1,0},{2,3},{3,2},{4,5},{5,4},{6,7},{7,6},{8,9},{9,8},{10,11... | collective-permute-start | bytes 12386312 | tf_op jit(solution)/shard_map/ppermute | solution.py:694
  335.3 53.5 %collective-permute-start.53 = (bf16[16,48,2688]{2,1,0:T(8,128)(2,1)}, bf16[16,48,2688]{2,1,0:T(8,128)(2,1)S(1)}, u32[]{:S(2)}, u32[]{:S(2)}) collective-permute-start(bf16[16,48,2688]{2,1,0:T(8,128)(2,1)} %get-tuple-element.131), channel_id=1, source_target_pairs={{0,1},{1,0},{2,3},{3,2},{4,5},{5,4},{6,7},{7,6},{8,9},{9,8},{10,11... | collective-permute-start | bytes 12386312 | tf_op jit(solution)/shard_map/ppermute | solution.py:694
  342.6 15.3 %collective-permute-start.46 = (bf16[4,2,48,512]{3,2,1,0:T(8,128)(2,1)S(1)}, bf16[4,2,48,512]{3,2,1,0:T(8,128)(2,1)S(1)}, u32[]{:S(2)}, u32[]{:S(2)}) collective-permute-start(bf16[4,2,48,512]{3,2,1,0:T(8,128)(2,1)S(1)} %slice_bitcast_fusion.18), channel_id=1, source_target_pairs={{0,4},{1,5},{2,6},{3,7},{4,0},{5,1},{6,2},{7,3},{8,12},{9,13},{10,... | collective-permute-start | bytes 1179656 | tf_op jit(solution)/shard_map/ppermute | solution.py:694
  351.4 14.9 %collective-permute-start.64 = (bf16[4,48,512]{2,1,0:T(8,128)(2,1)S(1)}, bf16[4,48,512]{2,1,0:T(8,128)(2,1)S(1)}, u32[]{:S(2)}, u32[]{:S(2)}) collective-permute-start(bf16[4,48,512]{2,1,0:T(8,128)(2,1)S(1)} %slice_bitcast_fusion.26), channel_id=1, source_target_pairs={{0,2},{1,3},{2,0},{3,1},{4,6},{5,7},{6,4},{7,5},{8,10},{9,11},{10,... | collective-permute-start | bytes 589832 | tf_op jit(solution)/shard_map/ppermute | solution.py:694
  387.5 16.1 %collective-permute-start.73 = (bf16[4,2,48,768]{3,2,1,0:T(8,128)(2,1)S(1)}, bf16[4,2,48,768]{3,2,1,0:T(8,128)(2,1)S(1)}, u32[]{:S(2)}, u32[]{:S(2)}) collective-permute-start(bf16[4,2,48,768]{3,2,1,0:T(8,128)(2,1)S(1)} %slice_bitcast_fusion.8), channel_id=1, source_target_pairs={{0,2},{1,3},{2,0},{3,1},{4,6},{5,7},{6,4},{7,5},{8,10},{9,11},{10,... | collective-permute-start | bytes 1769480 | tf_op jit(solution)/shard_map/ppermute | solution.py:694
  390.0 19.9 %collective-permute-start.56 = (bf16[4,2,48,768]{3,2,1,0:T(8,128)(2,1)S(1)}, bf16[4,2,48,768]{3,2,1,0:T(8,128)(2,1)S(1)}, u32[]{:S(2)}, u32[]{:S(2)}) collective-permute-start(bf16[4,2,48,768]{3,2,1,0:T(8,128)(2,1)S(1)} %slice_bitcast_fusion.10), channel_id=1, source_target_pairs={{0,2},{1,3},{2,0},{3,1},{4,6},{5,7},{6,4},{7,5},{8,10},{9,11},{10,... | collective-permute-start | bytes 1769480 | tf_op jit(solution)/shard_map/ppermute | solution.py:694
  391.1 48.0 %collective-permute-start.71 = (bf16[4,2,48,1920]{3,2,1,0:T(8,128)(2,1)S(1)}, bf16[4,2,48,1920]{3,2,1,0:T(8,128)(2,1)S(1)}, u32[]{:S(2)}, u32[]{:S(2)}) collective-permute-start(bf16[4,2,48,1920]{3,2,1,0:T(8,128)(2,1)S(1)} %slice_bitcast_fusion), channel_id=1, source_target_pairs={{0,4},{1,5},{2,6},{3,7},{4,0},{5,1},{6,2},{7,3},{8,12},{9,13},{10,... | collective-permute-start | bytes 4423688 | tf_op jit(solution)/shard_map/ppermute | solution.py:694
  403.8 28.9 %collective-permute-start.74 = (bf16[4,48,768]{2,1,0:T(8,128)(2,1)S(1)}, bf16[4,48,768]{2,1,0:T(8,128)(2,1)S(1)}, u32[]{:S(2)}, u32[]{:S(2)}) collective-permute-start(bf16[4,48,768]{2,1,0:T(8,128)(2,1)S(1)} %slice_bitcast_fusion.20), channel_id=1, source_target_pairs={{0,4},{1,5},{2,6},{3,7},{4,0},{5,1},{6,2},{7,3},{8,12},{9,13},{10,... | collective-permute-start | bytes 884744 | tf_op jit(solution)/shard_map/ppermute | solution.py:694
  410.1 28.9 %collective-permute-start.57 = (bf16[4,48,768]{2,1,0:T(8,128)(2,1)S(1)}, bf16[4,48,768]{2,1,0:T(8,128)(2,1)S(1)}, u32[]{:S(2)}, u32[]{:S(2)}) collective-permute-start(bf16[4,48,768]{2,1,0:T(8,128)(2,1)S(1)} %slice_bitcast_fusion.22), channel_id=1, source_target_pairs={{0,4},{1,5},{2,6},{3,7},{4,0},{5,1},{6,2},{7,3},{8,12},{9,13},{10,... | collective-permute-start | bytes 884744 | tf_op jit(solution)/shard_map/ppermute | solution.py:694
  411.1 52.4 %collective-permute-start.54 = (bf16[4,2,48,1920]{3,2,1,0:T(8,128)(2,1)S(1)}, bf16[4,2,48,1920]{3,2,1,0:T(8,128)(2,1)S(1)}, u32[]{:S(2)}, u32[]{:S(2)}) collective-permute-start(bf16[4,2,48,1920]{3,2,1,0:T(8,128)(2,1)S(1)} %slice_bitcast_fusion.2), channel_id=1, source_target_pairs={{0,4},{1,5},{2,6},{3,7},{4,0},{5,1},{6,2},{7,3},{8,12},{9,13},{10,... | collective-permute-start | bytes 4423688 | tf_op jit(solution)/shard_map/ppermute | solution.py:694
  439.6 25.2 %collective-permute-start.72 = (bf16[4,48,1920]{2,1,0:T(8,128)(2,1)S(1)}, bf16[4,48,1920]{2,1,0:T(8,128)(2,1)S(1)}, u32[]{:S(2)}, u32[]{:S(2)}) collective-permute-start(bf16[4,48,1920]{2,1,0:T(8,128)(2,1)S(1)} %slice_bitcast_fusion.4), channel_id=1, source_target_pairs={{0,2},{1,3},{2,0},{3,1},{4,6},{5,7},{6,4},{7,5},{8,10},{9,11},{10,... | collective-permute-start | bytes 2211848 | tf_op jit(solution)/shard_map/ppermute | solution.py:694
  466.9 28.4 %collective-permute-start.76 = (bf16[48,2688]{1,0:T(8,128)(2,1)S(1)}, bf16[48,2688]{1,0:T(8,128)(2,1)S(1)}, u32[]{:S(2)}, u32[]{:S(2)}) collective-permute-start(bf16[48,2688]{1,0:T(8,128)(2,1)S(1)} %get-tuple-element.175), channel_id=1, source_target_pairs={{0,16},{8,24},{16,0},{24,8},{1,17},{9,25},{17,1},{25,9},{2,18},{10... | collective-permute-start | bytes 774152 | tf_op jit(solution)/shard_map/ppermute | solution.py:698
  466.9 28.4 %collective-permute-start.75 = (bf16[48,2688]{1,0:T(8,128)(2,1)S(1)}, bf16[48,2688]{1,0:T(8,128)(2,1)S(1)}, u32[]{:S(2)}, u32[]{:S(2)}) collective-permute-start(bf16[48,2688]{1,0:T(8,128)(2,1)S(1)} %get-tuple-element.173), channel_id=1, source_target_pairs={{0,8},{8,0},{16,24},{24,16},{1,9},{9,1},{17,25},{25,17},{2,10},{10... | collective-permute-start | bytes 774152 | tf_op jit(solution)/shard_map/ppermute | solution.py:698
  476.6 26.5 %collective-permute-start.60 = (bf16[48,2688]{1,0:T(8,128)(2,1)}, bf16[48,2688]{1,0:T(8,128)(2,1)}, u32[]{:S(2)}, u32[]{:S(2)}) collective-permute-start(bf16[48,2688]{1,0:T(8,128)(2,1)} %get-tuple-element.171), channel_id=1, source_target_pairs={{0,24},{8,16},{16,8},{24,0},{1,25},{9,17},{17,9},{25,1},{2,26},{10... | collective-permute-start | bytes 774152 | tf_op jit(solution)/shard_map/ppermute | solution.py:698
  478.3 25.3 %collective-permute-start.59 = (bf16[48,2688]{1,0:T(8,128)(2,1)}, bf16[48,2688]{1,0:T(8,128)(2,1)}, u32[]{:S(2)}, u32[]{:S(2)}) collective-permute-start(bf16[48,2688]{1,0:T(8,128)(2,1)} %get-tuple-element.172), channel_id=1, source_target_pairs={{0,16},{8,24},{16,0},{24,8},{1,17},{9,25},{17,1},{25,9},{2,18},{10... | collective-permute-start | bytes 774152 | tf_op jit(solution)/shard_map/ppermute | solution.py:698
  478.3 25.3 %collective-permute-start.58 = (bf16[48,2688]{1,0:T(8,128)(2,1)}, bf16[48,2688]{1,0:T(8,128)(2,1)}, u32[]{:S(2)}, u32[]{:S(2)}) collective-permute-start(bf16[48,2688]{1,0:T(8,128)(2,1)} %get-tuple-element.170), channel_id=1, source_target_pairs={{0,8},{8,0},{16,24},{24,16},{1,9},{9,1},{17,25},{25,17},{2,10},{10... | collective-permute-start | bytes 774152 | tf_op jit(solution)/shard_map/ppermute | solution.py:698
  502.1 15.6 %collective-permute-start.78 = (f32[24,2944]{1,0:T(8,128)}, f32[24,2944]{1,0:T(8,128)}, u32[]{:S(2)}, u32[]{:S(2)}) collective-permute-start(f32[24,2944]{1,0:T(8,128)} %copy.79), channel_id=1, source_target_pairs={{0,1},{1,0},{2,3},{3,2},{4,5},{5,4},{6,7},{7,6},{8,9},{9,8},{10,11... | collective-permute-start | bytes 847880 | tf_op jit(solution)/shard_map/ppermute | solution.py:694
  (76 other events, 1101.3 us)

commit v2 on v1

v2 whole, which is shorter than its diff:
```python
import functools

import jax
import jax.numpy as jnp
from jax import lax
from jax.experimental import pallas as pl
from jax.experimental.pallas import tpu as pltpu
from jax.sharding import PartitionSpec as P

GROUP = 128
EPS = 1e-06
SUB = 8
UNIT = 48
HALVES = {"mix": 1024, "out": 384, "up": 1536}
ROWS = 32
F32 = jnp.float32
BF16 = jnp.bfloat16
ALL = ("dp", "seq")
VMEM = pl.BlockSpec(memory_space=pltpu.VMEM)
SMEM = pl.BlockSpec(memory_space=pltpu.SMEM)
ANY = pl.BlockSpec(memory_space=pl.ANY)


def sds(shape, dtype=F32):
    return jax.ShapeDtypeStruct(shape, dtype)


def over_rows(total, body):
    def step(i, _):
        body(pl.ds(pl.multiple_of(i * ROWS, ROWS), ROWS))
        return 0

    lax.fori_loop(0, total // ROWS, step, 0)


def dot(left, right):
    return jnp.dot(left, right, preferred_element_type=F32)


def dot_t(left, right):
    return lax.dot_general(left, right, (((1,), (1,)), ((), ())), preferred_element_type=F32)


def cmul(ar, ai, br, bi):
    return ar * br - ai * bi, ar * bi + ai * br


def power(cos, sin, times):
    while times > 1:
        cos, sin = cos * cos - sin * sin, 2.0 * cos * sin
        times //= 2
    return cos, sin


def turns(p_ref, half):
    cos, sin = p_ref[3:4, half:], p_ref[4:5, :half]
    return tuple(
        [jnp.broadcast_to(part[:, t * GROUP : (t + 1) * GROUP], (SUB, GROUP)) for t in range(half // GROUP)]
        for part in (cos, sin)
    )


def parts(ref, k, tiles):
    return [ref[k, :, t * GROUP : (t + 1) * GROUP] for t in range(tiles)]


def mix_width(plan, width):
    return 2 * width + width // 2 if plan is None else 2 * HALVES["mix"]


def load_start(pairs, sem):
    for source, target in pairs:
        pltpu.make_async_copy(source, target, sem).start()


def load_wait(pairs, sem):
    for source, target in pairs:
        pltpu.make_async_copy(source, target, sem).wait()


def pairs_of(plan, sources, me_ref, name, target):
    if plan is None:
        return [(sources[{"mix": 0, "out": 1, "up": 2, "down": 3}[name]], target)]
    chip, core = me_ref[1], me_ref[2]
    column, columns = plan[name]
    pairs = []
    for source, (other_core, rels) in enumerate(plan["sources"]):
        half = core ^ other_core
        for b, (zero, one) in enumerate(zip(*rels)):
            block = chip ^ (zero + half * (one - zero))
            if name == "down":
                row, left = block * (2 * UNIT) + half * UNIT, 0
            elif name == "small":
                row, left = block * UNIT, half * GROUP
            else:
                row, left = block * UNIT, half * HALVES[name]
            to = target.at[pl.ds(pl.multiple_of(row, UNIT), UNIT), pl.ds(pl.multiple_of(left, GROUP), columns)]
            pairs.append((sources[source].at[b, :, pl.ds(column, columns)], to))
    return pairs


def front_kernel(
    plan, count, me_ref, x_ref, p_ref, *refs
):
    w_hbm, refs = refs[:count], refs[count:]
    (
    normed_ref, cpre_ref, gate_ref, rate_ref, kept_ref, feed_ref, sub_ref, total_ref,
    w_ref, sem,
    ) = refs
    rows, width = x_ref.shape
    half = width // 2
    block = rows // SUB
    pairs = pairs_of(plan, w_hbm, me_ref, "mix", w_ref)
    load_start(pairs, sem)

    def norm(r):
        x = x_ref[r, :].astype(F32)
        scale = lax.rsqrt(jnp.mean(x * x, axis=1, keepdims=True) + EPS)
        normed_ref[r, :] = (x * scale * p_ref[0:1, :]).astype(BF16)

    over_rows(rows, norm)
    load_wait(pairs, sem)
    normed = normed_ref[...]
    rate = jax.nn.sigmoid(dot(normed, w_ref[:, 2 * width : 2 * width + half]) + p_ref[3:4, :half])
    rate_ref[...] = rate
    at = lax.broadcasted_iota(jnp.int32, (rows, GROUP), 0)
    fresh = at == me_ref[5]
    for j in range(6, me_ref.shape[0]):
        fresh = jnp.logical_or(fresh, at == me_ref[j])
    tiles = half // GROUP
    for t in range(tiles):
        kept_ref[t] = jnp.where(fresh, 0.0, rate[:, t * GROUP : (t + 1) * GROUP])
    for k in range(2):
        cols = slice(k * half, (k + 1) * half)
        pre = dot(normed, w_ref[:, cols])
        cpre_ref[:, cols] = pre
        feed = (1.0 - rate_ref[...]) * (pre * jax.nn.sigmoid(pre))
        for t in range(tiles):
            feed_ref[k * tiles + t] = feed[:, t * GROUP : (t + 1) * GROUP]
    cos, sin = turns(p_ref, half)

    mag = [jnp.ones((SUB, GROUP), F32)] * tiles
    br = [jnp.zeros((SUB, GROUP), F32)] * tiles
    bi = [jnp.zeros((SUB, GROUP), F32)] * tiles
    for j in range(block):
        at = pl.ds(j, SUB, stride=block)
        for t in range(tiles):
            kept = kept_ref[t, at, :]
            tr, ti = cmul(cos[t], sin[t], br[t], bi[t])
            br[t] = kept * tr + feed_ref[t, at, :]
            bi[t] = kept * ti + feed_ref[tiles + t, at, :]
            mag[t] = mag[t] * kept
    mag, br, bi = (jnp.concatenate(part, axis=1) for part in (mag, br, bi))
    far_cos, far_sin = power(jnp.concatenate(cos, axis=1), jnp.concatenate(sin, axis=1), block)
    ar, ai = mag * far_cos, mag * far_sin
    sub_ref[0] = ar
    sub_ref[1] = ai
    sub_ref[2] = br
    sub_ref[3] = bi
    one_r, one_i, sum_r, sum_i = (part[0:1] for part in (ar, ai, br, bi))
    for k in range(1, SUB):
        kr, ki = ar[k : k + 1], ai[k : k + 1]
        one_r, one_i = cmul(kr, ki, one_r, one_i)
        sum_r, sum_i = cmul(kr, ki, sum_r, sum_i)
        sum_r = sum_r + br[k : k + 1]
        sum_i = sum_i + bi[k : k + 1]
    total_ref[0:1, :] = one_r
    total_ref[1:2, :] = one_i
    total_ref[2:3, :] = sum_r
    total_ref[3:4, :] = sum_i
    for k in range(2):
        cols = slice(width + k * half, width + (k + 1) * half)
        gate_ref[:, k * half : (k + 1) * half] = jax.nn.sigmoid(dot(normed, w_ref[:, cols]))


def front(plan, me, x, params, weights):
    rows, width = x.shape
    half = width // 2
    return pl.pallas_call(
        functools.partial(front_kernel, plan, len(weights)),
        out_shape=(
            sds((rows, width), BF16),
            sds((rows, width)),
            sds((rows, width)),
            sds((rows, half)),
            sds((half // GROUP, rows, GROUP)),
            sds((width // GROUP, rows, GROUP)),
            sds((4, SUB, half)),
            sds((4, half)),
        ),
        in_specs=[SMEM, VMEM, VMEM] + [ANY] * len(weights),
        out_specs=(VMEM,) * 8,
        scratch_shapes=[pltpu.VMEM((width, mix_width(plan, width)), BF16), pltpu.SemaphoreType.DMA],
        compiler_params=pltpu.CompilerParams(vmem_limit_bytes=56 << 20),
        cost_estimate=pl.CostEstimate(flops=2 * rows * width * 5 * half, bytes_accessed=8 << 20, transcendentals=0),
        name="front",
    )(me, x, params, *weights)


def mid_kernel(plan, count, me_ref, x_ref, p_ref, gate_ref, kept_ref, feed_ref, sub_ref, every_ref, *refs):
    w_hbm, refs = refs[:count], refs[count:]
    states_ref, first_ref, gn_ref, rg_ref, gated_ref, after_ref, lifted_ref, out_ref, sem = refs
    rows, width = x_ref.shape
    half = width // 2
    block = rows // SUB
    pairs = pairs_of(plan, w_hbm, me_ref, "out", out_ref)
    load_start(pairs, sem)

    sr = jnp.zeros((1, half), F32)
    si = jnp.zeros((1, half), F32)
    for k in range(every_ref.shape[0]):
        at = k ^ me_ref[3]
        nr, ni = cmul(every_ref[at, 0:1, :], every_ref[at, 1:2, :], sr, si)
        earlier = k < me_ref[0]
        sr = jnp.where(earlier, nr + every_ref[at, 2:3, :], sr)
        si = jnp.where(earlier, ni + every_ref[at, 3:4, :], si)
    for k in range(SUB):
        first_ref[0, k : k + 1, :] = sr
        first_ref[1, k : k + 1, :] = si
        nr, ni = cmul(sub_ref[0, k : k + 1, :], sub_ref[1, k : k + 1, :], sr, si)
        sr = nr + sub_ref[2, k : k + 1, :]
        si = ni + sub_ref[3, k : k + 1, :]
    cos, sin = turns(p_ref, half)
    tiles = half // GROUP
    sr = parts(first_ref, 0, tiles)
    si = parts(first_ref, 1, tiles)
    for j in range(block):
        at = pl.ds(j, SUB, stride=block)
        for t in range(tiles):
            kept = kept_ref[t, at, :]
            tr, ti = cmul(cos[t], sin[t], sr[t], si[t])
            sr[t] = kept * tr + feed_ref[t, at, :]
            si[t] = kept * ti + feed_ref[tiles + t, at, :]
            states_ref[t, at, :] = sr[t]
            states_ref[tiles + t, at, :] = si[t]

    lane = lax.broadcasted_iota(jnp.int32, (ROWS, GROUP), 1)

    def group_norm(r):
        held = jnp.zeros((ROWS, GROUP), F32)
        for g in range(width // GROUP):
            cols = slice(g * GROUP, (g + 1) * GROUP)
            v = gate_ref[r, cols] * states_ref[g, r, :]
            centre = v - jnp.mean(v, axis=1, keepdims=True)
            scale = lax.rsqrt(jnp.mean(centre * centre, axis=1, keepdims=True) + EPS)
            gn = centre * scale
            gn_ref[r, cols] = gn
            gated_ref[r, cols] = (gn * p_ref[1:2, cols]).astype(BF16)
            held = jnp.where(lane == g, scale, held)
        rg_ref[r, :] = held

    over_rows(rows, group_norm)
    load_wait(pairs, sem)
    after_ref[...] = x_ref[...].astype(F32) + dot(gated_ref[...], out_ref[...])

    def norm(r):
        after = after_ref[r, :]
        scale = lax.rsqrt(jnp.mean(after * after, axis=1, keepdims=True) + EPS)
        lifted_ref[r, :] = (after * scale * p_ref[2:3, :]).astype(BF16)

    over_rows(rows, norm)


def mid(plan, me, x, params, gate, kept, feed, sub, every, weights):
    rows, width = x.shape
    half = width // 2
    return pl.pallas_call(
        functools.partial(mid_kernel, plan, len(weights)),
        out_shape=(
            sds((width // GROUP, rows, GROUP)),
            sds((2, SUB, half)),
            sds((rows, width)),
            sds((rows, GROUP)),
            sds((rows, width), BF16),
            sds((rows, width)),
            sds((rows, width), BF16),
        ),
        in_specs=[SMEM] + [VMEM] * 7 + [ANY] * len(weights),
        out_specs=(VMEM,) * 7,
        scratch_shapes=[pltpu.VMEM((width, width), BF16), pltpu.SemaphoreType.DMA],
        compiler_params=pltpu.CompilerParams(vmem_limit_bytes=56 << 20),
        cost_estimate=pl.CostEstimate(flops=2 * rows * width * width, bytes_accessed=8 << 20, transcendentals=0),
        name="mid",
    )(me, x, params, gate, kept, feed, sub, every, *weights)


def ffn_kernel(plan, count, me_ref, after_ref, lifted_ref, *refs):
    w_hbm, refs = refs[:count], refs[count:]
    both_ref, hidden_ref, next_ref, up_ref, down_ref, sems = refs
    inner = hidden_ref.shape[1]
    up_pairs = pairs_of(plan, w_hbm, me_ref, "up", up_ref)
    down_pairs = pairs_of(plan, w_hbm, me_ref, "down", down_ref)
    load_start(up_pairs, sems.at[0])
    load_start(down_pairs, sems.at[1])
    load_wait(up_pairs, sems.at[0])
    lifted = lifted_ref[...]
    step = after_ref.shape[1] // 2
    for k in range(inner // step):
        cols = slice(k * step, (k + 1) * step)
        more = slice(inner + k * step, inner + (k + 1) * step)
        a = dot(lifted, up_ref[:, cols])
        b = dot(lifted, up_ref[:, more])
        both_ref[:, cols] = a
        both_ref[:, more] = b
        hidden_ref[:, cols] = (a * jax.nn.sigmoid(a) * b).astype(BF16)
    load_wait(down_pairs, sems.at[1])
    next_ref[...] = (after_ref[...] + dot(hidden_ref[...], down_ref[...])).astype(next_ref.dtype)


def ffn(plan, me, after, lifted, weights, dtype):
    rows, width = after.shape
    inner = 2 * width
    return pl.pallas_call(
        functools.partial(ffn_kernel, plan, len(weights)),
        out_shape=(sds((rows, 2 * inner)), sds((rows, inner), BF16), sds((rows, width), dtype)),
        in_specs=[SMEM] + [VMEM] * 2 + [ANY] * len(weights),
        out_specs=(VMEM,) * 3,
        scratch_shapes=[
            pltpu.VMEM((width, 2 * inner), BF16),
            pltpu.VMEM((inner, width), BF16),
            pltpu.SemaphoreType.DMA((2,)),
        ],
        compiler_params=pltpu.CompilerParams(vmem_limit_bytes=56 << 20),
        cost_estimate=pl.CostEstimate(flops=2 * rows * width * 6 * width, bytes_accessed=14 << 20, transcendentals=0),
        name="ffn",
    )(me, after, lifted, *weights)


def back_ffn_kernel(plan, count, me_ref, dx_ref, p_ref, both_ref, after_ref, *refs):
    w_hbm, refs = refs[:count], refs[count:]
    dlow_ref, dboth_ref, dafter_ref, dmid_ref, gain_ref, work_ref, up_ref, down_ref, sems = refs
    rows, width = dx_ref.shape
    inner = down_ref.shape[0]
    up_pairs = pairs_of(plan, w_hbm, me_ref, "up", up_ref)
    down_pairs = pairs_of(plan, w_hbm, me_ref, "down", down_ref)
    load_start(down_pairs, sems.at[1])
    load_start(up_pairs, sems.at[0])
    if dx_ref.dtype == BF16:
        at = lax.broadcasted_iota(jnp.int32, (rows, GROUP), 0)
        live = at < me_ref[4]
        for t in range(width // GROUP):
            cols = slice(t * GROUP, (t + 1) * GROUP)
            dlow_ref[:, cols] = jnp.where(live, dx_ref[:, cols].astype(F32), 0.0).astype(BF16)
        grad_ref = dlow_ref
    else:
        dlow_ref[...] = dx_ref[...].astype(BF16)
        grad_ref = dx_ref
    dlow = dlow_ref[...]
    load_wait(down_pairs, sems.at[1])
    step = width // 2
    for k in range(inner // step):
        cols = slice(k * step, (k + 1) * step)
        more = slice(inner + k * step, inner + (k + 1) * step)
        dh = dot_t(dlow, down_ref[cols, :])
        a = both_ref[:, cols]
        sig = jax.nn.sigmoid(a)
        dboth_ref[:, cols] = (dh * both_ref[:, more] * (sig * (1.0 + a * (1.0 - sig)))).astype(BF16)
        dboth_ref[:, more] = (dh * (a * sig)).astype(BF16)
    load_wait(up_pairs, sems.at[0])
    work_ref[...] = dot_t(dboth_ref[...], up_ref[...])

    def norm_back(r):
        after = after_ref[r, :]
        scale = lax.rsqrt(jnp.mean(after * after, axis=1, keepdims=True) + EPS)
        normal = after * scale
        lift = work_ref[r, :]
        e = lift * p_ref[2:3, :]
        d = grad_ref[r, :].astype(F32) + scale * (e - normal * jnp.mean(e * normal, axis=1, keepdims=True))
        dafter_ref[r, :] = d
        dmid_ref[r, :] = d.astype(BF16)
        work_ref[r, :] = lift * normal

    over_rows(rows, norm_back)
    gain_ref[...] = jnp.sum(work_ref[...], axis=0, keepdims=True)


def back_ffn(plan, me, dx, params, both, after, weights):
    rows, width = dx.shape
    inner = 2 * width
    return pl.pallas_call(
        functools.partial(back_ffn_kernel, plan, len(weights)),
        out_shape=(
            sds((rows, width), BF16),
            sds((rows, 2 * inner), BF16),
            sds((rows, width)),
            sds((rows, width), BF16),
            sds((1, width)),
        ),
        in_specs=[SMEM] + [VMEM] * 4 + [ANY] * len(weights),
        out_specs=(VMEM,) * 5,
        scratch_shapes=[
            pltpu.VMEM((rows, width), F32),
            pltpu.VMEM((width, 2 * inner), BF16),
            pltpu.VMEM((inner, width), BF16),
            pltpu.SemaphoreType.DMA((2,)),
        ],
        compiler_params=pltpu.CompilerParams(vmem_limit_bytes=56 << 20),
        cost_estimate=pl.CostEstimate(flops=2 * rows * width * 6 * width, bytes_accessed=14 << 20, transcendentals=0),
        name="back_ffn",
    )(me, dx, params, both, after, *weights)


def back_mid_kernel(
    plan, count, me_ref, dmid_ref, p_ref, gn_ref, rg_ref, gate_ref, states_ref, kept_ref, sub_ref, *refs
):
    w_hbm, refs = refs[:count], refs[count:]
    dgpre_ref, dstates_ref, gain_ref, rsub_ref, rtotal_ref, work_ref, out_ref, sem = refs
    rows, width = dmid_ref.shape
    half = width // 2
    block = rows // SUB
    pairs = pairs_of(plan, w_hbm, me_ref, "out", out_ref)
    load_start(pairs, sem)
    load_wait(pairs, sem)
    work_ref[...] = dot_t(dmid_ref[...], out_ref[...])

    def group_back(r):
        held = rg_ref[r, :]
        for g in range(width // GROUP):
            cols = slice(g * GROUP, (g + 1) * GROUP)
            gn = gn_ref[r, cols]
            dg = work_ref[r, cols]
            e = dg * p_ref[1:2, cols]
            dv = held[:, g : g + 1] * (
                e - jnp.mean(e, axis=1, keepdims=True) - gn * jnp.mean(e * gn, axis=1, keepdims=True)
            )
            gate = gate_ref[r, cols]
            dgpre_ref[r, cols] = (dv * states_ref[g, r, :] * gate * (1.0 - gate)).astype(BF16)
            dstates_ref[g, r, :] = dv * gate
            work_ref[r, cols] = dg * gn

    over_rows(rows, group_back)
    gain_ref[...] = jnp.sum(work_ref[...], axis=0, keepdims=True)

    cos, sin = turns(p_ref, half)
    tiles = half // GROUP
    zr = [jnp.zeros((SUB, GROUP), F32)] * tiles
    zi = [jnp.zeros((SUB, GROUP), F32)] * tiles
    for j in reversed(range(block)):
        at = pl.ds(j, SUB, stride=block)
        for t in range(tiles):
            kept = kept_ref[t, at, :]
            qr = dstates_ref[t, at, :] + zr[t]
            qi = dstates_ref[tiles + t, at, :] + zi[t]
            zr[t] = kept * (cos[t] * qr + sin[t] * qi)
            zi[t] = kept * (cos[t] * qi - sin[t] * qr)
    zr, zi = jnp.concatenate(zr, axis=1), jnp.concatenate(zi, axis=1)
    rsub_ref[0] = zr
    rsub_ref[1] = zi
    tr = jnp.zeros((1, half), F32)
    ti = jnp.zeros((1, half), F32)
    for k in reversed(range(SUB)):
        ar, ai = sub_ref[0, k : k + 1, :], sub_ref[1, k : k + 1, :]
        tr, ti = ar * tr + ai * ti + zr[k : k + 1], ar * ti - ai * tr + zi[k : k + 1]
    rtotal_ref[0:1, :] = tr
    rtotal_ref[1:2, :] = ti


def back_mid(plan, me, dmid, params, gn, rg, gate, states, kept, sub, weights):
    rows, width = dmid.shape
    half = width // 2
    return pl.pallas_call(
        functools.partial(back_mid_kernel, plan, len(weights)),
        out_shape=(
            sds((rows, width), BF16),
            sds((width // GROUP, rows, GROUP)),
            sds((1, width)),
            sds((2, SUB, half)),
            sds((2, half)),
        ),
        in_specs=[SMEM] + [VMEM] * 8 + [ANY] * len(weights),
        out_specs=(VMEM,) * 5,
        scratch_shapes=[
            pltpu.VMEM((rows, width), F32),
            pltpu.VMEM((width, width), BF16),
            pltpu.SemaphoreType.DMA,
        ],
        compiler_params=pltpu.CompilerParams(vmem_limit_bytes=56 << 20),
        cost_estimate=pl.CostEstimate(flops=2 * rows * width * width, bytes_accessed=8 << 20, transcendentals=0),
        name="back_mid",
    )(me, dmid, params, gn, rg, gate, states, kept, sub, *weights)


def back_two_kernel(
    plan, count, me_ref, x_ref, p_ref, dafter_ref, dgpre_ref, dstates_ref, states_ref, kept_ref, rate_ref, cpre_ref,
    first_ref, sub_ref, rsub_ref, every_ref, revery_ref, *refs
):
    w_hbm, refs = refs[:count], refs[count:]
    (
    dmixin_ref, dx_ref, gains_ref,
    work_ref, q_ref, turn_ref, start_ref, w_ref, sem,
    ) = refs
    rows, width = x_ref.shape
    half = width // 2
    block = rows // SUB
    pairs = pairs_of(plan, w_hbm, me_ref, "mix", w_ref)
    load_start(pairs, sem)
    zr = jnp.zeros((1, half), F32)
    zi = jnp.zeros((1, half), F32)
    for k in reversed(range(every_ref.shape[0])):
        at = k ^ me_ref[3]
        ar, ai = every_ref[at, 0:1, :], every_ref[at, 1:2, :]
        later = k > me_ref[0]
        nr = ar * zr + ai * zi + revery_ref[at, 0:1, :]
        ni = ar * zi - ai * zr + revery_ref[at, 1:2, :]
        zr = jnp.where(later, nr, zr)
        zi = jnp.where(later, ni, zi)
    for k in reversed(range(SUB)):
        start_ref[0, k : k + 1, :] = zr
        start_ref[1, k : k + 1, :] = zi
        ar, ai = sub_ref[0, k : k + 1, :], sub_ref[1, k : k + 1, :]
        zr, zi = (
            ar * zr + ai * zi + rsub_ref[0, k : k + 1, :],
            ar * zi - ai * zr + rsub_ref[1, k : k + 1, :],
        )
    cos, sin = turns(p_ref, half)
    tiles = half // GROUP
    zr = parts(start_ref, 0, tiles)
    zi = parts(start_ref, 1, tiles)
    angle = [jnp.zeros((SUB, GROUP), F32)] * tiles
    for j in reversed(range(block)):
        at = pl.ds(j, SUB, stride=block)
        before = pl.ds(max(j - 1, 0), SUB, stride=block)
        for t in range(tiles):
            kept = kept_ref[t, at, :]
            qr = dstates_ref[t, at, :] + zr[t]
            qi = dstates_ref[tiles + t, at, :] + zi[t]
            q_ref[t, at, :] = qr
            q_ref[tiles + t, at, :] = qi
            zr[t] = kept * (cos[t] * qr + sin[t] * qi)
            zi[t] = kept * (cos[t] * qi - sin[t] * qr)
            if j:
                sr, si = states_ref[t, before, :], states_ref[tiles + t, before, :]
            else:
                sr, si = (first_ref[k, :, t * GROUP : (t + 1) * GROUP] for k in range(2))
            turn_ref[t, at, :] = zr[t] * sr + zi[t] * si
            angle[t] = angle[t] + (zi[t] * sr - zr[t] * si)
    gains_ref[1:2, half:] = jnp.sum(jnp.concatenate(angle, axis=1), axis=0, keepdims=True)

    def activations(r):
        for t in range(tiles):
            rate = rate_ref[r, t * GROUP : (t + 1) * GROUP]
            left = 1.0 - rate
            meet = jnp.zeros_like(rate)
            for k in range(2):
                cols = slice((k * tiles + t) * GROUP, (k * tiles + t + 1) * GROUP)
                pre = cpre_ref[r, cols]
                sig = jax.nn.sigmoid(pre)
                q = q_ref[k * tiles + t, r, :]
                meet = meet + q * (pre * sig)
                dmixin_ref[r, cols] = (left * q * (sig * (1.0 + pre * (1.0 - sig)))).astype(BF16)
            dfpre = left * (turn_ref[t, r, :] - rate * meet)
            dmixin_ref[r, 2 * width + t * GROUP : 2 * width + (t + 1) * GROUP] = dfpre.astype(BF16)
            turn_ref[t, r, :] = dfpre
        dmixin_ref[r, width : 2 * width] = dgpre_ref[r, :]

    over_rows(rows, activations)
    for t in range(tiles):
        gains_ref[1:2, t * GROUP : (t + 1) * GROUP] = jnp.sum(turn_ref[t], axis=0, keepdims=True)
    load_wait(pairs, sem)
    work_ref[...] = dot_t(dmixin_ref[...], w_ref[:, : dmixin_ref.shape[1]])

    def norm_back(r):
        x = x_ref[r, :].astype(F32)
        scale = lax.rsqrt(jnp.mean(x * x, axis=1, keepdims=True) + EPS)
        normal = x * scale
        dn = work_ref[r, :]
        e = dn * p_ref[0:1, :]
        dx_ref[r, :] = dafter_ref[r, :] + scale * (e - normal * jnp.mean(e * normal, axis=1, keepdims=True))
        work_ref[r, :] = dn * normal

    over_rows(rows, norm_back)
    gains_ref[0:1, :] = jnp.sum(work_ref[...], axis=0, keepdims=True)


def back_two(plan, me, x, params, dafter, dgpre, dstates, states, kept, rate, cpre, first, sub, rsub, every, revery, weights):
    rows, width = x.shape
    half = width // 2
    return pl.pallas_call(
        functools.partial(back_two_kernel, plan, len(weights)),
        out_shape=(
            sds((rows, 2 * width + half), BF16),
            sds((rows, width)),
            sds((2, width)),
        ),
        in_specs=[SMEM] + [VMEM] * 14 + [ANY] * len(weights),
        out_specs=(VMEM,) * 3,
        scratch_shapes=[
            pltpu.VMEM((rows, width), F32),
            pltpu.VMEM((width // GROUP, rows, GROUP), F32),
            pltpu.VMEM((half // GROUP, rows, GROUP), F32),
            pltpu.VMEM((2, SUB, half), F32),
            pltpu.VMEM((width, mix_width(plan, width)), BF16),
            pltpu.SemaphoreType.DMA,
        ],
        compiler_params=pltpu.CompilerParams(vmem_limit_bytes=56 << 20),
        cost_estimate=pl.CostEstimate(flops=2 * rows * width * 5 * half, bytes_accessed=10 << 20, transcendentals=0),
        name="back_two",
    )(me, x, params, dafter, dgpre, dstates, states, kept, rate, cpre, first, sub, rsub, every, revery, *weights)


def row_product(left, right):
    return lax.dot_general(left, right, (((0,), (0,)), ((), ())), preferred_element_type=F32)


def export(info_ref, rels, name, grad, column, columns, keep_ref, send_ref, sem):
    chip, core = info_ref[1], info_ref[2]
    pairs = []
    for half, target in ((1 - core, send_ref), (core, keep_ref)):
        for b, (zero, one) in enumerate(zip(*rels)):
            block = chip ^ (zero + half * (one - zero))
            if name == "down":
                row, left = block * (2 * UNIT) + half * UNIT, 0
            else:
                row, left = block * UNIT, half * HALVES[name]
            pairs.append(
                (
                    grad.at[pl.ds(pl.multiple_of(row, UNIT), UNIT), pl.ds(pl.multiple_of(left, GROUP), columns)],
                    target.at[b, :, pl.ds(column, columns)],
                )
            )
    load_start(pairs, sem)
    return pairs


def products(left, right_ref, grad_ref, size):
    step = HALVES["out"]
    for k in range(size // step):
        cols = slice(k * step, (k + 1) * step)
        grad_ref[:, cols] = row_product(left, right_ref[:, cols]).astype(BF16)


def grad_ud_kernel(
    rels, info_ref, lifted_ref, dboth_ref, hidden_ref, dlow_ref, keep_ref, send_ref, up_ref, down_ref, sem
):
    width = dlow_ref.shape[1]
    products(hidden_ref[...], dlow_ref, down_ref, width)
    pairs = export(info_ref, rels, "down", down_ref, HALVES["up"], width, keep_ref, send_ref, sem)
    products(lifted_ref[...], dboth_ref, up_ref, up_ref.shape[1])
    pairs += export(info_ref, rels, "up", up_ref, 0, HALVES["up"], keep_ref, send_ref, sem)
    load_wait(pairs, sem)


def grad_ud(rels, info, lifted, dboth, hidden, dlow):
    rows, width = dlow.shape
    inner = hidden.shape[1]
    shape = sds((len(rels[0]), UNIT, HALVES["up"] + width), BF16)
    return pl.pallas_call(
        functools.partial(grad_ud_kernel, rels),
        out_shape=(shape, shape),
        in_specs=[SMEM] + [VMEM] * 4,
        out_specs=(ANY, ANY),
        scratch_shapes=[
            pltpu.VMEM((width, 2 * inner), BF16),
            pltpu.VMEM((inner, width), BF16),
            pltpu.SemaphoreType.DMA,
        ],
        compiler_params=pltpu.CompilerParams(vmem_limit_bytes=56 << 20),
        cost_estimate=pl.CostEstimate(flops=2 * rows * width * 6 * width, bytes_accessed=12 << 20, transcendentals=0),
        name="grad_ud",
    )(info, lifted, dboth, hidden, dlow)


def grad_mo_kernel(rels, info_ref, gated_ref, dmid_ref, normed_ref, dmixin_ref, *refs):
    extra, (keep_ref, send_ref, out_ref, mix_ref, held_ref, sem) = refs[:-6], refs[-6:]
    width = dmid_ref.shape[1]
    products(gated_ref[...], dmid_ref, out_ref, width)
    pairs = export(info_ref, rels, "out", out_ref, HALVES["mix"], HALVES["out"], keep_ref, send_ref, sem)
    size = dmixin_ref.shape[1]
    held_ref[...] = jnp.zeros_like(held_ref)
    for k in range(len(extra) // 3):
        two, mid_gain, ffn_gain = extra[3 * k : 3 * k + 3]
        held_ref[4 * k : 4 * k + 1, :] = two[0:1, :]
        held_ref[4 * k + 1 : 4 * k + 2, :] = mid_gain[...]
        held_ref[4 * k + 2 : 4 * k + 3, :] = ffn_gain[...]
        held_ref[4 * k + 3 : 4 * k + 4, :] = two[1:2, :]
    mix_ref[:, size:] = jnp.transpose(held_ref[...]).astype(BF16)
    products(normed_ref[...], dmixin_ref, mix_ref, size)
    pairs += export(info_ref, rels, "mix", mix_ref, 0, HALVES["mix"], keep_ref, send_ref, sem)
    load_wait(pairs, sem)


def grad_mo(rels, info, gated, dmid, normed, dmixin, extra):
    rows, width = normed.shape
    shape = sds((len(rels[0]), UNIT, HALVES["mix"] + HALVES["out"]), BF16)
    return pl.pallas_call(
        functools.partial(grad_mo_kernel, rels),
        out_shape=(shape, shape),
        in_specs=[SMEM] + [VMEM] * (4 + len(extra)),
        out_specs=(ANY, ANY),
        scratch_shapes=[
            pltpu.VMEM((width, width), BF16),
            pltpu.VMEM((width, 2 * HALVES["mix"]), BF16),
            pltpu.VMEM((GROUP, width), F32),
            pltpu.SemaphoreType.DMA,
        ],
        compiler_params=pltpu.CompilerParams(vmem_limit_bytes=56 << 20),
        cost_estimate=pl.CostEstimate(flops=7 * rows * width * width, bytes_accessed=6 << 20, transcendentals=0),
        name="grad_mo",
    )(info, gated, dmid, normed, dmixin, *extra)


def table_kernel(plan, count, me_ref, *refs):
    sources, (table_ref, held_ref, sem) = refs[:count], refs[count:]
    pairs = pairs_of(plan, sources, me_ref, "small", held_ref)
    load_start(pairs, sem)
    load_wait(pairs, sem)
    depth = table_ref.shape[0]
    half = table_ref.shape[2] // 2
    table = jnp.transpose(held_ref[:, GROUP:].astype(F32))
    table_ref[...] = jnp.zeros_like(table_ref)
    for l in range(depth):
        chan = table[3 * depth + l : 3 * depth + l + 1]
        table_ref[l, 0:3, :] = table[3 * l : 3 * l + 3]
        table_ref[l, 3:4, :half] = chan[:, :half]
        table_ref[l, 3:4, half:] = jnp.cos(chan[:, half:])
        table_ref[l, 4:5, :half] = jnp.sin(chan[:, half:])


def table_of(plan, me, weights, depth, width):
    return pl.pallas_call(
        functools.partial(table_kernel, plan, len(weights)),
        out_shape=sds((depth, 8, width)),
        in_specs=[SMEM] + [ANY] * len(weights),
        out_specs=VMEM,
        scratch_shapes=[pltpu.VMEM((width, 2 * GROUP), BF16), pltpu.SemaphoreType.DMA],
        compiler_params=pltpu.CompilerParams(vmem_limit_bytes=16 << 20),
        cost_estimate=pl.CostEstimate(flops=1 << 20, bytes_accessed=1 << 20, transcendentals=0),
        name="table",
    )(me, *weights)


def swap(x, bits):
    count = lax.axis_size("dp") * lax.axis_size("seq")
    return lax.ppermute(x, ALL, [(i, i ^ bits[i % 2]) for i in range(count)])


def hold(values, *after):
    return lax.optimization_barrier(tuple(values) + after)[: len(values)]


def rels_of(stages):
    rels = ([0], [0])
    for bits in stages:
        for core in range(2):
            rels[core].extend([rel ^ bits[core] for rel in rels[core]])
    return rels


class Spread:
    def __init__(self, unit, stages):
        self.held, self.stages, self.at = unit[None], stages, 0
        self.got = None

    def join(self):
        if self.got is not None:
            self.held = jnp.concatenate([self.held, self.got])

    def next(self):
        self.join()
        one, two = self.stages[self.at]
        self.at += 1
        self.got = swap(self.held, (2 * one, 2 * two))

    def end(self):
        self.near, self.last = self.held, self.got
        self.last_core = swap(self.last, (1, 1))

    def near_core(self):
        self.held_core = swap(self.held, (1, 1))

    def arrays(self):
        return (self.near, self.held_core, self.last, self.last_core)

    def sources(self):
        rels = rels_of(self.stages)
        half = len(rels[0]) // 2
        low = tuple(tuple(rel[:half]) for rel in rels)
        high = tuple(tuple(rel[half:]) for rel in rels)
        return ((0, low), (1, low), (0, high), (1, high))


class Reduce:
    def __init__(self, keep, send, stages):
        self.held, self.stages = keep, list(stages)
        self.got = swap(send, (1, 1))

    def add(self):
        half = self.held.shape[0] // 2
        if not half:
            return self.held[0].astype(F32) + self.got[0].astype(F32)

        def joined(part):
            return (self.held[part].astype(F32) + self.got[part].astype(F32)).astype(BF16)

        self.low, self.high = joined(slice(0, half)), joined(slice(half, None))

    def next(self):
        self.add()
        one, two = self.stages.pop()
        self.got = swap(self.high, (2 * one, 2 * two))
        self.held = self.low


def exchange(x):
    pair = jnp.stack([x, swap(x, (1, 1))])
    got = [swap(pair, (k, k)) for k in range(2, lax.axis_size("seq"), 2)]
    return jnp.concatenate([pair] + got)


def finish_kernel(info_ref, *refs):
    depth = (len(refs) - 5) // 3
    mine, other, downs = refs[:depth], refs[depth : 2 * depth], refs[2 * depth : 3 * depth]
    mix_ref, out_ref, up_ref, down_ref, tail_ref = refs[3 * depth :]
    width = down_ref.shape[2]
    mix_cols = mix_ref.shape[2]
    size = HALVES["mix"]

    def place(first, second):
        for l in range(depth):
            mix_ref[l, :, :size] = first[l][:, :size]
            mix_ref[l, :, size:] = second[l][:, : mix_cols - size]
            at = size
            for name, ref in (("out", out_ref), ("up", up_ref)):
                step = HALVES[name]
                ref[l, :, :step] = first[l][:, at : at + step]
                ref[l, :, step:] = second[l][:, at : at + step]
                at += step
        tail_ref[...] = second[0][:, size - GROUP : size]

    @pl.when(info_ref[2] == 0)
    def _():
        place(mine, other)

    @pl.when(info_ref[2] == 1)
    def _():
        place(other, mine)

    for l in range(depth):
        down_ref[l] = downs[l][:, downs[l].shape[1] - width :]


def finish(info, mine, other, downs, shapes):
    share = mine[0].shape[0]
    return pl.pallas_call(
        finish_kernel,
        out_shape=tuple(sds(shape) for shape in shapes) + (sds((share, GROUP)),),
        in_specs=[SMEM] + [VMEM] * (3 * len(mine)),
        out_specs=(VMEM,) * 5,
        compiler_params=pltpu.CompilerParams(vmem_limit_bytes=32 << 20),
        cost_estimate=pl.CostEstimate(flops=1 << 20, bytes_accessed=6 << 20, transcendentals=0),
        name="finish",
    )(info, *mine, *other, *downs)


def layer_params(gains, chan):
    half = chan.shape[0] // 2
    angle = chan[half:]
    rows = [
        gains[0],
        gains[1],
        gains[2],
        jnp.concatenate([chan[:half], jnp.cos(angle)]),
        jnp.concatenate([jnp.sin(angle), jnp.zeros((half,), F32)]),
    ]
    return jnp.concatenate([jnp.stack(rows), jnp.zeros((3, 2 * half), F32)], axis=0)


STAGES = ((4, 8), (8, 4), (1, 2), (2, 1))


def small_of(gains, chan_params):
    depth, _, share = gains.shape
    return jnp.concatenate(
        [gains.reshape(depth * 3, share).T, chan_params.T, jnp.zeros((share, GROUP - 4 * depth), BF16)], axis=1
    )


def info_of(lengths, rows, turned):
    where = lax.axis_index("seq")
    base = where * rows
    ends = [lengths[0, 0]]
    for j in range(1, lengths.shape[1]):
        ends.append(ends[-1] + lengths[0, j])
    chip = (lax.axis_index("dp") * lax.axis_size("seq") + where) // 2
    values = [where, chip, where % 2, where if turned else jnp.zeros_like(where), ends[-1] - base]
    values += [end - lengths[0, j] - base for j, end in enumerate(ends)]
    return jnp.stack([value.astype(jnp.int32) for value in values])


def plain_body(stream, w_mix, w_out, w_up, w_down, gains, chan_params, lengths, cotangent):
    rows, width = stream.shape
    depth = w_mix.shape[0]
    info = info_of(lengths, rows, False)
    small = small_of(gains, chan_params)
    table = lax.all_gather(small, ALL, axis=0, tiled=True)[:, : 4 * depth].T.astype(F32)
    params = [layer_params(table[3 * l : 3 * l + 3], table[3 * depth + l]) for l in range(depth)]
    weights = [
        tuple(lax.all_gather(w[l], ALL, axis=0, tiled=True) for w in (w_mix, w_out, w_up, w_down))
        for l in range(depth)
    ]
    x = stream
    saved = []
    for l in range(depth):
        head = front(None, info, x, params[l], weights[l])
        every = lax.all_gather(head[-1], "seq")
        middle = mid(None, info, x, params[l], head[2], head[4], head[5], head[6], every, weights[l])
        tail = ffn(None, info, middle[5], middle[6], weights[l], F32)
        saved.append((x, every, head, middle, tail))
        x = tail[-1]
    mixed = x.astype(BF16)
    dx = cotangent
    sums = [None] * depth
    for l in reversed(range(depth)):
        x, every, (normed, cpre, gate, rate, kept, feed, sub, _), middle, (both, hidden, _) = saved[l]
        states, first, gn, rg, gated, after, lifted = middle
        dlow, dboth, dafter, dmid, ffn_gain = back_ffn(None, info, dx, params[l], both, after, weights[l])
        dgpre, dstates, mid_gain, rsub, rtotal = back_mid(
            None, info, dmid, params[l], gn, rg, gate, states, kept, sub, weights[l]
        )
        revery = lax.all_gather(rtotal, "seq")
        dmixin, dx, gains_b = back_two(
            None, info, x, params[l], dafter, dgpre, dstates, states, kept, rate, cpre, first, sub, rsub, every, revery,
            weights[l],
        )
        grads = [row_product(normed, dmixin), row_product(gated, dmid), row_product(lifted, dboth), row_product(hidden, dlow)]
        grads.append(jnp.stack([gains_b[0], mid_gain[0], ffn_gain[0], gains_b[1]], axis=1))
        sums[l] = [lax.psum_scatter(g.astype(BF16), ALL, scatter_dimension=0, tiled=True).astype(F32) for g in grads]
    outs = [jnp.stack([sums[l][k] for l in range(depth)]) for k in range(5)]
    tail = outs.pop()
    return (mixed, dx, *outs, jnp.swapaxes(tail[:, :, :3], 1, 2), tail[:, :, 3])


def fast_body(stream, w_mix, w_out, w_up, w_down, gains, chan_params, lengths, cotangent):
    rows, width = stream.shape
    depth, share, mix_cols = w_mix.shape
    info = info_of(lengths, rows, True)
    small = small_of(gains, chan_params)
    core = lax.axis_index("seq") % 2
    padding = jnp.zeros((share, 2 * HALVES["mix"] - mix_cols - GROUP), BF16)
    halves = ([], [])
    for l in range(depth):
        mix = jnp.concatenate([w_mix[l], padding, small if l == 0 else jnp.zeros_like(small)], axis=1)
        for h in range(2):
            for w, size in ((mix, HALVES["mix"]), (w_out[l], HALVES["out"]), (w_up[l], HALVES["up"])):
                halves[h].append(w[:, h * size : (h + 1) * size])
    halves = [jnp.concatenate(half, axis=1) for half in halves]
    mine = jnp.where(core == 0, halves[0], halves[1])
    other = swap(jnp.where(core == 0, halves[1], halves[0]), (1, 1))
    units = jnp.where(core == 0, jnp.concatenate([mine, other]), jnp.concatenate([other, mine]))
    joint = HALVES["mix"] + HALVES["out"]
    size = joint + HALVES["up"]
    mos, uds = [], []
    for l in range(depth):
        unit = units[:, l * size : (l + 1) * size]
        mos.append(Spread(unit[:, :joint], STAGES))
        uds.append(Spread(jnp.concatenate([unit[:, joint:], w_down[l]], axis=1), STAGES))
    rels = rels_of(STAGES)
    plan = {
        "sources": mos[0].sources(),
        "mix": (0, HALVES["mix"]),
        "out": (HALVES["mix"], HALVES["out"]),
        "small": (HALVES["mix"] - GROUP, GROUP),
        "up": (0, HALVES["up"]),
        "down": (HALVES["up"], width),
    }

    x = stream
    saved = []
    mo, ud = mos[0], uds[0]
    mo.next()
    mo.next()
    (ud.held,) = hold((ud.held,), mo.held)
    ud.next()
    mo.next()
    (ud.got,) = hold((ud.got,), mo.held)
    ud.next()
    mo.next()
    mo.near_core()
    mo.end()
    params = table_of(plan, info, mo.arrays(), depth, width)
    for l in range(depth):
        mo, ud = mos[l], uds[l]
        (ud.got,) = hold((ud.got,), mo.last)
        ud.next()
        if l + 1 < depth:
            (mos[l + 1].held,) = hold((mos[l + 1].held,), ud.held)
            mos[l + 1].next()
        head = front(plan, info, x, params[l], mo.arrays())
        every = exchange(head[-1])
        (ud.got,) = hold((ud.got,), every)
        ud.next()
        ud.near_core()
        if l + 1 < depth:
            (mos[l + 1].got,) = hold((mos[l + 1].got,), ud.held)
            mos[l + 1].next()
        middle = mid(plan, info, x, params[l], head[2], head[4], head[5], head[6], every, mo.arrays())
        (ud.got,) = hold((ud.got,), middle[-1])
        ud.end()
        if l + 1 < depth:
            (mos[l + 1].got,) = hold((mos[l + 1].got,), ud.last)
            mos[l + 1].next()
            (uds[l + 1].held,) = hold((uds[l + 1].held,), mos[l + 1].held)
            uds[l + 1].next()
        tail = ffn(plan, info, middle[5], middle[6], ud.arrays(), F32 if l + 1 < depth else BF16)
        saved.append((x, every, head, middle, tail))
        x = tail[-1]
        if l + 1 < depth:
            (mos[l + 1].got,) = hold((mos[l + 1].got,), x)
            mos[l + 1].next()
            mos[l + 1].near_core()
            (uds[l + 1].got,) = hold((uds[l + 1].got,), mos[l + 1].held)
            uds[l + 1].next()
            mos[l + 1].end()
    mixed = x
    dx = cotangent
    sums = [None] * depth
    extra = ()
    for l in reversed(range(depth)):
        x, every, (normed, cpre, gate, rate, kept, feed, sub, _), middle, (both, hidden, _) = saved[l]
        states, first, gn, rg, gated, after, lifted = middle
        dlow, dboth, dafter, dmid, ffn_gain = back_ffn(plan, info, dx, params[l], both, after, uds[l].arrays())
        above = sums[l + 1] if l + 1 < depth else None
        if above:
            above[0].got, above[1].got = hold((above[0].got, above[1].got), dlow)
            above[1].next()
            above[0].next()
            (lifted,) = hold((lifted,), above[1].high)
        ud = Reduce(*grad_ud(rels, info, lifted, dboth, hidden, dlow), STAGES)
        (dmid,) = hold((dmid,), ud.held)
        dgpre, dstates, mid_gain, rsub, rtotal = back_mid(
            plan, info, dmid, params[l], gn, rg, gate, states, kept, sub, mos[l].arrays()
        )
        revery = exchange(rtotal)
        (ud.got,) = hold((ud.got,), rtotal)
        if above:
            above[1].got, above[0].got = hold((above[1].got, above[0].got), rtotal)
            above[1].next()
            above[0].next()
        ud.next()
        (dstates,) = hold((dstates,), ud.high)
        dmixin, dx, gains_b = back_two(
            plan, info, x, params[l], dafter, dgpre, dstates, states, kept, rate, cpre, first, sub, rsub, every, revery,
            mos[l].arrays(),
        )
        extra = (gains_b, mid_gain, ffn_gain) + extra
        if above:
            above[1].got, above[0].got = hold((above[1].got, above[0].got), dmixin)
            above[0].next()
        mo = Reduce(*grad_mo(rels, info, gated, dmid, normed, dmixin, extra if l == 0 else ()), STAGES)
        (ud.got,) = hold((ud.got,), mo.held)
        ud.next()
        mo.next()
        if l:
            (dx,) = hold((dx,), mo.high, ud.high)
        sums[l] = (mo, ud)
    mo, ud = sums[0]
    mo.next()
    ud.next()
    mo.next()
    ud.next()
    mo.next()
    mine, other, downs = [], [], []
    for mo, ud in sums:
        ready = ud.add()
        line = jnp.concatenate([mo.add(), ready[:, : HALVES["up"]]], axis=1)
        first, second = line[:share], line[share:]
        mine.append(jnp.where(core == 0, first, second))
        other.append(swap(jnp.where(core == 0, second, first), (1, 1)))
        downs.append(ready)
    shapes = (w_mix.shape, w_out.shape, w_up.shape, w_down.shape)
    *grads, tail = finish(info, mine, other, downs, shapes)
    tail = tail[:, : 4 * depth].T.reshape(depth, 4, share)
    return (mixed, dx, *grads, tail[:, :3], tail[:, 3])


def body(stream, w_mix, *others):
    n_dp, n_seq = lax.axis_size("dp"), lax.axis_size("seq")
    fast = n_seq == 8 and n_dp & (n_dp - 1) == 0 and 2 * w_mix.shape[1] == UNIT
    return (fast_body if fast else plain_body)(stream, w_mix, *others)


def solution(mesh):
    placed = (
        P(ALL, None),
        P(None, ALL, None),
        P(None, ALL, None),
        P(None, ALL, None),
        P(None, ALL, None),
        P(None, None, ALL),
        P(None, ALL),
        P("dp", None),
        P(ALL, None),
    )
    return jax.shard_map(
        body,
        mesh=mesh,
        in_specs=placed,
        out_specs=(
            P(ALL, None),
            P(ALL, None),
            P(None, ALL, None),
            P(None, ALL, None),
            P(None, ALL, None),
            P(None, ALL, None),
            P(None, None, ALL),
            P(None, ALL),
        ),
        check_vma=False,
    )
```

time: 556 us -> 454 us (0.82)
  blocking collectives: 40.3 us -> 0 us
  local copies, waits for them, and re-layouts: 49.8 us -> 19.7 us
  starting transfers between devices: 90 us -> 63.7 us
  other arithmetic: 36.8 us -> 17.7 us
  Pallas kernels: 107 us -> 123 us
    all_gather x4 -> x0, blocking collectives: 40.3 us -> none  [the longest x2 20.6 us: body(): every = lax.all_gather(total, 'seq')]
    ppermute x79 -> x63, starting transfers between devices: 90 us -> 63.7 us  [swap(): return lax.ppermute(x, ALL, [(i, i ^ bits[i % 2]) for i in range(count)])]
    slice x41 -> x6, local copies, waits for them, and re-layouts: 19.2 us -> 1.2 us  [the longest x1 0.59 us: info_of(): ends.append(ends[-1] + lengths[0, j])]
    pallas_call x8 -> x13, Pallas kernels: 75.9 us -> 92 us  [the longest x2 20.5 us: back_ffn(): pl.pallas_call(functools.partial(back_ffn_kernel, plan, len(weights)), ou...]
    select_n x6 -> x4, other arithmetic: 7.47 us -> 0.25 us  [the longest x1 0.09 us: fast_body(): jnp.where(core == 0, jnp.concatenate([mine, other]), jnp.concatenate([oth...]
    concatenate x13 -> x7, other arithmetic: 6.77 us -> 0.44 us  [join(): self.held = jnp.concatenate([self.held, self.got])]
    ppermute x79 -> x63, waiting for transfers between devices: 220 us -> 217 us  [swap(): return lax.ppermute(x, ALL, [(i, i ^ bits[i % 2]) for i in range(count)])]
    convert_element_type x23 -> x16, other arithmetic: 12.2 us -> 13.7 us  [joined(): (self.held[part].astype(F32) + self.got[part].astype(F32)).astype(BF16)]
  transfers between devices with their start and end apart: 79 -> 63, of which waited for: 32 -> 35; matrix products, arithmetic and copies ran while one was open for 10% -> 3% of each run, Pallas kernels for 12% -> 14%
where the time goes in v2:
time: 454 us; the launch traced here: 445 us
  waiting for transfers between devices  217 us (48%)
  Pallas kernels  123 us (27%)
  starting transfers between devices  63.7 us (14%)
  local copies, waits for them, and re-layouts  19.7 us (4%)
  other arithmetic  17.7 us (4%)
  between operations  4.66 us (1%)
    ppermute x63, waiting for transfers between devices, swap(): return lax.ppermute(x, ALL, [(i, i ^ bits[i % 2]) for i in range(count)])  217 us
    ppermute x63, starting transfers between devices, swap(): return lax.ppermute(x, ALL, [(i, i ^ bits[i % 2]) for i in range(count)])  63.7 us
    pallas_call x2, Pallas kernels, back_ffn(): pl.pallas_call(functools.partial(back_ffn_kernel, plan, len(weights)), ou...  20.5 us
    pallas_call x2, Pallas kernels, back_two(): pl.pallas_call(functools.partial(back_two_kernel, plan, len(weights)), ou...  17.1 us
    pallas_call x2, Pallas kernels, back_mid(): pl.pallas_call(functools.partial(back_mid_kernel, plan, len(weights)), ou...  15.8 us
    pallas_call x2, Pallas kernels, ffn(): pl.pallas_call(functools.partial(ffn_kernel, plan, len(weights)), out_sha...  15.5 us
    pallas_call x2, Pallas kernels, mid(): pl.pallas_call(functools.partial(mid_kernel, plan, len(weights)), out_sha...  15 us
    convert_element_type x16, other arithmetic, joined(): (self.held[part].astype(F32) + self.got[part].astype(F32)).astype(BF16)  13.7 us
  transfers between devices with their start and end apart: 63, of which 35 were waited for; matrix products, arithmetic and copies ran while one was open for 3% of the time, Pallas kernels for 14%

profile of v2, /device:TPU:0, one launch (start us, length us, event | category | flops | bytes accessed | tf_op | source)
XLA Modules:
  0.0 445.5 jit_solution(9650815248462822796)
XLA Ops:
  7.1 3.0 collective-permute-start.1
  10.1 4.1 collective-permute-done.1
  16.7 6.3 %collective-permute-done.2 = bf16[2,48,1408]{2,1,0:T(8,128)(2,1)S(1)} collective-permute-done((bf16[2,48,1408]{2,1,0:T(8,128)(2,1)S(1)}, bf16[2,48,1408]{2,1,0:T(8,128)(2,1)S(1)}, u32[]{:S(2)}, u32[]{:S(2)}) %collective-permute-start.2) | collective-permute-done | bytes 270368 | tf_op jit(solution)/shard_map/ppermute | solution.py:734
  23.2 2.9 collective-permute-start.3
  26.0 7.3 %collective-permute-done.3 = bf16[4,48,1408]{2,1,0:T(8,128)(2,1)S(1)} collective-permute-done((bf16[4,48,1408]{2,1,0:T(8,128)(2,1)S(1)}, bf16[4,48,1408]{2,1,0:T(8,128)(2,1)S(1)}, u32[]{:S(2)}, u32[]{:S(2)}) %collective-permute-start.3) | collective-permute-done | bytes 540704 | tf_op jit(solution)/shard_map/ppermute | solution.py:734
  35.7 3.0 collective-permute-start.11
  42.9 5.8 %collective-permute-done.5.refs_2_ = bf16[8,48,1408]{2,1,0:T(8,128)(2,1)S(1)} collective-permute-done((bf16[8,48,1408]{2,1,0:T(8,128)(2,1)S(1)}, bf16[8,48,1408]{2,1,0:T(8,128)(2,1)S(1)}, u32[]{:S(2)}, u32[]{:S(2)}) %collective-permute-start.5) | collective-permute-done | bytes 1081376 | tf_op jit(solution)/shard_map/ppermute | solution.py:734
  51.6 8.1 %collective-permute-done.12 = bf16[2,48,2304]{2,1,0:T(8,128)(2,1)S(1)} collective-permute-done((bf16[2,48,2304]{2,1,0:T(8,128)(2,1)S(1)}, bf16[2,48,2304]{2,1,0:T(8,128)(2,1)S(1)}, u32[]{:S(2)}, u32[]{:S(2)}) %collective-permute-start.12) | collective-permute-done | bytes 442400 | tf_op jit(solution)/shard_map/ppermute | solution.py:734
  65.0 6.3 %front.2 = (bf16[256,768]{1,0:T(8,128)(2,1)}, f32[256,768]{1,0:T(8,128)}, f32[256,768]{1,0:T(8,128)}, f32[256,384]{1,0:T(8,128)}, f32[3,256,128]{2,1,0:T(8,128)}...) custom-call(s32[8]{0:T(128)} %copy-done.6, bf16[256,768]{1,0:T(8,128)(2,1)} %x_ref.5, ...), custom_call_target="tpu_custom_call" | custom-call | flops 754974720 | bytes 8388608 | tf_op jit(solution)/shard_map/front/pallas_call | solution.py:179
  78.6 3.1 collective-permute-done.8
  83.6 7.5 %mid.2 = (f32[6,256,128]{2,1,0:T(8,128)}, f32[2,8,384]{2,1,0:T(8,128)}, f32[256,768]{1,0:T(8,128)}, f32[256,128]{1,0:T(8,128)}, bf16[256,768]{1,0:T(8,128)(2,1)}...) custom-call(s32[8]{0:T(128)} %copy-done.6, bf16[256,768]{1,0:T(8,128)(2,1)} %x_ref.5, f32[8,768]{1,0:T(8,128)} %get-tuple-element.287.p_ref, ...), custom_call_target="tpu_custom_call" | custom-call | flops 301989888 | bytes 8388608 | tf_op jit(solution)/shard_map/mid/pallas_call | solution.py:267
  91.1 14.5 %collective-permute-done.15.refs_2_ = bf16[8,48,2304]{2,1,0:T(8,128)(2,1)S(1)} collective-permute-done((bf16[8,48,2304]{2,1,0:T(8,128)(2,1)S(1)}, bf16[8,48,2304]{2,1,0:T(8,128)(2,1)S(1)}, u32[]{:S(2)}, u32[]{:S(2)}) %collective-permute-start.15) | collective-permute-done | bytes 1769504 | tf_op jit(solution)/shard_map/ppermute | solution.py:734
  105.6 3.0 collective-permute-start.17
  108.7 4.2 collective-permute-done.17
  116.2 7.1 %collective-permute-done.18 = bf16[2,48,1408]{2,1,0:T(8,128)(2,1)S(1)} collective-permute-done((bf16[2,48,1408]{2,1,0:T(8,128)(2,1)S(1)}, bf16[2,48,1408]{2,1,0:T(8,128)(2,1)S(1)}, u32[]{:S(2)}, u32[]{:S(2)}) %collective-permute-start.18) | collective-permute-done | bytes 270368 | tf_op jit(solution)/shard_map/ppermute | solution.py:734
  126.4 7.8 %ffn.2 = (f32[256,3072]{1,0:T(8,128)}, bf16[256,1536]{1,0:T(8,128)(2,1)}, f32[256,768]{1,0:T(8,128)}) custom-call(s32[8]{0:T(128)} %copy-done.6, f32[256,768]{1,0:T(8,128)} %get-tuple-element.118.after_ref, bf16[256,768]{1,0:T(8,128)(2,1)} %get-tuple-element.177.lifted_ref, bf16[8,48,2304]{2,1,0:T(8,128)(2,1)} %copy-done.13, ...), custom_call_target="tpu_custom_call" | custom-call | flops 1811939328 | bytes 14680064 | tf_op jit(solution)/shard_map/ffn/pallas_call | solution.py:313
  135.8 6.6 %collective-permute-done.27 = bf16[1,48,2304]{2,1,0:T(8,128)(2,1)S(1)} collective-permute-done((bf16[1,48,2304]{2,1,0:T(8,128)(2,1)S(1)}, bf16[1,48,2304]{2,1,0:T(8,128)(2,1)S(1)}, u32[]{:S(2)}, u32[]{:S(2)}) %collective-permute-start.27) | collective-permute-done | bytes 221216 | tf_op jit(solution)/shard_map/ppermute | solution.py:734
  143.5 6.0 %collective-permute-done.21.refs_2_ = bf16[8,48,1408]{2,1,0:T(8,128)(2,1)S(1)} collective-permute-done((bf16[8,48,1408]{2,1,0:T(8,128)(2,1)S(1)}, bf16[8,48,1408]{2,1,0:T(8,128)(2,1)S(1)}, u32[]{:S(2)}, u32[]{:S(2)}) %collective-permute-start.21) | collective-permute-done | bytes 1081376 | tf_op jit(solution)/shard_map/ppermute | solution.py:734
  149.6 6.6 %collective-permute-done.28 = bf16[2,48,2304]{2,1,0:T(8,128)(2,1)S(1)} collective-permute-done((bf16[2,48,2304]{2,1,0:T(8,128)(2,1)S(1)}, bf16[2,48,2304]{2,1,0:T(8,128)(2,1)S(1)}, u32[]{:S(2)}, u32[]{:S(2)}) %collective-permute-start.28) | collective-permute-done | bytes 442400 | tf_op jit(solution)/shard_map/ppermute | solution.py:734
  159.0 6.4 %front.3 = (bf16[256,768]{1,0:T(8,128)(2,1)}, f32[256,768]{1,0:T(8,128)}, f32[256,768]{1,0:T(8,128)}, f32[256,384]{1,0:T(8,128)}, f32[3,256,128]{2,1,0:T(8,128)}...) custom-call(s32[8]{0:T(128)} %copy-done.6, f32[256,768]{1,0:T(8,128)} %get-tuple-element.125.x_ref, ...), custom_call_target="tpu_custom_call" | custom-call | flops 754974720 | bytes 8388608 | tf_op jit(solution)/shard_map/front/pallas_call | solution.py:179
  175.0 7.6 %mid.3 = (f32[6,256,128]{2,1,0:T(8,128)}, f32[2,8,384]{2,1,0:T(8,128)}, f32[256,768]{1,0:T(8,128)}, f32[256,128]{1,0:T(8,128)}, bf16[256,768]{1,0:T(8,128)(2,1)}...) custom-call(s32[8]{0:T(128)} %copy-done.6, f32[256,768]{1,0:T(8,128)} %get-tuple-element.125.x_ref, ...), custom_call_target="tpu_custom_call" | custom-call | flops 301989888 | bytes 8388608 | tf_op jit(solution)/shard_map/mid/pallas_call | solution.py:267
  182.6 13.7 %collective-permute-done.31.refs_2_ = bf16[8,48,2304]{2,1,0:T(8,128)(2,1)S(1)} collective-permute-done((bf16[8,48,2304]{2,1,0:T(8,128)(2,1)S(1)}, bf16[8,48,2304]{2,1,0:T(8,128)(2,1)S(1)}, u32[]{:S(2)}, u32[]{:S(2)}) %collective-permute-start.31) | collective-permute-done | bytes 1769504 | tf_op jit(solution)/shard_map/ppermute | solution.py:734
  196.3 3.7 collective-permute-done.32.refs_3_
  201.2 7.7 %ffn.3 = (f32[256,3072]{1,0:T(8,128)}, bf16[256,1536]{1,0:T(8,128)(2,1)}, bf16[256,768]{1,0:T(8,128)(2,1)}) custom-call(s32[8]{0:T(128)} %copy-done.6, f32[256,768]{1,0:T(8,128)} %get-tuple-element.135.after_ref, bf16[256,768]{1,0:T(8,128)(2,1)} %get-tuple-element.136.lifted_ref, bf16[8,48,2304]{2,1,0:T(8,128)(2,1)} %copy-done.12, ...), custom_call_target="tpu_custom_call" | custom-call | flops 1811939328 | bytes 14680064 | tf_op jit(solution)/shard_map/ffn/pallas_call | solution.py:313
  208.9 10.2 %back_ffn.2 = (bf16[256,768]{1,0:T(8,128)(2,1)}, bf16[256,3072]{1,0:T(8,128)(2,1)}, f32[256,768]{1,0:T(8,128)}, bf16[256,768]{1,0:T(8,128)(2,1)}, f32[1,768]{1,0:T(1,128)}) custom-call(s32[8]{0:T(128)} %copy-done.6, bf16[256,768]{1,0:T(8,128)(2,1)} %dx_ref.1, f32[8,768]{1,0:T(8,128)} %get-tuple-element.286.p_ref, f32[256,3072]{1,0:T(8,128)} %get-tuple-element.143.both_ref, ...), custom_call_target="tpu_custom_call" | custom-call | flops 1811939328 | bytes 14680064 | tf_op jit(solution)/shard_map/back_ffn/pallas_call | solution.py:380
  219.1 6.8 %grad_ud.2 = (bf16[16,48,2304]{2,1,0:T(8,128)(2,1)}, bf16[16,48,2304]{2,1,0:T(8,128)(2,1)}) custom-call(s32[8]{0:T(128)} %copy-done.6, bf16[256,768]{1,0:T(8,128)(2,1)} %get-tuple-element.136.lifted_ref, bf16[256,3072]{1,0:T(8,128)(2,1)} %get-tuple-element.146.dboth_ref, bf16[256,1536]{1,0:T(8,128)(2,1)} %get-tuple-element.147.hidden_ref, ...), custom_call_target="tpu_custom_call" | custom-call | flops 1811939328 | bytes 12582912 | tf_op jit(solution)/shard_map/grad_ud/pallas_call | solution.py:647
  226.1 7.6 %back_mid.2 = (bf16[256,768]{1,0:T(8,128)(2,1)}, f32[6,256,128]{2,1,0:T(8,128)}, f32[1,768]{1,0:T(1,128)}, f32[2,8,384]{2,1,0:T(8,128)}, f32[2,384]{1,0:T(2,128)}) custom-call(s32[8]{0:T(128)} %copy-done.6, bf16[256,768]{1,0:T(8,128)(2,1)} %get-tuple-element.150.dmid_ref, f32[8,768]{1,0:T(8,128)} %get-tuple-element.286.p_ref, ...), custom_call_target="tpu_custom_call" | custom-call | flops 301989888 | bytes 8388608 | tf_op jit(solution)/shard_map/back_mid/pallas_call | solution.py:461
  239.3 2.8 collective-permute-done.35
  242.2 2.8 add_convert_fusion.2
  245.1 8.6 %back_two.2 = (bf16[256,1920]{1,0:T(8,128)(2,1)}, f32[256,768]{1,0:T(8,128)}, f32[2,768]{1,0:T(2,128)}) custom-call(s32[8]{0:T(128)} %copy-done.6, f32[256,768]{1,0:T(8,128)} %get-tuple-element.125.x_ref, f32[8,768]{1,0:T(8,128)} %get-tuple-element.286.p_ref, f32[256,768]{1,0:T(8,128)} %get-tuple-element.144.dafter_ref, ...), custom_call_target="tpu_custom_call" | custom-call | flops 754974720 | bytes 10485760 | tf_op jit(solution)/shard_map/back_two/pallas_call | solution.py:578
  253.7 4.9 %grad_mo.2 = (bf16[16,48,1408]{2,1,0:T(8,128)(2,1)}, bf16[16,48,1408]{2,1,0:T(8,128)(2,1)}) custom-call(s32[8]{0:T(128)} %copy-done.6, bf16[256,768]{1,0:T(8,128)(2,1)} %get-tuple-element.165.gated_ref, bf16[256,768]{1,0:T(8,128)(2,1)} %get-tuple-element.150.dmid_ref, bf16[256,768]{1,0:T(8,128)(2,1)} %get-tuple-element.166.normed_ref, ...), custom_call_target="tpu_custom_call" | custom-call | flops 1056964608 | bytes 6291456 | tf_op jit(solution)/shard_map/grad_mo/pallas_call | solution.py:685
  260.5 20.8 %collective-permute-done.39 = bf16[8,48,2304]{2,1,0:T(8,128)(2,1)S(1)} collective-permute-done((bf16[8,48,2304]{2,1,0:T(8,128)(2,1)S(1)}, bf16[8,48,2304]{2,1,0:T(8,128)(2,1)S(1)}, u32[]{:S(2)}, u32[]{:S(2)}) %collective-permute-start.39) | collective-permute-done | bytes 1769504 | tf_op jit(solution)/shard_map/ppermute | solution.py:734
  286.0 10.4 %back_ffn.3 = (bf16[256,768]{1,0:T(8,128)(2,1)}, bf16[256,3072]{1,0:T(8,128)(2,1)}, f32[256,768]{1,0:T(8,128)}, bf16[256,768]{1,0:T(8,128)(2,1)}, f32[1,768]{1,0:T(1,128)}) custom-call(s32[8]{0:T(128)} %copy-done.6, f32[256,768]{1,0:T(8,128)} %get-tuple-element.171.dx_ref, f32[8,768]{1,0:T(8,128)} %get-tuple-element.287.p_ref, ...), custom_call_target="tpu_custom_call" | custom-call | flops 1811939328 | bytes 14680064 | tf_op jit(solution)/shard_map/back_ffn/pallas_call | solution.py:380
  296.3 10.4 %collective-permute-done.41 = bf16[4,48,2304]{2,1,0:T(8,128)(2,1)S(1)} collective-permute-done((bf16[4,48,2304]{2,1,0:T(8,128)(2,1)S(1)}, bf16[4,48,2304]{2,1,0:T(8,128)(2,1)S(1)}, u32[]{:S(2)}, u32[]{:S(2)}) %collective-permute-start.41) | collective-permute-done | bytes 884768 | tf_op jit(solution)/shard_map/ppermute | solution.py:734
  308.9 6.8 %grad_ud.3 = (bf16[16,48,2304]{2,1,0:T(8,128)(2,1)}, bf16[16,48,2304]{2,1,0:T(8,128)(2,1)}) custom-call(s32[8]{0:T(128)} %copy-done.6, bf16[256,768]{1,0:T(8,128)(2,1)} %get-tuple-element.177.lifted_ref, bf16[256,3072]{1,0:T(8,128)(2,1)} %get-tuple-element.178.dboth_ref, bf16[256,1536]{1,0:T(8,128)(2,1)} %get-tuple-element.179.hidden_ref, ...), custom_call_target="tpu_custom_call" | custom-call | flops 1811939328 | bytes 12582912 | tf_op jit(solution)/shard_map/grad_ud/pallas_call | solution.py:647
  315.8 8.1 %back_mid.3 = (bf16[256,768]{1,0:T(8,128)(2,1)}, f32[6,256,128]{2,1,0:T(8,128)}, f32[1,768]{1,0:T(1,128)}, f32[2,8,384]{2,1,0:T(8,128)}, f32[2,384]{1,0:T(2,128)}) custom-call(s32[8]{0:T(128)} %copy-done.6, bf16[256,768]{1,0:T(8,128)(2,1)} %get-tuple-element.181.dmid_ref, f32[8,768]{1,0:T(8,128)} %get-tuple-element.287.p_ref, ...), custom_call_target="tpu_custom_call" | custom-call | flops 301989888 | bytes 8388608 | tf_op jit(solution)/shard_map/back_mid/pallas_call | solution.py:461
  328.7 5.7 %collective-permute-done.44 = f32[2,2,384]{2,1,0:T(2,128)S(1)} collective-permute-done((f32[2,2,384]{2,1,0:T(2,128)S(1)}, f32[2,2,384]{2,1,0:T(2,128)S(1)}, u32[]{:S(2)}, u32[]{:S(2)}) %collective-permute-start.44) | collective-permute-done | bytes 6176 | tf_op jit(solution)/shard_map/ppermute | solution.py:734
  338.1 4.1 add_convert_fusion
  342.2 8.4 %back_two.3 = (bf16[256,1920]{1,0:T(8,128)(2,1)}, f32[256,768]{1,0:T(8,128)}, f32[2,768]{1,0:T(2,128)}) custom-call(s32[8]{0:T(128)} %copy-done.6, bf16[256,768]{1,0:T(8,128)(2,1)} %x_ref.5, f32[8,768]{1,0:T(8,128)} %get-tuple-element.287.p_ref, f32[256,768]{1,0:T(8,128)} %get-tuple-element.173.dafter_ref, bf16[256,768]{1,0:T(8,128)(2,1)} %get-tuple-element.185.dgpre_ref, ...), custom_call_target="tpu_custom_call" | custom-call | flops 754974720 | bytes 10485760 | tf_op jit(solution)/shard_map/back_two/pallas_call | solution.py:578
  350.7 5.0 %grad_mo.3 = (bf16[16,48,1408]{2,1,0:T(8,128)(2,1)}, bf16[16,48,1408]{2,1,0:T(8,128)(2,1)}) custom-call(s32[8]{0:T(128)} %copy-done.6, bf16[256,768]{1,0:T(8,128)(2,1)} %get-tuple-element.196.gated_ref, bf16[256,768]{1,0:T(8,128)(2,1)} %get-tuple-element.181.dmid_ref, bf16[256,768]{1,0:T(8,128)(2,1)} %get-tuple-element.197.normed_ref, ...), custom_call_target="tpu_custom_call" | custom-call | flops 1056964608 | bytes 6291456 | tf_op jit(solution)/shard_map/grad_mo/pallas_call | solution.py:685
  355.9 2.8 collective-permute-start.59
  361.3 8.6 %collective-permute-done.58 = bf16[1,48,2304]{2,1,0:T(8,128)(2,1)S(1)} collective-permute-done((bf16[1,48,2304]{2,1,0:T(8,128)(2,1)S(1)}, bf16[1,48,2304]{2,1,0:T(8,128)(2,1)S(1)}, u32[]{:S(2)}, u32[]{:S(2)}) %collective-permute-start.58) | collective-permute-done | bytes 221216 | tf_op jit(solution)/shard_map/ppermute | solution.py:734
  373.6 7.7 %collective-permute-done.52 = bf16[8,48,2304]{2,1,0:T(8,128)(2,1)S(1)} collective-permute-done((bf16[8,48,2304]{2,1,0:T(8,128)(2,1)S(1)}, bf16[8,48,2304]{2,1,0:T(8,128)(2,1)S(1)}, u32[]{:S(2)}, u32[]{:S(2)}) %collective-permute-start.52) | collective-permute-done | bytes 1769504 | tf_op jit(solution)/shard_map/ppermute | solution.py:734
  385.0 21.4 %collective-permute-done.48 = bf16[8,48,1408]{2,1,0:T(8,128)(2,1)S(1)} collective-permute-done((bf16[8,48,1408]{2,1,0:T(8,128)(2,1)S(1)}, bf16[8,48,1408]{2,1,0:T(8,128)(2,1)S(1)}, u32[]{:S(2)}, u32[]{:S(2)}) %collective-permute-start.48) | collective-permute-done | bytes 1081376 | tf_op jit(solution)/shard_map/ppermute | solution.py:734
  408.1 8.0 %collective-permute-done.49 = bf16[4,48,1408]{2,1,0:T(8,128)(2,1)S(1)} collective-permute-done((bf16[4,48,1408]{2,1,0:T(8,128)(2,1)S(1)}, bf16[4,48,1408]{2,1,0:T(8,128)(2,1)S(1)}, u32[]{:S(2)}, u32[]{:S(2)}) %collective-permute-start.49) | collective-permute-done | bytes 540704 | tf_op jit(solution)/shard_map/ppermute | solution.py:734
  416.6 14.3 %collective-permute-done.54 = bf16[2,48,2304]{2,1,0:T(8,128)(2,1)S(1)} collective-permute-done((bf16[2,48,2304]{2,1,0:T(8,128)(2,1)S(1)}, bf16[2,48,2304]{2,1,0:T(8,128)(2,1)S(1)}, u32[]{:S(2)}, u32[]{:S(2)}) %collective-permute-start.54) | collective-permute-done | bytes 442400 | tf_op jit(solution)/shard_map/ppermute | solution.py:734
  431.0 4.2 collective-permute-done.50
  437.6 2.7 collective-permute-done.51
  (259 shorter events, 95.3 us)
Async XLA Ops:
  7.1 7.1 %collective-permute-start.1 = (bf16[1,48,1408]{2,1,0:T(8,128)(2,1)S(1)}, bf16[1,48,1408]{2,1,0:T(8,128)(2,1)S(1)}, u32[]{:S(2)}, u32[]{:S(2)}) collective-permute-start(bf16[1,48,1408]{2,1,0:T(8,128)(2,1)S(1)} %get-tuple-element.257), channel_id=1, source_target_pairs={{0,8},{1,17},{2,10},{3,19},{4,12},{5,21},{6,14},{7,23},{8,0},{9,25... | collective-permute-start | bytes 405512 | tf_op jit(solution)/shard_map/ppermute | solution.py:734
  14.2 8.8 %collective-permute-start.2 = (bf16[2,48,1408]{2,1,0:T(8,128)(2,1)S(1)}, bf16[2,48,1408]{2,1,0:T(8,128)(2,1)S(1)}, u32[]{:S(2)}, u32[]{:S(2)}) collective-permute-start(bf16[2,48,1408]{2,1,0:T(8,128)(2,1)S(1)} %pad_maximum_fusion.7), channel_id=1, source_target_pairs={{0,16},{1,9},{2,18},{3,11},{4,20},{5,13},{6,22},{7,15},{8,24},{9,1... | collective-permute-start | bytes 811016 | tf_op jit(solution)/shard_map/ppermute | solution.py:734
  23.2 10.2 %collective-permute-start.3 = (bf16[4,48,1408]{2,1,0:T(8,128)(2,1)S(1)}, bf16[4,48,1408]{2,1,0:T(8,128)(2,1)S(1)}, u32[]{:S(2)}, u32[]{:S(2)}) collective-permute-start(bf16[4,48,1408]{2,1,0:T(8,128)(2,1)S(1)} %pad_maximum_fusion.2), channel_id=1, source_target_pairs={{0,2},{1,5},{2,0},{3,7},{4,6},{5,1},{6,4},{7,3},{8,10},{9,13},{10,... | collective-permute-start | bytes 1622024 | tf_op jit(solution)/shard_map/ppermute | solution.py:734
  33.5 15.2 %collective-permute-start.5 = (bf16[8,48,1408]{2,1,0:T(8,128)(2,1)S(1)}, bf16[8,48,1408]{2,1,0:T(8,128)(2,1)S(1)}, u32[]{:S(2)}, u32[]{:S(2)}) collective-permute-start(bf16[8,48,1408]{2,1,0:T(8,128)(2,1)S(1)} %pad_maximum_fusion.refs_0_), channel_id=1, source_target_pairs={{0,4},{1,3},{2,6},{3,1},{4,0},{5,7},{6,2},{7,5},{8,12},{9,11},{10,... | collective-permute-start | bytes 3244040 | tf_op jit(solution)/shard_map/ppermute | solution.py:734
  35.7 7.2 %collective-permute-start.11 = (bf16[1,48,2304]{2,1,0:T(8,128)(2,1)S(1)}, bf16[1,48,2304]{2,1,0:T(8,128)(2,1)S(1)}, u32[]{:S(2)}, u32[]{:S(2)}) collective-permute-start(bf16[1,48,2304]{2,1,0:T(8,128)(2,1)S(1)} %maximum_bitcast_fusion), channel_id=1, source_target_pairs={{0,8},{1,17},{2,10},{3,19},{4,12},{5,21},{6,14},{7,23},{8,0},{9,25... | collective-permute-start | bytes 663560 | tf_op jit(solution)/shard_map/ppermute | solution.py:734
  42.9 20.1 %collective-permute-start.4 = (bf16[8,48,1408]{2,1,0:T(8,128)(2,1)S(1)}, bf16[8,48,1408]{2,1,0:T(8,128)(2,1)S(1)}, u32[]{:S(2)}, u32[]{:S(2)}) collective-permute-start(bf16[8,48,1408]{2,1,0:T(8,128)(2,1)S(1)} %pad_maximum_fusion.refs_0_), channel_id=1, source_target_pairs={{0,1},{1,0},{2,3},{3,2},{4,5},{5,4},{6,7},{7,6},{8,9},{9,8},{10,11... | collective-permute-start | bytes 3244040 | tf_op jit(solution)/shard_map/ppermute | solution.py:734
  48.8 14.3 %collective-permute-start.6 = (bf16[8,48,1408]{2,1,0:T(8,128)(2,1)S(1)}, bf16[8,48,1408]{2,1,0:T(8,128)(2,1)S(1)}, u32[]{:S(2)}, u32[]{:S(2)}) collective-permute-start(bf16[8,48,1408]{2,1,0:T(8,128)(2,1)S(1)} %collective-permute-done.5.refs_2_), channel_id=1, source_target_pairs={{0,1},{1,0},{2,3},{3,2},{4,5},{5,4},{6,7},{7,6},{8,9},{9,8},{10,11... | collective-permute-start | bytes 3244040 | tf_op jit(solution)/shard_map/ppermute | solution.py:734
  48.8 10.9 %collective-permute-start.12 = (bf16[2,48,2304]{2,1,0:T(8,128)(2,1)S(1)}, bf16[2,48,2304]{2,1,0:T(8,128)(2,1)S(1)}, u32[]{:S(2)}, u32[]{:S(2)}) collective-permute-start(bf16[2,48,2304]{2,1,0:T(8,128)(2,1)S(1)} %pad_maximum_fusion.3), channel_id=1, source_target_pairs={{0,16},{1,9},{2,18},{3,11},{4,20},{5,13},{6,22},{7,15},{8,24},{9,1... | collective-permute-start | bytes 1327112 | tf_op jit(solution)/shard_map/ppermute | solution.py:734
  60.6 21.2 %collective-permute-start.13 = (bf16[4,48,2304]{2,1,0:T(8,128)(2,1)}, bf16[4,48,2304]{2,1,0:T(8,128)(2,1)}, u32[]{:S(2)}, u32[]{:S(2)}) collective-permute-start(bf16[4,48,2304]{2,1,0:T(8,128)(2,1)} %get-tuple-element.260), channel_id=1, source_target_pairs={{0,2},{1,5},{2,0},{3,7},{4,6},{5,1},{6,4},{7,3},{8,10},{9,13},{10,... | collective-permute-start | bytes 2654216 | tf_op jit(solution)/shard_map/ppermute | solution.py:734
  75.1 6.7 %collective-permute-start.10 = (f32[2,4,384]{2,1,0:T(4,128)S(1)}, f32[2,4,384]{2,1,0:T(4,128)S(1)}, u32[]{:S(2)}, u32[]{:S(2)}) collective-permute-start(f32[2,4,384]{2,1,0:T(4,128)S(1)} %pad_maximum_fusion.9), channel_id=1, source_target_pairs={{0,6},{1,7},{2,4},{3,5},{4,2},{5,3},{6,0},{7,1},{8,14},{9,15},{10,... | collective-permute-start | bytes 36872 | tf_op jit(solution)/shard_map/ppermute | solution.py:734
  83.1 22.6 %collective-permute-start.15 = (bf16[8,48,2304]{2,1,0:T(8,128)(2,1)S(1)}, bf16[8,48,2304]{2,1,0:T(8,128)(2,1)S(1)}, u32[]{:S(2)}, u32[]{:S(2)}) collective-permute-start(bf16[8,48,2304]{2,1,0:T(8,128)(2,1)S(1)} %constant_dynamic-update-slice_fusion.20.refs_0_), channel_id=1, source_target_pairs={{0,4},{1,3},{2,6},{3,1},{4,0},{5,7},{6,2},{7,5},{8,12},{9,11},{10,... | collective-permute-start | bytes 5308424 | tf_op jit(solution)/shard_map/ppermute | solution.py:734
  83.6 41.0 %collective-permute-start.14 = (bf16[8,48,2304]{2,1,0:T(8,128)(2,1)S(1)}, bf16[8,48,2304]{2,1,0:T(8,128)(2,1)S(1)}, u32[]{:S(2)}, u32[]{:S(2)}) collective-permute-start(bf16[8,48,2304]{2,1,0:T(8,128)(2,1)S(1)} %constant_dynamic-update-slice_fusion.20.refs_0_), channel_id=1, source_target_pairs={{0,1},{1,0},{2,3},{3,2},{4,5},{5,4},{6,7},{7,6},{8,9},{9,8},{10,11... | collective-permute-start | bytes 5308424 | tf_op jit(solution)/shard_map/ppermute | solution.py:734
  105.6 19.0 %collective-permute-start.16 = (bf16[8,48,2304]{2,1,0:T(8,128)(2,1)S(1)}, bf16[8,48,2304]{2,1,0:T(8,128)(2,1)S(1)}, u32[]{:S(2)}, u32[]{:S(2)}) collective-permute-start(bf16[8,48,2304]{2,1,0:T(8,128)(2,1)S(1)} %collective-permute-done.15.refs_2_), channel_id=1, source_target_pairs={{0,1},{1,0},{2,3},{3,2},{4,5},{5,4},{6,7},{7,6},{8,9},{9,8},{10,11... | collective-permute-start | bytes 5308424 | tf_op jit(solution)/shard_map/ppermute | solution.py:734
  105.6 7.3 %collective-permute-start.17 = (bf16[1,48,1408]{2,1,0:T(8,128)(2,1)S(1)}, bf16[1,48,1408]{2,1,0:T(8,128)(2,1)S(1)}, u32[]{:S(2)}, u32[]{:S(2)}) collective-permute-start(bf16[1,48,1408]{2,1,0:T(8,128)(2,1)S(1)} %get-tuple-element.126), channel_id=1, source_target_pairs={{0,8},{1,17},{2,10},{3,19},{4,12},{5,21},{6,14},{7,23},{8,0},{9,25... | collective-permute-start | bytes 405512 | tf_op jit(solution)/shard_map/ppermute | solution.py:734
  113.0 10.4 %collective-permute-start.18 = (bf16[2,48,1408]{2,1,0:T(8,128)(2,1)S(1)}, bf16[2,48,1408]{2,1,0:T(8,128)(2,1)S(1)}, u32[]{:S(2)}, u32[]{:S(2)}) collective-permute-start(bf16[2,48,1408]{2,1,0:T(8,128)(2,1)S(1)} %pad_maximum_fusion.8), channel_id=1, source_target_pairs={{0,16},{1,9},{2,18},{3,11},{4,20},{5,13},{6,22},{7,15},{8,24},{9,1... | collective-permute-start | bytes 811016 | tf_op jit(solution)/shard_map/ppermute | solution.py:734
  124.1 10.1 %collective-permute-start.19 = (bf16[4,48,1408]{2,1,0:T(8,128)(2,1)}, bf16[4,48,1408]{2,1,0:T(8,128)(2,1)S(1)}, u32[]{:S(2)}, u32[]{:S(2)}) collective-permute-start(bf16[4,48,1408]{2,1,0:T(8,128)(2,1)} %get-tuple-element.264), channel_id=1, source_target_pairs={{0,2},{1,5},{2,0},{3,7},{4,6},{5,1},{6,4},{7,3},{8,10},{9,13},{10,... | collective-permute-start | bytes 1622024 | tf_op jit(solution)/shard_map/ppermute | solution.py:734
  134.3 15.2 %collective-permute-start.21 = (bf16[8,48,1408]{2,1,0:T(8,128)(2,1)S(1)}, bf16[8,48,1408]{2,1,0:T(8,128)(2,1)S(1)}, u32[]{:S(2)}, u32[]{:S(2)}) collective-permute-start(bf16[8,48,1408]{2,1,0:T(8,128)(2,1)S(1)} %constant_dynamic-update-slice_fusion.27.refs_0_), channel_id=1, source_target_pairs={{0,4},{1,3},{2,6},{3,1},{4,0},{5,7},{6,2},{7,5},{8,12},{9,11},{10,... | collective-permute-start | bytes 3244040 | tf_op jit(solution)/shard_map/ppermute | solution.py:734
  135.6 6.7 %collective-permute-start.27 = (bf16[1,48,2304]{2,1,0:T(8,128)(2,1)S(1)}, bf16[1,48,2304]{2,1,0:T(8,128)(2,1)S(1)}, u32[]{:S(2)}, u32[]{:S(2)}) collective-permute-start(bf16[1,48,2304]{2,1,0:T(8,128)(2,1)S(1)} %maximum_bitcast_fusion.1), channel_id=1, source_target_pairs={{0,8},{1,17},{2,10},{3,19},{4,12},{5,21},{6,14},{7,23},{8,0},{9,25... | collective-permute-start | bytes 663560 | tf_op jit(solution)/shard_map/ppermute | solution.py:734
  135.7 22.0 %collective-permute-start.20 = (bf16[8,48,1408]{2,1,0:T(8,128)(2,1)S(1)}, bf16[8,48,1408]{2,1,0:T(8,128)(2,1)S(1)}, u32[]{:S(2)}, u32[]{:S(2)}) collective-permute-start(bf16[8,48,1408]{2,1,0:T(8,128)(2,1)S(1)} %constant_dynamic-update-slice_fusion.27.refs_0_), channel_id=1, source_target_pairs={{0,1},{1,0},{2,3},{3,2},{4,5},{5,4},{6,7},{7,6},{8,9},{9,8},{10,11... | collective-permute-start | bytes 3244040 | tf_op jit(solution)/shard_map/ppermute | solution.py:734
  142.4 13.8 %collective-permute-start.28 = (bf16[2,48,2304]{2,1,0:T(8,128)(2,1)S(1)}, bf16[2,48,2304]{2,1,0:T(8,128)(2,1)S(1)}, u32[]{:S(2)}, u32[]{:S(2)}) collective-permute-start(bf16[2,48,2304]{2,1,0:T(8,128)(2,1)S(1)} %pad_maximum_fusion.4), channel_id=1, source_target_pairs={{0,16},{1,9},{2,18},{3,11},{4,20},{5,13},{6,22},{7,15},{8,24},{9,1... | collective-permute-start | bytes 1327112 | tf_op jit(solution)/shard_map/ppermute | solution.py:734
  149.5 8.1 %collective-permute-start.22 = (bf16[8,48,1408]{2,1,0:T(8,128)(2,1)S(1)}, bf16[8,48,1408]{2,1,0:T(8,128)(2,1)S(1)}, u32[]{:S(2)}, u32[]{:S(2)}) collective-permute-start(bf16[8,48,1408]{2,1,0:T(8,128)(2,1)S(1)} %collective-permute-done.21.refs_2_), channel_id=1, source_target_pairs={{0,1},{1,0},{2,3},{3,2},{4,5},{5,4},{6,7},{7,6},{8,9},{9,8},{10,11... | collective-permute-start | bytes 3244040 | tf_op jit(solution)/shard_map/ppermute | solution.py:734
  156.3 17.3 %collective-permute-start.29 = (bf16[4,48,2304]{2,1,0:T(8,128)(2,1)S(1)}, bf16[4,48,2304]{2,1,0:T(8,128)(2,1)S(1)}, u32[]{:S(2)}, u32[]{:S(2)}) collective-permute-start(bf16[4,48,2304]{2,1,0:T(8,128)(2,1)S(1)} %pad_maximum_fusion.1), channel_id=1, source_target_pairs={{0,2},{1,5},{2,0},{3,7},{4,6},{5,1},{6,4},{7,3},{8,10},{9,13},{10,... | collective-permute-start | bytes 2654216 | tf_op jit(solution)/shard_map/ppermute | solution.py:734
  167.6 6.0 %collective-permute-start.26 = (f32[2,4,384]{2,1,0:T(4,128)S(1)}, f32[2,4,384]{2,1,0:T(4,128)S(1)}, u32[]{:S(2)}, u32[]{:S(2)}) collective-permute-start(f32[2,4,384]{2,1,0:T(4,128)S(1)} %pad_maximum_fusion.10), channel_id=1, source_target_pairs={{0,6},{1,7},{2,4},{3,5},{4,2},{5,3},{6,0},{7,1},{8,14},{9,15},{10,... | collective-permute-start | bytes 36872 | tf_op jit(solution)/shard_map/ppermute | solution.py:734
  173.7 22.6 %collective-permute-start.31 = (bf16[8,48,2304]{2,1,0:T(8,128)(2,1)S(1)}, bf16[8,48,2304]{2,1,0:T(8,128)(2,1)S(1)}, u32[]{:S(2)}, u32[]{:S(2)}) collective-permute-start(bf16[8,48,2304]{2,1,0:T(8,128)(2,1)S(1)} %constant_dynamic-update-slice_fusion.36.refs_0_), channel_id=1, source_target_pairs={{0,4},{1,3},{2,6},{3,1},{4,0},{5,7},{6,2},{7,5},{8,12},{9,11},{10,... | collective-permute-start | bytes 5308424 | tf_op jit(solution)/shard_map/ppermute | solution.py:734
  175.0 21.3 %collective-permute-start.30 = (bf16[8,48,2304]{2,1,0:T(8,128)(2,1)S(1)}, bf16[8,48,2304]{2,1,0:T(8,128)(2,1)S(1)}, u32[]{:S(2)}, u32[]{:S(2)}) collective-permute-start(bf16[8,48,2304]{2,1,0:T(8,128)(2,1)S(1)} %constant_dynamic-update-slice_fusion.36.refs_0_), channel_id=1, source_target_pairs={{0,1},{1,0},{2,3},{3,2},{4,5},{5,4},{6,7},{7,6},{8,9},{9,8},{10,11... | collective-permute-start | bytes 5308424 | tf_op jit(solution)/shard_map/ppermute | solution.py:734
  225.9 16.3 %collective-permute-start.33 = (bf16[16,48,2304]{2,1,0:T(8,128)(2,1)}, bf16[16,48,2304]{2,1,0:T(8,128)(2,1)}, u32[]{:S(2)}, u32[]{:S(2)}) collective-permute-start(bf16[16,48,2304]{2,1,0:T(8,128)(2,1)} %get-tuple-element.156), channel_id=1, source_target_pairs={{0,1},{1,0},{2,3},{3,2},{4,5},{5,4},{6,7},{7,6},{8,9},{9,8},{10,11... | collective-permute-start | bytes 10616840 | tf_op jit(solution)/shard_map/ppermute | solution.py:734
  235.8 6.3 %collective-permute-start.37 = (f32[2,2,384]{2,1,0:T(2,128)S(1)}, f32[2,2,384]{2,1,0:T(2,128)S(1)}, u32[]{:S(2)}, u32[]{:S(2)}) collective-permute-start(f32[2,2,384]{2,1,0:T(2,128)S(1)} %pad_maximum_fusion.11), channel_id=1, source_target_pairs={{0,6},{1,7},{2,4},{3,5},{4,2},{5,3},{6,0},{7,1},{8,14},{9,15},{10,... | collective-permute-start | bytes 18440 | tf_op jit(solution)/shard_map/ppermute | solution.py:734
  258.6 22.7 %collective-permute-start.38 = (bf16[16,48,1408]{2,1,0:T(8,128)(2,1)}, bf16[16,48,1408]{2,1,0:T(8,128)(2,1)S(1)}, u32[]{:S(2)}, u32[]{:S(2)}) collective-permute-start(bf16[16,48,1408]{2,1,0:T(8,128)(2,1)} %get-tuple-element.169), channel_id=1, source_target_pairs={{0,1},{1,0},{2,3},{3,2},{4,5},{5,4},{6,7},{7,6},{8,9},{9,8},{10,11... | collective-permute-start | bytes 6488072 | tf_op jit(solution)/shard_map/ppermute | solution.py:734
  258.7 22.6 %collective-permute-start.39 = (bf16[8,48,2304]{2,1,0:T(8,128)(2,1)S(1)}, bf16[8,48,2304]{2,1,0:T(8,128)(2,1)S(1)}, u32[]{:S(2)}, u32[]{:S(2)}) collective-permute-start(bf16[8,48,2304]{2,1,0:T(8,128)(2,1)S(1)} %get-tuple-element.229), channel_id=1, source_target_pairs={{0,4},{1,3},{2,6},{3,1},{4,0},{5,7},{6,2},{7,5},{8,12},{9,11},{10,... | collective-permute-start | bytes 5308424 | tf_op jit(solution)/shard_map/ppermute | solution.py:734
  283.4 24.3 %collective-permute-start.40 = (bf16[8,48,1408]{2,1,0:T(8,128)(2,1)S(1)}, bf16[8,48,1408]{2,1,0:T(8,128)(2,1)S(1)}, u32[]{:S(2)}, u32[]{:S(2)}) collective-permute-start(bf16[8,48,1408]{2,1,0:T(8,128)(2,1)S(1)} %get-tuple-element.231), channel_id=1, source_target_pairs={{0,4},{1,3},{2,6},{3,1},{4,0},{5,7},{6,2},{7,5},{8,12},{9,11},{10,... | collective-permute-start | bytes 3244040 | tf_op jit(solution)/shard_map/ppermute | solution.py:734
  285.6 21.1 %collective-permute-start.41 = (bf16[4,48,2304]{2,1,0:T(8,128)(2,1)S(1)}, bf16[4,48,2304]{2,1,0:T(8,128)(2,1)S(1)}, u32[]{:S(2)}, u32[]{:S(2)}) collective-permute-start(bf16[4,48,2304]{2,1,0:T(8,128)(2,1)S(1)} %get-tuple-element.237), channel_id=1, source_target_pairs={{0,2},{1,5},{2,0},{3,7},{4,6},{5,1},{6,4},{7,3},{8,10},{9,13},{10,... | collective-permute-start | bytes 2654216 | tf_op jit(solution)/shard_map/ppermute | solution.py:734
  315.7 22.5 %collective-permute-start.42 = (bf16[16,48,2304]{2,1,0:T(8,128)(2,1)}, bf16[16,48,2304]{2,1,0:T(8,128)(2,1)}, u32[]{:S(2)}, u32[]{:S(2)}) collective-permute-start(bf16[16,48,2304]{2,1,0:T(8,128)(2,1)} %get-tuple-element.187), channel_id=1, source_target_pairs={{0,1},{1,0},{2,3},{3,2},{4,5},{5,4},{6,7},{7,6},{8,9},{9,8},{10,11... | collective-permute-start | bytes 10616840 | tf_op jit(solution)/shard_map/ppermute | solution.py:734
  315.7 22.4 %collective-permute-start.56 = (bf16[2,48,2304]{2,1,0:T(8,128)(2,1)}, bf16[2,48,2304]{2,1,0:T(8,128)(2,1)}, u32[]{:S(2)}, u32[]{:S(2)}) collective-permute-start(bf16[2,48,2304]{2,1,0:T(8,128)(2,1)} %get-tuple-element.243), channel_id=1, source_target_pairs={{0,16},{1,9},{2,18},{3,11},{4,20},{5,13},{6,22},{7,15},{8,24},{9,1... | collective-permute-start | bytes 1327112 | tf_op jit(solution)/shard_map/ppermute | solution.py:734
  324.8 13.4 %collective-permute-start.57 = (bf16[4,48,1408]{2,1,0:T(8,128)(2,1)S(1)}, bf16[4,48,1408]{2,1,0:T(8,128)(2,1)S(1)}, u32[]{:S(2)}, u32[]{:S(2)}) collective-permute-start(bf16[4,48,1408]{2,1,0:T(8,128)(2,1)S(1)} %get-tuple-element.239), channel_id=1, source_target_pairs={{0,2},{1,5},{2,0},{3,7},{4,6},{5,1},{6,4},{7,3},{8,10},{9,13},{10,... | collective-permute-start | bytes 1622024 | tf_op jit(solution)/shard_map/ppermute | solution.py:734
  326.0 12.1 %collective-permute-start.46 = (f32[2,2,384]{2,1,0:T(2,128)S(1)}, f32[2,2,384]{2,1,0:T(2,128)S(1)}, u32[]{:S(2)}, u32[]{:S(2)}) collective-permute-start(f32[2,2,384]{2,1,0:T(2,128)S(1)} %pad_maximum_fusion.12), channel_id=1, source_target_pairs={{0,6},{1,7},{2,4},{3,5},{4,2},{5,3},{6,0},{7,1},{8,14},{9,15},{10,... | collective-permute-start | bytes 18440 | tf_op jit(solution)/shard_map/ppermute | solution.py:734
  327.6 6.8 %collective-permute-start.44 = (f32[2,2,384]{2,1,0:T(2,128)S(1)}, f32[2,2,384]{2,1,0:T(2,128)S(1)}, u32[]{:S(2)}, u32[]{:S(2)}) collective-permute-start(f32[2,2,384]{2,1,0:T(2,128)S(1)} %pad_maximum_fusion.12), channel_id=1, source_target_pairs={{0,2},{1,3},{2,0},{3,1},{4,6},{5,7},{6,4},{7,5},{8,10},{9,11},{10,... | collective-permute-start | bytes 18440 | tf_op jit(solution)/shard_map/ppermute | solution.py:734
  355.7 25.6 %collective-permute-start.47 = (bf16[16,48,1408]{2,1,0:T(8,128)(2,1)}, bf16[16,48,1408]{2,1,0:T(8,128)(2,1)S(1)}, u32[]{:S(2)}, u32[]{:S(2)}) collective-permute-start(bf16[16,48,1408]{2,1,0:T(8,128)(2,1)} %get-tuple-element.206), channel_id=1, source_target_pairs={{0,1},{1,0},{2,3},{3,2},{4,5},{5,4},{6,7},{7,6},{8,9},{9,8},{10,11... | collective-permute-start | bytes 6488072 | tf_op jit(solution)/shard_map/ppermute | solution.py:734
  355.9 14.1 %collective-permute-start.59 = (bf16[2,48,1408]{2,1,0:T(8,128)(2,1)S(1)}, bf16[2,48,1408]{2,1,0:T(8,128)(2,1)S(1)}, u32[]{:S(2)}, u32[]{:S(2)}) collective-permute-start(bf16[2,48,1408]{2,1,0:T(8,128)(2,1)S(1)} %get-tuple-element.247), channel_id=1, source_target_pairs={{0,16},{1,9},{2,18},{3,11},{4,20},{5,13},{6,22},{7,15},{8,24},{9,1... | collective-permute-start | bytes 811016 | tf_op jit(solution)/shard_map/ppermute | solution.py:734
  358.7 22.5 %collective-permute-start.52 = (bf16[8,48,2304]{2,1,0:T(8,128)(2,1)S(1)}, bf16[8,48,2304]{2,1,0:T(8,128)(2,1)S(1)}, u32[]{:S(2)}, u32[]{:S(2)}) collective-permute-start(bf16[8,48,2304]{2,1,0:T(8,128)(2,1)S(1)} %copy-done.23), channel_id=1, source_target_pairs={{0,4},{1,3},{2,6},{3,1},{4,0},{5,7},{6,2},{7,5},{8,12},{9,11},{10,... | collective-permute-start | bytes 5308424 | tf_op jit(solution)/shard_map/ppermute | solution.py:734
  361.0 9.0 %collective-permute-start.58 = (bf16[1,48,2304]{2,1,0:T(8,128)(2,1)S(1)}, bf16[1,48,2304]{2,1,0:T(8,128)(2,1)S(1)}, u32[]{:S(2)}, u32[]{:S(2)}) collective-permute-start(bf16[1,48,2304]{2,1,0:T(8,128)(2,1)S(1)} %add_convert_fusion.25), channel_id=1, source_target_pairs={{0,8},{1,17},{2,10},{3,19},{4,12},{5,21},{6,14},{7,23},{8,0},{9,25... | collective-permute-start | bytes 663560 | tf_op jit(solution)/shard_map/ppermute | solution.py:734
  370.0 14.8 %collective-permute-start.60 = (bf16[1,48,1408]{2,1,0:T(8,128)(2,1)S(1)}, bf16[1,48,1408]{2,1,0:T(8,128)(2,1)S(1)}, u32[]{:S(2)}, u32[]{:S(2)}) collective-permute-start(bf16[1,48,1408]{2,1,0:T(8,128)(2,1)S(1)} %add_convert_fusion.28), channel_id=1, source_target_pairs={{0,8},{1,17},{2,10},{3,19},{4,12},{5,21},{6,14},{7,23},{8,0},{9,25... | collective-permute-start | bytes 405512 | tf_op jit(solution)/shard_map/ppermute | solution.py:734
  381.8 24.6 %collective-permute-start.48 = (bf16[8,48,1408]{2,1,0:T(8,128)(2,1)S(1)}, bf16[8,48,1408]{2,1,0:T(8,128)(2,1)S(1)}, u32[]{:S(2)}, u32[]{:S(2)}) collective-permute-start(bf16[8,48,1408]{2,1,0:T(8,128)(2,1)S(1)} %get-tuple-element.233), channel_id=1, source_target_pairs={{0,4},{1,3},{2,6},{3,1},{4,0},{5,7},{6,2},{7,5},{8,12},{9,11},{10,... | collective-permute-start | bytes 3244040 | tf_op jit(solution)/shard_map/ppermute | solution.py:734
  383.6 24.0 %collective-permute-start.53 = (bf16[4,48,2304]{2,1,0:T(8,128)(2,1)S(1)}, bf16[4,48,2304]{2,1,0:T(8,128)(2,1)S(1)}, u32[]{:S(2)}, u32[]{:S(2)}) collective-permute-start(bf16[4,48,2304]{2,1,0:T(8,128)(2,1)S(1)} %get-tuple-element.235), channel_id=1, source_target_pairs={{0,2},{1,5},{2,0},{3,7},{4,6},{5,1},{6,4},{7,3},{8,10},{9,13},{10,... | collective-permute-start | bytes 2654216 | tf_op jit(solution)/shard_map/ppermute | solution.py:734
  384.9 55.6 %collective-permute-start.62 = (f32[24,2944]{1,0:T(8,128)S(1)}, f32[24,2944]{1,0:T(8,128)S(1)}, u32[]{:S(2)}, u32[]{:S(2)}) collective-permute-start(f32[24,2944]{1,0:T(8,128)S(1)} %get-tuple-element.250), channel_id=1, source_target_pairs={{0,1},{1,0},{2,3},{3,2},{4,5},{5,4},{6,7},{7,6},{8,9},{9,8},{10,11... | collective-permute-start | bytes 847880 | tf_op jit(solution)/shard_map/ppermute | solution.py:734
  406.7 9.4 %collective-permute-start.49 = (bf16[4,48,1408]{2,1,0:T(8,128)(2,1)S(1)}, bf16[4,48,1408]{2,1,0:T(8,128)(2,1)S(1)}, u32[]{:S(2)}, u32[]{:S(2)}) collective-permute-start(bf16[4,48,1408]{2,1,0:T(8,128)(2,1)S(1)} %get-tuple-element.241), channel_id=1, source_target_pairs={{0,2},{1,5},{2,0},{3,7},{4,6},{5,1},{6,4},{7,3},{8,10},{9,13},{10,... | collective-permute-start | bytes 1622024 | tf_op jit(solution)/shard_map/ppermute | solution.py:734
  407.8 23.1 %collective-permute-start.54 = (bf16[2,48,2304]{2,1,0:T(8,128)(2,1)S(1)}, bf16[2,48,2304]{2,1,0:T(8,128)(2,1)S(1)}, u32[]{:S(2)}, u32[]{:S(2)}) collective-permute-start(bf16[2,48,2304]{2,1,0:T(8,128)(2,1)S(1)} %get-tuple-element.245), channel_id=1, source_target_pairs={{0,16},{1,9},{2,18},{3,11},{4,20},{5,13},{6,22},{7,15},{8,24},{9,1... | collective-permute-start | bytes 1327112 | tf_op jit(solution)/shard_map/ppermute | solution.py:734
  416.2 19.0 %collective-permute-start.50 = (bf16[2,48,1408]{2,1,0:T(8,128)(2,1)S(1)}, bf16[2,48,1408]{2,1,0:T(8,128)(2,1)S(1)}, u32[]{:S(2)}, u32[]{:S(2)}) collective-permute-start(bf16[2,48,1408]{2,1,0:T(8,128)(2,1)S(1)} %get-tuple-element.249), channel_id=1, source_target_pairs={{0,16},{1,9},{2,18},{3,11},{4,20},{5,13},{6,22},{7,15},{8,24},{9,1... | collective-permute-start | bytes 811016 | tf_op jit(solution)/shard_map/ppermute | solution.py:734
  430.9 6.6 %collective-permute-start.55 = (bf16[1,48,2304]{2,1,0:T(8,128)(2,1)S(1)}, bf16[1,48,2304]{2,1,0:T(8,128)(2,1)S(1)}, u32[]{:S(2)}, u32[]{:S(2)}) collective-permute-start(bf16[1,48,2304]{2,1,0:T(8,128)(2,1)S(1)} %add_convert_fusion.26), channel_id=1, source_target_pairs={{0,8},{1,17},{2,10},{3,19},{4,12},{5,21},{6,14},{7,23},{8,0},{9,25... | collective-permute-start | bytes 663560 | tf_op jit(solution)/shard_map/ppermute | solution.py:734
  (49 other events, 364.1 us)

commit v3 on v2

--- a/solution.py
+++ b/solution.py
@@ -19,6 +19,7 @@
 VMEM = pl.BlockSpec(memory_space=pltpu.VMEM)
 SMEM = pl.BlockSpec(memory_space=pltpu.SMEM)
 ANY = pl.BlockSpec(memory_space=pl.ANY)
+COST = pl.CostEstimate(flops=1000, bytes_accessed=1000, transcendentals=0)
 
 
 def sds(shape, dtype=F32):
@@ -191,8 +192,8 @@
         in_specs=[SMEM, VMEM, VMEM] + [ANY] * len(weights),
         out_specs=(VMEM,) * 8,
         scratch_shapes=[pltpu.VMEM((width, mix_width(plan, width)), BF16), pltpu.SemaphoreType.DMA],
-        compiler_params=pltpu.CompilerParams(vmem_limit_bytes=56 << 20),
-        cost_estimate=pl.CostEstimate(flops=2 * rows * width * 5 * half, bytes_accessed=8 << 20, transcendentals=0),
+        compiler_params=pltpu.CompilerParams(vmem_limit_bytes=24 << 20),
+        cost_estimate=COST,
         name="front",
     )(me, x, params, *weights)
 
@@ -278,8 +279,8 @@
         in_specs=[SMEM] + [VMEM] * 7 + [ANY] * len(weights),
         out_specs=(VMEM,) * 7,
         scratch_shapes=[pltpu.VMEM((width, width), BF16), pltpu.SemaphoreType.DMA],
-        compiler_params=pltpu.CompilerParams(vmem_limit_bytes=56 << 20),
-        cost_estimate=pl.CostEstimate(flops=2 * rows * width * width, bytes_accessed=8 << 20, transcendentals=0),
+        compiler_params=pltpu.CompilerParams(vmem_limit_bytes=24 << 20),
+        cost_estimate=COST,
         name="mid",
     )(me, x, params, gate, kept, feed, sub, every, *weights)
 
@@ -320,8 +321,8 @@
             pltpu.VMEM((inner, width), BF16),
             pltpu.SemaphoreType.DMA((2,)),
         ],
-        compiler_params=pltpu.CompilerParams(vmem_limit_bytes=56 << 20),
-        cost_estimate=pl.CostEstimate(flops=2 * rows * width * 6 * width, bytes_accessed=14 << 20, transcendentals=0),
+        compiler_params=pltpu.CompilerParams(vmem_limit_bytes=24 << 20),
+        cost_estimate=COST,
         name="ffn",
     )(me, after, lifted, *weights)
 
@@ -394,8 +395,8 @@
             pltpu.VMEM((inner, width), BF16),
             pltpu.SemaphoreType.DMA((2,)),
         ],
-        compiler_params=pltpu.CompilerParams(vmem_limit_bytes=56 << 20),
-        cost_estimate=pl.CostEstimate(flops=2 * rows * width * 6 * width, bytes_accessed=14 << 20, transcendentals=0),
+        compiler_params=pltpu.CompilerParams(vmem_limit_bytes=24 << 20),
+        cost_estimate=COST,
         name="back_ffn",
     )(me, dx, params, both, after, *weights)
 
@@ -474,8 +475,8 @@
             pltpu.VMEM((width, width), BF16),
             pltpu.SemaphoreType.DMA,
         ],
-        compiler_params=pltpu.CompilerParams(vmem_limit_bytes=56 << 20),
-        cost_estimate=pl.CostEstimate(flops=2 * rows * width * width, bytes_accessed=8 << 20, transcendentals=0),
+        compiler_params=pltpu.CompilerParams(vmem_limit_bytes=24 << 20),
+        cost_estimate=COST,
         name="back_mid",
     )(me, dmid, params, gn, rg, gate, states, kept, sub, *weights)
 
@@ -592,8 +593,8 @@
             pltpu.VMEM((width, mix_width(plan, width)), BF16),
             pltpu.SemaphoreType.DMA,
         ],
-        compiler_params=pltpu.CompilerParams(vmem_limit_bytes=56 << 20),
-        cost_estimate=pl.CostEstimate(flops=2 * rows * width * 5 * half, bytes_accessed=10 << 20, transcendentals=0),
+        compiler_params=pltpu.CompilerParams(vmem_limit_bytes=24 << 20),
+        cost_estimate=COST,
         name="back_two",
     )(me, x, params, dafter, dgpre, dstates, states, kept, rate, cpre, first, sub, rsub, every, revery, *weights)
 
@@ -654,8 +655,8 @@
             pltpu.VMEM((inner, width), BF16),
             pltpu.SemaphoreType.DMA,
         ],
-        compiler_params=pltpu.CompilerParams(vmem_limit_bytes=56 << 20),
-        cost_estimate=pl.CostEstimate(flops=2 * rows * width * 6 * width, bytes_accessed=12 << 20, transcendentals=0),
+        compiler_params=pltpu.CompilerParams(vmem_limit_bytes=24 << 20),
+        cost_estimate=COST,
         name="grad_ud",
     )(info, lifted, dboth, hidden, dlow)
 
@@ -693,8 +694,8 @@
             pltpu.VMEM((GROUP, width), F32),
             pltpu.SemaphoreType.DMA,
         ],
-        compiler_params=pltpu.CompilerParams(vmem_limit_bytes=56 << 20),
-        cost_estimate=pl.CostEstimate(flops=7 * rows * width * width, bytes_accessed=6 << 20, transcendentals=0),
+        compiler_params=pltpu.CompilerParams(vmem_limit_bytes=24 << 20),
+        cost_estimate=COST,
         name="grad_mo",
     )(info, gated, dmid, normed, dmixin, *extra)
 
@@ -724,7 +725,7 @@
         out_specs=VMEM,
         scratch_shapes=[pltpu.VMEM((width, 2 * GROUP), BF16), pltpu.SemaphoreType.DMA],
         compiler_params=pltpu.CompilerParams(vmem_limit_bytes=16 << 20),
-        cost_estimate=pl.CostEstimate(flops=1 << 20, bytes_accessed=1 << 20, transcendentals=0),
+        cost_estimate=COST,
         name="table",
     )(me, *weights)
 
@@ -734,8 +735,22 @@
     return lax.ppermute(x, ALL, [(i, i ^ bits[i % 2]) for i in range(count)])
 
 
-def hold(values, *after):
-    return lax.optimization_barrier(tuple(values) + after)[: len(values)]
+class Order:
+    def __init__(self):
+        self.last = None
+
+    def step(self, *values):
+        if self.last is not None:
+            values = lax.optimization_barrier(values + (self.last,))[: len(values)]
+        self.last = values[0]
+        return values
+
+    def join(self, *moves):
+        for move in moves:
+            (move.got,) = self.step(move.got)
+
+    def join_core(self, move):
+        (move.last_core, move.held_core) = self.step(move.last_core, move.held_core)
 
 
 def rels_of(stages):
@@ -794,11 +809,14 @@
 
         self.low, self.high = joined(slice(0, half)), joined(slice(half, None))
 
-    def next(self):
-        self.add()
+    def send(self):
         one, two = self.stages.pop()
         self.got = swap(self.high, (2 * one, 2 * two))
         self.held = self.low
+
+    def next(self):
+        self.add()
+        self.send()
 
 
 def exchange(x):
@@ -847,7 +865,7 @@
         in_specs=[SMEM] + [VMEM] * (3 * len(mine)),
         out_specs=(VMEM,) * 5,
         compiler_params=pltpu.CompilerParams(vmem_limit_bytes=32 << 20),
-        cost_estimate=pl.CostEstimate(flops=1 << 20, bytes_accessed=6 << 20, transcendentals=0),
+        cost_estimate=COST,
         name="finish",
     )(info, *mine, *other, *downs)
 
@@ -964,109 +982,129 @@
         "down": (HALVES["up"], width),
     }
 
+    order = Order()
+
+    def go(move):
+        order.join(move)
+        move.next()
+
+    mo, ud = mos[0], uds[0]
+    more = depth > 1
+    ud.next()
+    mo.next()
+    go(ud)
+    go(mo)
+    go(mo)
+    if more:
+        mos[1].next()
+    go(mo)
+    mo.near_core()
+    go(ud)
+    if more:
+        go(mos[1])
+        uds[1].next()
+        order.join(mos[1])
+        go(uds[1])
+    order.join(ud)
+    order.join(mo)
+    mo.end()
+    ud.next()
+    ud.near_core()
     x = stream
     saved = []
-    mo, ud = mos[0], uds[0]
-    mo.next()
-    mo.next()
-    (ud.held,) = hold((ud.held,), mo.held)
-    ud.next()
-    mo.next()
-    (ud.got,) = hold((ud.got,), mo.held)
-    ud.next()
-    mo.next()
-    mo.near_core()
-    mo.end()
-    params = table_of(plan, info, mo.arrays(), depth, width)
+    params = None
     for l in range(depth):
         mo, ud = mos[l], uds[l]
-        (ud.got,) = hold((ud.got,), mo.last)
-        ud.next()
-        if l + 1 < depth:
-            (mos[l + 1].held,) = hold((mos[l + 1].held,), ud.held)
+        more = l + 1 < depth
+        order.join_core(mo)
+        if l == 0:
+            params = table_of(plan, info, mo.arrays(), depth, width)
+        (layer,) = order.step(params[l])
+        head = front(plan, info, x, layer, mo.arrays())
+        (total,) = order.step(head[-1])
+        every = exchange(total)
+        (every,) = order.step(every)
+        order.join(ud)
+        ud.end()
+        if more:
             mos[l + 1].next()
-        head = front(plan, info, x, params[l], mo.arrays())
-        every = exchange(head[-1])
-        (ud.got,) = hold((ud.got,), every)
-        ud.next()
-        ud.near_core()
-        if l + 1 < depth:
-            (mos[l + 1].got,) = hold((mos[l + 1].got,), ud.held)
-            mos[l + 1].next()
-        middle = mid(plan, info, x, params[l], head[2], head[4], head[5], head[6], every, mo.arrays())
-        (ud.got,) = hold((ud.got,), middle[-1])
-        ud.end()
-        if l + 1 < depth:
-            (mos[l + 1].got,) = hold((mos[l + 1].got,), ud.last)
-            mos[l + 1].next()
-            (uds[l + 1].held,) = hold((uds[l + 1].held,), mos[l + 1].held)
             uds[l + 1].next()
-        tail = ffn(plan, info, middle[5], middle[6], ud.arrays(), F32 if l + 1 < depth else BF16)
-        saved.append((x, every, head, middle, tail))
-        x = tail[-1]
-        if l + 1 < depth:
-            (mos[l + 1].got,) = hold((mos[l + 1].got,), x)
-            mos[l + 1].next()
+        middle = mid(plan, info, x, layer, head[2], head[4], head[5], head[6], order.step(every)[0], mo.arrays())
+        middle = (*middle[:-1], *order.step(middle[-1]))
+        if more:
+            go(mos[l + 1])
             mos[l + 1].near_core()
-            (uds[l + 1].got,) = hold((uds[l + 1].got,), mos[l + 1].held)
-            uds[l + 1].next()
+        order.join_core(ud)
+        tail = ffn(plan, info, middle[5], middle[6], ud.arrays(), F32 if more else BF16)
+        saved.append((x, every, head, middle, tail, layer))
+        (x,) = order.step(tail[-1])
+        if more:
+            go(uds[l + 1])
+            uds[l + 1].near_core()
+            order.join(mos[l + 1])
             mos[l + 1].end()
     mixed = x
     dx = cotangent
     sums = [None] * depth
     extra = ()
     for l in reversed(range(depth)):
-        x, every, (normed, cpre, gate, rate, kept, feed, sub, _), middle, (both, hidden, _) = saved[l]
+        x, every, (normed, cpre, gate, rate, kept, feed, sub, _), middle, (both, hidden, _), layer = saved[l]
         states, first, gn, rg, gated, after, lifted = middle
-        dlow, dboth, dafter, dmid, ffn_gain = back_ffn(plan, info, dx, params[l], both, after, uds[l].arrays())
-        above = sums[l + 1] if l + 1 < depth else None
-        if above:
-            above[0].got, above[1].got = hold((above[0].got, above[1].got), dlow)
-            above[1].next()
-            above[0].next()
-            (lifted,) = hold((lifted,), above[1].high)
+        mo_up, ud_up = sums[l + 1] if l + 1 < depth else (None, None)
+        (dx,) = order.step(dx)
+        dlow, dboth, dafter, dmid, ffn_gain = back_ffn(plan, info, dx, layer, both, after, uds[l].arrays())
+        (dlow,) = order.step(dlow)
+        if mo_up:
+            go(ud_up)
+            go(mo_up)
+        (lifted,) = order.step(lifted)
         ud = Reduce(*grad_ud(rels, info, lifted, dboth, hidden, dlow), STAGES)
-        (dmid,) = hold((dmid,), ud.held)
+        (ud.held,) = order.step(ud.held)
+        (dmid,) = order.step(dmid)
         dgpre, dstates, mid_gain, rsub, rtotal = back_mid(
-            plan, info, dmid, params[l], gn, rg, gate, states, kept, sub, mos[l].arrays()
+            plan, info, dmid, layer, gn, rg, gate, states, kept, sub, mos[l].arrays()
         )
+        (rtotal,) = order.step(rtotal)
         revery = exchange(rtotal)
-        (ud.got,) = hold((ud.got,), rtotal)
-        if above:
-            above[1].got, above[0].got = hold((above[1].got, above[0].got), rtotal)
-            above[1].next()
-            above[0].next()
-        ud.next()
-        (dstates,) = hold((dstates,), ud.high)
+        order.join(ud)
+        ud.add()
+        (revery,) = order.step(revery)
+        (ud.high,) = order.step(ud.high)
+        ud.send()
+        if mo_up:
+            go(ud_up)
+            go(mo_up)
+        (dstates,) = order.step(dstates)
         dmixin, dx, gains_b = back_two(
-            plan, info, x, params[l], dafter, dgpre, dstates, states, kept, rate, cpre, first, sub, rsub, every, revery,
+            plan, info, x, layer, dafter, dgpre, dstates, states, kept, rate, cpre, first, sub, rsub, every, revery,
             mos[l].arrays(),
         )
+        (dmixin,) = order.step(dmixin)
         extra = (gains_b, mid_gain, ffn_gain) + extra
-        if above:
-            above[1].got, above[0].got = hold((above[1].got, above[0].got), dmixin)
-            above[0].next()
         mo = Reduce(*grad_mo(rels, info, gated, dmid, normed, dmixin, extra if l == 0 else ()), STAGES)
-        (ud.got,) = hold((ud.got,), mo.held)
-        ud.next()
-        mo.next()
-        if l:
-            (dx,) = hold((dx,), mo.high, ud.high)
+        (mo.held,) = order.step(mo.held)
+        if mo_up:
+            go(ud_up)
+            go(mo_up)
         sums[l] = (mo, ud)
     mo, ud = sums[0]
-    mo.next()
-    ud.next()
-    mo.next()
-    ud.next()
-    mo.next()
+    go(ud)
+    go(mo)
+    if depth > 1:
+        go(sums[1][0])
+    go(ud)
+    go(mo)
+    go(ud)
+    go(mo)
+    go(mo)
     mine, other, downs = [], [], []
-    for mo, ud in sums:
+    for mo, ud in reversed(sums):
         ready = ud.add()
         line = jnp.concatenate([mo.add(), ready[:, : HALVES["up"]]], axis=1)
         first, second = line[:share], line[share:]
-        mine.append(jnp.where(core == 0, first, second))
-        other.append(swap(jnp.where(core == 0, second, first), (1, 1)))
-        downs.append(ready)
+        mine.insert(0, jnp.where(core == 0, first, second))
+        other.insert(0, swap(jnp.where(core == 0, second, first), (1, 1)))
+        downs.insert(0, ready)
     shapes = (w_mix.shape, w_out.shape, w_up.shape, w_down.shape)
     *grads, tail = finish(info, mine, other, downs, shapes)
     tail = tail[:, : 4 * depth].T.reshape(depth, 4, share)

time: 454 us -> 362 us (0.80); the launches traced: 445 us -> 358 us
  waiting for transfers between devices: 217 us -> 170 us
  Pallas kernels: 123 us -> 91.7 us
  other arithmetic: 17.7 us -> 12.4 us
    ppermute x63, waiting for transfers between devices: 217 us -> 170 us  [swap(): return lax.ppermute(x, ALL, [(i, i ^ bits[i % 2]) for i in range(count)])]
    pallas_call x2, Pallas kernels: 20.5 us -> 14.7 us  [back_ffn(): pl.pallas_call(functools.partial(back_ffn_kernel, plan, len(weights)), ou...]
    pallas_call x2, Pallas kernels: 15.8 us -> 10.1 us  [back_mid(): pl.pallas_call(functools.partial(back_mid_kernel, plan, len(weights)), ou...]
    convert_element_type x16, other arithmetic: 13.7 us -> 8.46 us  [joined(): (self.held[part].astype(F32) + self.got[part].astype(F32)).astype(BF16)]
    pallas_call x2, Pallas kernels: 15 us -> 9.84 us  [mid(): pl.pallas_call(functools.partial(mid_kernel, plan, len(weights)), out_sha...]
    unnamed x97 -> x118, local copies, waits for them, and re-layouts: 11.8 us -> 11 us
  transfers between devices with their start and end apart: 63 -> 63, of which waited for: 35 -> 33; matrix products, arithmetic and copies ran while one was open for 3% -> 2% of each run, Pallas kernels for 14% -> 15%
where the time goes in v3:
time: 362 us; the launch traced here: 358 us
  waiting for transfers between devices  170 us (47%)
  Pallas kernels  91.7 us (25%)
  starting transfers between devices  63.7 us (18%)
  local copies, waits for them, and re-layouts  15.6 us (4%)
  other arithmetic  12.4 us (3%)
  between operations  4.61 us (1%)
    ppermute x63, waiting for transfers between devices, swap(): return lax.ppermute(x, ALL, [(i, i ^ bits[i % 2]) for i in range(count)])  170 us
    ppermute x63, starting transfers between devices, swap(): return lax.ppermute(x, ALL, [(i, i ^ bits[i % 2]) for i in range(count)])  63.7 us
    pallas_call x2, Pallas kernels, back_ffn(): pl.pallas_call(functools.partial(back_ffn_kernel, plan, len(weights)), ou...  14.7 us
    pallas_call x2, Pallas kernels, back_two(): pl.pallas_call(functools.partial(back_two_kernel, plan, len(weights)), ou...  13.8 us
    pallas_call x2, Pallas kernels, ffn(): pl.pallas_call(functools.partial(ffn_kernel, plan, len(weights)), out_sha...  11.6 us
    unnamed x118, local copies, waits for them, and re-layouts  11 us
    pallas_call x2, Pallas kernels, front(): pl.pallas_call(functools.partial(front_kernel, plan, len(weights)), out_s...  10.6 us
    pallas_call x2, Pallas kernels, grad_ud(): pl.pallas_call(functools.partial(grad_ud_kernel, rels), out_shape=(shape,...  10.6 us
  transfers between devices with their start and end apart: 63, of which 33 were waited for; matrix products, arithmetic and copies ran while one was open for 2% of the time, Pallas kernels for 15%

profile of v3, /device:TPU:0, one launch (start us, length us, event | category | flops | bytes accessed | tf_op | source)
XLA Modules:
  0.0 358.2 jit_solution(9076783746601857233)
XLA Ops:
  7.1 3.0 collective-permute-start.2
  10.3 8.6 %collective-permute-done.1 = bf16[1,48,1408]{2,1,0:T(8,128)(2,1)S(1)} collective-permute-done((bf16[1,48,1408]{2,1,0:T(8,128)(2,1)S(1)}, bf16[1,48,1408]{2,1,0:T(8,128)(2,1)S(1)}, u32[]{:S(2)}, u32[]{:S(2)}) %collective-permute-start.1) | collective-permute-done | bytes 135200 | tf_op jit(solution)/shard_map/ppermute | solution.py:735
  21.5 6.2 %collective-permute-done.3 = bf16[2,48,1408]{2,1,0:T(8,128)(2,1)S(1)} collective-permute-done((bf16[2,48,1408]{2,1,0:T(8,128)(2,1)S(1)}, bf16[2,48,1408]{2,1,0:T(8,128)(2,1)S(1)}, u32[]{:S(2)}, u32[]{:S(2)}) %collective-permute-start.3) | collective-permute-done | bytes 270368 | tf_op jit(solution)/shard_map/ppermute | solution.py:735
  27.8 3.0 collective-permute-start.4
  31.7 3.7 %collective-permute-start.9 = (bf16[1,48,1408]{2,1,0:T(8,128)(2,1)S(1)}, bf16[1,48,1408]{2,1,0:T(8,128)(2,1)S(1)}, u32[]{:S(2)}, u32[]{:S(2)}) collective-permute-start(bf16[1,48,1408]{2,1,0:T(8,128)(2,1)S(1)} %get-tuple-element.338), channel_id=1, source_target_pairs={{0,8},{1,17},{2,10},{3,19},{4,12},{5,21},{6,14},{7,23},{8,0},{9,25... | collective-permute-start | bytes 405512 | tf_op jit(solution)/shard_map/ppermute | solution.py:735
  38.3 8.1 %collective-permute-done.6 = bf16[2,48,2304]{2,1,0:T(8,128)(2,1)S(1)} collective-permute-done((bf16[2,48,2304]{2,1,0:T(8,128)(2,1)S(1)}, bf16[2,48,2304]{2,1,0:T(8,128)(2,1)S(1)}, u32[]{:S(2)}, u32[]{:S(2)}) %collective-permute-start.6) | collective-permute-done | bytes 442400 | tf_op jit(solution)/shard_map/ppermute | solution.py:735
  48.7 3.3 collective-permute-start.8
  52.1 7.1 %collective-permute-done.10 = bf16[2,48,1408]{2,1,0:T(8,128)(2,1)S(1)} collective-permute-done((bf16[2,48,1408]{2,1,0:T(8,128)(2,1)S(1)}, bf16[2,48,1408]{2,1,0:T(8,128)(2,1)S(1)}, u32[]{:S(2)}, u32[]{:S(2)}) %collective-permute-start.10) | collective-permute-done | bytes 270368 | tf_op jit(solution)/shard_map/ppermute | solution.py:735
  59.2 7.6 %collective-permute-done.7 = bf16[4,48,2304]{2,1,0:T(8,128)(2,1)S(1)} collective-permute-done((bf16[4,48,2304]{2,1,0:T(8,128)(2,1)S(1)}, bf16[4,48,2304]{2,1,0:T(8,128)(2,1)S(1)}, u32[]{:S(2)}, u32[]{:S(2)}) %collective-permute-start.7) | collective-permute-done | bytes 884768 | tf_op jit(solution)/shard_map/ppermute | solution.py:735
  76.9 5.3 %front.2 = (bf16[256,768]{1,0:T(8,128)(2,1)S(1)}, f32[256,768]{1,0:T(8,128)S(1)}, f32[256,768]{1,0:T(8,128)S(1)}, f32[256,384]{1,0:T(8,128)S(1)}, f32[3,256,128]...) custom-call(s32[8]{0:T(128)S(1)} %stack.68.me_ref.info_ref, ...), custom_call_target="tpu_custom_call" | custom-call | flops 1000 | bytes 1000 | tf_op jit(solution)/shard_map/front/pallas_call | solution.py:180
  84.3 2.9 collective-permute-start.16
  87.5 3.6 %collective-permute-done.14 = f32[2,4,384]{2,1,0:T(4,128)S(1)} collective-permute-done((f32[2,4,384]{2,1,0:T(4,128)S(1)}, f32[2,4,384]{2,1,0:T(4,128)S(1)}, u32[]{:S(2)}, u32[]{:S(2)}) %collective-permute-start.14) | collective-permute-done | bytes 12320 | tf_op jit(solution)/shard_map/ppermute | solution.py:735
  92.3 6.5 %collective-permute-done.15 = f32[2,4,384]{2,1,0:T(4,128)S(1)} collective-permute-done((f32[2,4,384]{2,1,0:T(4,128)S(1)}, f32[2,4,384]{2,1,0:T(4,128)S(1)}, u32[]{:S(2)}, u32[]{:S(2)}) %collective-permute-start.15) | collective-permute-done | bytes 12320 | tf_op jit(solution)/shard_map/ppermute | solution.py:735
  101.6 4.9 %mid.2 = (f32[6,256,128]{2,1,0:T(8,128)S(1)}, f32[2,8,384]{2,1,0:T(8,128)S(1)}, f32[256,768]{1,0:T(8,128)S(1)}, f32[256,128]{1,0:T(8,128)S(1)}, bf16[256,768]{1,...) custom-call(s32[8]{0:T(128)S(1)} %stack.68.me_ref.info_ref, bf16[256,768]{1,0:T(8,128)(2,1)S(1)} %copy-done, ...), custom_call_target="tpu_custom_call" | custom-call | flops 1000 | bytes 1000 | tf_op jit(solution)/shard_map/mid/pallas_call | solution.py:268
  107.0 7.9 %collective-permute-done.22 = bf16[2,48,2304]{2,1,0:T(8,128)(2,1)S(1)} collective-permute-done((bf16[2,48,2304]{2,1,0:T(8,128)(2,1)S(1)}, bf16[2,48,2304]{2,1,0:T(8,128)(2,1)S(1)}, u32[]{:S(2)}, u32[]{:S(2)}) %collective-permute-start.22) | collective-permute-done | bytes 442400 | tf_op jit(solution)/shard_map/ppermute | solution.py:735
  115.5 5.3 %ffn.2 = (f32[256,3072]{1,0:T(8,128)S(1)}, bf16[256,1536]{1,0:T(8,128)(2,1)S(1)}, f32[256,768]{1,0:T(8,128)S(1)}) custom-call(s32[8]{0:T(128)S(1)} %stack.68.me_ref.info_ref, f32[256,768]{1,0:T(8,128)S(1)} %get-tuple-element.176.after_ref, bf16[256,768]{1,0:T(8,128)(2,1)S(1)} %get-tuple-element.249.lifted_ref, bf16[8,48,2304]{2,1,0:T(8,128)(2,1)} %pad_maximum_fusion.refs_0_, ...), custom_call_target="tpu_custom_call" | custom-call | flops 1000 | bytes 1000 | tf_op jit(solution)/shard_map/ffn/pallas_call | solution.py:314
  121.7 8.8 %collective-permute-done.23 = bf16[4,48,2304]{2,1,0:T(8,128)(2,1)S(1)} collective-permute-done((bf16[4,48,2304]{2,1,0:T(8,128)(2,1)S(1)}, bf16[4,48,2304]{2,1,0:T(8,128)(2,1)S(1)}, u32[]{:S(2)}, u32[]{:S(2)}) %collective-permute-start.23) | collective-permute-done | bytes 884768 | tf_op jit(solution)/shard_map/ppermute | solution.py:735
  133.5 5.3 %front.3 = (bf16[256,768]{1,0:T(8,128)(2,1)S(1)}, f32[256,768]{1,0:T(8,128)S(1)}, f32[256,768]{1,0:T(8,128)S(1)}, f32[256,384]{1,0:T(8,128)S(1)}, f32[3,256,128]...) custom-call(s32[8]{0:T(128)S(1)} %stack.68.me_ref.info_ref, ...), custom_call_target="tpu_custom_call" | custom-call | flops 1000 | bytes 1000 | tf_op jit(solution)/shard_map/front/pallas_call | solution.py:180
  146.5 8.0 %collective-permute-done.28 = f32[2,4,384]{2,1,0:T(4,128)S(1)} collective-permute-done((f32[2,4,384]{2,1,0:T(4,128)S(1)}, f32[2,4,384]{2,1,0:T(4,128)S(1)}, u32[]{:S(2)}, u32[]{:S(2)}) %collective-permute-start.28) | collective-permute-done | bytes 12320 | tf_op jit(solution)/shard_map/ppermute | solution.py:735
  154.6 5.0 %mid.3 = (f32[6,256,128]{2,1,0:T(8,128)S(1)}, f32[2,8,384]{2,1,0:T(8,128)S(1)}, f32[256,768]{1,0:T(8,128)S(1)}, f32[256,128]{1,0:T(8,128)S(1)}, bf16[256,768]{1,...) custom-call(s32[8]{0:T(128)S(1)} %stack.68.me_ref.info_ref, ...), custom_call_target="tpu_custom_call" | custom-call | flops 1000 | bytes 1000 | tf_op jit(solution)/shard_map/mid/pallas_call | solution.py:268
  160.4 6.3 %ffn.3 = (f32[256,3072]{1,0:T(8,128)S(1)}, bf16[256,1536]{1,0:T(8,128)(2,1)S(1)}, bf16[256,768]{1,0:T(8,128)(2,1)}) custom-call(s32[8]{0:T(128)S(1)} %stack.68.me_ref.info_ref, f32[256,768]{1,0:T(8,128)S(1)} %get-tuple-element.198.after_ref, bf16[256,768]{1,0:T(8,128)(2,1)S(1)} %get-tuple-element.211.lifted_ref, ...), custom_call_target="tpu_custom_call" | custom-call | flops 1000 | bytes 1000 | tf_op jit(solution)/shard_map/ffn/pallas_call | solution.py:314
  167.6 7.9 %back_ffn.2 = (bf16[256,768]{1,0:T(8,128)(2,1)S(1)}, bf16[256,3072]{1,0:T(8,128)(2,1)S(1)}, f32[256,768]{1,0:T(8,128)S(1)}, bf16[256,768]{1,0:T(8,128)(2,1)S(1)}, f32[1,768]{1,0:T(1,128)S(1)}) custom-call(s32[8]{0:T(128)S(1)} %stack.68.me_ref.info_ref, bf16[256,768]{1,0:T(8,128)(2,1)S(1)} %copy-done.19, f32[8,768]{1,0:T(8,128)S(1)} %get-tuple-element.187.p_ref, ...), custom_call_target="tpu_custom_call" | custom-call | flops 1000 | bytes 1000 | tf_op jit(solution)/shard_map/back_ffn/pallas_call | solution.py:381
  179.3 5.3 %grad_ud.2 = (bf16[16,48,2304]{2,1,0:T(8,128)(2,1)S(1)}, bf16[16,48,2304]{2,1,0:T(8,128)(2,1)S(1)}) custom-call(s32[8]{0:T(128)S(1)} %stack.68.me_ref.info_ref, bf16[256,768]{1,0:T(8,128)(2,1)S(1)} %get-tuple-element.211.lifted_ref, bf16[256,3072]{1,0:T(8,128)(2,1)S(1)} %get-tuple-element.212.dboth_ref, bf16[256,1536]{1,0:T(8,128)(2,1)S(1)} %copy-done.18, ...), custom_call_target="tpu_custom_call" | custom-call | flops 1000 | bytes 1000 | tf_op jit(solution)/shard_map/grad_ud/pallas_call | solution.py:648
  185.2 4.6 %back_mid.2 = (bf16[256,768]{1,0:T(8,128)(2,1)S(1)}, f32[6,256,128]{2,1,0:T(8,128)S(1)}, f32[1,768]{1,0:T(1,128)S(1)}, f32[2,8,384]{2,1,0:T(8,128)S(1)}, f32[2,384]{1,0:T(2,128)S(1)}) custom-call(s32[8]{0:T(128)S(1)} %stack.68.me_ref.info_ref, bf16[256,768]{1,0:T(8,128)(2,1)S(1)} %get-tuple-element.216.dmid_ref, f32[8,768]{1,0:T(8,128)S(1)} %get-tuple-element.187.p_ref, ...), custom_call_target="tpu_custom_call" | custom-call | flops 1000 | bytes 1000 | tf_op jit(solution)/shard_map/back_mid/pallas_call | solution.py:462
  196.5 4.2 %add_convert_fusion.2 = (bf16[8,48,2304]{2,1,0:T(8,128)(2,1)S(1)}, bf16[8,48,2304]{2,1,0:T(8,128)(2,1)}) fusion(bf16[16,48,2304]{2,1,0:T(8,128)(2,1)} %collective-permute-done.33, bf16[16,48,2304]{2,1,0:T(8,128)(2,1)S(1)} %get-tuple-element.215), kind=kLoop, calls=%fused_computation.2 | loop fusion | flops 7077888 | bytes 10616832 | tf_op jit(solution)/shard_map/convert_element_type | solution.py:808
  200.8 6.4 %back_two.2 = (bf16[256,1920]{1,0:T(8,128)(2,1)S(1)}, f32[256,768]{1,0:T(8,128)S(1)}, f32[2,768]{1,0:T(2,128)S(1)}) custom-call(s32[8]{0:T(128)S(1)} %stack.68.me_ref.info_ref, f32[256,768]{1,0:T(8,128)S(1)} %get-tuple-element.183.x_ref, f32[8,768]{1,0:T(8,128)S(1)} %get-tuple-element.187.p_ref, f32[256,768]{1,0:T(8,128)S(1)} %copy-done.12, ...), custom_call_target="tpu_custom_call" | custom-call | flops 1000 | bytes 1000 | tf_op jit(solution)/shard_map/back_two/pallas_call | solution.py:579
  207.2 3.6 grad_mo.2
  211.3 6.8 %back_ffn.3 = (bf16[256,768]{1,0:T(8,128)(2,1)S(1)}, bf16[256,3072]{1,0:T(8,128)(2,1)S(1)}, f32[256,768]{1,0:T(8,128)S(1)}, bf16[256,768]{1,0:T(8,128)(2,1)S(1)}, f32[1,768]{1,0:T(1,128)S(1)}) custom-call(s32[8]{0:T(128)S(1)} %stack.68.me_ref.info_ref, f32[256,768]{1,0:T(8,128)S(1)} %get-tuple-element.240.dx_ref, f32[8,768]{1,0:T(8,128)S(1)} %get-tuple-element.166.p_ref, ...), custom_call_target="tpu_custom_call" | custom-call | flops 1000 | bytes 1000 | tf_op jit(solution)/shard_map/back_ffn/pallas_call | solution.py:381
  218.1 15.4 %collective-permute-done.39 = bf16[8,48,2304]{2,1,0:T(8,128)(2,1)S(1)} collective-permute-done((bf16[8,48,2304]{2,1,0:T(8,128)(2,1)S(1)}, bf16[8,48,2304]{2,1,0:T(8,128)(2,1)S(1)}, u32[]{:S(2)}, u32[]{:S(2)}) %collective-permute-start.39) | collective-permute-done | bytes 1769504 | tf_op jit(solution)/shard_map/ppermute | solution.py:735
  233.5 5.3 %grad_ud.3 = (bf16[16,48,2304]{2,1,0:T(8,128)(2,1)S(1)}, bf16[16,48,2304]{2,1,0:T(8,128)(2,1)S(1)}) custom-call(s32[8]{0:T(128)S(1)} %stack.68.me_ref.info_ref, bf16[256,768]{1,0:T(8,128)(2,1)S(1)} %copy-done.6, bf16[256,3072]{1,0:T(8,128)(2,1)S(1)} %get-tuple-element.250.dboth_ref, bf16[256,1536]{1,0:T(8,128)(2,1)S(1)} %copy-done.16, ...), custom_call_target="tpu_custom_call" | custom-call | flops 1000 | bytes 1000 | tf_op jit(solution)/shard_map/grad_ud/pallas_call | solution.py:648
  241.1 5.4 %back_mid.3 = (bf16[256,768]{1,0:T(8,128)(2,1)S(1)}, f32[6,256,128]{2,1,0:T(8,128)S(1)}, f32[1,768]{1,0:T(1,128)S(1)}, f32[2,8,384]{2,1,0:T(8,128)S(1)}, f32[2,384]{1,0:T(2,128)S(1)}) custom-call(s32[8]{0:T(128)S(1)} %stack.68.me_ref.info_ref, bf16[256,768]{1,0:T(8,128)(2,1)S(1)} %get-tuple-element.254.dmid_ref, f32[8,768]{1,0:T(8,128)S(1)} %get-tuple-element.166.p_ref, ...), custom_call_target="tpu_custom_call" | custom-call | flops 1000 | bytes 1000 | tf_op jit(solution)/shard_map/back_mid/pallas_call | solution.py:462
  250.9 4.1 %collective-permute-done.44 = f32[2,2,384]{2,1,0:T(2,128)S(1)} collective-permute-done((f32[2,2,384]{2,1,0:T(2,128)S(1)}, f32[2,2,384]{2,1,0:T(2,128)S(1)}, u32[]{:S(2)}, u32[]{:S(2)}) %collective-permute-start.44) | collective-permute-done | bytes 6176 | tf_op jit(solution)/shard_map/ppermute | solution.py:735
  255.2 8.5 %collective-permute-done.45 = f32[2,2,384]{2,1,0:T(2,128)S(1)} collective-permute-done((f32[2,2,384]{2,1,0:T(2,128)S(1)}, f32[2,2,384]{2,1,0:T(2,128)S(1)}, u32[]{:S(2)}, u32[]{:S(2)}) %collective-permute-start.45) | collective-permute-done | bytes 6176 | tf_op jit(solution)/shard_map/ppermute | solution.py:735
  265.8 7.3 %back_two.3 = (bf16[256,1920]{1,0:T(8,128)(2,1)S(1)}, f32[256,768]{1,0:T(8,128)}, f32[2,768]{1,0:T(2,128)S(1)}) custom-call(s32[8]{0:T(128)S(1)} %stack.68.me_ref.info_ref, bf16[256,768]{1,0:T(8,128)(2,1)S(1)} %copy-done, f32[8,768]{1,0:T(8,128)S(1)} %get-tuple-element.166.p_ref, f32[256,768]{1,0:T(8,128)S(1)} %get-tuple-element.242.dafter_ref, ...), custom_call_target="tpu_custom_call" | custom-call | flops 1000 | bytes 1000 | tf_op jit(solution)/shard_map/back_two/pallas_call | solution.py:579
  273.1 2.8 collective-permute-start.50
  278.0 3.5 grad_mo.3
  281.6 5.6 %collective-permute-done.50 = bf16[2,48,2304]{2,1,0:T(8,128)(2,1)S(1)} collective-permute-done((bf16[2,48,2304]{2,1,0:T(8,128)(2,1)S(1)}, bf16[2,48,2304]{2,1,0:T(8,128)(2,1)S(1)}, u32[]{:S(2)}, u32[]{:S(2)}) %collective-permute-start.50) | collective-permute-done | bytes 442400 | tf_op jit(solution)/shard_map/ppermute | solution.py:735
  287.4 4.1 %collective-permute-done.49 = bf16[4,48,1408]{2,1,0:T(8,128)(2,1)S(1)} collective-permute-done((bf16[4,48,1408]{2,1,0:T(8,128)(2,1)S(1)}, bf16[4,48,1408]{2,1,0:T(8,128)(2,1)S(1)}, u32[]{:S(2)}, u32[]{:S(2)}) %collective-permute-start.49) | collective-permute-done | bytes 540704 | tf_op jit(solution)/shard_map/ppermute | solution.py:735
  291.8 2.7 collective-permute-done.60
  295.4 3.2 collective-permute-start.52
  298.6 3.6 collective-permute-done.53
  305.1 9.2 %collective-permute-done.52 = bf16[4,48,2304]{2,1,0:T(8,128)(2,1)S(1)} collective-permute-done((bf16[4,48,2304]{2,1,0:T(8,128)(2,1)S(1)}, bf16[4,48,2304]{2,1,0:T(8,128)(2,1)S(1)}, u32[]{:S(2)}, u32[]{:S(2)}) %collective-permute-start.52) | collective-permute-done | bytes 884768 | tf_op jit(solution)/shard_map/ppermute | solution.py:735
  314.6 3.4 collective-permute-start.55
  317.9 3.7 %collective-permute-done.51 = bf16[8,48,1408]{2,1,0:T(8,128)(2,1)S(1)} collective-permute-done((bf16[8,48,1408]{2,1,0:T(8,128)(2,1)S(1)}, bf16[8,48,1408]{2,1,0:T(8,128)(2,1)S(1)}, u32[]{:S(2)}, u32[]{:S(2)}) %collective-permute-start.51) | collective-permute-done | bytes 1081376 | tf_op jit(solution)/shard_map/ppermute | solution.py:735
  324.6 3.5 collective-permute-done.55
  328.2 3.2 collective-permute-done.54
  334.5 13.7 %collective-permute-done.56 = bf16[2,48,1408]{2,1,0:T(8,128)(2,1)S(1)} collective-permute-done((bf16[2,48,1408]{2,1,0:T(8,128)(2,1)S(1)}, bf16[2,48,1408]{2,1,0:T(8,128)(2,1)S(1)}, u32[]{:S(2)}, u32[]{:S(2)}) %collective-permute-start.56) | collective-permute-done | bytes 270368 | tf_op jit(solution)/shard_map/ppermute | solution.py:735
  348.4 4.9 %collective-permute-done.57 = bf16[1,48,1408]{2,1,0:T(8,128)(2,1)S(1)} collective-permute-done((bf16[1,48,1408]{2,1,0:T(8,128)(2,1)S(1)}, bf16[1,48,1408]{2,1,0:T(8,128)(2,1)S(1)}, u32[]{:S(2)}, u32[]{:S(2)}) %collective-permute-start.57) | collective-permute-done | bytes 135200 | tf_op jit(solution)/shard_map/ppermute | solution.py:735
  (280 shorter events, 81.1 us)
Async XLA Ops:
  7.1 11.8 %collective-permute-start.2 = (bf16[1,48,2304]{2,1,0:T(8,128)(2,1)S(1)}, bf16[1,48,2304]{2,1,0:T(8,128)(2,1)S(1)}, u32[]{:S(2)}, u32[]{:S(2)}) collective-permute-start(bf16[1,48,2304]{2,1,0:T(8,128)(2,1)S(1)} %maximum_bitcast_fusion), channel_id=1, source_target_pairs={{0,8},{1,17},{2,10},{3,19},{4,12},{5,21},{6,14},{7,23},{8,0},{9,25... | collective-permute-start | bytes 663560 | tf_op jit(solution)/shard_map/ppermute | solution.py:735
  10.2 8.7 %collective-permute-start.1 = (bf16[1,48,1408]{2,1,0:T(8,128)(2,1)S(1)}, bf16[1,48,1408]{2,1,0:T(8,128)(2,1)S(1)}, u32[]{:S(2)}, u32[]{:S(2)}) collective-permute-start(bf16[1,48,1408]{2,1,0:T(8,128)(2,1)S(1)} %get-tuple-element.339), channel_id=1, source_target_pairs={{0,8},{1,17},{2,10},{3,19},{4,12},{5,21},{6,14},{7,23},{8,0},{9,25... | collective-permute-start | bytes 405512 | tf_op jit(solution)/shard_map/ppermute | solution.py:735
  19.0 8.7 %collective-permute-start.3 = (bf16[2,48,1408]{2,1,0:T(8,128)(2,1)S(1)}, bf16[2,48,1408]{2,1,0:T(8,128)(2,1)S(1)}, u32[]{:S(2)}, u32[]{:S(2)}) collective-permute-start(bf16[2,48,1408]{2,1,0:T(8,128)(2,1)S(1)} %pad_maximum_fusion.12), channel_id=1, source_target_pairs={{0,16},{1,9},{2,18},{3,11},{4,20},{5,13},{6,22},{7,15},{8,24},{9,1... | collective-permute-start | bytes 811016 | tf_op jit(solution)/shard_map/ppermute | solution.py:735
  27.8 10.4 %collective-permute-start.4 = (bf16[4,48,1408]{2,1,0:T(8,128)(2,1)S(1)}, bf16[4,48,1408]{2,1,0:T(8,128)(2,1)S(1)}, u32[]{:S(2)}, u32[]{:S(2)}) collective-permute-start(bf16[4,48,1408]{2,1,0:T(8,128)(2,1)S(1)} %pad_maximum_fusion.6), channel_id=1, source_target_pairs={{0,2},{1,5},{2,0},{3,7},{4,6},{5,1},{6,4},{7,3},{8,10},{9,13},{10,... | collective-permute-start | bytes 1622024 | tf_op jit(solution)/shard_map/ppermute | solution.py:735
  30.9 15.5 %collective-permute-start.6 = (bf16[2,48,2304]{2,1,0:T(8,128)(2,1)S(1)}, bf16[2,48,2304]{2,1,0:T(8,128)(2,1)S(1)}, u32[]{:S(2)}, u32[]{:S(2)}) collective-permute-start(bf16[2,48,2304]{2,1,0:T(8,128)(2,1)S(1)} %pad_maximum_fusion.8), channel_id=1, source_target_pairs={{0,16},{1,9},{2,18},{3,11},{4,20},{5,13},{6,22},{7,15},{8,24},{9,1... | collective-permute-start | bytes 1327112 | tf_op jit(solution)/shard_map/ppermute | solution.py:735
  31.7 16.8 %collective-permute-start.9 = (bf16[1,48,1408]{2,1,0:T(8,128)(2,1)S(1)}, bf16[1,48,1408]{2,1,0:T(8,128)(2,1)S(1)}, u32[]{:S(2)}, u32[]{:S(2)}) collective-permute-start(bf16[1,48,1408]{2,1,0:T(8,128)(2,1)S(1)} %get-tuple-element.338), channel_id=1, source_target_pairs={{0,8},{1,17},{2,10},{3,19},{4,12},{5,21},{6,14},{7,23},{8,0},{9,25... | collective-permute-start | bytes 405512 | tf_op jit(solution)/shard_map/ppermute | solution.py:735
  46.4 22.1 %collective-permute-start.5 = (bf16[8,48,1408]{2,1,0:T(8,128)(2,1)S(1)}, bf16[8,48,1408]{2,1,0:T(8,128)(2,1)S(1)}, u32[]{:S(2)}, u32[]{:S(2)}) collective-permute-start(bf16[8,48,1408]{2,1,0:T(8,128)(2,1)S(1)} %pad_maximum_fusion.2.refs_0_), channel_id=1, source_target_pairs={{0,4},{1,3},{2,6},{3,1},{4,0},{5,7},{6,2},{7,5},{8,12},{9,11},{10,... | collective-permute-start | bytes 3244040 | tf_op jit(solution)/shard_map/ppermute | solution.py:735
  48.0 18.8 %collective-permute-start.7 = (bf16[4,48,2304]{2,1,0:T(8,128)(2,1)S(1)}, bf16[4,48,2304]{2,1,0:T(8,128)(2,1)S(1)}, u32[]{:S(2)}, u32[]{:S(2)}) collective-permute-start(bf16[4,48,2304]{2,1,0:T(8,128)(2,1)S(1)} %pad_maximum_fusion.4), channel_id=1, source_target_pairs={{0,2},{1,5},{2,0},{3,7},{4,6},{5,1},{6,4},{7,3},{8,10},{9,13},{10,... | collective-permute-start | bytes 2654216 | tf_op jit(solution)/shard_map/ppermute | solution.py:735
  48.6 10.6 %collective-permute-start.10 = (bf16[2,48,1408]{2,1,0:T(8,128)(2,1)S(1)}, bf16[2,48,1408]{2,1,0:T(8,128)(2,1)S(1)}, u32[]{:S(2)}, u32[]{:S(2)}) collective-permute-start(bf16[2,48,1408]{2,1,0:T(8,128)(2,1)S(1)} %pad_maximum_fusion.13), channel_id=1, source_target_pairs={{0,16},{1,9},{2,18},{3,11},{4,20},{5,13},{6,22},{7,15},{8,24},{9,1... | collective-permute-start | bytes 811016 | tf_op jit(solution)/shard_map/ppermute | solution.py:735
  48.7 10.4 %collective-permute-start.8 = (bf16[1,48,2304]{2,1,0:T(8,128)(2,1)S(1)}, bf16[1,48,2304]{2,1,0:T(8,128)(2,1)S(1)}, u32[]{:S(2)}, u32[]{:S(2)}) collective-permute-start(bf16[1,48,2304]{2,1,0:T(8,128)(2,1)S(1)} %maximum_bitcast_fusion.1), channel_id=1, source_target_pairs={{0,8},{1,17},{2,10},{3,19},{4,12},{5,21},{6,14},{7,23},{8,0},{9,25... | collective-permute-start | bytes 663560 | tf_op jit(solution)/shard_map/ppermute | solution.py:735
  52.1 23.1 %collective-permute-start.12 = (bf16[8,48,1408]{2,1,0:T(8,128)(2,1)S(1)}, bf16[8,48,1408]{2,1,0:T(8,128)(2,1)S(1)}, u32[]{:S(2)}, u32[]{:S(2)}) collective-permute-start(bf16[8,48,1408]{2,1,0:T(8,128)(2,1)S(1)} %pad_maximum_fusion.2.refs_0_), channel_id=1, source_target_pairs={{0,1},{1,0},{2,3},{3,2},{4,5},{5,4},{6,7},{7,6},{8,9},{9,8},{10,11... | collective-permute-start | bytes 3244040 | tf_op jit(solution)/shard_map/ppermute | solution.py:735
  68.5 6.7 %collective-permute-start.11 = (bf16[8,48,1408]{2,1,0:T(8,128)(2,1)S(1)}, bf16[8,48,1408]{2,1,0:T(8,128)(2,1)}, u32[]{:S(2)}, u32[]{:S(2)}) collective-permute-start(bf16[8,48,1408]{2,1,0:T(8,128)(2,1)S(1)} %collective-permute-done.5.refs_2_), channel_id=1, source_target_pairs={{0,1},{1,0},{2,3},{3,2},{4,5},{5,4},{6,7},{7,6},{8,9},{9,8},{10,11... | collective-permute-start | bytes 3244040 | tf_op jit(solution)/shard_map/ppermute | solution.py:735
  69.9 28.9 %collective-permute-start.17 = (bf16[8,48,2304]{2,1,0:T(8,128)(2,1)}, bf16[8,48,2304]{2,1,0:T(8,128)(2,1)}, u32[]{:S(2)}, u32[]{:S(2)}) collective-permute-start(bf16[8,48,2304]{2,1,0:T(8,128)(2,1)} %pad_maximum_fusion.refs_0_), channel_id=1, source_target_pairs={{0,4},{1,3},{2,6},{3,1},{4,0},{5,7},{6,2},{7,5},{8,12},{9,11},{10,... | collective-permute-start | bytes 5308424 | tf_op jit(solution)/shard_map/ppermute | solution.py:735
  74.8 31.7 %collective-permute-start.20 = (bf16[4,48,1408]{2,1,0:T(8,128)(2,1)S(1)}, bf16[4,48,1408]{2,1,0:T(8,128)(2,1)S(1)}, u32[]{:S(2)}, u32[]{:S(2)}) collective-permute-start(bf16[4,48,1408]{2,1,0:T(8,128)(2,1)S(1)} %pad_maximum_fusion.7), channel_id=1, source_target_pairs={{0,2},{1,5},{2,0},{3,7},{4,6},{5,1},{6,4},{7,3},{8,10},{9,13},{10,... | collective-permute-start | bytes 1622024 | tf_op jit(solution)/shard_map/ppermute | solution.py:735
  75.1 40.3 %collective-permute-start.19 = (bf16[8,48,2304]{2,1,0:T(8,128)(2,1)}, bf16[8,48,2304]{2,1,0:T(8,128)(2,1)S(1)}, u32[]{:S(2)}, u32[]{:S(2)}) collective-permute-start(bf16[8,48,2304]{2,1,0:T(8,128)(2,1)} %pad_maximum_fusion.refs_0_), channel_id=1, source_target_pairs={{0,1},{1,0},{2,3},{3,2},{4,5},{5,4},{6,7},{7,6},{8,9},{9,8},{10,11... | collective-permute-start | bytes 5308424 | tf_op jit(solution)/shard_map/ppermute | solution.py:735
  84.3 14.6 %collective-permute-start.16 = (f32[2,4,384]{2,1,0:T(4,128)S(1)}, f32[2,4,384]{2,1,0:T(4,128)S(1)}, u32[]{:S(2)}, u32[]{:S(2)}) collective-permute-start(f32[2,4,384]{2,1,0:T(4,128)S(1)} %pad_maximum_fusion.14), channel_id=1, source_target_pairs={{0,6},{1,7},{2,4},{3,5},{4,2},{5,3},{6,0},{7,1},{8,14},{9,15},{10,... | collective-permute-start | bytes 36872 | tf_op jit(solution)/shard_map/ppermute | solution.py:735
  91.1 7.7 %collective-permute-start.15 = (f32[2,4,384]{2,1,0:T(4,128)S(1)}, f32[2,4,384]{2,1,0:T(4,128)S(1)}, u32[]{:S(2)}, u32[]{:S(2)}) collective-permute-start(f32[2,4,384]{2,1,0:T(4,128)S(1)} %pad_maximum_fusion.14), channel_id=1, source_target_pairs={{0,4},{1,5},{2,6},{3,7},{4,0},{5,1},{6,2},{7,3},{8,12},{9,13},{10,... | collective-permute-start | bytes 36872 | tf_op jit(solution)/shard_map/ppermute | solution.py:735
  98.9 16.5 %collective-permute-start.18 = (bf16[8,48,2304]{2,1,0:T(8,128)(2,1)}, bf16[8,48,2304]{2,1,0:T(8,128)(2,1)S(1)}, u32[]{:S(2)}, u32[]{:S(2)}) collective-permute-start(bf16[8,48,2304]{2,1,0:T(8,128)(2,1)} %collective-permute-done.17.refs_2_), channel_id=1, source_target_pairs={{0,1},{1,0},{2,3},{3,2},{4,5},{5,4},{6,7},{7,6},{8,9},{9,8},{10,11... | collective-permute-start | bytes 5308424 | tf_op jit(solution)/shard_map/ppermute | solution.py:735
  101.4 13.5 %collective-permute-start.22 = (bf16[2,48,2304]{2,1,0:T(8,128)(2,1)S(1)}, bf16[2,48,2304]{2,1,0:T(8,128)(2,1)S(1)}, u32[]{:S(2)}, u32[]{:S(2)}) collective-permute-start(bf16[2,48,2304]{2,1,0:T(8,128)(2,1)S(1)} %pad_maximum_fusion.9), channel_id=1, source_target_pairs={{0,16},{1,9},{2,18},{3,11},{4,20},{5,13},{6,22},{7,15},{8,24},{9,1... | collective-permute-start | bytes 1327112 | tf_op jit(solution)/shard_map/ppermute | solution.py:735
  106.7 23.8 %collective-permute-start.21 = (bf16[8,48,1408]{2,1,0:T(8,128)(2,1)S(1)}, bf16[8,48,1408]{2,1,0:T(8,128)(2,1)S(1)}, u32[]{:S(2)}, u32[]{:S(2)}) collective-permute-start(bf16[8,48,1408]{2,1,0:T(8,128)(2,1)S(1)} %pad_maximum_fusion.3.refs_0_), channel_id=1, source_target_pairs={{0,4},{1,3},{2,6},{3,1},{4,0},{5,7},{6,2},{7,5},{8,12},{9,11},{10,... | collective-permute-start | bytes 3244040 | tf_op jit(solution)/shard_map/ppermute | solution.py:735
  115.1 15.4 %collective-permute-start.23 = (bf16[4,48,2304]{2,1,0:T(8,128)(2,1)S(1)}, bf16[4,48,2304]{2,1,0:T(8,128)(2,1)S(1)}, u32[]{:S(2)}, u32[]{:S(2)}) collective-permute-start(bf16[4,48,2304]{2,1,0:T(8,128)(2,1)S(1)} %pad_maximum_fusion.5), channel_id=1, source_target_pairs={{0,2},{1,5},{2,0},{3,7},{4,6},{5,1},{6,4},{7,3},{8,10},{9,13},{10,... | collective-permute-start | bytes 2654216 | tf_op jit(solution)/shard_map/ppermute | solution.py:735
  115.4 16.3 %collective-permute-start.25 = (bf16[8,48,1408]{2,1,0:T(8,128)(2,1)S(1)}, bf16[8,48,1408]{2,1,0:T(8,128)(2,1)S(1)}, u32[]{:S(2)}, u32[]{:S(2)}) collective-permute-start(bf16[8,48,1408]{2,1,0:T(8,128)(2,1)S(1)} %pad_maximum_fusion.3.refs_0_), channel_id=1, source_target_pairs={{0,1},{1,0},{2,3},{3,2},{4,5},{5,4},{6,7},{7,6},{8,9},{9,8},{10,11... | collective-permute-start | bytes 3244040 | tf_op jit(solution)/shard_map/ppermute | solution.py:735
  131.4 23.1 %collective-permute-start.30 = (bf16[8,48,2304]{2,1,0:T(8,128)(2,1)S(1)}, bf16[8,48,2304]{2,1,0:T(8,128)(2,1)S(1)}, u32[]{:S(2)}, u32[]{:S(2)}) collective-permute-start(bf16[8,48,2304]{2,1,0:T(8,128)(2,1)S(1)} %pad_maximum_fusion.1.refs_0_), channel_id=1, source_target_pairs={{0,4},{1,3},{2,6},{3,1},{4,0},{5,7},{6,2},{7,5},{8,12},{9,11},{10,... | collective-permute-start | bytes 5308424 | tf_op jit(solution)/shard_map/ppermute | solution.py:735
  131.7 28.6 %collective-permute-start.32 = (bf16[8,48,2304]{2,1,0:T(8,128)(2,1)S(1)}, bf16[8,48,2304]{2,1,0:T(8,128)(2,1)S(1)}, u32[]{:S(2)}, u32[]{:S(2)}) collective-permute-start(bf16[8,48,2304]{2,1,0:T(8,128)(2,1)S(1)} %pad_maximum_fusion.1.refs_0_), channel_id=1, source_target_pairs={{0,1},{1,0},{2,3},{3,2},{4,5},{5,4},{6,7},{7,6},{8,9},{9,8},{10,11... | collective-permute-start | bytes 5308424 | tf_op jit(solution)/shard_map/ppermute | solution.py:735
  140.8 13.7 %collective-permute-start.29 = (f32[2,4,384]{2,1,0:T(4,128)S(1)}, f32[2,4,384]{2,1,0:T(4,128)S(1)}, u32[]{:S(2)}, u32[]{:S(2)}) collective-permute-start(f32[2,4,384]{2,1,0:T(4,128)S(1)} %pad_maximum_fusion.15), channel_id=1, source_target_pairs={{0,6},{1,7},{2,4},{3,5},{4,2},{5,3},{6,0},{7,1},{8,14},{9,15},{10,... | collective-permute-start | bytes 36872 | tf_op jit(solution)/shard_map/ppermute | solution.py:735
  140.9 13.7 %collective-permute-start.28 = (f32[2,4,384]{2,1,0:T(4,128)S(1)}, f32[2,4,384]{2,1,0:T(4,128)S(1)}, u32[]{:S(2)}, u32[]{:S(2)}) collective-permute-start(f32[2,4,384]{2,1,0:T(4,128)S(1)} %pad_maximum_fusion.15), channel_id=1, source_target_pairs={{0,4},{1,5},{2,6},{3,7},{4,0},{5,1},{6,2},{7,3},{8,12},{9,13},{10,... | collective-permute-start | bytes 36872 | tf_op jit(solution)/shard_map/ppermute | solution.py:735
  184.6 11.9 %collective-permute-start.33 = (bf16[16,48,2304]{2,1,0:T(8,128)(2,1)S(1)}, bf16[16,48,2304]{2,1,0:T(8,128)(2,1)}, u32[]{:S(2)}, u32[]{:S(2)}) collective-permute-start(bf16[16,48,2304]{2,1,0:T(8,128)(2,1)S(1)} %get-tuple-element.222), channel_id=1, source_target_pairs={{0,1},{1,0},{2,3},{3,2},{4,5},{5,4},{6,7},{7,6},{8,9},{9,8},{10,11... | collective-permute-start | bytes 10616840 | tf_op jit(solution)/shard_map/ppermute | solution.py:735
  210.8 22.7 %collective-permute-start.38 = (bf16[16,48,1408]{2,1,0:T(8,128)(2,1)S(1)}, bf16[16,48,1408]{2,1,0:T(8,128)(2,1)S(1)}, u32[]{:S(2)}, u32[]{:S(2)}) collective-permute-start(bf16[16,48,1408]{2,1,0:T(8,128)(2,1)S(1)} %get-tuple-element.244), channel_id=1, source_target_pairs={{0,1},{1,0},{2,3},{3,2},{4,5},{5,4},{6,7},{7,6},{8,9},{9,8},{10,11... | collective-permute-start | bytes 6488072 | tf_op jit(solution)/shard_map/ppermute | solution.py:735
  210.9 22.6 %collective-permute-start.39 = (bf16[8,48,2304]{2,1,0:T(8,128)(2,1)S(1)}, bf16[8,48,2304]{2,1,0:T(8,128)(2,1)S(1)}, u32[]{:S(2)}, u32[]{:S(2)}) collective-permute-start(bf16[8,48,2304]{2,1,0:T(8,128)(2,1)S(1)} %copy-done.40), channel_id=1, source_target_pairs={{0,4},{1,3},{2,6},{3,1},{4,0},{5,7},{6,2},{7,5},{8,12},{9,11},{10,... | collective-permute-start | bytes 5308424 | tf_op jit(solution)/shard_map/ppermute | solution.py:735
  238.8 24.9 %collective-permute-start.42 = (bf16[16,48,2304]{2,1,0:T(8,128)(2,1)S(1)}, bf16[16,48,2304]{2,1,0:T(8,128)(2,1)S(1)}, u32[]{:S(2)}, u32[]{:S(2)}) collective-permute-start(bf16[16,48,2304]{2,1,0:T(8,128)(2,1)S(1)} %get-tuple-element.260), channel_id=1, source_target_pairs={{0,1},{1,0},{2,3},{3,2},{4,5},{5,4},{6,7},{7,6},{8,9},{9,8},{10,11... | collective-permute-start | bytes 10616840 | tf_op jit(solution)/shard_map/ppermute | solution.py:735
  239.3 25.6 %collective-permute-start.41 = (bf16[4,48,2304]{2,1,0:T(8,128)(2,1)S(1)}, bf16[4,48,2304]{2,1,0:T(8,128)(2,1)S(1)}, u32[]{:S(2)}, u32[]{:S(2)}) collective-permute-start(bf16[4,48,2304]{2,1,0:T(8,128)(2,1)S(1)} %get-tuple-element.321), channel_id=1, source_target_pairs={{0,2},{1,5},{2,0},{3,7},{4,6},{5,1},{6,4},{7,3},{8,10},{9,13},{10,... | collective-permute-start | bytes 2654216 | tf_op jit(solution)/shard_map/ppermute | solution.py:735
  247.3 17.9 %collective-permute-start.40 = (bf16[8,48,1408]{2,1,0:T(8,128)(2,1)S(1)}, bf16[8,48,1408]{2,1,0:T(8,128)(2,1)S(1)}, u32[]{:S(2)}, u32[]{:S(2)}) collective-permute-start(bf16[8,48,1408]{2,1,0:T(8,128)(2,1)S(1)} %get-tuple-element.317), channel_id=1, source_target_pairs={{0,4},{1,3},{2,6},{3,1},{4,0},{5,7},{6,2},{7,5},{8,12},{9,11},{10,... | collective-permute-start | bytes 3244040 | tf_op jit(solution)/shard_map/ppermute | solution.py:735
  247.8 15.9 %collective-permute-start.46 = (f32[2,2,384]{2,1,0:T(2,128)S(1)}, f32[2,2,384]{2,1,0:T(2,128)S(1)}, u32[]{:S(2)}, u32[]{:S(2)}) collective-permute-start(f32[2,2,384]{2,1,0:T(2,128)S(1)} %pad_maximum_fusion.17), channel_id=1, source_target_pairs={{0,6},{1,7},{2,4},{3,5},{4,2},{5,3},{6,0},{7,1},{8,14},{9,15},{10,... | collective-permute-start | bytes 18440 | tf_op jit(solution)/shard_map/ppermute | solution.py:735
  255.0 8.7 %collective-permute-start.45 = (f32[2,2,384]{2,1,0:T(2,128)S(1)}, f32[2,2,384]{2,1,0:T(2,128)S(1)}, u32[]{:S(2)}, u32[]{:S(2)}) collective-permute-start(f32[2,2,384]{2,1,0:T(2,128)S(1)} %pad_maximum_fusion.17), channel_id=1, source_target_pairs={{0,4},{1,5},{2,6},{3,7},{4,0},{5,1},{6,2},{7,3},{8,12},{9,13},{10,... | collective-permute-start | bytes 18440 | tf_op jit(solution)/shard_map/ppermute | solution.py:735
  264.6 30.1 %collective-permute-start.48 = (bf16[8,48,2304]{2,1,0:T(8,128)(2,1)S(1)}, bf16[8,48,2304]{2,1,0:T(8,128)(2,1)S(1)}, u32[]{:S(2)}, u32[]{:S(2)}) collective-permute-start(bf16[8,48,2304]{2,1,0:T(8,128)(2,1)S(1)} %get-tuple-element.265), channel_id=1, source_target_pairs={{0,4},{1,3},{2,6},{3,1},{4,0},{5,7},{6,2},{7,5},{8,12},{9,11},{10,... | collective-permute-start | bytes 5308424 | tf_op jit(solution)/shard_map/ppermute | solution.py:735
  273.1 14.1 %collective-permute-start.50 = (bf16[2,48,2304]{2,1,0:T(8,128)(2,1)S(1)}, bf16[2,48,2304]{2,1,0:T(8,128)(2,1)S(1)}, u32[]{:S(2)}, u32[]{:S(2)}) collective-permute-start(bf16[2,48,2304]{2,1,0:T(8,128)(2,1)S(1)} %get-tuple-element.327), channel_id=1, source_target_pairs={{0,16},{1,9},{2,18},{3,11},{4,20},{5,13},{6,22},{7,15},{8,24},{9,1... | collective-permute-start | bytes 1327112 | tf_op jit(solution)/shard_map/ppermute | solution.py:735
  276.2 15.3 %collective-permute-start.49 = (bf16[4,48,1408]{2,1,0:T(8,128)(2,1)S(1)}, bf16[4,48,1408]{2,1,0:T(8,128)(2,1)S(1)}, u32[]{:S(2)}, u32[]{:S(2)}) collective-permute-start(bf16[4,48,1408]{2,1,0:T(8,128)(2,1)S(1)} %get-tuple-element.325), channel_id=1, source_target_pairs={{0,2},{1,5},{2,0},{3,7},{4,6},{5,1},{6,4},{7,3},{8,10},{9,13},{10,... | collective-permute-start | bytes 1622024 | tf_op jit(solution)/shard_map/ppermute | solution.py:735
  281.6 17.0 %collective-permute-start.47 = (bf16[16,48,1408]{2,1,0:T(8,128)(2,1)S(1)}, bf16[16,48,1408]{2,1,0:T(8,128)(2,1)S(1)}, u32[]{:S(2)}, u32[]{:S(2)}) collective-permute-start(bf16[16,48,1408]{2,1,0:T(8,128)(2,1)S(1)} %get-tuple-element.286), channel_id=1, source_target_pairs={{0,1},{1,0},{2,3},{3,2},{4,5},{5,4},{6,7},{7,6},{8,9},{9,8},{10,11... | collective-permute-start | bytes 6488072 | tf_op jit(solution)/shard_map/ppermute | solution.py:735
  287.3 7.2 %collective-permute-start.60 = (bf16[1,48,2304]{2,1,0:T(8,128)(2,1)S(1)}, bf16[1,48,2304]{2,1,0:T(8,128)(2,1)S(1)}, u32[]{:S(2)}, u32[]{:S(2)}) collective-permute-start(bf16[1,48,2304]{2,1,0:T(8,128)(2,1)S(1)} %add_convert_fusion.24), channel_id=1, source_target_pairs={{0,8},{1,17},{2,10},{3,19},{4,12},{5,21},{6,14},{7,23},{8,0},{9,25... | collective-permute-start | bytes 663560 | tf_op jit(solution)/shard_map/ppermute | solution.py:735
  291.6 10.6 %collective-permute-start.53 = (bf16[2,48,1408]{2,1,0:T(8,128)(2,1)S(1)}, bf16[2,48,1408]{2,1,0:T(8,128)(2,1)S(1)}, u32[]{:S(2)}, u32[]{:S(2)}) collective-permute-start(bf16[2,48,1408]{2,1,0:T(8,128)(2,1)S(1)} %get-tuple-element.331), channel_id=1, source_target_pairs={{0,16},{1,9},{2,18},{3,11},{4,20},{5,13},{6,22},{7,15},{8,24},{9,1... | collective-permute-start | bytes 811016 | tf_op jit(solution)/shard_map/ppermute | solution.py:735
  295.4 19.0 %collective-permute-start.52 = (bf16[4,48,2304]{2,1,0:T(8,128)(2,1)S(1)}, bf16[4,48,2304]{2,1,0:T(8,128)(2,1)S(1)}, u32[]{:S(2)}, u32[]{:S(2)}) collective-permute-start(bf16[4,48,2304]{2,1,0:T(8,128)(2,1)S(1)} %get-tuple-element.318), channel_id=1, source_target_pairs={{0,2},{1,5},{2,0},{3,7},{4,6},{5,1},{6,4},{7,3},{8,10},{9,13},{10,... | collective-permute-start | bytes 2654216 | tf_op jit(solution)/shard_map/ppermute | solution.py:735
  302.7 18.9 %collective-permute-start.51 = (bf16[8,48,1408]{2,1,0:T(8,128)(2,1)S(1)}, bf16[8,48,1408]{2,1,0:T(8,128)(2,1)S(1)}, u32[]{:S(2)}, u32[]{:S(2)}) collective-permute-start(bf16[8,48,1408]{2,1,0:T(8,128)(2,1)S(1)} %get-tuple-element.315), channel_id=1, source_target_pairs={{0,4},{1,3},{2,6},{3,1},{4,0},{5,7},{6,2},{7,5},{8,12},{9,11},{10,... | collective-permute-start | bytes 3244040 | tf_op jit(solution)/shard_map/ppermute | solution.py:735
  302.8 19.7 %collective-permute-start.59 = (bf16[1,48,1408]{2,1,0:T(8,128)(2,1)S(1)}, bf16[1,48,1408]{2,1,0:T(8,128)(2,1)S(1)}, u32[]{:S(2)}, u32[]{:S(2)}) collective-permute-start(bf16[1,48,1408]{2,1,0:T(8,128)(2,1)S(1)} %add_convert_fusion.28), channel_id=1, source_target_pairs={{0,8},{1,17},{2,10},{3,19},{4,12},{5,21},{6,14},{7,23},{8,0},{9,25... | collective-permute-start | bytes 405512 | tf_op jit(solution)/shard_map/ppermute | solution.py:735
  314.6 13.6 %collective-permute-start.55 = (bf16[2,48,2304]{2,1,0:T(8,128)(2,1)S(1)}, bf16[2,48,2304]{2,1,0:T(8,128)(2,1)S(1)}, u32[]{:S(2)}, u32[]{:S(2)}) collective-permute-start(bf16[2,48,2304]{2,1,0:T(8,128)(2,1)S(1)} %get-tuple-element.328), channel_id=1, source_target_pairs={{0,16},{1,9},{2,18},{3,11},{4,20},{5,13},{6,22},{7,15},{8,24},{9,1... | collective-permute-start | bytes 1327112 | tf_op jit(solution)/shard_map/ppermute | solution.py:735
  321.9 9.4 %collective-permute-start.54 = (bf16[4,48,1408]{2,1,0:T(8,128)(2,1)S(1)}, bf16[4,48,1408]{2,1,0:T(8,128)(2,1)S(1)}, u32[]{:S(2)}, u32[]{:S(2)}) collective-permute-start(bf16[4,48,1408]{2,1,0:T(8,128)(2,1)S(1)} %get-tuple-element.322), channel_id=1, source_target_pairs={{0,2},{1,5},{2,0},{3,7},{4,6},{5,1},{6,4},{7,3},{8,10},{9,13},{10,... | collective-permute-start | bytes 1622024 | tf_op jit(solution)/shard_map/ppermute | solution.py:735
  322.7 30.8 %collective-permute-start.62 = (f32[24,2944]{1,0:T(8,128)S(1)}, f32[24,2944]{1,0:T(8,128)S(1)}, u32[]{:S(2)}, u32[]{:S(2)}) collective-permute-start(f32[24,2944]{1,0:T(8,128)S(1)} %get-tuple-element.334), channel_id=1, source_target_pairs={{0,1},{1,0},{2,3},{3,2},{4,5},{5,4},{6,7},{7,6},{8,9},{9,8},{10,11... | collective-permute-start | bytes 847880 | tf_op jit(solution)/shard_map/ppermute | solution.py:735
  331.5 16.7 %collective-permute-start.56 = (bf16[2,48,1408]{2,1,0:T(8,128)(2,1)S(1)}, bf16[2,48,1408]{2,1,0:T(8,128)(2,1)S(1)}, u32[]{:S(2)}, u32[]{:S(2)}) collective-permute-start(bf16[2,48,1408]{2,1,0:T(8,128)(2,1)S(1)} %get-tuple-element.332), channel_id=1, source_target_pairs={{0,16},{1,9},{2,18},{3,11},{4,20},{5,13},{6,22},{7,15},{8,24},{9,1... | collective-permute-start | bytes 811016 | tf_op jit(solution)/shard_map/ppermute | solution.py:735
  331.9 16.4 %collective-permute-start.58 = (bf16[1,48,2304]{2,1,0:T(8,128)(2,1)S(1)}, bf16[1,48,2304]{2,1,0:T(8,128)(2,1)S(1)}, u32[]{:S(2)}, u32[]{:S(2)}) collective-permute-start(bf16[1,48,2304]{2,1,0:T(8,128)(2,1)S(1)} %add_convert_fusion.26), channel_id=1, source_target_pairs={{0,8},{1,17},{2,10},{3,19},{4,12},{5,21},{6,14},{7,23},{8,0},{9,25... | collective-permute-start | bytes 663560 | tf_op jit(solution)/shard_map/ppermute | solution.py:735
  (63 other events, 475.5 us)

commit v4 on v3

--- a/solution.py
+++ b/solution.py
@@ -11,7 +11,7 @@
 EPS = 1e-06
 SUB = 8
 UNIT = 48
-HALVES = {"mix": 1024, "out": 384, "up": 1536}
+HALVES = {"mix": 1024, "out": 384, "up": 1536, "gate": 384, "cell": 640}
 ROWS = 32
 F32 = jnp.float32
 BF16 = jnp.bfloat16
@@ -192,7 +192,7 @@
         in_specs=[SMEM, VMEM, VMEM] + [ANY] * len(weights),
         out_specs=(VMEM,) * 8,
         scratch_shapes=[pltpu.VMEM((width, mix_width(plan, width)), BF16), pltpu.SemaphoreType.DMA],
-        compiler_params=pltpu.CompilerParams(vmem_limit_bytes=24 << 20),
+        compiler_params=pltpu.CompilerParams(vmem_limit_bytes=12 << 20),
         cost_estimate=COST,
         name="front",
     )(me, x, params, *weights)
@@ -279,7 +279,7 @@
         in_specs=[SMEM] + [VMEM] * 7 + [ANY] * len(weights),
         out_specs=(VMEM,) * 7,
         scratch_shapes=[pltpu.VMEM((width, width), BF16), pltpu.SemaphoreType.DMA],
-        compiler_params=pltpu.CompilerParams(vmem_limit_bytes=24 << 20),
+        compiler_params=pltpu.CompilerParams(vmem_limit_bytes=12 << 20),
         cost_estimate=COST,
         name="mid",
     )(me, x, params, gate, kept, feed, sub, every, *weights)
@@ -321,31 +321,56 @@
             pltpu.VMEM((inner, width), BF16),
             pltpu.SemaphoreType.DMA((2,)),
         ],
-        compiler_params=pltpu.CompilerParams(vmem_limit_bytes=24 << 20),
+        compiler_params=pltpu.CompilerParams(vmem_limit_bytes=17 << 20),
         cost_estimate=COST,
         name="ffn",
     )(me, after, lifted, *weights)
 
 
-def back_ffn_kernel(plan, count, me_ref, dx_ref, p_ref, both_ref, after_ref, *refs):
+def lower(me_ref, dx_ref, dlow_ref):
+    rows, width = dx_ref.shape
+    if dx_ref.dtype == BF16:
+        at = lax.broadcasted_iota(jnp.int32, (rows, GROUP), 0)
+        live = at < me_ref[4]
+        for t in range(width // GROUP):
+            cols = slice(t * GROUP, (t + 1) * GROUP)
+            dlow_ref[:, cols] = jnp.where(live, dx_ref[:, cols].astype(F32), 0.0).astype(BF16)
+        return dlow_ref
+    dlow_ref[...] = dx_ref[...].astype(BF16)
+    return dx_ref
+
+
+def lift_back(grad_ref, p_ref, after_ref, work_ref, dafter_ref, dmid_ref, gain_ref):
+    def norm_back(r):
+        after = after_ref[r, :]
+        scale = lax.rsqrt(jnp.mean(after * after, axis=1, keepdims=True) + EPS)
+        normal = after * scale
+        lift = work_ref[r, :]
+        e = lift * p_ref[2:3, :]
+        d = grad_ref[r, :].astype(F32) + scale * (e - normal * jnp.mean(e * normal, axis=1, keepdims=True))
+        dafter_ref[r, :] = d
+        dmid_ref[r, :] = d.astype(BF16)
+        work_ref[r, :] = lift * normal
+
+    over_rows(after_ref.shape[0], norm_back)
+    gain_ref[...] = jnp.sum(work_ref[...], axis=0, keepdims=True)
+
+
+def back_ffn_kernel(plan, count, rels, me_ref, dx_ref, p_ref, both_ref, after_ref, *refs):
     w_hbm, refs = refs[:count], refs[count:]
-    dlow_ref, dboth_ref, dafter_ref, dmid_ref, gain_ref, work_ref, up_ref, down_ref, sems = refs
+    if rels is not None:
+        lifted_ref, keep_ref, send_ref, *refs, dboth_ref, grad_up_ref, out_sem = refs
+        dlow_ref, *refs = refs
+    else:
+        dlow_ref, dboth_ref, *refs = refs
+    dafter_ref, dmid_ref, gain_ref, work_ref, up_ref, down_ref, sems = refs
     rows, width = dx_ref.shape
     inner = down_ref.shape[0]
     up_pairs = pairs_of(plan, w_hbm, me_ref, "up", up_ref)
     down_pairs = pairs_of(plan, w_hbm, me_ref, "down", down_ref)
     load_start(down_pairs, sems.at[1])
     load_start(up_pairs, sems.at[0])
-    if dx_ref.dtype == BF16:
-        at = lax.broadcasted_iota(jnp.int32, (rows, GROUP), 0)
-        live = at < me_ref[4]
-        for t in range(width // GROUP):
-            cols = slice(t * GROUP, (t + 1) * GROUP)
-            dlow_ref[:, cols] = jnp.where(live, dx_ref[:, cols].astype(F32), 0.0).astype(BF16)
-        grad_ref = dlow_ref
-    else:
-        dlow_ref[...] = dx_ref[...].astype(BF16)
-        grad_ref = dx_ref
+    grad_ref = lower(me_ref, dx_ref, dlow_ref)
     dlow = dlow_ref[...]
     load_wait(down_pairs, sems.at[1])
     step = width // 2
@@ -357,48 +382,105 @@
         sig = jax.nn.sigmoid(a)
         dboth_ref[:, cols] = (dh * both_ref[:, more] * (sig * (1.0 + a * (1.0 - sig)))).astype(BF16)
         dboth_ref[:, more] = (dh * (a * sig)).astype(BF16)
+    if rels is not None:
+        products(lifted_ref[...], dboth_ref, grad_up_ref, grad_up_ref.shape[1])
+        pairs = export(me_ref, rels, "up", grad_up_ref, 0, HALVES["up"], keep_ref, send_ref, out_sem)
     load_wait(up_pairs, sems.at[0])
     work_ref[...] = dot_t(dboth_ref[...], up_ref[...])
 
-    def norm_back(r):
-        after = after_ref[r, :]
-        scale = lax.rsqrt(jnp.mean(after * after, axis=1, keepdims=True) + EPS)
-        normal = after * scale
-        lift = work_ref[r, :]
-        e = lift * p_ref[2:3, :]
-        d = grad_ref[r, :].astype(F32) + scale * (e - normal * jnp.mean(e * normal, axis=1, keepdims=True))
-        dafter_ref[r, :] = d
-        dmid_ref[r, :] = d.astype(BF16)
-        work_ref[r, :] = lift * normal
-
-    over_rows(rows, norm_back)
-    gain_ref[...] = jnp.sum(work_ref[...], axis=0, keepdims=True)
-
-
-def back_ffn(plan, me, dx, params, both, after, weights):
+    lift_back(grad_ref, p_ref, after_ref, work_ref, dafter_ref, dmid_ref, gain_ref)
+    if rels is not None:
+        load_wait(pairs, out_sem)
+
+
+def turn_kernel(plan, count, rels, me_ref, dx_ref, p_ref, after_ref, lifted_ref, *refs):
+    w_hbm, refs = refs[:count], refs[count:]
+    (
+        keep_ref, send_ref, next_ref, hidden_ref, dlow_ref, dafter_ref, dmid_ref, gain_ref,
+        dboth_ref, grad_up_ref, work_ref, up_ref, down_ref, sems, out_sem,
+    ) = refs
+    width = dx_ref.shape[1]
+    inner = down_ref.shape[0]
+    up_pairs = pairs_of(plan, w_hbm, me_ref, "up", up_ref)
+    down_pairs = pairs_of(plan, w_hbm, me_ref, "down", down_ref)
+    load_start(up_pairs, sems.at[0])
+    load_start(down_pairs, sems.at[1])
+    grad_ref = lower(me_ref, dx_ref, dlow_ref)
+    dlow = dlow_ref[...]
+    lifted = lifted_ref[...]
+    load_wait(up_pairs, sems.at[0])
+    load_wait(down_pairs, sems.at[1])
+    step = width // 2
+    for k in range(inner // step):
+        cols = slice(k * step, (k + 1) * step)
+        more = slice(inner + k * step, inner + (k + 1) * step)
+        a = dot(lifted, up_ref[:, cols])
+        b = dot(lifted, up_ref[:, more])
+        dh = dot_t(dlow, down_ref[cols, :])
+        sig = jax.nn.sigmoid(a)
+        gated = a * sig
+        hidden_ref[:, cols] = (gated * b).astype(BF16)
+        dboth_ref[:, cols] = (dh * b * (sig * (1.0 + a * (1.0 - sig)))).astype(BF16)
+        dboth_ref[:, more] = (dh * gated).astype(BF16)
+    products(lifted, dboth_ref, grad_up_ref, grad_up_ref.shape[1])
+    pairs = export(me_ref, rels, "up", grad_up_ref, 0, HALVES["up"], keep_ref, send_ref, out_sem)
+    work_ref[...] = dot_t(dboth_ref[...], up_ref[...])
+    lift_back(grad_ref, p_ref, after_ref, work_ref, dafter_ref, dmid_ref, gain_ref)
+    next_ref[...] = (after_ref[...] + dot(hidden_ref[...], down_ref[...])).astype(next_ref.dtype)
+    load_wait(pairs, out_sem)
+
+
+def turn(plan, rels, me, dx, params, after, lifted, weights):
     rows, width = dx.shape
     inner = 2 * width
+    block = sds((2 ** len(STAGES), UNIT, HALVES["up"]), BF16)
+    low = sds((rows, width), BF16)
     return pl.pallas_call(
-        functools.partial(back_ffn_kernel, plan, len(weights)),
-        out_shape=(
-            sds((rows, width), BF16),
-            sds((rows, 2 * inner), BF16),
-            sds((rows, width)),
-            sds((rows, width), BF16),
-            sds((1, width)),
-        ),
+        functools.partial(turn_kernel, plan, len(weights), rels),
+        out_shape=(block, block, low, sds((rows, inner), BF16), low, sds((rows, width)), low, sds((1, width))),
         in_specs=[SMEM] + [VMEM] * 4 + [ANY] * len(weights),
-        out_specs=(VMEM,) * 5,
+        out_specs=(ANY, ANY) + (VMEM,) * 6,
+        scratch_shapes=[
+            pltpu.VMEM((rows, 2 * inner), BF16),
+            pltpu.VMEM((width, 2 * inner), BF16),
+            pltpu.VMEM((rows, width), F32),
+            pltpu.VMEM((width, 2 * inner), BF16),
+            pltpu.VMEM((inner, width), BF16),
+            pltpu.SemaphoreType.DMA((2,)),
+            pltpu.SemaphoreType.DMA,
+        ],
+        compiler_params=pltpu.CompilerParams(vmem_limit_bytes=22 << 20),
+        cost_estimate=COST,
+        name="turn",
+    )(me, dx, params, after, lifted, *weights)
+
+
+def back_ffn(plan, me, dx, params, both, after, weights, rels=None, lifted=()):
+    rows, width = dx.shape
+    inner = 2 * width
+    block = sds((2 ** len(STAGES), UNIT, HALVES["up"]), BF16)
+    dboth = (rows, 2 * inner)
+    outs = (sds((rows, width), BF16), sds(dboth, BF16), sds((rows, width)), sds((rows, width), BF16), sds((1, width)))
+    specs, more = (VMEM,) * 5, []
+    if rels is not None:
+        outs, specs = (block, block, outs[0], *outs[2:]), (ANY, ANY, *specs[1:])
+        more = [pltpu.VMEM(dboth, BF16), pltpu.VMEM((width, 2 * inner), BF16), pltpu.SemaphoreType.DMA]
+    return pl.pallas_call(
+        functools.partial(back_ffn_kernel, plan, len(weights), rels),
+        out_shape=outs,
+        in_specs=[SMEM] + [VMEM] * 4 + [ANY] * len(weights) + [VMEM] * len(lifted),
+        out_specs=specs,
         scratch_shapes=[
             pltpu.VMEM((rows, width), F32),
             pltpu.VMEM((width, 2 * inner), BF16),
             pltpu.VMEM((inner, width), BF16),
             pltpu.SemaphoreType.DMA((2,)),
-        ],
-        compiler_params=pltpu.CompilerParams(vmem_limit_bytes=24 << 20),
+        ]
+        + more,
+        compiler_params=pltpu.CompilerParams(vmem_limit_bytes=25 << 20),
         cost_estimate=COST,
         name="back_ffn",
-    )(me, dx, params, both, after, *weights)
+    )(me, dx, params, both, after, *weights, *lifted)
 
 
 def back_mid_kernel(
@@ -475,21 +557,24 @@
             pltpu.VMEM((width, width), BF16),
             pltpu.SemaphoreType.DMA,
         ],
-        compiler_params=pltpu.CompilerParams(vmem_limit_bytes=24 << 20),
+        compiler_params=pltpu.CompilerParams(vmem_limit_bytes=11 << 20),
         cost_estimate=COST,
         name="back_mid",
     )(me, dmid, params, gn, rg, gate, states, kept, sub, *weights)
 
 
 def back_two_kernel(
-    plan, count, me_ref, x_ref, p_ref, dafter_ref, dgpre_ref, dstates_ref, states_ref, kept_ref, rate_ref, cpre_ref,
+    plan, count, rels, spare, me_ref, x_ref, p_ref, dafter_ref, dgpre_ref, dstates_ref, states_ref, kept_ref, rate_ref, cpre_ref,
     first_ref, sub_ref, rsub_ref, every_ref, revery_ref, *refs
 ):
-    w_hbm, refs = refs[:count], refs[count:]
-    (
-    dmixin_ref, dx_ref, gains_ref,
-    work_ref, q_ref, turn_ref, start_ref, w_ref, sem,
-    ) = refs
+    w_hbm, extra, refs = refs[:count], refs[count : count + spare], refs[count + spare :]
+    if rels is not None:
+        normed_ref, *extra = extra
+        keep_ref, send_ref, dx_ref, gains_ref, *refs, mix_ref, held_ref, out_sem = refs
+        dmixin_ref, *refs = refs
+    else:
+        dmixin_ref, dx_ref, gains_ref, *refs = refs
+    work_ref, q_ref, turn_ref, start_ref, w_ref, sem = refs
     rows, width = x_ref.shape
     half = width // 2
     block = rows // SUB
@@ -572,31 +657,52 @@
     over_rows(rows, norm_back)
     gains_ref[0:1, :] = jnp.sum(work_ref[...], axis=0, keepdims=True)
 
-
-def back_two(plan, me, x, params, dafter, dgpre, dstates, states, kept, rate, cpre, first, sub, rsub, every, revery, weights):
+    if rels is None:
+        return
+    held_ref[...] = jnp.zeros_like(held_ref)
+    for k in range(spare // 3):
+        two, mid_gain, ffn_gain = (gains_ref, *extra)[3 * k : 3 * k + 3]
+        held_ref[4 * k : 4 * k + 1, :] = two[0:1, :]
+        held_ref[4 * k + 1 : 4 * k + 2, :] = mid_gain[...]
+        held_ref[4 * k + 2 : 4 * k + 3, :] = ffn_gain[...]
+        held_ref[4 * k + 3 : 4 * k + 4, :] = two[1:2, :]
+    normed = normed_ref[...]
+    products(normed, dmixin_ref, mix_ref, width)
+    products(normed, dmixin_ref, mix_ref, half, 2 * width, width)
+    mix_ref[:, width + half :] = jnp.transpose(held_ref[...]).astype(BF16)
+    pairs = export(me_ref, rels, "cell", mix_ref, 0, HALVES["cell"], keep_ref, send_ref, out_sem)
+    load_wait(pairs, out_sem)
+
+
+def back_two(plan, me, x, params, dafter, dgpre, dstates, states, kept, rate, cpre, first, sub, rsub, every, revery, weights, rels=None, extra=()):
     rows, width = x.shape
     half = width // 2
+    size = 2 * width + half
+    block = sds((2 ** len(STAGES), UNIT, HALVES["cell"]), BF16)
+    scratch = [
+        pltpu.VMEM((rows, width), F32),
+        pltpu.VMEM((width // GROUP, rows, GROUP), F32),
+        pltpu.VMEM((half // GROUP, rows, GROUP), F32),
+        pltpu.VMEM((2, SUB, half), F32),
+        pltpu.VMEM((width, mix_width(plan, width)), BF16),
+        pltpu.SemaphoreType.DMA,
+    ]
+    if rels is None:
+        first_out, specs, more = (sds((rows, size), BF16),), (VMEM,), []
+    else:
+        first_out, specs = (block, block), (ANY, ANY)
+        scratch.insert(0, pltpu.VMEM((rows, size), BF16))
+        more = [pltpu.VMEM((width, 2 * HALVES["cell"]), BF16), pltpu.VMEM((GROUP, width), F32), pltpu.SemaphoreType.DMA]
     return pl.pallas_call(
-        functools.partial(back_two_kernel, plan, len(weights)),
-        out_shape=(
-            sds((rows, 2 * width + half), BF16),
-            sds((rows, width)),
-            sds((2, width)),
-        ),
-        in_specs=[SMEM] + [VMEM] * 14 + [ANY] * len(weights),
-        out_specs=(VMEM,) * 3,
-        scratch_shapes=[
-            pltpu.VMEM((rows, width), F32),
-            pltpu.VMEM((width // GROUP, rows, GROUP), F32),
-            pltpu.VMEM((half // GROUP, rows, GROUP), F32),
-            pltpu.VMEM((2, SUB, half), F32),
-            pltpu.VMEM((width, mix_width(plan, width)), BF16),
-            pltpu.SemaphoreType.DMA,
-        ],
-        compiler_params=pltpu.CompilerParams(vmem_limit_bytes=24 << 20),
+        functools.partial(back_two_kernel, plan, len(weights), rels, len(extra)),
+        out_shape=first_out + (sds((rows, width)), sds((2, width))),
+        in_specs=[SMEM] + [VMEM] * 14 + [ANY] * len(weights) + [VMEM] * len(extra),
+        out_specs=specs + (VMEM, VMEM),
+        scratch_shapes=scratch + more,
+        compiler_params=pltpu.CompilerParams(vmem_limit_bytes=18 << 20),
         cost_estimate=COST,
         name="back_two",
-    )(me, x, params, dafter, dgpre, dstates, states, kept, rate, cpre, first, sub, rsub, every, revery, *weights)
+    )(me, x, params, dafter, dgpre, dstates, states, kept, rate, cpre, first, sub, rsub, every, revery, *weights, *extra)
 
 
 def row_product(left, right):
@@ -623,81 +729,46 @@
     return pairs
 
 
-def products(left, right_ref, grad_ref, size):
+def products(left, right_ref, grad_ref, size, source=0, target=0):
     step = HALVES["out"]
-    for k in range(size // step):
-        cols = slice(k * step, (k + 1) * step)
-        grad_ref[:, cols] = row_product(left, right_ref[:, cols]).astype(BF16)
-
-
-def grad_ud_kernel(
-    rels, info_ref, lifted_ref, dboth_ref, hidden_ref, dlow_ref, keep_ref, send_ref, up_ref, down_ref, sem
+    for k in range(0, size, step):
+        right = right_ref[:, source + k : source + k + step]
+        grad_ref[:, target + k : target + k + step] = row_product(left, right).astype(BF16)
+
+
+def grad_od_kernel(
+    rels, info_ref, gated_ref, dmid_ref, hidden_ref, dlow_ref, normed_ref, dgpre_ref, keep_ref, send_ref,
+    out_ref, gate_ref, down_ref, sem,
 ):
     width = dlow_ref.shape[1]
     products(hidden_ref[...], dlow_ref, down_ref, width)
-    pairs = export(info_ref, rels, "down", down_ref, HALVES["up"], width, keep_ref, send_ref, sem)
-    products(lifted_ref[...], dboth_ref, up_ref, up_ref.shape[1])
-    pairs += export(info_ref, rels, "up", up_ref, 0, HALVES["up"], keep_ref, send_ref, sem)
+    at = HALVES["out"] + HALVES["gate"]
+    pairs = export(info_ref, rels, "down", down_ref, at, width, keep_ref, send_ref, sem)
+    products(gated_ref[...], dmid_ref, out_ref, width)
+    pairs += export(info_ref, rels, "out", out_ref, 0, HALVES["out"], keep_ref, send_ref, sem)
+    products(normed_ref[...], dgpre_ref, gate_ref, width)
+    pairs += export(info_ref, rels, "gate", gate_ref, HALVES["out"], HALVES["gate"], keep_ref, send_ref, sem)
     load_wait(pairs, sem)
 
 
-def grad_ud(rels, info, lifted, dboth, hidden, dlow):
-    rows, width = dlow.shape
-    inner = hidden.shape[1]
-    shape = sds((len(rels[0]), UNIT, HALVES["up"] + width), BF16)
+def grad_od(rels, info, gated, dmid, hidden, dlow, normed, dgpre):
+    width = dlow.shape[1]
+    shape = sds((len(rels[0]), UNIT, HALVES["out"] + HALVES["gate"] + width), BF16)
     return pl.pallas_call(
-        functools.partial(grad_ud_kernel, rels),
+        functools.partial(grad_od_kernel, rels),
         out_shape=(shape, shape),
-        in_specs=[SMEM] + [VMEM] * 4,
-        out_specs=(ANY, ANY),
-        scratch_shapes=[
-            pltpu.VMEM((width, 2 * inner), BF16),
-            pltpu.VMEM((inner, width), BF16),
-            pltpu.SemaphoreType.DMA,
-        ],
-        compiler_params=pltpu.CompilerParams(vmem_limit_bytes=24 << 20),
-        cost_estimate=COST,
-        name="grad_ud",
-    )(info, lifted, dboth, hidden, dlow)
-
-
-def grad_mo_kernel(rels, info_ref, gated_ref, dmid_ref, normed_ref, dmixin_ref, *refs):
-    extra, (keep_ref, send_ref, out_ref, mix_ref, held_ref, sem) = refs[:-6], refs[-6:]
-    width = dmid_ref.shape[1]
-    products(gated_ref[...], dmid_ref, out_ref, width)
-    pairs = export(info_ref, rels, "out", out_ref, HALVES["mix"], HALVES["out"], keep_ref, send_ref, sem)
-    size = dmixin_ref.shape[1]
-    held_ref[...] = jnp.zeros_like(held_ref)
-    for k in range(len(extra) // 3):
-        two, mid_gain, ffn_gain = extra[3 * k : 3 * k + 3]
-        held_ref[4 * k : 4 * k + 1, :] = two[0:1, :]
-        held_ref[4 * k + 1 : 4 * k + 2, :] = mid_gain[...]
-        held_ref[4 * k + 2 : 4 * k + 3, :] = ffn_gain[...]
-        held_ref[4 * k + 3 : 4 * k + 4, :] = two[1:2, :]
-    mix_ref[:, size:] = jnp.transpose(held_ref[...]).astype(BF16)
-    products(normed_ref[...], dmixin_ref, mix_ref, size)
-    pairs += export(info_ref, rels, "mix", mix_ref, 0, HALVES["mix"], keep_ref, send_ref, sem)
-    load_wait(pairs, sem)
-
-
-def grad_mo(rels, info, gated, dmid, normed, dmixin, extra):
-    rows, width = normed.shape
-    shape = sds((len(rels[0]), UNIT, HALVES["mix"] + HALVES["out"]), BF16)
-    return pl.pallas_call(
-        functools.partial(grad_mo_kernel, rels),
-        out_shape=(shape, shape),
-        in_specs=[SMEM] + [VMEM] * (4 + len(extra)),
+        in_specs=[SMEM] + [VMEM] * 6,
         out_specs=(ANY, ANY),
         scratch_shapes=[
             pltpu.VMEM((width, width), BF16),
-            pltpu.VMEM((width, 2 * HALVES["mix"]), BF16),
-            pltpu.VMEM((GROUP, width), F32),
+            pltpu.VMEM((width, width), BF16),
+            pltpu.VMEM((hidden.shape[1], width), BF16),
             pltpu.SemaphoreType.DMA,
         ],
-        compiler_params=pltpu.CompilerParams(vmem_limit_bytes=24 << 20),
+        compiler_params=pltpu.CompilerParams(vmem_limit_bytes=11 << 20),
         cost_estimate=COST,
-        name="grad_mo",
-    )(info, gated, dmid, normed, dmixin, *extra)
+        name="grad_od",
+    )(info, gated, dmid, hidden, dlow, normed, dgpre)
 
 
 def table_kernel(plan, count, me_ref, *refs):
@@ -724,7 +795,7 @@
         in_specs=[SMEM] + [ANY] * len(weights),
         out_specs=VMEM,
         scratch_shapes=[pltpu.VMEM((width, 2 * GROUP), BF16), pltpu.SemaphoreType.DMA],
-        compiler_params=pltpu.CompilerParams(vmem_limit_bytes=16 << 20),
+        compiler_params=pltpu.CompilerParams(vmem_limit_bytes=6 << 20),
         cost_estimate=COST,
         name="table",
     )(me, *weights)
@@ -745,12 +816,23 @@
         self.last = values[0]
         return values
 
-    def join(self, *moves):
+    def join(self, *moves, cores=()):
+        values = [move.got for move in moves]
+        for move in cores:
+            values += [move.last_core, move.held_core]
+        values = list(self.step(*values))
         for move in moves:
-            (move.got,) = self.step(move.got)
-
-    def join_core(self, move):
-        (move.last_core, move.held_core) = self.step(move.last_core, move.held_core)
+            move.got = values.pop(0)
+        for move in cores:
+            move.last_core, move.held_core = values.pop(0), values.pop(0)
+
+
+    def pass_on(self, *moves):
+        for move in moves:
+            move.ready()
+        for move, value in zip(moves, self.step(*(move.out for move in moves))):
+            move.out = value
+            move.send()
 
 
 def rels_of(stages):
@@ -770,8 +852,12 @@
         if self.got is not None:
             self.held = jnp.concatenate([self.held, self.got])
 
-    def next(self):
+    def ready(self):
         self.join()
+        self.out = self.held
+
+    def send(self):
+        self.held = self.out
         one, two = self.stages[self.at]
         self.at += 1
         self.got = swap(self.held, (2 * one, 2 * two))
@@ -807,20 +893,23 @@
         def joined(part):
             return (self.held[part].astype(F32) + self.got[part].astype(F32)).astype(BF16)
 
-        self.low, self.high = joined(slice(0, half)), joined(slice(half, None))
+        self.held, self.out = joined(slice(0, half)), joined(slice(half, None))
+        self.got = None
+
+    def ready(self):
+        if self.got is not None:
+            self.add()
 
     def send(self):
         one, two = self.stages.pop()
-        self.got = swap(self.high, (2 * one, 2 * two))
-        self.held = self.low
-
-    def next(self):
-        self.add()
-        self.send()
-
-
-def exchange(x):
-    pair = jnp.stack([x, swap(x, (1, 1))])
+        self.got = swap(self.out, (2 * one, 2 * two))
+
+
+def exchange(x, order=None):
+    other = swap(x, (1, 1))
+    if order is not None:
+        (other,) = order.step(other)
+    pair = jnp.stack([x, other])
     got = [swap(pair, (k, k)) for k in range(2, lax.axis_size("seq"), 2)]
     return jnp.concatenate([pair] + got)
 
@@ -830,18 +919,19 @@
     mine, other, downs = refs[:depth], refs[depth : 2 * depth], refs[2 * depth : 3 * depth]
     mix_ref, out_ref, up_ref, down_ref, tail_ref = refs[3 * depth :]
     width = down_ref.shape[2]
-    mix_cols = mix_ref.shape[2]
-    size = HALVES["mix"]
+    size = HALVES["cell"]
 
     def place(first, second):
         for l in range(depth):
+            rest = width - size
             mix_ref[l, :, :size] = first[l][:, :size]
-            mix_ref[l, :, size:] = second[l][:, : mix_cols - size]
+            mix_ref[l, :, size:width] = second[l][:, :rest]
+            mix_ref[l, :, 2 * width :] = second[l][:, rest : size - GROUP]
             at = size
-            for name, ref in (("out", out_ref), ("up", up_ref)):
+            for name, ref, begin in (("out", out_ref, 0), ("gate", mix_ref, width), ("up", up_ref, 0)):
                 step = HALVES[name]
-                ref[l, :, :step] = first[l][:, at : at + step]
-                ref[l, :, step:] = second[l][:, at : at + step]
+                ref[l, :, begin : begin + step] = first[l][:, at : at + step]
+                ref[l, :, begin + step : begin + 2 * step] = second[l][:, at : at + step]
                 at += step
         tail_ref[...] = second[0][:, size - GROUP : size]
 
@@ -864,7 +954,7 @@
         out_shape=tuple(sds(shape) for shape in shapes) + (sds((share, GROUP)),),
         in_specs=[SMEM] + [VMEM] * (3 * len(mine)),
         out_specs=(VMEM,) * 5,
-        compiler_params=pltpu.CompilerParams(vmem_limit_bytes=32 << 20),
+        compiler_params=pltpu.CompilerParams(vmem_limit_bytes=8 << 20),
         cost_estimate=COST,
         name="finish",
     )(info, *mine, *other, *downs)
@@ -884,6 +974,8 @@
 
 
 STAGES = ((4, 8), (8, 4), (1, 2), (2, 1))
+LATER = ((1, 2), (4, 8), (8, 4), (2, 1))
+UPPER = (STAGES, LATER, STAGES)
 
 
 def small_of(gains, chan_params):
@@ -970,137 +1062,139 @@
     mos, uds = [], []
     for l in range(depth):
         unit = units[:, l * size : (l + 1) * size]
-        mos.append(Spread(unit[:, :joint], STAGES))
-        uds.append(Spread(jnp.concatenate([unit[:, joint:], w_down[l]], axis=1), STAGES))
-    rels = rels_of(STAGES)
+        stages = LATER if l else STAGES
+        mos.append(Spread(unit[:, :joint], stages))
+        uds.append(Spread(jnp.concatenate([unit[:, joint:], w_down[l]], axis=1), stages))
     plan = {
-        "sources": mos[0].sources(),
         "mix": (0, HALVES["mix"]),
         "out": (HALVES["mix"], HALVES["out"]),
         "small": (HALVES["mix"] - GROUP, GROUP),
         "up": (0, HALVES["up"]),
         "down": (HALVES["up"], width),
     }
+    plans = [dict(plan, sources=mo.sources()) for mo in mos]
 
     order = Order()
-
-    def go(move):
-        order.join(move)
-        move.next()
-
     mo, ud = mos[0], uds[0]
-    more = depth > 1
-    ud.next()
-    mo.next()
-    go(ud)
-    go(mo)
-    go(mo)
-    if more:
-        mos[1].next()
-    go(mo)
+    later = [move for l in range(1, depth) for move in (mos[l], uds[l])]
+    order.pass_on(ud, mo, *later)
+    order.join(ud, mo, *later)
+    order.pass_on(mo, ud, *later)
+    order.join(mo, ud)
+    order.pass_on(mo, ud)
+    order.join(mo, *later[:1])
+    order.pass_on(mo, *later[:1])
     mo.near_core()
-    go(ud)
-    if more:
-        go(mos[1])
-        uds[1].next()
-        order.join(mos[1])
-        go(uds[1])
-    order.join(ud)
-    order.join(mo)
+    order.join(ud, *later[1:2])
+    if later:
+        order.pass_on(*later[1:2])
+    order.join(mo, *later[:1])
     mo.end()
-    ud.next()
+    order.pass_on(ud)
     ud.near_core()
     x = stream
     saved = []
     params = None
     for l in range(depth):
-        mo, ud = mos[l], uds[l]
+        mo, ud, plan = mos[l], uds[l], plans[l]
         more = l + 1 < depth
-        order.join_core(mo)
+        order.join(cores=(mo,))
         if l == 0:
             params = table_of(plan, info, mo.arrays(), depth, width)
         (layer,) = order.step(params[l])
         head = front(plan, info, x, layer, mo.arrays())
         (total,) = order.step(head[-1])
-        every = exchange(total)
+        if more:
+            order.join(ud, uds[l + 1])
+        else:
+            order.join(ud)
+        ud.end()
+        every = exchange(order.step(total)[0])
         (every,) = order.step(every)
-        order.join(ud)
-        ud.end()
         if more:
-            mos[l + 1].next()
-            uds[l + 1].next()
+            order.pass_on(mos[l + 1])
+            mos[l + 1].near_core()
         middle = mid(plan, info, x, layer, head[2], head[4], head[5], head[6], order.step(every)[0], mo.arrays())
         middle = (*middle[:-1], *order.step(middle[-1]))
         if more:
-            go(mos[l + 1])
-            mos[l + 1].near_core()
-        order.join_core(ud)
-        tail = ffn(plan, info, middle[5], middle[6], ud.arrays(), F32 if more else BF16)
-        saved.append((x, every, head, middle, tail, layer))
-        (x,) = order.step(tail[-1])
+            order.join(mos[l + 1], cores=(ud,))
+            mos[l + 1].end()
+            order.pass_on(uds[l + 1])
+            uds[l + 1].near_core()
+        else:
+            order.join(cores=(ud,))
         if more:
-            go(uds[l + 1])
-            uds[l + 1].near_core()
-            order.join(mos[l + 1])
-            mos[l + 1].end()
-    mixed = x
-    dx = cotangent
+            tail = ffn(plan, info, middle[5], middle[6], ud.arrays(), F32)
+            saved.append((x, every, head, middle, tail, layer))
+            (x,) = order.step(tail[-1])
+    later_stages = UPPER if depth > 1 else (STAGES,) * 3
+    keep, send, mixed, hidden, dlow, dafter, dmid, ffn_gain = turn(
+        plan, rels_of(later_stages[0]), info, cotangent, layer, middle[5], middle[6], ud.arrays()
+    )
+    saved.append((x, every, head, middle, (None, hidden, None), layer))
+    above = None
     sums = [None] * depth
     extra = ()
     for l in reversed(range(depth)):
         x, every, (normed, cpre, gate, rate, kept, feed, sub, _), middle, (both, hidden, _), layer = saved[l]
         states, first, gn, rg, gated, after, lifted = middle
-        mo_up, ud_up = sums[l + 1] if l + 1 < depth else (None, None)
-        (dx,) = order.step(dx)
-        dlow, dboth, dafter, dmid, ffn_gain = back_ffn(plan, info, dx, layer, both, after, uds[l].arrays())
-        (dlow,) = order.step(dlow)
-        if mo_up:
-            go(ud_up)
-            go(mo_up)
-        (lifted,) = order.step(lifted)
-        ud = Reduce(*grad_ud(rels, info, lifted, dboth, hidden, dlow), STAGES)
-        (ud.held,) = order.step(ud.held)
+        plan = plans[l]
+        u_stages, od_stages, c_stages = UPPER if l else (STAGES,) * 3
+        if above:
+            (dx,) = order.step(dx)
+            keep, send, dlow, dafter, dmid, ffn_gain = back_ffn(
+                plan, info, dx, layer, both, after, uds[l].arrays(), rels_of(u_stages), (lifted,)
+            )
+        (keep,) = order.step(keep)
+        u = Reduce(keep, send, u_stages)
+        if above:
+            u_up, od_up, c_up = above
+            order.join(od_up, c_up, u_up)
+            od_up.ready()
+            order.pass_on(c_up, u_up)
         (dmid,) = order.step(dmid)
         dgpre, dstates, mid_gain, rsub, rtotal = back_mid(
             plan, info, dmid, layer, gn, rg, gate, states, kept, sub, mos[l].arrays()
         )
         (rtotal,) = order.step(rtotal)
-        revery = exchange(rtotal)
-        order.join(ud)
-        ud.add()
+        order.join(u, *((c_up, u_up) if above else ()))
+        revery = exchange(rtotal, order)
+        waiting = [u] + ([od_up, c_up, u_up] if above else [])
+        for move in waiting:
+            move.ready()
+        (dlow,) = order.step(dlow)
+        od = Reduce(
+            *grad_od(rels_of(od_stages), info, gated, dmid, hidden, dlow, normed, dgpre), od_stages
+        )
+        (od.held,) = order.step(od.held)
         (revery,) = order.step(revery)
-        (ud.high,) = order.step(ud.high)
-        ud.send()
-        if mo_up:
-            go(ud_up)
-            go(mo_up)
+        order.pass_on(*waiting)
         (dstates,) = order.step(dstates)
-        dmixin, dx, gains_b = back_two(
+        more = (normed,)
+        if l == 0:
+            more = (normed, mid_gain, ffn_gain, *extra)
+        keep, send, dx, gains_b = back_two(
             plan, info, x, layer, dafter, dgpre, dstates, states, kept, rate, cpre, first, sub, rsub, every, revery,
-            mos[l].arrays(),
+            mos[l].arrays(), rels_of(c_stages), more,
         )
-        (dmixin,) = order.step(dmixin)
         extra = (gains_b, mid_gain, ffn_gain) + extra
-        mo = Reduce(*grad_mo(rels, info, gated, dmid, normed, dmixin, extra if l == 0 else ()), STAGES)
-        (mo.held,) = order.step(mo.held)
-        if mo_up:
-            go(ud_up)
-            go(mo_up)
-        sums[l] = (mo, ud)
-    mo, ud = sums[0]
-    go(ud)
-    go(mo)
+        (keep,) = order.step(keep)
+        c = Reduce(keep, send, c_stages)
+        order.join(*waiting, od)
+        order.pass_on(od, u, *((od_up, c_up) if above else ()))
+        above = sums[l] = (u, od, c)
+    u, od, c = sums[0]
+    others = ()
     if depth > 1:
-        go(sums[1][0])
-    go(ud)
-    go(mo)
-    go(ud)
-    go(mo)
-    go(mo)
+        u_up, od_up, c_up = sums[1]
+        others = (od_up, c_up)
+    for moves in ((c,), (od, *others), (u,), (c,), (od,), (u,), (c,), (od,), (c,)):
+        order.join(*moves)
+        order.pass_on(*moves)
     mine, other, downs = [], [], []
-    for mo, ud in reversed(sums):
-        ready = ud.add()
-        line = jnp.concatenate([mo.add(), ready[:, : HALVES["up"]]], axis=1)
+    for u, od, c in reversed(sums):
+        ready = od.add()
+        line = jnp.concatenate([c.add(), ready[:, : HALVES["out"] + HALVES["gate"]], u.add()], axis=1)
         first, second = line[:share], line[share:]
         mine.insert(0, jnp.where(core == 0, first, second))
         other.insert(0, swap(jnp.where(core == 0, second, first), (1, 1)))
@@ -1113,7 +1207,7 @@
 
 def body(stream, w_mix, *others):
     n_dp, n_seq = lax.axis_size("dp"), lax.axis_size("seq")
-    fast = n_seq == 8 and n_dp & (n_dp - 1) == 0 and 2 * w_mix.shape[1] == UNIT
+    fast = n_seq == 8 and n_dp == 4 and 2 * w_mix.shape[1] == UNIT and w_mix.shape[0] == 2
     return (fast_body if fast else plain_body)(stream, w_mix, *others)
 
 

time: 362 us -> 348 us (0.961)
  waiting for transfers between devices: 170 us -> 150 us
  starting transfers between devices: 63.7 us -> 75.8 us
  local copies, waits for them, and re-layouts: 15.6 us -> 10.2 us
    ppermute x63 -> x73, waiting for transfers between devices: 170 us -> 150 us  [swap(): return lax.ppermute(x, ALL, [(i, i ^ bits[i % 2]) for i in range(count)])]
    ppermute x63 -> x73, starting transfers between devices: 63.7 us -> 75.8 us  [swap(): return lax.ppermute(x, ALL, [(i, i ^ bits[i % 2]) for i in range(count)])]
    pallas_call x2 -> x1, Pallas kernels: 11.6 us -> 5.29 us  [ffn(): pl.pallas_call(functools.partial(ffn_kernel, plan, len(weights)), out_sha...]
    unnamed x118 -> x52, local copies, waits for them, and re-layouts: 11 us -> 5.81 us
    pallas_call x8 -> x6, Pallas kernels: 46.1 us -> 49.9 us  [the longest x2 17.2 us: back_two(): pl.pallas_call(functools.partial(back_two_kernel, plan, len(weights), rel...]
    convert_element_type x16 -> x24, other arithmetic: 8.46 us -> 7.58 us  [joined(): (self.held[part].astype(F32) + self.got[part].astype(F32)).astype(BF16)]
  transfers between devices with their start and end apart: 63 -> 73, of which waited for: 33 -> 32; matrix products, arithmetic and copies ran while one was open for 2% -> 3% of each run, Pallas kernels for 15% -> 20%
where the time goes in v4:
time: 348 us; the launch traced here: 343 us
  waiting for transfers between devices  150 us (43%)
  Pallas kernels  89.5 us (26%)
  starting transfers between devices  75.8 us (22%)
  other arithmetic  13.9 us (4%)
  local copies, waits for them, and re-layouts  10.2 us (3%)
  between operations  4.27 us (1%)
    ppermute x73, waiting for transfers between devices, swap(): return lax.ppermute(x, ALL, [(i, i ^ bits[i % 2]) for i in range(count)])  150 us
    ppermute x73, starting transfers between devices, swap(): return lax.ppermute(x, ALL, [(i, i ^ bits[i % 2]) for i in range(count)])  75.8 us
    pallas_call x2, Pallas kernels, back_two(): pl.pallas_call(functools.partial(back_two_kernel, plan, len(weights), rel...  17.2 us
    pallas_call x1, Pallas kernels, turn(): pl.pallas_call(functools.partial(turn_kernel, plan, len(weights), rels),...  14 us
    pallas_call x2, Pallas kernels, front(): pl.pallas_call(functools.partial(front_kernel, plan, len(weights)), out_s...  10.6 us
    pallas_call x1, Pallas kernels, back_ffn(): pl.pallas_call(functools.partial(back_ffn_kernel, plan, len(weights), rel...  10.4 us
    pallas_call x2, Pallas kernels, mid(): pl.pallas_call(functools.partial(mid_kernel, plan, len(weights)), out_sha...  10.1 us
    pallas_call x2, Pallas kernels, back_mid(): pl.pallas_call(functools.partial(back_mid_kernel, plan, len(weights)), ou...  10.1 us
  transfers between devices with their start and end apart: 73, of which 32 were waited for; matrix products, arithmetic and copies ran while one was open for 3% of the time, Pallas kernels for 20%

profile of v4, /device:TPU:0, one launch (start us, length us, event | category | flops | bytes accessed | tf_op | source)
XLA Modules:
  0.0 343.5 jit_solution(2107459865361578457)
XLA Ops:
  7.1 3.0 collective-permute-start.1
  12.3 5.2 %collective-permute-done.3 = bf16[1,48,1408]{2,1,0:T(8,128)(2,1)S(1)} collective-permute-done((bf16[1,48,1408]{2,1,0:T(8,128)(2,1)S(1)}, bf16[1,48,1408]{2,1,0:T(8,128)(2,1)S(1)}, u32[]{:S(2)}, u32[]{:S(2)}) %collective-permute-start.3) | collective-permute-done | bytes 135200 | tf_op jit(solution)/shard_map/ppermute | solution.py:806
  19.2 2.4 collective-permute-start.6
  22.2 15.4 %collective-permute-done.5 = bf16[2,48,1408]{2,1,0:T(8,128)(2,1)S(1)} collective-permute-done((bf16[2,48,1408]{2,1,0:T(8,128)(2,1)S(1)}, bf16[2,48,1408]{2,1,0:T(8,128)(2,1)S(1)}, u32[]{:S(2)}, u32[]{:S(2)}) %collective-permute-start.5) | collective-permute-done | bytes 270368 | tf_op jit(solution)/shard_map/ppermute | solution.py:806
  37.8 3.6 %collective-permute-start.7 = (bf16[4,48,1408]{2,1,0:T(8,128)(2,1)S(1)}, bf16[4,48,1408]{2,1,0:T(8,128)(2,1)S(1)}, u32[]{:S(2)}, u32[]{:S(2)}) collective-permute-start(bf16[4,48,1408]{2,1,0:T(8,128)(2,1)S(1)} %pad_maximum_fusion.8), channel_id=1, source_target_pairs={{0,2},{1,5},{2,0},{3,7},{4,6},{5,1},{6,4},{7,3},{8,10},{9,13},{10,... | collective-permute-start | bytes 1622024 | tf_op jit(solution)/shard_map/ppermute | solution.py:806
  43.5 6.0 %collective-permute-done.8 = bf16[2,48,1408]{2,1,0:T(8,128)(2,1)S(1)} collective-permute-done((bf16[2,48,1408]{2,1,0:T(8,128)(2,1)S(1)}, bf16[2,48,1408]{2,1,0:T(8,128)(2,1)S(1)}, u32[]{:S(2)}, u32[]{:S(2)}) %collective-permute-start.8) | collective-permute-done | bytes 270368 | tf_op jit(solution)/shard_map/ppermute | solution.py:806
  51.3 2.7 collective-permute-start.10
  54.0 15.2 %collective-permute-done.12 = bf16[2,48,2304]{2,1,0:T(8,128)(2,1)S(1)} collective-permute-done((bf16[2,48,2304]{2,1,0:T(8,128)(2,1)S(1)}, bf16[2,48,2304]{2,1,0:T(8,128)(2,1)S(1)}, u32[]{:S(2)}, u32[]{:S(2)}) %collective-permute-start.12) | collective-permute-done | bytes 442400 | tf_op jit(solution)/shard_map/ppermute | solution.py:806
  82.0 5.7 %front.2 = (bf16[256,768]{1,0:T(8,128)(2,1)S(1)}, f32[256,768]{1,0:T(8,128)S(1)}, f32[256,768]{1,0:T(8,128)S(1)}, f32[256,384]{1,0:T(8,128)S(1)}, f32[3,256,128]...) custom-call(s32[8]{0:T(128)S(1)} %stack.68.me_ref.info_ref, ...), custom_call_target="tpu_custom_call" | custom-call | flops 1000 | bytes 1000 | tf_op jit(solution)/shard_map/front/pallas_call | solution.py:180
  88.5 9.2 %collective-permute-done.16 = bf16[4,48,2304]{2,1,0:T(8,128)(2,1)} collective-permute-done((bf16[4,48,2304]{2,1,0:T(8,128)(2,1)}, bf16[4,48,2304]{2,1,0:T(8,128)(2,1)}, u32[]{:S(2)}, u32[]{:S(2)}) %collective-permute-start.16) | collective-permute-done | bytes 884768 | tf_op jit(solution)/shard_map/ppermute | solution.py:806
  98.3 2.8 collective-permute-done.17
  102.0 2.6 collective-permute-start.18
  108.8 5.0 %mid.2 = (f32[6,256,128]{2,1,0:T(8,128)S(1)}, f32[2,8,384]{2,1,0:T(8,128)S(1)}, f32[256,768]{1,0:T(8,128)S(1)}, f32[256,128]{1,0:T(8,128)S(1)}, bf16[256,768]{1,...) custom-call(s32[8]{0:T(128)S(1)} %stack.68.me_ref.info_ref, bf16[256,768]{1,0:T(8,128)(2,1)S(1)} %copy-done, ...), custom_call_target="tpu_custom_call" | custom-call | flops 1000 | bytes 1000 | tf_op jit(solution)/shard_map/mid/pallas_call | solution.py:268
  114.6 6.9 %collective-permute-done.21.refs_2_ = bf16[8,48,1408]{2,1,0:T(8,128)(2,1)S(1)} collective-permute-done((bf16[8,48,1408]{2,1,0:T(8,128)(2,1)S(1)}, bf16[8,48,1408]{2,1,0:T(8,128)(2,1)S(1)}, u32[]{:S(2)}, u32[]{:S(2)}) %collective-permute-start.21) | collective-permute-done | bytes 1081376 | tf_op jit(solution)/shard_map/ppermute | solution.py:806
  122.8 5.3 %ffn.1 = (f32[256,3072]{1,0:T(8,128)S(1)}, bf16[256,1536]{1,0:T(8,128)(2,1)S(1)}, f32[256,768]{1,0:T(8,128)S(1)}) custom-call(s32[8]{0:T(128)S(1)} %stack.68.me_ref.info_ref, f32[256,768]{1,0:T(8,128)S(1)} %get-tuple-element.237.after_ref, bf16[256,768]{1,0:T(8,128)(2,1)S(1)} %get-tuple-element.235.lifted_ref.refs_4_, ...), custom_call_target="tpu_custom_call" | custom-call | flops 1000 | bytes 1000 | tf_op jit(solution)/shard_map/ffn/pallas_call | solution.py:314
  128.2 4.9 %front.3 = (bf16[256,768]{1,0:T(8,128)(2,1)S(1)}, f32[256,768]{1,0:T(8,128)S(1)}, f32[256,768]{1,0:T(8,128)S(1)}, f32[256,384]{1,0:T(8,128)S(1)}, f32[3,256,128]...) custom-call(s32[8]{0:T(128)S(1)} %stack.68.me_ref.info_ref, ...), custom_call_target="tpu_custom_call" | custom-call | flops 1000 | bytes 1000 | tf_op jit(solution)/shard_map/front/pallas_call | solution.py:180
  133.1 11.0 %collective-permute-done.26.refs_2_ = bf16[8,48,2304]{2,1,0:T(8,128)(2,1)S(1)} collective-permute-done((bf16[8,48,2304]{2,1,0:T(8,128)(2,1)S(1)}, bf16[8,48,2304]{2,1,0:T(8,128)(2,1)S(1)}, u32[]{:S(2)}, u32[]{:S(2)}) %collective-permute-start.26) | collective-permute-done | bytes 1769504 | tf_op jit(solution)/shard_map/ppermute | solution.py:806
  144.6 3.2 collective-permute-done.27
  147.8 2.2 collective-permute-start.30
  151.3 3.7 %collective-permute-done.28 = f32[2,4,384]{2,1,0:T(4,128)S(1)} collective-permute-done((f32[2,4,384]{2,1,0:T(4,128)S(1)}, f32[2,4,384]{2,1,0:T(4,128)S(1)}, u32[]{:S(2)}, u32[]{:S(2)}) %collective-permute-start.28) | collective-permute-done | bytes 12320 | tf_op jit(solution)/shard_map/ppermute | solution.py:806
  155.0 5.2 %mid.3 = (f32[6,256,128]{2,1,0:T(8,128)S(1)}, f32[2,8,384]{2,1,0:T(8,128)S(1)}, f32[256,768]{1,0:T(8,128)S(1)}, f32[256,128]{1,0:T(8,128)S(1)}, bf16[256,768]{1,...) custom-call(s32[8]{0:T(128)S(1)} %stack.68.me_ref.info_ref, ...), custom_call_target="tpu_custom_call" | custom-call | flops 1000 | bytes 1000 | tf_op jit(solution)/shard_map/mid/pallas_call | solution.py:268
  160.2 14.0 %turn.1 = (bf16[16,48,1536]{2,1,0:T(8,128)(2,1)S(1)}, bf16[16,48,1536]{2,1,0:T(8,128)(2,1)S(1)}, bf16[256,768]{1,0:T(8,128)(2,1)}, bf16[256,1536]{1,0:T(8,128)(2...) custom-call(s32[8]{0:T(128)S(1)} %stack.68.me_ref.info_ref, ...), custom_call_target="tpu_custom_call" | custom-call | flops 1000 | bytes 1000 | tf_op jit(solution)/shard_map/turn/pallas_call | solution.py:438
  174.3 4.6 %back_mid.2 = (bf16[256,768]{1,0:T(8,128)(2,1)S(1)}, f32[6,256,128]{2,1,0:T(8,128)S(1)}, f32[1,768]{1,0:T(1,128)S(1)}, f32[2,8,384]{2,1,0:T(8,128)S(1)}, f32[2,384]{1,0:T(2,128)S(1)}) custom-call(s32[8]{0:T(128)S(1)} %stack.68.me_ref.info_ref, bf16[256,768]{1,0:T(8,128)(2,1)S(1)} %get-tuple-element.267.dmid_ref, f32[8,768]{1,0:T(8,128)S(1)} %get-tuple-element.245.p_ref, ...), custom_call_target="tpu_custom_call" | custom-call | flops 1000 | bytes 1000 | tf_op jit(solution)/shard_map/back_mid/pallas_call | solution.py:544
  180.3 4.3 %grad_od.2 = (bf16[16,48,1536]{2,1,0:T(8,128)(2,1)S(1)}, bf16[16,48,1536]{2,1,0:T(8,128)(2,1)S(1)}) custom-call(s32[8]{0:T(128)S(1)} %stack.68.me_ref.info_ref, bf16[256,768]{1,0:T(8,128)(2,1)S(1)} %get-tuple-element.278.gated_ref, bf16[256,768]{1,0:T(8,128)(2,1)S(1)} %get-tuple-element.267.dmid_ref, bf16[256,1536]{1,0:T(8,128)(2,1)S(1)} %get-tuple-element.279.hidden_ref, ...), custom_call_target="tpu_custom_call" | custom-call | flops 1000 | bytes 1000 | tf_op jit(solution)/shard_map/grad_od/pallas_call | solution.py:757
  186.5 2.0 collective-permute-start.35
  191.0 8.2 %back_two.2 = (bf16[16,48,640]{2,1,0:T(8,128)(2,1)S(1)}, bf16[16,48,640]{2,1,0:T(8,128)(2,1)S(1)}, f32[256,768]{1,0:T(8,128)S(1)}, f32[2,768]{1,0:T(2,128)S(1)}) custom-call(s32[8]{0:T(128)S(1)} %stack.68.me_ref.info_ref, f32[256,768]{1,0:T(8,128)S(1)} %get-tuple-element.243.x_ref, f32[8,768]{1,0:T(8,128)S(1)} %get-tuple-element.245.p_ref, ...), custom_call_target="tpu_custom_call" | custom-call | flops 1000 | bytes 1000 | tf_op jit(solution)/shard_map/back_two/pallas_call | solution.py:696
  199.2 7.2 %collective-permute-done.38 = bf16[8,48,1536]{2,1,0:T(8,128)(2,1)S(1)} collective-permute-done((bf16[8,48,1536]{2,1,0:T(8,128)(2,1)S(1)}, bf16[8,48,1536]{2,1,0:T(8,128)(2,1)S(1)}, u32[]{:S(2)}, u32[]{:S(2)}) %collective-permute-start.38) | collective-permute-done | bytes 1179680 | tf_op jit(solution)/shard_map/ppermute | solution.py:806
  206.4 2.4 add_convert_fusion.3
  210.1 10.4 %back_ffn.1 = (bf16[16,48,1536]{2,1,0:T(8,128)(2,1)S(1)}, bf16[16,48,1536]{2,1,0:T(8,128)(2,1)S(1)}, bf16[256,768]{1,0:T(8,128)(2,1)S(1)}, f32[256,768]{1,0:T(8,...) custom-call(s32[8]{0:T(128)S(1)} %stack.68.me_ref.info_ref, f32[256,768]{1,0:T(8,128)S(1)} %get-tuple-element.299.dx_ref, ...), custom_call_target="tpu_custom_call" | custom-call | flops 1000 | bytes 1000 | tf_op jit(solution)/shard_map/back_ffn/pallas_call | solution.py:468
  221.0 2.0 collective-permute-start.42
  223.1 7.9 %collective-permute-done.42 = bf16[4,48,1536]{2,1,0:T(8,128)(2,1)S(1)} collective-permute-done((bf16[4,48,1536]{2,1,0:T(8,128)(2,1)S(1)}, bf16[4,48,1536]{2,1,0:T(8,128)(2,1)S(1)}, u32[]{:S(2)}, u32[]{:S(2)}) %collective-permute-start.42) | collective-permute-done | bytes 589856 | tf_op jit(solution)/shard_map/ppermute | solution.py:806
  234.5 5.5 %back_mid.3 = (bf16[256,768]{1,0:T(8,128)(2,1)S(1)}, f32[6,256,128]{2,1,0:T(8,128)S(1)}, f32[1,768]{1,0:T(1,128)S(1)}, f32[2,8,384]{2,1,0:T(8,128)S(1)}, f32[2,384]{1,0:T(2,128)S(1)}) custom-call(s32[8]{0:T(128)S(1)} %stack.68.me_ref.info_ref, bf16[256,768]{1,0:T(8,128)(2,1)S(1)} %get-tuple-element.311.dmid_ref, f32[8,768]{1,0:T(8,128)S(1)} %get-tuple-element.222.p_ref, ...), custom_call_target="tpu_custom_call" | custom-call | flops 1000 | bytes 1000 | tf_op jit(solution)/shard_map/back_mid/pallas_call | solution.py:544
  242.2 2.8 collective-permute-start.49
  245.8 4.1 %grad_od.3 = (bf16[16,48,1536]{2,1,0:T(8,128)(2,1)S(1)}, bf16[16,48,1536]{2,1,0:T(8,128)(2,1)S(1)}) custom-call(s32[8]{0:T(128)S(1)} %stack.68.me_ref.info_ref, bf16[256,768]{1,0:T(8,128)(2,1)S(1)} %get-tuple-element.325.gated_ref, bf16[256,768]{1,0:T(8,128)(2,1)S(1)} %get-tuple-element.311.dmid_ref, bf16[256,1536]{1,0:T(8,128)(2,1)S(1)} %copy-done.4, ...), custom_call_target="tpu_custom_call" | custom-call | flops 1000 | bytes 1000 | tf_op jit(solution)/shard_map/grad_od/pallas_call | solution.py:757
  256.7 9.0 %back_two.3 = (bf16[16,48,640]{2,1,0:T(8,128)(2,1)S(1)}, bf16[16,48,640]{2,1,0:T(8,128)(2,1)S(1)}, f32[256,768]{1,0:T(8,128)}, f32[2,768]{1,0:T(2,128)}) custom-call(s32[8]{0:T(128)S(1)} %stack.68.me_ref.info_ref, bf16[256,768]{1,0:T(8,128)(2,1)S(1)} %copy-done, f32[8,768]{1,0:T(8,128)S(1)} %get-tuple-element.222.p_ref, ...), custom_call_target="tpu_custom_call" | custom-call | flops 1000 | bytes 1000 | tf_op jit(solution)/shard_map/back_two/pallas_call | solution.py:696
  265.7 4.7 %collective-permute-done.54 = bf16[1,48,1536]{2,1,0:T(8,128)(2,1)S(1)} collective-permute-done((bf16[1,48,1536]{2,1,0:T(8,128)(2,1)S(1)}, bf16[1,48,1536]{2,1,0:T(8,128)(2,1)S(1)}, u32[]{:S(2)}, u32[]{:S(2)}) %collective-permute-start.54) | collective-permute-done | bytes 147488 | tf_op jit(solution)/shard_map/ppermute | solution.py:806
  280.6 4.1 %collective-permute-done.60 = bf16[2,48,640]{2,1,0:T(8,128)(2,1)S(1)} collective-permute-done((bf16[2,48,640]{2,1,0:T(8,128)(2,1)S(1)}, bf16[2,48,640]{2,1,0:T(8,128)(2,1)S(1)}, u32[]{:S(2)}, u32[]{:S(2)}) %collective-permute-start.60) | collective-permute-done | bytes 122912 | tf_op jit(solution)/shard_map/ppermute | solution.py:806
  285.4 11.0 %collective-permute-done.58 = bf16[8,48,1536]{2,1,0:T(8,128)(2,1)S(1)} collective-permute-done((bf16[8,48,1536]{2,1,0:T(8,128)(2,1)S(1)}, bf16[8,48,1536]{2,1,0:T(8,128)(2,1)S(1)}, u32[]{:S(2)}, u32[]{:S(2)}) %collective-permute-start.58) | collective-permute-done | bytes 1179680 | tf_op jit(solution)/shard_map/ppermute | solution.py:806
  296.8 4.3 %collective-permute-start.63 = (bf16[4,48,1536]{2,1,0:T(8,128)(2,1)S(1)}, bf16[4,48,1536]{2,1,0:T(8,128)(2,1)S(1)}, u32[]{:S(2)}, u32[]{:S(2)}) collective-permute-start(bf16[4,48,1536]{2,1,0:T(8,128)(2,1)S(1)} %get-tuple-element.365), channel_id=1, source_target_pairs={{0,2},{1,5},{2,0},{3,7},{4,6},{5,1},{6,4},{7,3},{8,10},{9,13},{10,... | collective-permute-start | bytes 1769480 | tf_op jit(solution)/shard_map/ppermute | solution.py:806
  301.4 5.4 %collective-permute-done.56 = bf16[8,48,640]{2,1,0:T(8,128)(2,1)S(1)} collective-permute-done((bf16[8,48,640]{2,1,0:T(8,128)(2,1)S(1)}, bf16[8,48,640]{2,1,0:T(8,128)(2,1)S(1)}, u32[]{:S(2)}, u32[]{:S(2)}) %collective-permute-start.56) | collective-permute-done | bytes 491552 | tf_op jit(solution)/shard_map/ppermute | solution.py:806
  306.9 4.6 %collective-permute-start.70 = (bf16[1,48,1536]{2,1,0:T(8,128)(2,1)S(1)}, bf16[1,48,1536]{2,1,0:T(8,128)(2,1)S(1)}, u32[]{:S(2)}, u32[]{:S(2)}) collective-permute-start(bf16[1,48,1536]{2,1,0:T(8,128)(2,1)S(1)} %add_convert_fusion.38), channel_id=1, source_target_pairs={{0,2},{1,5},{2,0},{3,7},{4,6},{5,1},{6,4},{7,3},{8,10},{9,13},{10,... | collective-permute-start | bytes 442376 | tf_op jit(solution)/shard_map/ppermute | solution.py:806
  311.6 2.9 collective-permute-done.70
  317.7 2.5 collective-permute-start.64
  320.2 8.9 %collective-permute-done.65 = bf16[2,48,1536]{2,1,0:T(8,128)(2,1)S(1)} collective-permute-done((bf16[2,48,1536]{2,1,0:T(8,128)(2,1)S(1)}, bf16[2,48,1536]{2,1,0:T(8,128)(2,1)S(1)}, u32[]{:S(2)}, u32[]{:S(2)}) %collective-permute-start.65) | collective-permute-done | bytes 294944 | tf_op jit(solution)/shard_map/ppermute | solution.py:806
  329.1 2.5 collective-permute-done.64
  332.1 1.8 collective-permute-start.67
  333.9 2.1 collective-permute-done.66
  336.0 2.6 collective-permute-done.67
  (242 shorter events, 76.3 us)
Async XLA Ops:
  7.1 12.0 %collective-permute-start.1 = (bf16[1,48,2304]{2,1,0:T(8,128)(2,1)S(1)}, bf16[1,48,2304]{2,1,0:T(8,128)(2,1)S(1)}, u32[]{:S(2)}, u32[]{:S(2)}) collective-permute-start(bf16[1,48,2304]{2,1,0:T(8,128)(2,1)S(1)} %maximum_bitcast_fusion), channel_id=1, source_target_pairs={{0,8},{1,17},{2,10},{3,19},{4,12},{5,21},{6,14},{7,23},{8,0},{9,25... | collective-permute-start | bytes 663560 | tf_op jit(solution)/shard_map/ppermute | solution.py:806
  10.1 9.0 %collective-permute-start.4 = (bf16[1,48,2304]{2,1,0:T(8,128)(2,1)S(1)}, bf16[1,48,2304]{2,1,0:T(8,128)(2,1)S(1)}, u32[]{:S(2)}, u32[]{:S(2)}) collective-permute-start(bf16[1,48,2304]{2,1,0:T(8,128)(2,1)S(1)} %maximum_bitcast_fusion.1), channel_id=1, source_target_pairs={{0,2},{1,5},{2,0},{3,7},{4,6},{5,1},{6,4},{7,3},{8,10},{9,13},{10,... | collective-permute-start | bytes 663560 | tf_op jit(solution)/shard_map/ppermute | solution.py:806
  12.3 6.8 %collective-permute-start.2 = (bf16[1,48,1408]{2,1,0:T(8,128)(2,1)S(1)}, bf16[1,48,1408]{2,1,0:T(8,128)(2,1)S(1)}, u32[]{:S(2)}, u32[]{:S(2)}) collective-permute-start(bf16[1,48,1408]{2,1,0:T(8,128)(2,1)S(1)} %get-tuple-element.435), channel_id=1, source_target_pairs={{0,8},{1,17},{2,10},{3,19},{4,12},{5,21},{6,14},{7,23},{8,0},{9,25... | collective-permute-start | bytes 405512 | tf_op jit(solution)/shard_map/ppermute | solution.py:806
  19.2 18.4 %collective-permute-start.6 = (bf16[2,48,2304]{2,1,0:T(8,128)(2,1)S(1)}, bf16[2,48,2304]{2,1,0:T(8,128)(2,1)S(1)}, u32[]{:S(2)}, u32[]{:S(2)}) collective-permute-start(bf16[2,48,2304]{2,1,0:T(8,128)(2,1)S(1)} %pad_maximum_fusion.10), channel_id=1, source_target_pairs={{0,16},{1,9},{2,18},{3,11},{4,20},{5,13},{6,22},{7,15},{8,24},{9,1... | collective-permute-start | bytes 1327112 | tf_op jit(solution)/shard_map/ppermute | solution.py:806
  21.6 16.0 %collective-permute-start.5 = (bf16[2,48,1408]{2,1,0:T(8,128)(2,1)S(1)}, bf16[2,48,1408]{2,1,0:T(8,128)(2,1)S(1)}, u32[]{:S(2)}, u32[]{:S(2)}) collective-permute-start(bf16[2,48,1408]{2,1,0:T(8,128)(2,1)S(1)} %pad_maximum_fusion.12), channel_id=1, source_target_pairs={{0,16},{1,9},{2,18},{3,11},{4,20},{5,13},{6,22},{7,15},{8,24},{9,1... | collective-permute-start | bytes 811016 | tf_op jit(solution)/shard_map/ppermute | solution.py:806
  37.8 11.8 %collective-permute-start.7 = (bf16[4,48,1408]{2,1,0:T(8,128)(2,1)S(1)}, bf16[4,48,1408]{2,1,0:T(8,128)(2,1)S(1)}, u32[]{:S(2)}, u32[]{:S(2)}) collective-permute-start(bf16[4,48,1408]{2,1,0:T(8,128)(2,1)S(1)} %pad_maximum_fusion.8), channel_id=1, source_target_pairs={{0,2},{1,5},{2,0},{3,7},{4,6},{5,1},{6,4},{7,3},{8,10},{9,13},{10,... | collective-permute-start | bytes 1622024 | tf_op jit(solution)/shard_map/ppermute | solution.py:806
  41.4 8.2 %collective-permute-start.8 = (bf16[2,48,1408]{2,1,0:T(8,128)(2,1)S(1)}, bf16[2,48,1408]{2,1,0:T(8,128)(2,1)S(1)}, u32[]{:S(2)}, u32[]{:S(2)}) collective-permute-start(bf16[2,48,1408]{2,1,0:T(8,128)(2,1)S(1)} %pad_maximum_fusion.13), channel_id=1, source_target_pairs={{0,8},{1,17},{2,10},{3,19},{4,12},{5,21},{6,14},{7,23},{8,0},{9,25... | collective-permute-start | bytes 811016 | tf_op jit(solution)/shard_map/ppermute | solution.py:806
  41.9 27.3 %collective-permute-start.11 = (bf16[4,48,2304]{2,1,0:T(8,128)(2,1)S(1)}, bf16[4,48,2304]{2,1,0:T(8,128)(2,1)S(1)}, u32[]{:S(2)}, u32[]{:S(2)}) collective-permute-start(bf16[4,48,2304]{2,1,0:T(8,128)(2,1)S(1)} %pad_maximum_fusion.4), channel_id=1, source_target_pairs={{0,2},{1,5},{2,0},{3,7},{4,6},{5,1},{6,4},{7,3},{8,10},{9,13},{10,... | collective-permute-start | bytes 2654216 | tf_op jit(solution)/shard_map/ppermute | solution.py:806
  42.5 26.8 %collective-permute-start.12 = (bf16[2,48,2304]{2,1,0:T(8,128)(2,1)S(1)}, bf16[2,48,2304]{2,1,0:T(8,128)(2,1)S(1)}, u32[]{:S(2)}, u32[]{:S(2)}) collective-permute-start(bf16[2,48,2304]{2,1,0:T(8,128)(2,1)S(1)} %pad_maximum_fusion.11), channel_id=1, source_target_pairs={{0,8},{1,17},{2,10},{3,19},{4,12},{5,21},{6,14},{7,23},{8,0},{9,25... | collective-permute-start | bytes 1327112 | tf_op jit(solution)/shard_map/ppermute | solution.py:806
  49.8 21.9 %collective-permute-start.9 = (bf16[8,48,1408]{2,1,0:T(8,128)(2,1)S(1)}, bf16[8,48,1408]{2,1,0:T(8,128)(2,1)S(1)}, u32[]{:S(2)}, u32[]{:S(2)}) collective-permute-start(bf16[8,48,1408]{2,1,0:T(8,128)(2,1)S(1)} %pad_maximum_fusion.2.refs_0_), channel_id=1, source_target_pairs={{0,4},{1,3},{2,6},{3,1},{4,0},{5,7},{6,2},{7,5},{8,12},{9,11},{10,... | collective-permute-start | bytes 3244040 | tf_op jit(solution)/shard_map/ppermute | solution.py:806
  51.3 20.3 %collective-permute-start.10 = (bf16[4,48,1408]{2,1,0:T(8,128)(2,1)S(1)}, bf16[4,48,1408]{2,1,0:T(8,128)(2,1)S(1)}, u32[]{:S(2)}, u32[]{:S(2)}) collective-permute-start(bf16[4,48,1408]{2,1,0:T(8,128)(2,1)S(1)} %pad_maximum_fusion.9), channel_id=1, source_target_pairs={{0,16},{1,9},{2,18},{3,11},{4,20},{5,13},{6,22},{7,15},{8,24},{9,1... | collective-permute-start | bytes 1622024 | tf_op jit(solution)/shard_map/ppermute | solution.py:806
  72.4 25.4 %collective-permute-start.15 = (bf16[8,48,2304]{2,1,0:T(8,128)(2,1)}, bf16[8,48,2304]{2,1,0:T(8,128)(2,1)}, u32[]{:S(2)}, u32[]{:S(2)}) collective-permute-start(bf16[8,48,2304]{2,1,0:T(8,128)(2,1)} %pad_maximum_fusion.refs_0_), channel_id=1, source_target_pairs={{0,4},{1,3},{2,6},{3,1},{4,0},{5,7},{6,2},{7,5},{8,12},{9,11},{10,... | collective-permute-start | bytes 5308424 | tf_op jit(solution)/shard_map/ppermute | solution.py:806
  73.5 6.7 %collective-permute-start.14 = (bf16[8,48,1408]{2,1,0:T(8,128)(2,1)S(1)}, bf16[8,48,1408]{2,1,0:T(8,128)(2,1)S(1)}, u32[]{:S(2)}, u32[]{:S(2)}) collective-permute-start(bf16[8,48,1408]{2,1,0:T(8,128)(2,1)S(1)} %pad_maximum_fusion.2.refs_0_), channel_id=1, source_target_pairs={{0,1},{1,0},{2,3},{3,2},{4,5},{5,4},{6,7},{7,6},{8,9},{9,8},{10,11... | collective-permute-start | bytes 3244040 | tf_op jit(solution)/shard_map/ppermute | solution.py:806
  73.5 6.7 %collective-permute-start.13 = (bf16[8,48,1408]{2,1,0:T(8,128)(2,1)S(1)}, bf16[8,48,1408]{2,1,0:T(8,128)(2,1)}, u32[]{:S(2)}, u32[]{:S(2)}) collective-permute-start(bf16[8,48,1408]{2,1,0:T(8,128)(2,1)S(1)} %collective-permute-done.9.refs_2_), channel_id=1, source_target_pairs={{0,1},{1,0},{2,3},{3,2},{4,5},{5,4},{6,7},{7,6},{8,9},{9,8},{10,11... | collective-permute-start | bytes 3244040 | tf_op jit(solution)/shard_map/ppermute | solution.py:806
  74.0 23.7 %collective-permute-start.16 = (bf16[4,48,2304]{2,1,0:T(8,128)(2,1)}, bf16[4,48,2304]{2,1,0:T(8,128)(2,1)}, u32[]{:S(2)}, u32[]{:S(2)}) collective-permute-start(bf16[4,48,2304]{2,1,0:T(8,128)(2,1)} %pad_maximum_fusion.5), channel_id=1, source_target_pairs={{0,16},{1,9},{2,18},{3,11},{4,20},{5,13},{6,22},{7,15},{8,24},{9,1... | collective-permute-start | bytes 2654216 | tf_op jit(solution)/shard_map/ppermute | solution.py:806
  78.9 35.8 %collective-permute-start.23 = (bf16[8,48,2304]{2,1,0:T(8,128)(2,1)}, bf16[8,48,2304]{2,1,0:T(8,128)(2,1)S(1)}, u32[]{:S(2)}, u32[]{:S(2)}) collective-permute-start(bf16[8,48,2304]{2,1,0:T(8,128)(2,1)} %pad_maximum_fusion.refs_0_), channel_id=1, source_target_pairs={{0,1},{1,0},{2,3},{3,2},{4,5},{5,4},{6,7},{7,6},{8,9},{9,8},{10,11... | collective-permute-start | bytes 5308424 | tf_op jit(solution)/shard_map/ppermute | solution.py:806
  97.8 23.8 %collective-permute-start.22 = (bf16[8,48,2304]{2,1,0:T(8,128)(2,1)}, bf16[8,48,2304]{2,1,0:T(8,128)(2,1)S(1)}, u32[]{:S(2)}, u32[]{:S(2)}) collective-permute-start(bf16[8,48,2304]{2,1,0:T(8,128)(2,1)} %collective-permute-done.15.refs_2_), channel_id=1, source_target_pairs={{0,1},{1,0},{2,3},{3,2},{4,5},{5,4},{6,7},{7,6},{8,9},{9,8},{10,11... | collective-permute-start | bytes 5308424 | tf_op jit(solution)/shard_map/ppermute | solution.py:806
  106.3 15.2 %collective-permute-start.21 = (bf16[8,48,1408]{2,1,0:T(8,128)(2,1)S(1)}, bf16[8,48,1408]{2,1,0:T(8,128)(2,1)S(1)}, u32[]{:S(2)}, u32[]{:S(2)}) collective-permute-start(bf16[8,48,1408]{2,1,0:T(8,128)(2,1)S(1)} %pad_maximum_fusion.3.refs_0_), channel_id=1, source_target_pairs={{0,4},{1,3},{2,6},{3,1},{4,0},{5,7},{6,2},{7,5},{8,12},{9,11},{10,... | collective-permute-start | bytes 3244040 | tf_op jit(solution)/shard_map/ppermute | solution.py:806
  121.6 22.5 %collective-permute-start.26 = (bf16[8,48,2304]{2,1,0:T(8,128)(2,1)S(1)}, bf16[8,48,2304]{2,1,0:T(8,128)(2,1)S(1)}, u32[]{:S(2)}, u32[]{:S(2)}) collective-permute-start(bf16[8,48,2304]{2,1,0:T(8,128)(2,1)S(1)} %pad_maximum_fusion.1.refs_0_), channel_id=1, source_target_pairs={{0,4},{1,3},{2,6},{3,1},{4,0},{5,7},{6,2},{7,5},{8,12},{9,11},{10,... | collective-permute-start | bytes 5308424 | tf_op jit(solution)/shard_map/ppermute | solution.py:806
  122.8 37.4 %collective-permute-start.32 = (bf16[8,48,2304]{2,1,0:T(8,128)(2,1)S(1)}, bf16[8,48,2304]{2,1,0:T(8,128)(2,1)S(1)}, u32[]{:S(2)}, u32[]{:S(2)}) collective-permute-start(bf16[8,48,2304]{2,1,0:T(8,128)(2,1)S(1)} %pad_maximum_fusion.1.refs_0_), channel_id=1, source_target_pairs={{0,1},{1,0},{2,3},{3,2},{4,5},{5,4},{6,7},{7,6},{8,9},{9,8},{10,11... | collective-permute-start | bytes 5308424 | tf_op jit(solution)/shard_map/ppermute | solution.py:806
  144.1 16.1 %collective-permute-start.31 = (bf16[8,48,2304]{2,1,0:T(8,128)(2,1)S(1)}, bf16[8,48,2304]{2,1,0:T(8,128)(2,1)S(1)}, u32[]{:S(2)}, u32[]{:S(2)}) collective-permute-start(bf16[8,48,2304]{2,1,0:T(8,128)(2,1)S(1)} %collective-permute-done.26.refs_2_), channel_id=1, source_target_pairs={{0,1},{1,0},{2,3},{3,2},{4,5},{5,4},{6,7},{7,6},{8,9},{9,8},{10,11... | collective-permute-start | bytes 5308424 | tf_op jit(solution)/shard_map/ppermute | solution.py:806
  147.8 7.2 %collective-permute-start.30 = (f32[2,4,384]{2,1,0:T(4,128)S(1)}, f32[2,4,384]{2,1,0:T(4,128)S(1)}, u32[]{:S(2)}, u32[]{:S(2)}) collective-permute-start(f32[2,4,384]{2,1,0:T(4,128)S(1)} %pad_maximum_fusion.15), channel_id=1, source_target_pairs={{0,6},{1,7},{2,4},{3,5},{4,2},{5,3},{6,0},{7,1},{8,14},{9,15},{10,... | collective-permute-start | bytes 36872 | tf_op jit(solution)/shard_map/ppermute | solution.py:806
  184.6 21.8 %collective-permute-start.39 = (bf16[16,48,1536]{2,1,0:T(8,128)(2,1)S(1)}, bf16[16,48,1536]{2,1,0:T(8,128)(2,1)}, u32[]{:S(2)}, u32[]{:S(2)}) collective-permute-start(bf16[16,48,1536]{2,1,0:T(8,128)(2,1)S(1)} %get-tuple-element.293), channel_id=1, source_target_pairs={{0,1},{1,0},{2,3},{3,2},{4,5},{5,4},{6,7},{7,6},{8,9},{9,8},{10,11... | collective-permute-start | bytes 7077896 | tf_op jit(solution)/shard_map/ppermute | solution.py:806
  190.2 16.3 %collective-permute-start.38 = (bf16[8,48,1536]{2,1,0:T(8,128)(2,1)S(1)}, bf16[8,48,1536]{2,1,0:T(8,128)(2,1)S(1)}, u32[]{:S(2)}, u32[]{:S(2)}) collective-permute-start(bf16[8,48,1536]{2,1,0:T(8,128)(2,1)S(1)} %get-tuple-element.286), channel_id=1, source_target_pairs={{0,4},{1,3},{2,6},{3,1},{4,0},{5,7},{6,2},{7,5},{8,12},{9,11},{10,... | collective-permute-start | bytes 3538952 | tf_op jit(solution)/shard_map/ppermute | solution.py:806
  209.2 21.7 %collective-permute-start.40 = (bf16[8,48,1536]{2,1,0:T(8,128)(2,1)S(1)}, bf16[8,48,1536]{2,1,0:T(8,128)(2,1)S(1)}, u32[]{:S(2)}, u32[]{:S(2)}) collective-permute-start(bf16[8,48,1536]{2,1,0:T(8,128)(2,1)S(1)} %get-tuple-element.298), channel_id=1, source_target_pairs={{0,4},{1,3},{2,6},{3,1},{4,0},{5,7},{6,2},{7,5},{8,12},{9,11},{10,... | collective-permute-start | bytes 3538952 | tf_op jit(solution)/shard_map/ppermute | solution.py:806
  210.1 13.0 %collective-permute-start.41 = (bf16[16,48,640]{2,1,0:T(8,128)(2,1)S(1)}, bf16[16,48,640]{2,1,0:T(8,128)(2,1)S(1)}, u32[]{:S(2)}, u32[]{:S(2)}) collective-permute-start(bf16[16,48,640]{2,1,0:T(8,128)(2,1)S(1)} %get-tuple-element.303), channel_id=1, source_target_pairs={{0,1},{1,0},{2,3},{3,2},{4,5},{5,4},{6,7},{7,6},{8,9},{9,8},{10,11... | collective-permute-start | bytes 2949128 | tf_op jit(solution)/shard_map/ppermute | solution.py:806
  220.5 21.7 %collective-permute-start.43 = (bf16[16,48,1536]{2,1,0:T(8,128)(2,1)S(1)}, bf16[16,48,1536]{2,1,0:T(8,128)(2,1)S(1)}, u32[]{:S(2)}, u32[]{:S(2)}) collective-permute-start(bf16[16,48,1536]{2,1,0:T(8,128)(2,1)S(1)} %get-tuple-element.317), channel_id=1, source_target_pairs={{0,1},{1,0},{2,3},{3,2},{4,5},{5,4},{6,7},{7,6},{8,9},{9,8},{10,11... | collective-permute-start | bytes 7077896 | tf_op jit(solution)/shard_map/ppermute | solution.py:806
  221.0 9.9 %collective-permute-start.42 = (bf16[4,48,1536]{2,1,0:T(8,128)(2,1)S(1)}, bf16[4,48,1536]{2,1,0:T(8,128)(2,1)S(1)}, u32[]{:S(2)}, u32[]{:S(2)}) collective-permute-start(bf16[4,48,1536]{2,1,0:T(8,128)(2,1)S(1)} %get-tuple-element.304), channel_id=1, source_target_pairs={{0,2},{1,5},{2,0},{3,7},{4,6},{5,1},{6,4},{7,3},{8,10},{9,13},{10,... | collective-permute-start | bytes 1769480 | tf_op jit(solution)/shard_map/ppermute | solution.py:806
  231.3 10.8 %collective-permute-start.45 = (bf16[2,48,1536]{2,1,0:T(8,128)(2,1)S(1)}, bf16[2,48,1536]{2,1,0:T(8,128)(2,1)S(1)}, u32[]{:S(2)}, u32[]{:S(2)}) collective-permute-start(bf16[2,48,1536]{2,1,0:T(8,128)(2,1)S(1)} %get-tuple-element.318), channel_id=1, source_target_pairs={{0,16},{1,9},{2,18},{3,11},{4,20},{5,13},{6,22},{7,15},{8,24},{9,1... | collective-permute-start | bytes 884744 | tf_op jit(solution)/shard_map/ppermute | solution.py:806
  231.9 10.3 %collective-permute-start.44 = (bf16[8,48,640]{2,1,0:T(8,128)(2,1)S(1)}, bf16[8,48,640]{2,1,0:T(8,128)(2,1)S(1)}, u32[]{:S(2)}, u32[]{:S(2)}) collective-permute-start(bf16[8,48,640]{2,1,0:T(8,128)(2,1)S(1)} %get-tuple-element.310), channel_id=1, source_target_pairs={{0,4},{1,3},{2,6},{3,1},{4,0},{5,7},{6,2},{7,5},{8,12},{9,11},{10,... | collective-permute-start | bytes 1474568 | tf_op jit(solution)/shard_map/ppermute | solution.py:806
  242.2 8.7 %collective-permute-start.49 = (f32[2,2,384]{2,1,0:T(2,128)S(1)}, f32[2,2,384]{2,1,0:T(2,128)S(1)}, u32[]{:S(2)}, u32[]{:S(2)}) collective-permute-start(f32[2,2,384]{2,1,0:T(2,128)S(1)} %pad_maximum_fusion.17), channel_id=1, source_target_pairs={{0,6},{1,7},{2,4},{3,5},{4,2},{5,3},{6,0},{7,1},{8,14},{9,15},{10,... | collective-permute-start | bytes 18440 | tf_op jit(solution)/shard_map/ppermute | solution.py:806
  249.8 22.7 %collective-permute-start.55 = (bf16[16,48,1536]{2,1,0:T(8,128)(2,1)S(1)}, bf16[16,48,1536]{2,1,0:T(8,128)(2,1)S(1)}, u32[]{:S(2)}, u32[]{:S(2)}) collective-permute-start(bf16[16,48,1536]{2,1,0:T(8,128)(2,1)S(1)} %get-tuple-element.351), channel_id=1, source_target_pairs={{0,1},{1,0},{2,3},{3,2},{4,5},{5,4},{6,7},{7,6},{8,9},{9,8},{10,11... | collective-permute-start | bytes 7077896 | tf_op jit(solution)/shard_map/ppermute | solution.py:806
  250.9 21.6 %collective-permute-start.51 = (bf16[8,48,1536]{2,1,0:T(8,128)(2,1)S(1)}, bf16[8,48,1536]{2,1,0:T(8,128)(2,1)S(1)}, u32[]{:S(2)}, u32[]{:S(2)}) collective-permute-start(bf16[8,48,1536]{2,1,0:T(8,128)(2,1)S(1)} %get-tuple-element.333), channel_id=1, source_target_pairs={{0,4},{1,3},{2,6},{3,1},{4,0},{5,7},{6,2},{7,5},{8,12},{9,11},{10,... | collective-permute-start | bytes 3538952 | tf_op jit(solution)/shard_map/ppermute | solution.py:806
  252.2 20.3 %collective-permute-start.52 = (bf16[4,48,1536]{2,1,0:T(8,128)(2,1)S(1)}, bf16[4,48,1536]{2,1,0:T(8,128)(2,1)S(1)}, u32[]{:S(2)}, u32[]{:S(2)}) collective-permute-start(bf16[4,48,1536]{2,1,0:T(8,128)(2,1)S(1)} %get-tuple-element.348), channel_id=1, source_target_pairs={{0,16},{1,9},{2,18},{3,11},{4,20},{5,13},{6,22},{7,15},{8,24},{9,1... | collective-permute-start | bytes 1769480 | tf_op jit(solution)/shard_map/ppermute | solution.py:806
  253.8 17.0 %collective-permute-start.53 = (bf16[4,48,640]{2,1,0:T(8,128)(2,1)S(1)}, bf16[4,48,640]{2,1,0:T(8,128)(2,1)S(1)}, u32[]{:S(2)}, u32[]{:S(2)}) collective-permute-start(bf16[4,48,640]{2,1,0:T(8,128)(2,1)S(1)} %get-tuple-element.349), channel_id=1, source_target_pairs={{0,2},{1,5},{2,0},{3,7},{4,6},{5,1},{6,4},{7,3},{8,10},{9,13},{10,... | collective-permute-start | bytes 737288 | tf_op jit(solution)/shard_map/ppermute | solution.py:806
  255.2 15.2 %collective-permute-start.54 = (bf16[1,48,1536]{2,1,0:T(8,128)(2,1)S(1)}, bf16[1,48,1536]{2,1,0:T(8,128)(2,1)S(1)}, u32[]{:S(2)}, u32[]{:S(2)}) collective-permute-start(bf16[1,48,1536]{2,1,0:T(8,128)(2,1)S(1)} %add_convert_fusion.39), channel_id=1, source_target_pairs={{0,8},{1,17},{2,10},{3,19},{4,12},{5,21},{6,14},{7,23},{8,0},{9,25... | collective-permute-start | bytes 442376 | tf_op jit(solution)/shard_map/ppermute | solution.py:806
  273.8 22.6 %collective-permute-start.58 = (bf16[8,48,1536]{2,1,0:T(8,128)(2,1)S(1)}, bf16[8,48,1536]{2,1,0:T(8,128)(2,1)S(1)}, u32[]{:S(2)}, u32[]{:S(2)}) collective-permute-start(bf16[8,48,1536]{2,1,0:T(8,128)(2,1)S(1)} %get-tuple-element.356), channel_id=1, source_target_pairs={{0,4},{1,3},{2,6},{3,1},{4,0},{5,7},{6,2},{7,5},{8,12},{9,11},{10,... | collective-permute-start | bytes 3538952 | tf_op jit(solution)/shard_map/ppermute | solution.py:806
  274.7 10.7 %collective-permute-start.59 = (bf16[2,48,1536]{2,1,0:T(8,128)(2,1)S(1)}, bf16[2,48,1536]{2,1,0:T(8,128)(2,1)S(1)}, u32[]{:S(2)}, u32[]{:S(2)}) collective-permute-start(bf16[2,48,1536]{2,1,0:T(8,128)(2,1)S(1)} %get-tuple-element.360), channel_id=1, source_target_pairs={{0,8},{1,17},{2,10},{3,19},{4,12},{5,21},{6,14},{7,23},{8,0},{9,25... | collective-permute-start | bytes 884744 | tf_op jit(solution)/shard_map/ppermute | solution.py:806
  275.9 8.8 %collective-permute-start.60 = (bf16[2,48,640]{2,1,0:T(8,128)(2,1)S(1)}, bf16[2,48,640]{2,1,0:T(8,128)(2,1)S(1)}, u32[]{:S(2)}, u32[]{:S(2)}) collective-permute-start(bf16[2,48,640]{2,1,0:T(8,128)(2,1)S(1)} %get-tuple-element.361), channel_id=1, source_target_pairs={{0,16},{1,9},{2,18},{3,11},{4,20},{5,13},{6,22},{7,15},{8,24},{9,1... | collective-permute-start | bytes 368648 | tf_op jit(solution)/shard_map/ppermute | solution.py:806
  277.3 29.5 %collective-permute-start.56 = (bf16[8,48,640]{2,1,0:T(8,128)(2,1)S(1)}, bf16[8,48,640]{2,1,0:T(8,128)(2,1)S(1)}, u32[]{:S(2)}, u32[]{:S(2)}) collective-permute-start(bf16[8,48,640]{2,1,0:T(8,128)(2,1)S(1)} %get-tuple-element.358), channel_id=1, source_target_pairs={{0,4},{1,3},{2,6},{3,1},{4,0},{5,7},{6,2},{7,5},{8,12},{9,11},{10,... | collective-permute-start | bytes 1474568 | tf_op jit(solution)/shard_map/ppermute | solution.py:806
  279.0 22.1 %collective-permute-start.57 = (bf16[4,48,1536]{2,1,0:T(8,128)(2,1)S(1)}, bf16[4,48,1536]{2,1,0:T(8,128)(2,1)S(1)}, u32[]{:S(2)}, u32[]{:S(2)}) collective-permute-start(bf16[4,48,1536]{2,1,0:T(8,128)(2,1)S(1)} %get-tuple-element.359), channel_id=1, source_target_pairs={{0,2},{1,5},{2,0},{3,7},{4,6},{5,1},{6,4},{7,3},{8,10},{9,13},{10,... | collective-permute-start | bytes 1769480 | tf_op jit(solution)/shard_map/ppermute | solution.py:806
  296.8 18.0 %collective-permute-start.63 = (bf16[4,48,1536]{2,1,0:T(8,128)(2,1)S(1)}, bf16[4,48,1536]{2,1,0:T(8,128)(2,1)S(1)}, u32[]{:S(2)}, u32[]{:S(2)}) collective-permute-start(bf16[4,48,1536]{2,1,0:T(8,128)(2,1)S(1)} %get-tuple-element.365), channel_id=1, source_target_pairs={{0,2},{1,5},{2,0},{3,7},{4,6},{5,1},{6,4},{7,3},{8,10},{9,13},{10,... | collective-permute-start | bytes 1769480 | tf_op jit(solution)/shard_map/ppermute | solution.py:806
  301.3 15.3 %collective-permute-start.62 = (bf16[2,48,1536]{2,1,0:T(8,128)(2,1)S(1)}, bf16[2,48,1536]{2,1,0:T(8,128)(2,1)S(1)}, u32[]{:S(2)}, u32[]{:S(2)}) collective-permute-start(bf16[2,48,1536]{2,1,0:T(8,128)(2,1)S(1)} %get-tuple-element.367), channel_id=1, source_target_pairs={{0,16},{1,9},{2,18},{3,11},{4,20},{5,13},{6,22},{7,15},{8,24},{9,1... | collective-permute-start | bytes 884744 | tf_op jit(solution)/shard_map/ppermute | solution.py:806
  306.9 7.7 %collective-permute-start.70 = (bf16[1,48,1536]{2,1,0:T(8,128)(2,1)S(1)}, bf16[1,48,1536]{2,1,0:T(8,128)(2,1)S(1)}, u32[]{:S(2)}, u32[]{:S(2)}) collective-permute-start(bf16[1,48,1536]{2,1,0:T(8,128)(2,1)S(1)} %add_convert_fusion.38), channel_id=1, source_target_pairs={{0,2},{1,5},{2,0},{3,7},{4,6},{5,1},{6,4},{7,3},{8,10},{9,13},{10,... | collective-permute-start | bytes 442376 | tf_op jit(solution)/shard_map/ppermute | solution.py:806
  314.7 24.1 %collective-permute-start.72 = (f32[24,2944]{1,0:T(8,128)S(1)}, f32[24,2944]{1,0:T(8,128)S(1)}, u32[]{:S(2)}, u32[]{:S(2)}) collective-permute-start(f32[24,2944]{1,0:T(8,128)S(1)} %get-tuple-element.428), channel_id=1, source_target_pairs={{0,1},{1,0},{2,3},{3,2},{4,5},{5,4},{6,7},{7,6},{8,9},{9,8},{10,11... | collective-permute-start | bytes 847880 | tf_op jit(solution)/shard_map/ppermute | solution.py:806
  314.9 14.2 %collective-permute-start.65 = (bf16[2,48,1536]{2,1,0:T(8,128)(2,1)S(1)}, bf16[2,48,1536]{2,1,0:T(8,128)(2,1)S(1)}, u32[]{:S(2)}, u32[]{:S(2)}) collective-permute-start(bf16[2,48,1536]{2,1,0:T(8,128)(2,1)S(1)} %get-tuple-element.371), channel_id=1, source_target_pairs={{0,16},{1,9},{2,18},{3,11},{4,20},{5,13},{6,22},{7,15},{8,24},{9,1... | collective-permute-start | bytes 884744 | tf_op jit(solution)/shard_map/ppermute | solution.py:806
  316.7 15.4 %collective-permute-start.68 = (bf16[1,48,1536]{2,1,0:T(8,128)(2,1)S(1)}, bf16[1,48,1536]{2,1,0:T(8,128)(2,1)S(1)}, u32[]{:S(2)}, u32[]{:S(2)}) collective-permute-start(bf16[1,48,1536]{2,1,0:T(8,128)(2,1)S(1)} %add_convert_fusion.37), channel_id=1, source_target_pairs={{0,8},{1,17},{2,10},{3,19},{4,12},{5,21},{6,14},{7,23},{8,0},{9,25... | collective-permute-start | bytes 442376 | tf_op jit(solution)/shard_map/ppermute | solution.py:806
  317.7 14.0 %collective-permute-start.64 = (bf16[2,48,640]{2,1,0:T(8,128)(2,1)S(1)}, bf16[2,48,640]{2,1,0:T(8,128)(2,1)S(1)}, u32[]{:S(2)}, u32[]{:S(2)}) collective-permute-start(bf16[2,48,640]{2,1,0:T(8,128)(2,1)S(1)} %get-tuple-element.375), channel_id=1, source_target_pairs={{0,16},{1,9},{2,18},{3,11},{4,20},{5,13},{6,22},{7,15},{8,24},{9,1... | collective-permute-start | bytes 368648 | tf_op jit(solution)/shard_map/ppermute | solution.py:806
  (39 other events, 201.0 us)

commit v5 on v4

--- a/solution.py
+++ b/solution.py
@@ -976,6 +976,7 @@
 STAGES = ((4, 8), (8, 4), (1, 2), (2, 1))
 LATER = ((1, 2), (4, 8), (8, 4), (2, 1))
 UPPER = (STAGES, LATER, STAGES)
+LOWER = (LATER, STAGES, STAGES)
 
 
 def small_of(gains, chan_params):
@@ -1139,7 +1140,7 @@
         x, every, (normed, cpre, gate, rate, kept, feed, sub, _), middle, (both, hidden, _), layer = saved[l]
         states, first, gn, rg, gated, after, lifted = middle
         plan = plans[l]
-        u_stages, od_stages, c_stages = UPPER if l else (STAGES,) * 3
+        u_stages, od_stages, c_stages = UPPER if l else LOWER
         if above:
             (dx,) = order.step(dx)
             keep, send, dlow, dafter, dmid, ffn_gain = back_ffn(

time: 348 us -> 339 us (0.974)
  waiting for transfers between devices: 150 us -> 146 us
  starting transfers between devices: 75.8 us -> 72.1 us
    ppermute x73, waiting for transfers between devices: 150 us -> 146 us  [swap(): return lax.ppermute(x, ALL, [(i, i ^ bits[i % 2]) for i in range(count)])]
    ppermute x73, starting transfers between devices: 75.8 us -> 72.1 us  [swap(): return lax.ppermute(x, ALL, [(i, i ^ bits[i % 2]) for i in range(count)])]
  transfers between devices with their start and end apart: 73 -> 73, of which waited for: 32 -> 29; matrix products, arithmetic and copies ran while one was open for 3% -> 3% of each run, Pallas kernels for 20% -> 21%
where the time goes in v5:
time: 339 us; the launch traced here: 336 us
  waiting for transfers between devices  146 us (43%)
  Pallas kernels  89.4 us (26%)
  starting transfers between devices  72.1 us (21%)
  other arithmetic  13.9 us (4%)
  local copies, waits for them, and re-layouts  10.2 us (3%)
  between operations  4.29 us (1%)
    ppermute x73, waiting for transfers between devices, swap(): return lax.ppermute(x, ALL, [(i, i ^ bits[i % 2]) for i in range(count)])  146 us
    ppermute x73, starting transfers between devices, swap(): return lax.ppermute(x, ALL, [(i, i ^ bits[i % 2]) for i in range(count)])  72.1 us
    pallas_call x2, Pallas kernels, back_two(): pl.pallas_call(functools.partial(back_two_kernel, plan, len(weights), rel...  17.2 us
    pallas_call x1, Pallas kernels, turn(): pl.pallas_call(functools.partial(turn_kernel, plan, len(weights), rels),...  14 us
    pallas_call x2, Pallas kernels, front(): pl.pallas_call(functools.partial(front_kernel, plan, len(weights)), out_s...  10.6 us
    pallas_call x1, Pallas kernels, back_ffn(): pl.pallas_call(functools.partial(back_ffn_kernel, plan, len(weights), rel...  10.4 us
    pallas_call x2, Pallas kernels, mid(): pl.pallas_call(functools.partial(mid_kernel, plan, len(weights)), out_sha...  10.1 us
    pallas_call x2, Pallas kernels, back_mid(): pl.pallas_call(functools.partial(back_mid_kernel, plan, len(weights)), ou...  10.1 us
  transfers between devices with their start and end apart: 73, of which 29 were waited for; matrix products, arithmetic and copies ran while one was open for 3% of the time, Pallas kernels for 21%

profile of v5, /device:TPU:0, one launch (start us, length us, event | category | flops | bytes accessed | tf_op | source)
XLA Modules:
  0.0 335.6 jit_solution(5835579780667888299)
XLA Ops:
  7.1 3.0 collective-permute-start.1
  12.3 5.2 %collective-permute-done.3 = bf16[1,48,1408]{2,1,0:T(8,128)(2,1)S(1)} collective-permute-done((bf16[1,48,1408]{2,1,0:T(8,128)(2,1)S(1)}, bf16[1,48,1408]{2,1,0:T(8,128)(2,1)S(1)}, u32[]{:S(2)}, u32[]{:S(2)}) %collective-permute-start.3) | collective-permute-done | bytes 135200 | tf_op jit(solution)/shard_map/ppermute | solution.py:806
  19.2 2.4 collective-permute-start.6
  22.2 15.4 %collective-permute-done.5 = bf16[2,48,1408]{2,1,0:T(8,128)(2,1)S(1)} collective-permute-done((bf16[2,48,1408]{2,1,0:T(8,128)(2,1)S(1)}, bf16[2,48,1408]{2,1,0:T(8,128)(2,1)S(1)}, u32[]{:S(2)}, u32[]{:S(2)}) %collective-permute-start.5) | collective-permute-done | bytes 270368 | tf_op jit(solution)/shard_map/ppermute | solution.py:806
  37.8 3.6 %collective-permute-start.7 = (bf16[4,48,1408]{2,1,0:T(8,128)(2,1)S(1)}, bf16[4,48,1408]{2,1,0:T(8,128)(2,1)S(1)}, u32[]{:S(2)}, u32[]{:S(2)}) collective-permute-start(bf16[4,48,1408]{2,1,0:T(8,128)(2,1)S(1)} %pad_maximum_fusion.8), channel_id=1, source_target_pairs={{0,2},{1,5},{2,0},{3,7},{4,6},{5,1},{6,4},{7,3},{8,10},{9,13},{10,... | collective-permute-start | bytes 1622024 | tf_op jit(solution)/shard_map/ppermute | solution.py:806
  43.5 6.0 %collective-permute-done.8 = bf16[2,48,1408]{2,1,0:T(8,128)(2,1)S(1)} collective-permute-done((bf16[2,48,1408]{2,1,0:T(8,128)(2,1)S(1)}, bf16[2,48,1408]{2,1,0:T(8,128)(2,1)S(1)}, u32[]{:S(2)}, u32[]{:S(2)}) %collective-permute-start.8) | collective-permute-done | bytes 270368 | tf_op jit(solution)/shard_map/ppermute | solution.py:806
  51.3 2.7 collective-permute-start.10
  54.0 15.2 %collective-permute-done.12 = bf16[2,48,2304]{2,1,0:T(8,128)(2,1)S(1)} collective-permute-done((bf16[2,48,2304]{2,1,0:T(8,128)(2,1)S(1)}, bf16[2,48,2304]{2,1,0:T(8,128)(2,1)S(1)}, u32[]{:S(2)}, u32[]{:S(2)}) %collective-permute-start.12) | collective-permute-done | bytes 442400 | tf_op jit(solution)/shard_map/ppermute | solution.py:806
  82.0 5.7 %front.2 = (bf16[256,768]{1,0:T(8,128)(2,1)S(1)}, f32[256,768]{1,0:T(8,128)S(1)}, f32[256,768]{1,0:T(8,128)S(1)}, f32[256,384]{1,0:T(8,128)S(1)}, f32[3,256,128]...) custom-call(s32[8]{0:T(128)S(1)} %stack.68.me_ref.info_ref, ...), custom_call_target="tpu_custom_call" | custom-call | flops 1000 | bytes 1000 | tf_op jit(solution)/shard_map/front/pallas_call | solution.py:180
  88.5 9.2 %collective-permute-done.16 = bf16[4,48,2304]{2,1,0:T(8,128)(2,1)} collective-permute-done((bf16[4,48,2304]{2,1,0:T(8,128)(2,1)}, bf16[4,48,2304]{2,1,0:T(8,128)(2,1)}, u32[]{:S(2)}, u32[]{:S(2)}) %collective-permute-start.16) | collective-permute-done | bytes 884768 | tf_op jit(solution)/shard_map/ppermute | solution.py:806
  98.3 2.8 collective-permute-done.17
  102.0 2.6 collective-permute-start.18
  108.8 5.0 %mid.2 = (f32[6,256,128]{2,1,0:T(8,128)S(1)}, f32[2,8,384]{2,1,0:T(8,128)S(1)}, f32[256,768]{1,0:T(8,128)S(1)}, f32[256,128]{1,0:T(8,128)S(1)}, bf16[256,768]{1,...) custom-call(s32[8]{0:T(128)S(1)} %stack.68.me_ref.info_ref, bf16[256,768]{1,0:T(8,128)(2,1)S(1)} %copy-done, ...), custom_call_target="tpu_custom_call" | custom-call | flops 1000 | bytes 1000 | tf_op jit(solution)/shard_map/mid/pallas_call | solution.py:268
  114.6 6.9 %collective-permute-done.21.refs_2_ = bf16[8,48,1408]{2,1,0:T(8,128)(2,1)S(1)} collective-permute-done((bf16[8,48,1408]{2,1,0:T(8,128)(2,1)S(1)}, bf16[8,48,1408]{2,1,0:T(8,128)(2,1)S(1)}, u32[]{:S(2)}, u32[]{:S(2)}) %collective-permute-start.21) | collective-permute-done | bytes 1081376 | tf_op jit(solution)/shard_map/ppermute | solution.py:806
  122.8 5.3 %ffn.1 = (f32[256,3072]{1,0:T(8,128)S(1)}, bf16[256,1536]{1,0:T(8,128)(2,1)S(1)}, f32[256,768]{1,0:T(8,128)S(1)}) custom-call(s32[8]{0:T(128)S(1)} %stack.68.me_ref.info_ref, f32[256,768]{1,0:T(8,128)S(1)} %get-tuple-element.237.after_ref, bf16[256,768]{1,0:T(8,128)(2,1)S(1)} %get-tuple-element.235.lifted_ref.refs_4_, ...), custom_call_target="tpu_custom_call" | custom-call | flops 1000 | bytes 1000 | tf_op jit(solution)/shard_map/ffn/pallas_call | solution.py:314
  128.2 4.9 %front.3 = (bf16[256,768]{1,0:T(8,128)(2,1)S(1)}, f32[256,768]{1,0:T(8,128)S(1)}, f32[256,768]{1,0:T(8,128)S(1)}, f32[256,384]{1,0:T(8,128)S(1)}, f32[3,256,128]...) custom-call(s32[8]{0:T(128)S(1)} %stack.68.me_ref.info_ref, ...), custom_call_target="tpu_custom_call" | custom-call | flops 1000 | bytes 1000 | tf_op jit(solution)/shard_map/front/pallas_call | solution.py:180
  133.1 11.0 %collective-permute-done.26.refs_2_ = bf16[8,48,2304]{2,1,0:T(8,128)(2,1)S(1)} collective-permute-done((bf16[8,48,2304]{2,1,0:T(8,128)(2,1)S(1)}, bf16[8,48,2304]{2,1,0:T(8,128)(2,1)S(1)}, u32[]{:S(2)}, u32[]{:S(2)}) %collective-permute-start.26) | collective-permute-done | bytes 1769504 | tf_op jit(solution)/shard_map/ppermute | solution.py:806
  144.6 3.2 collective-permute-done.27
  147.8 2.2 collective-permute-start.30
  151.3 3.7 %collective-permute-done.28 = f32[2,4,384]{2,1,0:T(4,128)S(1)} collective-permute-done((f32[2,4,384]{2,1,0:T(4,128)S(1)}, f32[2,4,384]{2,1,0:T(4,128)S(1)}, u32[]{:S(2)}, u32[]{:S(2)}) %collective-permute-start.28) | collective-permute-done | bytes 12320 | tf_op jit(solution)/shard_map/ppermute | solution.py:806
  155.0 5.2 %mid.3 = (f32[6,256,128]{2,1,0:T(8,128)S(1)}, f32[2,8,384]{2,1,0:T(8,128)S(1)}, f32[256,768]{1,0:T(8,128)S(1)}, f32[256,128]{1,0:T(8,128)S(1)}, bf16[256,768]{1,...) custom-call(s32[8]{0:T(128)S(1)} %stack.68.me_ref.info_ref, ...), custom_call_target="tpu_custom_call" | custom-call | flops 1000 | bytes 1000 | tf_op jit(solution)/shard_map/mid/pallas_call | solution.py:268
  160.2 14.0 %turn.1 = (bf16[16,48,1536]{2,1,0:T(8,128)(2,1)S(1)}, bf16[16,48,1536]{2,1,0:T(8,128)(2,1)S(1)}, bf16[256,768]{1,0:T(8,128)(2,1)}, bf16[256,1536]{1,0:T(8,128)(2...) custom-call(s32[8]{0:T(128)S(1)} %stack.68.me_ref.info_ref, ...), custom_call_target="tpu_custom_call" | custom-call | flops 1000 | bytes 1000 | tf_op jit(solution)/shard_map/turn/pallas_call | solution.py:438
  174.3 4.6 %back_mid.2 = (bf16[256,768]{1,0:T(8,128)(2,1)S(1)}, f32[6,256,128]{2,1,0:T(8,128)S(1)}, f32[1,768]{1,0:T(1,128)S(1)}, f32[2,8,384]{2,1,0:T(8,128)S(1)}, f32[2,384]{1,0:T(2,128)S(1)}) custom-call(s32[8]{0:T(128)S(1)} %stack.68.me_ref.info_ref, bf16[256,768]{1,0:T(8,128)(2,1)S(1)} %get-tuple-element.267.dmid_ref, f32[8,768]{1,0:T(8,128)S(1)} %get-tuple-element.245.p_ref, ...), custom_call_target="tpu_custom_call" | custom-call | flops 1000 | bytes 1000 | tf_op jit(solution)/shard_map/back_mid/pallas_call | solution.py:544
  180.3 4.3 %grad_od.2 = (bf16[16,48,1536]{2,1,0:T(8,128)(2,1)S(1)}, bf16[16,48,1536]{2,1,0:T(8,128)(2,1)S(1)}) custom-call(s32[8]{0:T(128)S(1)} %stack.68.me_ref.info_ref, bf16[256,768]{1,0:T(8,128)(2,1)S(1)} %get-tuple-element.278.gated_ref, bf16[256,768]{1,0:T(8,128)(2,1)S(1)} %get-tuple-element.267.dmid_ref, bf16[256,1536]{1,0:T(8,128)(2,1)S(1)} %get-tuple-element.279.hidden_ref, ...), custom_call_target="tpu_custom_call" | custom-call | flops 1000 | bytes 1000 | tf_op jit(solution)/shard_map/grad_od/pallas_call | solution.py:757
  186.5 2.0 collective-permute-start.35
  191.0 8.2 %back_two.2 = (bf16[16,48,640]{2,1,0:T(8,128)(2,1)S(1)}, bf16[16,48,640]{2,1,0:T(8,128)(2,1)S(1)}, f32[256,768]{1,0:T(8,128)S(1)}, f32[2,768]{1,0:T(2,128)S(1)}) custom-call(s32[8]{0:T(128)S(1)} %stack.68.me_ref.info_ref, f32[256,768]{1,0:T(8,128)S(1)} %get-tuple-element.243.x_ref, f32[8,768]{1,0:T(8,128)S(1)} %get-tuple-element.245.p_ref, ...), custom_call_target="tpu_custom_call" | custom-call | flops 1000 | bytes 1000 | tf_op jit(solution)/shard_map/back_two/pallas_call | solution.py:696
  199.2 7.2 %collective-permute-done.38 = bf16[8,48,1536]{2,1,0:T(8,128)(2,1)S(1)} collective-permute-done((bf16[8,48,1536]{2,1,0:T(8,128)(2,1)S(1)}, bf16[8,48,1536]{2,1,0:T(8,128)(2,1)S(1)}, u32[]{:S(2)}, u32[]{:S(2)}) %collective-permute-start.38) | collective-permute-done | bytes 1179680 | tf_op jit(solution)/shard_map/ppermute | solution.py:806
  206.4 2.4 add_convert_fusion.3
  210.1 10.4 %back_ffn.1 = (bf16[16,48,1536]{2,1,0:T(8,128)(2,1)S(1)}, bf16[16,48,1536]{2,1,0:T(8,128)(2,1)S(1)}, bf16[256,768]{1,0:T(8,128)(2,1)S(1)}, f32[256,768]{1,0:T(8,...) custom-call(s32[8]{0:T(128)S(1)} %stack.68.me_ref.info_ref, f32[256,768]{1,0:T(8,128)S(1)} %get-tuple-element.299.dx_ref, ...), custom_call_target="tpu_custom_call" | custom-call | flops 1000 | bytes 1000 | tf_op jit(solution)/shard_map/back_ffn/pallas_call | solution.py:468
  221.0 2.0 collective-permute-start.42
  223.1 7.9 %collective-permute-done.42 = bf16[4,48,1536]{2,1,0:T(8,128)(2,1)S(1)} collective-permute-done((bf16[4,48,1536]{2,1,0:T(8,128)(2,1)S(1)}, bf16[4,48,1536]{2,1,0:T(8,128)(2,1)S(1)}, u32[]{:S(2)}, u32[]{:S(2)}) %collective-permute-start.42) | collective-permute-done | bytes 589856 | tf_op jit(solution)/shard_map/ppermute | solution.py:806
  234.5 5.5 %back_mid.3 = (bf16[256,768]{1,0:T(8,128)(2,1)S(1)}, f32[6,256,128]{2,1,0:T(8,128)S(1)}, f32[1,768]{1,0:T(1,128)S(1)}, f32[2,8,384]{2,1,0:T(8,128)S(1)}, f32[2,384]{1,0:T(2,128)S(1)}) custom-call(s32[8]{0:T(128)S(1)} %stack.68.me_ref.info_ref, bf16[256,768]{1,0:T(8,128)(2,1)S(1)} %get-tuple-element.311.dmid_ref, f32[8,768]{1,0:T(8,128)S(1)} %get-tuple-element.222.p_ref, ...), custom_call_target="tpu_custom_call" | custom-call | flops 1000 | bytes 1000 | tf_op jit(solution)/shard_map/back_mid/pallas_call | solution.py:544
  242.2 2.8 collective-permute-start.49
  245.8 4.1 %grad_od.3 = (bf16[16,48,1536]{2,1,0:T(8,128)(2,1)S(1)}, bf16[16,48,1536]{2,1,0:T(8,128)(2,1)S(1)}) custom-call(s32[8]{0:T(128)S(1)} %stack.68.me_ref.info_ref, bf16[256,768]{1,0:T(8,128)(2,1)S(1)} %get-tuple-element.325.gated_ref, bf16[256,768]{1,0:T(8,128)(2,1)S(1)} %get-tuple-element.311.dmid_ref, bf16[256,1536]{1,0:T(8,128)(2,1)S(1)} %copy-done.4, ...), custom_call_target="tpu_custom_call" | custom-call | flops 1000 | bytes 1000 | tf_op jit(solution)/shard_map/grad_od/pallas_call | solution.py:757
  256.7 9.0 %back_two.3 = (bf16[16,48,640]{2,1,0:T(8,128)(2,1)S(1)}, bf16[16,48,640]{2,1,0:T(8,128)(2,1)S(1)}, f32[256,768]{1,0:T(8,128)}, f32[2,768]{1,0:T(2,128)}) custom-call(s32[8]{0:T(128)S(1)} %stack.68.me_ref.info_ref, bf16[256,768]{1,0:T(8,128)(2,1)S(1)} %copy-done, f32[8,768]{1,0:T(8,128)S(1)} %get-tuple-element.222.p_ref, ...), custom_call_target="tpu_custom_call" | custom-call | flops 1000 | bytes 1000 | tf_op jit(solution)/shard_map/back_two/pallas_call | solution.py:696
  265.7 4.7 %collective-permute-done.54 = bf16[1,48,1536]{2,1,0:T(8,128)(2,1)S(1)} collective-permute-done((bf16[1,48,1536]{2,1,0:T(8,128)(2,1)S(1)}, bf16[1,48,1536]{2,1,0:T(8,128)(2,1)S(1)}, u32[]{:S(2)}, u32[]{:S(2)}) %collective-permute-start.54) | collective-permute-done | bytes 147488 | tf_op jit(solution)/shard_map/ppermute | solution.py:806
  277.3 1.8 collective-permute-start.56
  279.7 6.2 %collective-permute-done.60 = bf16[2,48,640]{2,1,0:T(8,128)(2,1)S(1)} collective-permute-done((bf16[2,48,640]{2,1,0:T(8,128)(2,1)S(1)}, bf16[2,48,640]{2,1,0:T(8,128)(2,1)S(1)}, u32[]{:S(2)}, u32[]{:S(2)}) %collective-permute-start.60) | collective-permute-done | bytes 122912 | tf_op jit(solution)/shard_map/ppermute | solution.py:806
  285.9 6.0 %collective-permute-done.59 = bf16[2,48,1536]{2,1,0:T(8,128)(2,1)S(1)} collective-permute-done((bf16[2,48,1536]{2,1,0:T(8,128)(2,1)S(1)}, bf16[2,48,1536]{2,1,0:T(8,128)(2,1)S(1)}, u32[]{:S(2)}, u32[]{:S(2)}) %collective-permute-start.59) | collective-permute-done | bytes 294944 | tf_op jit(solution)/shard_map/ppermute | solution.py:806
  293.2 4.2 %collective-permute-done.57 = bf16[4,48,1536]{2,1,0:T(8,128)(2,1)S(1)} collective-permute-done((bf16[4,48,1536]{2,1,0:T(8,128)(2,1)S(1)}, bf16[4,48,1536]{2,1,0:T(8,128)(2,1)S(1)}, u32[]{:S(2)}, u32[]{:S(2)}) %collective-permute-start.57) | collective-permute-done | bytes 589856 | tf_op jit(solution)/shard_map/ppermute | solution.py:806
  297.5 3.2 collective-permute-start.62
  300.9 2.5 collective-permute-start.70
  303.4 6.2 %collective-permute-done.69 = bf16[1,48,640]{2,1,0:T(8,128)(2,1)S(1)} collective-permute-done((bf16[1,48,640]{2,1,0:T(8,128)(2,1)S(1)}, bf16[1,48,640]{2,1,0:T(8,128)(2,1)S(1)}, u32[]{:S(2)}, u32[]{:S(2)}) %collective-permute-start.69) | collective-permute-done | bytes 61472 | tf_op jit(solution)/shard_map/ppermute | solution.py:806
  310.7 2.4 collective-permute-start.68
  314.6 6.3 %collective-permute-done.65 = bf16[2,48,1536]{2,1,0:T(8,128)(2,1)S(1)} collective-permute-done((bf16[2,48,1536]{2,1,0:T(8,128)(2,1)S(1)}, bf16[2,48,1536]{2,1,0:T(8,128)(2,1)S(1)}, u32[]{:S(2)}, u32[]{:S(2)}) %collective-permute-start.65) | collective-permute-done | bytes 294944 | tf_op jit(solution)/shard_map/ppermute | solution.py:806
  321.0 2.6 collective-permute-done.64
  323.7 2.1 collective-permute-start.67
  325.8 3.3 collective-permute-done.66
  (242 shorter events, 74.3 us)
Async XLA Ops:
  7.1 12.0 %collective-permute-start.1 = (bf16[1,48,2304]{2,1,0:T(8,128)(2,1)S(1)}, bf16[1,48,2304]{2,1,0:T(8,128)(2,1)S(1)}, u32[]{:S(2)}, u32[]{:S(2)}) collective-permute-start(bf16[1,48,2304]{2,1,0:T(8,128)(2,1)S(1)} %maximum_bitcast_fusion), channel_id=1, source_target_pairs={{0,8},{1,17},{2,10},{3,19},{4,12},{5,21},{6,14},{7,23},{8,0},{9,25... | collective-permute-start | bytes 663560 | tf_op jit(solution)/shard_map/ppermute | solution.py:806
  10.1 9.0 %collective-permute-start.4 = (bf16[1,48,2304]{2,1,0:T(8,128)(2,1)S(1)}, bf16[1,48,2304]{2,1,0:T(8,128)(2,1)S(1)}, u32[]{:S(2)}, u32[]{:S(2)}) collective-permute-start(bf16[1,48,2304]{2,1,0:T(8,128)(2,1)S(1)} %maximum_bitcast_fusion.1), channel_id=1, source_target_pairs={{0,2},{1,5},{2,0},{3,7},{4,6},{5,1},{6,4},{7,3},{8,10},{9,13},{10,... | collective-permute-start | bytes 663560 | tf_op jit(solution)/shard_map/ppermute | solution.py:806
  19.2 18.4 %collective-permute-start.6 = (bf16[2,48,2304]{2,1,0:T(8,128)(2,1)S(1)}, bf16[2,48,2304]{2,1,0:T(8,128)(2,1)S(1)}, u32[]{:S(2)}, u32[]{:S(2)}) collective-permute-start(bf16[2,48,2304]{2,1,0:T(8,128)(2,1)S(1)} %pad_maximum_fusion.10), channel_id=1, source_target_pairs={{0,16},{1,9},{2,18},{3,11},{4,20},{5,13},{6,22},{7,15},{8,24},{9,1... | collective-permute-start | bytes 1327112 | tf_op jit(solution)/shard_map/ppermute | solution.py:806
  21.6 16.0 %collective-permute-start.5 = (bf16[2,48,1408]{2,1,0:T(8,128)(2,1)S(1)}, bf16[2,48,1408]{2,1,0:T(8,128)(2,1)S(1)}, u32[]{:S(2)}, u32[]{:S(2)}) collective-permute-start(bf16[2,48,1408]{2,1,0:T(8,128)(2,1)S(1)} %pad_maximum_fusion.12), channel_id=1, source_target_pairs={{0,16},{1,9},{2,18},{3,11},{4,20},{5,13},{6,22},{7,15},{8,24},{9,1... | collective-permute-start | bytes 811016 | tf_op jit(solution)/shard_map/ppermute | solution.py:806
  37.8 11.8 %collective-permute-start.7 = (bf16[4,48,1408]{2,1,0:T(8,128)(2,1)S(1)}, bf16[4,48,1408]{2,1,0:T(8,128)(2,1)S(1)}, u32[]{:S(2)}, u32[]{:S(2)}) collective-permute-start(bf16[4,48,1408]{2,1,0:T(8,128)(2,1)S(1)} %pad_maximum_fusion.8), channel_id=1, source_target_pairs={{0,2},{1,5},{2,0},{3,7},{4,6},{5,1},{6,4},{7,3},{8,10},{9,13},{10,... | collective-permute-start | bytes 1622024 | tf_op jit(solution)/shard_map/ppermute | solution.py:806
  41.4 8.2 %collective-permute-start.8 = (bf16[2,48,1408]{2,1,0:T(8,128)(2,1)S(1)}, bf16[2,48,1408]{2,1,0:T(8,128)(2,1)S(1)}, u32[]{:S(2)}, u32[]{:S(2)}) collective-permute-start(bf16[2,48,1408]{2,1,0:T(8,128)(2,1)S(1)} %pad_maximum_fusion.13), channel_id=1, source_target_pairs={{0,8},{1,17},{2,10},{3,19},{4,12},{5,21},{6,14},{7,23},{8,0},{9,25... | collective-permute-start | bytes 811016 | tf_op jit(solution)/shard_map/ppermute | solution.py:806
  41.9 27.3 %collective-permute-start.11 = (bf16[4,48,2304]{2,1,0:T(8,128)(2,1)S(1)}, bf16[4,48,2304]{2,1,0:T(8,128)(2,1)S(1)}, u32[]{:S(2)}, u32[]{:S(2)}) collective-permute-start(bf16[4,48,2304]{2,1,0:T(8,128)(2,1)S(1)} %pad_maximum_fusion.4), channel_id=1, source_target_pairs={{0,2},{1,5},{2,0},{3,7},{4,6},{5,1},{6,4},{7,3},{8,10},{9,13},{10,... | collective-permute-start | bytes 2654216 | tf_op jit(solution)/shard_map/ppermute | solution.py:806
  42.5 26.8 %collective-permute-start.12 = (bf16[2,48,2304]{2,1,0:T(8,128)(2,1)S(1)}, bf16[2,48,2304]{2,1,0:T(8,128)(2,1)S(1)}, u32[]{:S(2)}, u32[]{:S(2)}) collective-permute-start(bf16[2,48,2304]{2,1,0:T(8,128)(2,1)S(1)} %pad_maximum_fusion.11), channel_id=1, source_target_pairs={{0,8},{1,17},{2,10},{3,19},{4,12},{5,21},{6,14},{7,23},{8,0},{9,25... | collective-permute-start | bytes 1327112 | tf_op jit(solution)/shard_map/ppermute | solution.py:806
  49.8 21.9 %collective-permute-start.9 = (bf16[8,48,1408]{2,1,0:T(8,128)(2,1)S(1)}, bf16[8,48,1408]{2,1,0:T(8,128)(2,1)S(1)}, u32[]{:S(2)}, u32[]{:S(2)}) collective-permute-start(bf16[8,48,1408]{2,1,0:T(8,128)(2,1)S(1)} %pad_maximum_fusion.2.refs_0_), channel_id=1, source_target_pairs={{0,4},{1,3},{2,6},{3,1},{4,0},{5,7},{6,2},{7,5},{8,12},{9,11},{10,... | collective-permute-start | bytes 3244040 | tf_op jit(solution)/shard_map/ppermute | solution.py:806
  51.3 20.3 %collective-permute-start.10 = (bf16[4,48,1408]{2,1,0:T(8,128)(2,1)S(1)}, bf16[4,48,1408]{2,1,0:T(8,128)(2,1)S(1)}, u32[]{:S(2)}, u32[]{:S(2)}) collective-permute-start(bf16[4,48,1408]{2,1,0:T(8,128)(2,1)S(1)} %pad_maximum_fusion.9), channel_id=1, source_target_pairs={{0,16},{1,9},{2,18},{3,11},{4,20},{5,13},{6,22},{7,15},{8,24},{9,1... | collective-permute-start | bytes 1622024 | tf_op jit(solution)/shard_map/ppermute | solution.py:806
  72.4 25.4 %collective-permute-start.15 = (bf16[8,48,2304]{2,1,0:T(8,128)(2,1)}, bf16[8,48,2304]{2,1,0:T(8,128)(2,1)}, u32[]{:S(2)}, u32[]{:S(2)}) collective-permute-start(bf16[8,48,2304]{2,1,0:T(8,128)(2,1)} %pad_maximum_fusion.refs_0_), channel_id=1, source_target_pairs={{0,4},{1,3},{2,6},{3,1},{4,0},{5,7},{6,2},{7,5},{8,12},{9,11},{10,... | collective-permute-start | bytes 5308424 | tf_op jit(solution)/shard_map/ppermute | solution.py:806
  74.0 23.7 %collective-permute-start.16 = (bf16[4,48,2304]{2,1,0:T(8,128)(2,1)}, bf16[4,48,2304]{2,1,0:T(8,128)(2,1)}, u32[]{:S(2)}, u32[]{:S(2)}) collective-permute-start(bf16[4,48,2304]{2,1,0:T(8,128)(2,1)} %pad_maximum_fusion.5), channel_id=1, source_target_pairs={{0,16},{1,9},{2,18},{3,11},{4,20},{5,13},{6,22},{7,15},{8,24},{9,1... | collective-permute-start | bytes 2654216 | tf_op jit(solution)/shard_map/ppermute | solution.py:806
  78.9 35.8 %collective-permute-start.23 = (bf16[8,48,2304]{2,1,0:T(8,128)(2,1)}, bf16[8,48,2304]{2,1,0:T(8,128)(2,1)S(1)}, u32[]{:S(2)}, u32[]{:S(2)}) collective-permute-start(bf16[8,48,2304]{2,1,0:T(8,128)(2,1)} %pad_maximum_fusion.refs_0_), channel_id=1, source_target_pairs={{0,1},{1,0},{2,3},{3,2},{4,5},{5,4},{6,7},{7,6},{8,9},{9,8},{10,11... | collective-permute-start | bytes 5308424 | tf_op jit(solution)/shard_map/ppermute | solution.py:806
  97.8 23.8 %collective-permute-start.22 = (bf16[8,48,2304]{2,1,0:T(8,128)(2,1)}, bf16[8,48,2304]{2,1,0:T(8,128)(2,1)S(1)}, u32[]{:S(2)}, u32[]{:S(2)}) collective-permute-start(bf16[8,48,2304]{2,1,0:T(8,128)(2,1)} %collective-permute-done.15.refs_2_), channel_id=1, source_target_pairs={{0,1},{1,0},{2,3},{3,2},{4,5},{5,4},{6,7},{7,6},{8,9},{9,8},{10,11... | collective-permute-start | bytes 5308424 | tf_op jit(solution)/shard_map/ppermute | solution.py:806
  106.3 15.2 %collective-permute-start.21 = (bf16[8,48,1408]{2,1,0:T(8,128)(2,1)S(1)}, bf16[8,48,1408]{2,1,0:T(8,128)(2,1)S(1)}, u32[]{:S(2)}, u32[]{:S(2)}) collective-permute-start(bf16[8,48,1408]{2,1,0:T(8,128)(2,1)S(1)} %pad_maximum_fusion.3.refs_0_), channel_id=1, source_target_pairs={{0,4},{1,3},{2,6},{3,1},{4,0},{5,7},{6,2},{7,5},{8,12},{9,11},{10,... | collective-permute-start | bytes 3244040 | tf_op jit(solution)/shard_map/ppermute | solution.py:806
  121.6 22.5 %collective-permute-start.26 = (bf16[8,48,2304]{2,1,0:T(8,128)(2,1)S(1)}, bf16[8,48,2304]{2,1,0:T(8,128)(2,1)S(1)}, u32[]{:S(2)}, u32[]{:S(2)}) collective-permute-start(bf16[8,48,2304]{2,1,0:T(8,128)(2,1)S(1)} %pad_maximum_fusion.1.refs_0_), channel_id=1, source_target_pairs={{0,4},{1,3},{2,6},{3,1},{4,0},{5,7},{6,2},{7,5},{8,12},{9,11},{10,... | collective-permute-start | bytes 5308424 | tf_op jit(solution)/shard_map/ppermute | solution.py:806
  122.8 37.4 %collective-permute-start.32 = (bf16[8,48,2304]{2,1,0:T(8,128)(2,1)S(1)}, bf16[8,48,2304]{2,1,0:T(8,128)(2,1)S(1)}, u32[]{:S(2)}, u32[]{:S(2)}) collective-permute-start(bf16[8,48,2304]{2,1,0:T(8,128)(2,1)S(1)} %pad_maximum_fusion.1.refs_0_), channel_id=1, source_target_pairs={{0,1},{1,0},{2,3},{3,2},{4,5},{5,4},{6,7},{7,6},{8,9},{9,8},{10,11... | collective-permute-start | bytes 5308424 | tf_op jit(solution)/shard_map/ppermute | solution.py:806
  144.1 16.1 %collective-permute-start.31 = (bf16[8,48,2304]{2,1,0:T(8,128)(2,1)S(1)}, bf16[8,48,2304]{2,1,0:T(8,128)(2,1)S(1)}, u32[]{:S(2)}, u32[]{:S(2)}) collective-permute-start(bf16[8,48,2304]{2,1,0:T(8,128)(2,1)S(1)} %collective-permute-done.26.refs_2_), channel_id=1, source_target_pairs={{0,1},{1,0},{2,3},{3,2},{4,5},{5,4},{6,7},{7,6},{8,9},{9,8},{10,11... | collective-permute-start | bytes 5308424 | tf_op jit(solution)/shard_map/ppermute | solution.py:806
  147.8 7.2 %collective-permute-start.30 = (f32[2,4,384]{2,1,0:T(4,128)S(1)}, f32[2,4,384]{2,1,0:T(4,128)S(1)}, u32[]{:S(2)}, u32[]{:S(2)}) collective-permute-start(f32[2,4,384]{2,1,0:T(4,128)S(1)} %pad_maximum_fusion.15), channel_id=1, source_target_pairs={{0,6},{1,7},{2,4},{3,5},{4,2},{5,3},{6,0},{7,1},{8,14},{9,15},{10,... | collective-permute-start | bytes 36872 | tf_op jit(solution)/shard_map/ppermute | solution.py:806
  184.6 21.8 %collective-permute-start.39 = (bf16[16,48,1536]{2,1,0:T(8,128)(2,1)S(1)}, bf16[16,48,1536]{2,1,0:T(8,128)(2,1)}, u32[]{:S(2)}, u32[]{:S(2)}) collective-permute-start(bf16[16,48,1536]{2,1,0:T(8,128)(2,1)S(1)} %get-tuple-element.293), channel_id=1, source_target_pairs={{0,1},{1,0},{2,3},{3,2},{4,5},{5,4},{6,7},{7,6},{8,9},{9,8},{10,11... | collective-permute-start | bytes 7077896 | tf_op jit(solution)/shard_map/ppermute | solution.py:806
  190.2 16.3 %collective-permute-start.38 = (bf16[8,48,1536]{2,1,0:T(8,128)(2,1)S(1)}, bf16[8,48,1536]{2,1,0:T(8,128)(2,1)S(1)}, u32[]{:S(2)}, u32[]{:S(2)}) collective-permute-start(bf16[8,48,1536]{2,1,0:T(8,128)(2,1)S(1)} %get-tuple-element.286), channel_id=1, source_target_pairs={{0,4},{1,3},{2,6},{3,1},{4,0},{5,7},{6,2},{7,5},{8,12},{9,11},{10,... | collective-permute-start | bytes 3538952 | tf_op jit(solution)/shard_map/ppermute | solution.py:806
  209.2 21.7 %collective-permute-start.40 = (bf16[8,48,1536]{2,1,0:T(8,128)(2,1)S(1)}, bf16[8,48,1536]{2,1,0:T(8,128)(2,1)S(1)}, u32[]{:S(2)}, u32[]{:S(2)}) collective-permute-start(bf16[8,48,1536]{2,1,0:T(8,128)(2,1)S(1)} %get-tuple-element.298), channel_id=1, source_target_pairs={{0,4},{1,3},{2,6},{3,1},{4,0},{5,7},{6,2},{7,5},{8,12},{9,11},{10,... | collective-permute-start | bytes 3538952 | tf_op jit(solution)/shard_map/ppermute | solution.py:806
  210.1 13.0 %collective-permute-start.41 = (bf16[16,48,640]{2,1,0:T(8,128)(2,1)S(1)}, bf16[16,48,640]{2,1,0:T(8,128)(2,1)S(1)}, u32[]{:S(2)}, u32[]{:S(2)}) collective-permute-start(bf16[16,48,640]{2,1,0:T(8,128)(2,1)S(1)} %get-tuple-element.303), channel_id=1, source_target_pairs={{0,1},{1,0},{2,3},{3,2},{4,5},{5,4},{6,7},{7,6},{8,9},{9,8},{10,11... | collective-permute-start | bytes 2949128 | tf_op jit(solution)/shard_map/ppermute | solution.py:806
  220.5 21.7 %collective-permute-start.43 = (bf16[16,48,1536]{2,1,0:T(8,128)(2,1)S(1)}, bf16[16,48,1536]{2,1,0:T(8,128)(2,1)S(1)}, u32[]{:S(2)}, u32[]{:S(2)}) collective-permute-start(bf16[16,48,1536]{2,1,0:T(8,128)(2,1)S(1)} %get-tuple-element.317), channel_id=1, source_target_pairs={{0,1},{1,0},{2,3},{3,2},{4,5},{5,4},{6,7},{7,6},{8,9},{9,8},{10,11... | collective-permute-start | bytes 7077896 | tf_op jit(solution)/shard_map/ppermute | solution.py:806
  221.0 9.9 %collective-permute-start.42 = (bf16[4,48,1536]{2,1,0:T(8,128)(2,1)S(1)}, bf16[4,48,1536]{2,1,0:T(8,128)(2,1)S(1)}, u32[]{:S(2)}, u32[]{:S(2)}) collective-permute-start(bf16[4,48,1536]{2,1,0:T(8,128)(2,1)S(1)} %get-tuple-element.304), channel_id=1, source_target_pairs={{0,2},{1,5},{2,0},{3,7},{4,6},{5,1},{6,4},{7,3},{8,10},{9,13},{10,... | collective-permute-start | bytes 1769480 | tf_op jit(solution)/shard_map/ppermute | solution.py:806
  231.3 10.8 %collective-permute-start.45 = (bf16[2,48,1536]{2,1,0:T(8,128)(2,1)S(1)}, bf16[2,48,1536]{2,1,0:T(8,128)(2,1)S(1)}, u32[]{:S(2)}, u32[]{:S(2)}) collective-permute-start(bf16[2,48,1536]{2,1,0:T(8,128)(2,1)S(1)} %get-tuple-element.318), channel_id=1, source_target_pairs={{0,16},{1,9},{2,18},{3,11},{4,20},{5,13},{6,22},{7,15},{8,24},{9,1... | collective-permute-start | bytes 884744 | tf_op jit(solution)/shard_map/ppermute | solution.py:806
  231.9 10.3 %collective-permute-start.44 = (bf16[8,48,640]{2,1,0:T(8,128)(2,1)S(1)}, bf16[8,48,640]{2,1,0:T(8,128)(2,1)S(1)}, u32[]{:S(2)}, u32[]{:S(2)}) collective-permute-start(bf16[8,48,640]{2,1,0:T(8,128)(2,1)S(1)} %get-tuple-element.310), channel_id=1, source_target_pairs={{0,4},{1,3},{2,6},{3,1},{4,0},{5,7},{6,2},{7,5},{8,12},{9,11},{10,... | collective-permute-start | bytes 1474568 | tf_op jit(solution)/shard_map/ppermute | solution.py:806
  242.2 8.7 %collective-permute-start.49 = (f32[2,2,384]{2,1,0:T(2,128)S(1)}, f32[2,2,384]{2,1,0:T(2,128)S(1)}, u32[]{:S(2)}, u32[]{:S(2)}) collective-permute-start(f32[2,2,384]{2,1,0:T(2,128)S(1)} %pad_maximum_fusion.17), channel_id=1, source_target_pairs={{0,6},{1,7},{2,4},{3,5},{4,2},{5,3},{6,0},{7,1},{8,14},{9,15},{10,... | collective-permute-start | bytes 18440 | tf_op jit(solution)/shard_map/ppermute | solution.py:806
  249.8 22.7 %collective-permute-start.55 = (bf16[16,48,1536]{2,1,0:T(8,128)(2,1)S(1)}, bf16[16,48,1536]{2,1,0:T(8,128)(2,1)S(1)}, u32[]{:S(2)}, u32[]{:S(2)}) collective-permute-start(bf16[16,48,1536]{2,1,0:T(8,128)(2,1)S(1)} %get-tuple-element.351), channel_id=1, source_target_pairs={{0,1},{1,0},{2,3},{3,2},{4,5},{5,4},{6,7},{7,6},{8,9},{9,8},{10,11... | collective-permute-start | bytes 7077896 | tf_op jit(solution)/shard_map/ppermute | solution.py:806
  250.9 21.6 %collective-permute-start.51 = (bf16[8,48,1536]{2,1,0:T(8,128)(2,1)S(1)}, bf16[8,48,1536]{2,1,0:T(8,128)(2,1)S(1)}, u32[]{:S(2)}, u32[]{:S(2)}) collective-permute-start(bf16[8,48,1536]{2,1,0:T(8,128)(2,1)S(1)} %get-tuple-element.333), channel_id=1, source_target_pairs={{0,4},{1,3},{2,6},{3,1},{4,0},{5,7},{6,2},{7,5},{8,12},{9,11},{10,... | collective-permute-start | bytes 3538952 | tf_op jit(solution)/shard_map/ppermute | solution.py:806
  252.2 20.3 %collective-permute-start.52 = (bf16[4,48,1536]{2,1,0:T(8,128)(2,1)S(1)}, bf16[4,48,1536]{2,1,0:T(8,128)(2,1)S(1)}, u32[]{:S(2)}, u32[]{:S(2)}) collective-permute-start(bf16[4,48,1536]{2,1,0:T(8,128)(2,1)S(1)} %get-tuple-element.348), channel_id=1, source_target_pairs={{0,16},{1,9},{2,18},{3,11},{4,20},{5,13},{6,22},{7,15},{8,24},{9,1... | collective-permute-start | bytes 1769480 | tf_op jit(solution)/shard_map/ppermute | solution.py:806
  253.8 17.0 %collective-permute-start.53 = (bf16[4,48,640]{2,1,0:T(8,128)(2,1)S(1)}, bf16[4,48,640]{2,1,0:T(8,128)(2,1)S(1)}, u32[]{:S(2)}, u32[]{:S(2)}) collective-permute-start(bf16[4,48,640]{2,1,0:T(8,128)(2,1)S(1)} %get-tuple-element.349), channel_id=1, source_target_pairs={{0,2},{1,5},{2,0},{3,7},{4,6},{5,1},{6,4},{7,3},{8,10},{9,13},{10,... | collective-permute-start | bytes 737288 | tf_op jit(solution)/shard_map/ppermute | solution.py:806
  255.2 15.2 %collective-permute-start.54 = (bf16[1,48,1536]{2,1,0:T(8,128)(2,1)S(1)}, bf16[1,48,1536]{2,1,0:T(8,128)(2,1)S(1)}, u32[]{:S(2)}, u32[]{:S(2)}) collective-permute-start(bf16[1,48,1536]{2,1,0:T(8,128)(2,1)S(1)} %add_convert_fusion.39), channel_id=1, source_target_pairs={{0,8},{1,17},{2,10},{3,19},{4,12},{5,21},{6,14},{7,23},{8,0},{9,25... | collective-permute-start | bytes 442376 | tf_op jit(solution)/shard_map/ppermute | solution.py:806
  273.8 18.0 %collective-permute-start.58 = (bf16[8,48,1536]{2,1,0:T(8,128)(2,1)S(1)}, bf16[8,48,1536]{2,1,0:T(8,128)(2,1)S(1)}, u32[]{:S(2)}, u32[]{:S(2)}) collective-permute-start(bf16[8,48,1536]{2,1,0:T(8,128)(2,1)S(1)} %get-tuple-element.356), channel_id=1, source_target_pairs={{0,4},{1,3},{2,6},{3,1},{4,0},{5,7},{6,2},{7,5},{8,12},{9,11},{10,... | collective-permute-start | bytes 3538952 | tf_op jit(solution)/shard_map/ppermute | solution.py:806
  274.7 17.2 %collective-permute-start.59 = (bf16[2,48,1536]{2,1,0:T(8,128)(2,1)S(1)}, bf16[2,48,1536]{2,1,0:T(8,128)(2,1)S(1)}, u32[]{:S(2)}, u32[]{:S(2)}) collective-permute-start(bf16[2,48,1536]{2,1,0:T(8,128)(2,1)S(1)} %get-tuple-element.360), channel_id=1, source_target_pairs={{0,8},{1,17},{2,10},{3,19},{4,12},{5,21},{6,14},{7,23},{8,0},{9,25... | collective-permute-start | bytes 884744 | tf_op jit(solution)/shard_map/ppermute | solution.py:806
  275.9 10.0 %collective-permute-start.60 = (bf16[2,48,640]{2,1,0:T(8,128)(2,1)S(1)}, bf16[2,48,640]{2,1,0:T(8,128)(2,1)S(1)}, u32[]{:S(2)}, u32[]{:S(2)}) collective-permute-start(bf16[2,48,640]{2,1,0:T(8,128)(2,1)S(1)} %get-tuple-element.361), channel_id=1, source_target_pairs={{0,16},{1,9},{2,18},{3,11},{4,20},{5,13},{6,22},{7,15},{8,24},{9,1... | collective-permute-start | bytes 368648 | tf_op jit(solution)/shard_map/ppermute | solution.py:806
  277.3 23.4 %collective-permute-start.56 = (bf16[8,48,640]{2,1,0:T(8,128)(2,1)S(1)}, bf16[8,48,640]{2,1,0:T(8,128)(2,1)S(1)}, u32[]{:S(2)}, u32[]{:S(2)}) collective-permute-start(bf16[8,48,640]{2,1,0:T(8,128)(2,1)S(1)} %get-tuple-element.358), channel_id=1, source_target_pairs={{0,4},{1,3},{2,6},{3,1},{4,0},{5,7},{6,2},{7,5},{8,12},{9,11},{10,... | collective-permute-start | bytes 1474568 | tf_op jit(solution)/shard_map/ppermute | solution.py:806
  279.0 18.3 %collective-permute-start.57 = (bf16[4,48,1536]{2,1,0:T(8,128)(2,1)S(1)}, bf16[4,48,1536]{2,1,0:T(8,128)(2,1)S(1)}, u32[]{:S(2)}, u32[]{:S(2)}) collective-permute-start(bf16[4,48,1536]{2,1,0:T(8,128)(2,1)S(1)} %get-tuple-element.359), channel_id=1, source_target_pairs={{0,16},{1,9},{2,18},{3,11},{4,20},{5,13},{6,22},{7,15},{8,24},{9,1... | collective-permute-start | bytes 1769480 | tf_op jit(solution)/shard_map/ppermute | solution.py:806
  292.2 17.8 %collective-permute-start.63 = (bf16[4,48,1536]{2,1,0:T(8,128)(2,1)S(1)}, bf16[4,48,1536]{2,1,0:T(8,128)(2,1)S(1)}, u32[]{:S(2)}, u32[]{:S(2)}) collective-permute-start(bf16[4,48,1536]{2,1,0:T(8,128)(2,1)S(1)} %get-tuple-element.365), channel_id=1, source_target_pairs={{0,2},{1,5},{2,0},{3,7},{4,6},{5,1},{6,4},{7,3},{8,10},{9,13},{10,... | collective-permute-start | bytes 1769480 | tf_op jit(solution)/shard_map/ppermute | solution.py:806
  297.5 13.2 %collective-permute-start.62 = (bf16[2,48,1536]{2,1,0:T(8,128)(2,1)S(1)}, bf16[2,48,1536]{2,1,0:T(8,128)(2,1)S(1)}, u32[]{:S(2)}, u32[]{:S(2)}) collective-permute-start(bf16[2,48,1536]{2,1,0:T(8,128)(2,1)S(1)} %get-tuple-element.367), channel_id=1, source_target_pairs={{0,8},{1,17},{2,10},{3,19},{4,12},{5,21},{6,14},{7,23},{8,0},{9,25... | collective-permute-start | bytes 884744 | tf_op jit(solution)/shard_map/ppermute | solution.py:806
  300.7 9.0 %collective-permute-start.69 = (bf16[1,48,640]{2,1,0:T(8,128)(2,1)S(1)}, bf16[1,48,640]{2,1,0:T(8,128)(2,1)S(1)}, u32[]{:S(2)}, u32[]{:S(2)}) collective-permute-start(bf16[1,48,640]{2,1,0:T(8,128)(2,1)S(1)} %add_convert_fusion.47), channel_id=1, source_target_pairs={{0,8},{1,17},{2,10},{3,19},{4,12},{5,21},{6,14},{7,23},{8,0},{9,25... | collective-permute-start | bytes 184328 | tf_op jit(solution)/shard_map/ppermute | solution.py:806
  300.9 8.8 %collective-permute-start.70 = (bf16[1,48,1536]{2,1,0:T(8,128)(2,1)S(1)}, bf16[1,48,1536]{2,1,0:T(8,128)(2,1)S(1)}, u32[]{:S(2)}, u32[]{:S(2)}) collective-permute-start(bf16[1,48,1536]{2,1,0:T(8,128)(2,1)S(1)} %add_convert_fusion.38), channel_id=1, source_target_pairs={{0,2},{1,5},{2,0},{3,7},{4,6},{5,1},{6,4},{7,3},{8,10},{9,13},{10,... | collective-permute-start | bytes 442376 | tf_op jit(solution)/shard_map/ppermute | solution.py:806
  303.4 9.8 %collective-permute-start.61 = (bf16[4,48,640]{2,1,0:T(8,128)(2,1)S(1)}, bf16[4,48,640]{2,1,0:T(8,128)(2,1)S(1)}, u32[]{:S(2)}, u32[]{:S(2)}) collective-permute-start(bf16[4,48,640]{2,1,0:T(8,128)(2,1)S(1)} %get-tuple-element.369), channel_id=1, source_target_pairs={{0,2},{1,5},{2,0},{3,7},{4,6},{5,1},{6,4},{7,3},{8,10},{9,13},{10,... | collective-permute-start | bytes 737288 | tf_op jit(solution)/shard_map/ppermute | solution.py:806
  309.9 21.1 %collective-permute-start.72 = (f32[24,2944]{1,0:T(8,128)S(1)}, f32[24,2944]{1,0:T(8,128)S(1)}, u32[]{:S(2)}, u32[]{:S(2)}) collective-permute-start(f32[24,2944]{1,0:T(8,128)S(1)} %get-tuple-element.428), channel_id=1, source_target_pairs={{0,1},{1,0},{2,3},{3,2},{4,5},{5,4},{6,7},{7,6},{8,9},{9,8},{10,11... | collective-permute-start | bytes 847880 | tf_op jit(solution)/shard_map/ppermute | solution.py:806
  310.1 10.8 %collective-permute-start.65 = (bf16[2,48,1536]{2,1,0:T(8,128)(2,1)S(1)}, bf16[2,48,1536]{2,1,0:T(8,128)(2,1)S(1)}, u32[]{:S(2)}, u32[]{:S(2)}) collective-permute-start(bf16[2,48,1536]{2,1,0:T(8,128)(2,1)S(1)} %get-tuple-element.371), channel_id=1, source_target_pairs={{0,16},{1,9},{2,18},{3,11},{4,20},{5,13},{6,22},{7,15},{8,24},{9,1... | collective-permute-start | bytes 884744 | tf_op jit(solution)/shard_map/ppermute | solution.py:806
  310.7 12.9 %collective-permute-start.68 = (bf16[1,48,1536]{2,1,0:T(8,128)(2,1)S(1)}, bf16[1,48,1536]{2,1,0:T(8,128)(2,1)S(1)}, u32[]{:S(2)}, u32[]{:S(2)}) collective-permute-start(bf16[1,48,1536]{2,1,0:T(8,128)(2,1)S(1)} %add_convert_fusion.37), channel_id=1, source_target_pairs={{0,2},{1,5},{2,0},{3,7},{4,6},{5,1},{6,4},{7,3},{8,10},{9,13},{10,... | collective-permute-start | bytes 442376 | tf_op jit(solution)/shard_map/ppermute | solution.py:806
  313.2 10.4 %collective-permute-start.64 = (bf16[2,48,640]{2,1,0:T(8,128)(2,1)S(1)}, bf16[2,48,640]{2,1,0:T(8,128)(2,1)S(1)}, u32[]{:S(2)}, u32[]{:S(2)}) collective-permute-start(bf16[2,48,640]{2,1,0:T(8,128)(2,1)S(1)} %get-tuple-element.375), channel_id=1, source_target_pairs={{0,16},{1,9},{2,18},{3,11},{4,20},{5,13},{6,22},{7,15},{8,24},{9,1... | collective-permute-start | bytes 368648 | tf_op jit(solution)/shard_map/ppermute | solution.py:806
  323.7 7.0 %collective-permute-start.67 = (bf16[1,48,1536]{2,1,0:T(8,128)(2,1)S(1)}, bf16[1,48,1536]{2,1,0:T(8,128)(2,1)S(1)}, u32[]{:S(2)}, u32[]{:S(2)}) collective-permute-start(bf16[1,48,1536]{2,1,0:T(8,128)(2,1)S(1)} %add_convert_fusion.36), channel_id=1, source_target_pairs={{0,8},{1,17},{2,10},{3,19},{4,12},{5,21},{6,14},{7,23},{8,0},{9,25... | collective-permute-start | bytes 442376 | tf_op jit(solution)/shard_map/ppermute | solution.py:806
  (39 other events, 204.9 us)

commit v6 on v5

--- a/solution.py
+++ b/solution.py
@@ -12,7 +12,7 @@
 SUB = 8
 UNIT = 48
 HALVES = {"mix": 1024, "out": 384, "up": 1536, "gate": 384, "cell": 640}
-ROWS = 32
+ROWS = 256
 F32 = jnp.float32
 BF16 = jnp.bfloat16
 ALL = ("dp", "seq")
@@ -27,11 +27,8 @@
 
 
 def over_rows(total, body):
-    def step(i, _):
-        body(pl.ds(pl.multiple_of(i * ROWS, ROWS), ROWS))
-        return 0
-
-    lax.fori_loop(0, total // ROWS, step, 0)
+    for i in range(total // ROWS):
+        body(pl.ds(i * ROWS, ROWS))
 
 
 def dot(left, right):

time: 339 us -> 332 us (0.979)
  Pallas kernels: 89.4 us -> 75.2 us
  starting transfers between devices: 72.1 us -> 76.5 us
    ppermute x73, starting transfers between devices: 72.1 us -> 76.5 us  [swap(): return lax.ppermute(x, ALL, [(i, i ^ bits[i % 2]) for i in range(count)])]
    pallas_call x2, Pallas kernels: 17.2 us -> 13.7 us  [back_two(): pl.pallas_call(functools.partial(back_two_kernel, plan, len(weights), rel...]
  transfers between devices with their start and end apart: 73 -> 73, of which waited for: 29 -> 29; matrix products, arithmetic and copies ran while one was open for 3% -> 4% of each run, Pallas kernels for 21% -> 17%
where the time goes in v6:
time: 332 us; the launch traced here: 329 us
  waiting for transfers between devices  148 us (45%)
  starting transfers between devices  76.5 us (23%)
  Pallas kernels  75.2 us (23%)
  other arithmetic  13.9 us (4%)
  local copies, waits for them, and re-layouts  10.2 us (3%)
  between operations  4.35 us (1%)
    ppermute x73, waiting for transfers between devices, swap(): return lax.ppermute(x, ALL, [(i, i ^ bits[i % 2]) for i in range(count)])  148 us
    ppermute x73, starting transfers between devices, swap(): return lax.ppermute(x, ALL, [(i, i ^ bits[i % 2]) for i in range(count)])  76.5 us
    pallas_call x2, Pallas kernels, back_two(): pl.pallas_call(functools.partial(back_two_kernel, plan, len(weights), rel...  13.7 us
    pallas_call x1, Pallas kernels, turn(): pl.pallas_call(functools.partial(turn_kernel, plan, len(weights), rels),...  12.4 us
    pallas_call x2, Pallas kernels, front(): pl.pallas_call(functools.partial(front_kernel, plan, len(weights)), out_s...  9.84 us
    pallas_call x1, Pallas kernels, back_ffn(): pl.pallas_call(functools.partial(back_ffn_kernel, plan, len(weights), rel...  8.63 us
    pallas_call x2, Pallas kernels, grad_od(): pl.pallas_call(functools.partial(grad_od_kernel, rels), out_shape=(shape,...  8.13 us
    convert_element_type x24, other arithmetic, joined(): (self.held[part].astype(F32) + self.got[part].astype(F32)).astype(BF16)  7.57 us
  transfers between devices with their start and end apart: 73, of which 29 were waited for; matrix products, arithmetic and copies ran while one was open for 4% of the time, Pallas kernels for 17%

profile of v6, /device:TPU:0, one launch (start us, length us, event | category | flops | bytes accessed | tf_op | source)
XLA Modules:
  0.0 328.5 jit_solution(3033444502580939831)
XLA Ops:
  7.1 3.0 collective-permute-start.1
  12.3 5.2 %collective-permute-done.3 = bf16[1,48,1408]{2,1,0:T(8,128)(2,1)S(1)} collective-permute-done((bf16[1,48,1408]{2,1,0:T(8,128)(2,1)S(1)}, bf16[1,48,1408]{2,1,0:T(8,128)(2,1)S(1)}, u32[]{:S(2)}, u32[]{:S(2)}) %collective-permute-start.3) | collective-permute-done | bytes 135200 | tf_op jit(solution)/shard_map/ppermute | solution.py:803
  19.2 2.4 collective-permute-start.6
  22.2 15.4 %collective-permute-done.5 = bf16[2,48,1408]{2,1,0:T(8,128)(2,1)S(1)} collective-permute-done((bf16[2,48,1408]{2,1,0:T(8,128)(2,1)S(1)}, bf16[2,48,1408]{2,1,0:T(8,128)(2,1)S(1)}, u32[]{:S(2)}, u32[]{:S(2)}) %collective-permute-start.5) | collective-permute-done | bytes 270368 | tf_op jit(solution)/shard_map/ppermute | solution.py:803
  37.8 3.6 %collective-permute-start.7 = (bf16[4,48,1408]{2,1,0:T(8,128)(2,1)S(1)}, bf16[4,48,1408]{2,1,0:T(8,128)(2,1)S(1)}, u32[]{:S(2)}, u32[]{:S(2)}) collective-permute-start(bf16[4,48,1408]{2,1,0:T(8,128)(2,1)S(1)} %pad_maximum_fusion.8), channel_id=1, source_target_pairs={{0,2},{1,5},{2,0},{3,7},{4,6},{5,1},{6,4},{7,3},{8,10},{9,13},{10,... | collective-permute-start | bytes 1622024 | tf_op jit(solution)/shard_map/ppermute | solution.py:803
  43.5 6.0 %collective-permute-done.8 = bf16[2,48,1408]{2,1,0:T(8,128)(2,1)S(1)} collective-permute-done((bf16[2,48,1408]{2,1,0:T(8,128)(2,1)S(1)}, bf16[2,48,1408]{2,1,0:T(8,128)(2,1)S(1)}, u32[]{:S(2)}, u32[]{:S(2)}) %collective-permute-start.8) | collective-permute-done | bytes 270368 | tf_op jit(solution)/shard_map/ppermute | solution.py:803
  51.3 2.7 collective-permute-start.10
  54.0 15.2 %collective-permute-done.12 = bf16[2,48,2304]{2,1,0:T(8,128)(2,1)S(1)} collective-permute-done((bf16[2,48,2304]{2,1,0:T(8,128)(2,1)S(1)}, bf16[2,48,2304]{2,1,0:T(8,128)(2,1)S(1)}, u32[]{:S(2)}, u32[]{:S(2)}) %collective-permute-start.12) | collective-permute-done | bytes 442400 | tf_op jit(solution)/shard_map/ppermute | solution.py:803
  82.0 5.4 %front.2 = (bf16[256,768]{1,0:T(8,128)(2,1)S(1)}, f32[256,768]{1,0:T(8,128)S(1)}, f32[256,768]{1,0:T(8,128)S(1)}, f32[256,384]{1,0:T(8,128)S(1)}, f32[3,256,128]...) custom-call(s32[8]{0:T(128)S(1)} %stack.68.me_ref.info_ref, ...), custom_call_target="tpu_custom_call" | custom-call | flops 1000 | bytes 1000 | tf_op jit(solution)/shard_map/front/pallas_call | solution.py:177
  88.2 9.5 %collective-permute-done.16 = bf16[4,48,2304]{2,1,0:T(8,128)(2,1)} collective-permute-done((bf16[4,48,2304]{2,1,0:T(8,128)(2,1)}, bf16[4,48,2304]{2,1,0:T(8,128)(2,1)}, u32[]{:S(2)}, u32[]{:S(2)}) %collective-permute-start.16) | collective-permute-done | bytes 884768 | tf_op jit(solution)/shard_map/ppermute | solution.py:803
  98.3 2.8 collective-permute-done.17
  102.0 2.6 collective-permute-start.18
  108.8 3.8 %mid.2 = (f32[6,256,128]{2,1,0:T(8,128)S(1)}, f32[2,8,384]{2,1,0:T(8,128)S(1)}, f32[256,768]{1,0:T(8,128)S(1)}, f32[256,128]{1,0:T(8,128)S(1)}, bf16[256,768]{1,...) custom-call(s32[8]{0:T(128)S(1)} %stack.68.me_ref.info_ref, bf16[256,768]{1,0:T(8,128)(2,1)S(1)} %copy-done, ...), custom_call_target="tpu_custom_call" | custom-call | flops 1000 | bytes 1000 | tf_op jit(solution)/shard_map/mid/pallas_call | solution.py:265
  113.5 8.0 %collective-permute-done.21.refs_2_ = bf16[8,48,1408]{2,1,0:T(8,128)(2,1)S(1)} collective-permute-done((bf16[8,48,1408]{2,1,0:T(8,128)(2,1)S(1)}, bf16[8,48,1408]{2,1,0:T(8,128)(2,1)S(1)}, u32[]{:S(2)}, u32[]{:S(2)}) %collective-permute-start.21) | collective-permute-done | bytes 1081376 | tf_op jit(solution)/shard_map/ppermute | solution.py:803
  122.8 5.3 %ffn.1 = (f32[256,3072]{1,0:T(8,128)S(1)}, bf16[256,1536]{1,0:T(8,128)(2,1)S(1)}, f32[256,768]{1,0:T(8,128)S(1)}) custom-call(s32[8]{0:T(128)S(1)} %stack.68.me_ref.info_ref, f32[256,768]{1,0:T(8,128)S(1)} %get-tuple-element.237.after_ref, bf16[256,768]{1,0:T(8,128)(2,1)S(1)} %get-tuple-element.235.lifted_ref.refs_4_, ...), custom_call_target="tpu_custom_call" | custom-call | flops 1000 | bytes 1000 | tf_op jit(solution)/shard_map/ffn/pallas_call | solution.py:311
  128.2 4.5 %front.3 = (bf16[256,768]{1,0:T(8,128)(2,1)S(1)}, f32[256,768]{1,0:T(8,128)S(1)}, f32[256,768]{1,0:T(8,128)S(1)}, f32[256,384]{1,0:T(8,128)S(1)}, f32[3,256,128]...) custom-call(s32[8]{0:T(128)S(1)} %stack.68.me_ref.info_ref, ...), custom_call_target="tpu_custom_call" | custom-call | flops 1000 | bytes 1000 | tf_op jit(solution)/shard_map/front/pallas_call | solution.py:177
  132.7 11.4 %collective-permute-done.26.refs_2_ = bf16[8,48,2304]{2,1,0:T(8,128)(2,1)S(1)} collective-permute-done((bf16[8,48,2304]{2,1,0:T(8,128)(2,1)S(1)}, bf16[8,48,2304]{2,1,0:T(8,128)(2,1)S(1)}, u32[]{:S(2)}, u32[]{:S(2)}) %collective-permute-start.26) | collective-permute-done | bytes 1769504 | tf_op jit(solution)/shard_map/ppermute | solution.py:803
  144.6 3.2 collective-permute-done.27
  147.8 2.2 collective-permute-start.30
  151.3 3.7 %collective-permute-done.28 = f32[2,4,384]{2,1,0:T(4,128)S(1)} collective-permute-done((f32[2,4,384]{2,1,0:T(4,128)S(1)}, f32[2,4,384]{2,1,0:T(4,128)S(1)}, u32[]{:S(2)}, u32[]{:S(2)}) %collective-permute-start.28) | collective-permute-done | bytes 12320 | tf_op jit(solution)/shard_map/ppermute | solution.py:803
  155.0 3.2 mid.3
  158.3 12.4 %turn.1 = (bf16[16,48,1536]{2,1,0:T(8,128)(2,1)S(1)}, bf16[16,48,1536]{2,1,0:T(8,128)(2,1)S(1)}, bf16[256,768]{1,0:T(8,128)(2,1)}, bf16[256,1536]{1,0:T(8,128)(2...) custom-call(s32[8]{0:T(128)S(1)} %stack.68.me_ref.info_ref, ...), custom_call_target="tpu_custom_call" | custom-call | flops 1000 | bytes 1000 | tf_op jit(solution)/shard_map/turn/pallas_call | solution.py:435
  170.7 2.9 back_mid.2
  175.3 4.1 %grad_od.2 = (bf16[16,48,1536]{2,1,0:T(8,128)(2,1)S(1)}, bf16[16,48,1536]{2,1,0:T(8,128)(2,1)S(1)}) custom-call(s32[8]{0:T(128)S(1)} %stack.68.me_ref.info_ref, bf16[256,768]{1,0:T(8,128)(2,1)S(1)} %get-tuple-element.278.gated_ref, bf16[256,768]{1,0:T(8,128)(2,1)S(1)} %get-tuple-element.267.dmid_ref, bf16[256,1536]{1,0:T(8,128)(2,1)S(1)} %get-tuple-element.279.hidden_ref, ...), custom_call_target="tpu_custom_call" | custom-call | flops 1000 | bytes 1000 | tf_op jit(solution)/shard_map/grad_od/pallas_call | solution.py:754
  181.0 2.0 collective-permute-start.35
  185.5 6.5 %back_two.2 = (bf16[16,48,640]{2,1,0:T(8,128)(2,1)S(1)}, bf16[16,48,640]{2,1,0:T(8,128)(2,1)S(1)}, f32[256,768]{1,0:T(8,128)S(1)}, f32[2,768]{1,0:T(2,128)S(1)}) custom-call(s32[8]{0:T(128)S(1)} %stack.68.me_ref.info_ref, f32[256,768]{1,0:T(8,128)S(1)} %get-tuple-element.243.x_ref, f32[8,768]{1,0:T(8,128)S(1)} %get-tuple-element.245.p_ref, ...), custom_call_target="tpu_custom_call" | custom-call | flops 1000 | bytes 1000 | tf_op jit(solution)/shard_map/back_two/pallas_call | solution.py:693
  192.0 8.9 %collective-permute-done.38 = bf16[8,48,1536]{2,1,0:T(8,128)(2,1)S(1)} collective-permute-done((bf16[8,48,1536]{2,1,0:T(8,128)(2,1)S(1)}, bf16[8,48,1536]{2,1,0:T(8,128)(2,1)S(1)}, u32[]{:S(2)}, u32[]{:S(2)}) %collective-permute-start.38) | collective-permute-done | bytes 1179680 | tf_op jit(solution)/shard_map/ppermute | solution.py:803
  201.0 2.4 add_convert_fusion.3
  204.6 8.6 %back_ffn.1 = (bf16[16,48,1536]{2,1,0:T(8,128)(2,1)S(1)}, bf16[16,48,1536]{2,1,0:T(8,128)(2,1)S(1)}, bf16[256,768]{1,0:T(8,128)(2,1)S(1)}, f32[256,768]{1,0:T(8,...) custom-call(s32[8]{0:T(128)S(1)} %stack.68.me_ref.info_ref, f32[256,768]{1,0:T(8,128)S(1)} %get-tuple-element.299.dx_ref, ...), custom_call_target="tpu_custom_call" | custom-call | flops 1000 | bytes 1000 | tf_op jit(solution)/shard_map/back_ffn/pallas_call | solution.py:465
  215.8 7.9 %collective-permute-done.42 = bf16[4,48,1536]{2,1,0:T(8,128)(2,1)S(1)} collective-permute-done((bf16[4,48,1536]{2,1,0:T(8,128)(2,1)S(1)}, bf16[4,48,1536]{2,1,0:T(8,128)(2,1)S(1)}, u32[]{:S(2)}, u32[]{:S(2)}) %collective-permute-start.42) | collective-permute-done | bytes 589856 | tf_op jit(solution)/shard_map/ppermute | solution.py:803
  227.3 3.9 %back_mid.3 = (bf16[256,768]{1,0:T(8,128)(2,1)S(1)}, f32[6,256,128]{2,1,0:T(8,128)S(1)}, f32[1,768]{1,0:T(1,128)S(1)}, f32[2,8,384]{2,1,0:T(8,128)S(1)}, f32[2,384]{1,0:T(2,128)S(1)}) custom-call(s32[8]{0:T(128)S(1)} %stack.68.me_ref.info_ref, bf16[256,768]{1,0:T(8,128)(2,1)S(1)} %get-tuple-element.311.dmid_ref, f32[8,768]{1,0:T(8,128)S(1)} %get-tuple-element.222.p_ref, ...), custom_call_target="tpu_custom_call" | custom-call | flops 1000 | bytes 1000 | tf_op jit(solution)/shard_map/back_mid/pallas_call | solution.py:541
  231.2 2.4 collective-permute-start.46
  235.1 2.6 collective-permute-start.49
  238.7 4.1 %grad_od.3 = (bf16[16,48,1536]{2,1,0:T(8,128)(2,1)S(1)}, bf16[16,48,1536]{2,1,0:T(8,128)(2,1)S(1)}) custom-call(s32[8]{0:T(128)S(1)} %stack.68.me_ref.info_ref, bf16[256,768]{1,0:T(8,128)(2,1)S(1)} %get-tuple-element.325.gated_ref, bf16[256,768]{1,0:T(8,128)(2,1)S(1)} %get-tuple-element.311.dmid_ref, bf16[256,1536]{1,0:T(8,128)(2,1)S(1)} %copy-done.4, ...), custom_call_target="tpu_custom_call" | custom-call | flops 1000 | bytes 1000 | tf_op jit(solution)/shard_map/grad_od/pallas_call | solution.py:754
  249.0 7.2 %back_two.3 = (bf16[16,48,640]{2,1,0:T(8,128)(2,1)S(1)}, bf16[16,48,640]{2,1,0:T(8,128)(2,1)S(1)}, f32[256,768]{1,0:T(8,128)}, f32[2,768]{1,0:T(2,128)}) custom-call(s32[8]{0:T(128)S(1)} %stack.68.me_ref.info_ref, bf16[256,768]{1,0:T(8,128)(2,1)S(1)} %copy-done, f32[8,768]{1,0:T(8,128)S(1)} %get-tuple-element.222.p_ref, ...), custom_call_target="tpu_custom_call" | custom-call | flops 1000 | bytes 1000 | tf_op jit(solution)/shard_map/back_two/pallas_call | solution.py:693
  256.2 6.7 %collective-permute-done.54 = bf16[1,48,1536]{2,1,0:T(8,128)(2,1)S(1)} collective-permute-done((bf16[1,48,1536]{2,1,0:T(8,128)(2,1)S(1)}, bf16[1,48,1536]{2,1,0:T(8,128)(2,1)S(1)}, u32[]{:S(2)}, u32[]{:S(2)}) %collective-permute-start.54) | collective-permute-done | bytes 147488 | tf_op jit(solution)/shard_map/ppermute | solution.py:803
  268.7 2.1 collective-permute-start.60
  272.3 6.4 %collective-permute-done.60 = bf16[2,48,640]{2,1,0:T(8,128)(2,1)S(1)} collective-permute-done((bf16[2,48,640]{2,1,0:T(8,128)(2,1)S(1)}, bf16[2,48,640]{2,1,0:T(8,128)(2,1)S(1)}, u32[]{:S(2)}, u32[]{:S(2)}) %collective-permute-start.60) | collective-permute-done | bytes 122912 | tf_op jit(solution)/shard_map/ppermute | solution.py:803
  278.6 5.8 %collective-permute-done.59 = bf16[2,48,1536]{2,1,0:T(8,128)(2,1)S(1)} collective-permute-done((bf16[2,48,1536]{2,1,0:T(8,128)(2,1)S(1)}, bf16[2,48,1536]{2,1,0:T(8,128)(2,1)S(1)}, u32[]{:S(2)}, u32[]{:S(2)}) %collective-permute-start.59) | collective-permute-done | bytes 294944 | tf_op jit(solution)/shard_map/ppermute | solution.py:803
  284.8 3.6 %collective-permute-start.63 = (bf16[4,48,1536]{2,1,0:T(8,128)(2,1)S(1)}, bf16[4,48,1536]{2,1,0:T(8,128)(2,1)S(1)}, u32[]{:S(2)}, u32[]{:S(2)}) collective-permute-start(bf16[4,48,1536]{2,1,0:T(8,128)(2,1)S(1)} %get-tuple-element.365), channel_id=1, source_target_pairs={{0,2},{1,5},{2,0},{3,7},{4,6},{5,1},{6,4},{7,3},{8,10},{9,13},{10,... | collective-permute-start | bytes 1769480 | tf_op jit(solution)/shard_map/ppermute | solution.py:803
  290.5 3.0 collective-permute-start.62
  293.7 2.3 collective-permute-start.70
  296.1 4.8 %collective-permute-done.69 = bf16[1,48,640]{2,1,0:T(8,128)(2,1)S(1)} collective-permute-done((bf16[1,48,640]{2,1,0:T(8,128)(2,1)S(1)}, bf16[1,48,640]{2,1,0:T(8,128)(2,1)S(1)}, u32[]{:S(2)}, u32[]{:S(2)}) %collective-permute-start.69) | collective-permute-done | bytes 61472 | tf_op jit(solution)/shard_map/ppermute | solution.py:803
  307.1 6.2 %collective-permute-done.65 = bf16[2,48,1536]{2,1,0:T(8,128)(2,1)S(1)} collective-permute-done((bf16[2,48,1536]{2,1,0:T(8,128)(2,1)S(1)}, bf16[2,48,1536]{2,1,0:T(8,128)(2,1)S(1)}, u32[]{:S(2)}, u32[]{:S(2)}) %collective-permute-start.65) | collective-permute-done | bytes 294944 | tf_op jit(solution)/shard_map/ppermute | solution.py:803
  313.3 3.0 collective-permute-done.64
  316.4 2.1 collective-permute-start.67
  318.5 2.6 collective-permute-done.66
  321.1 2.4 collective-permute-done.67
  (242 shorter events, 78.0 us)
Async XLA Ops:
  7.1 12.0 %collective-permute-start.1 = (bf16[1,48,2304]{2,1,0:T(8,128)(2,1)S(1)}, bf16[1,48,2304]{2,1,0:T(8,128)(2,1)S(1)}, u32[]{:S(2)}, u32[]{:S(2)}) collective-permute-start(bf16[1,48,2304]{2,1,0:T(8,128)(2,1)S(1)} %maximum_bitcast_fusion), channel_id=1, source_target_pairs={{0,8},{1,17},{2,10},{3,19},{4,12},{5,21},{6,14},{7,23},{8,0},{9,25... | collective-permute-start | bytes 663560 | tf_op jit(solution)/shard_map/ppermute | solution.py:803
  10.1 9.0 %collective-permute-start.4 = (bf16[1,48,2304]{2,1,0:T(8,128)(2,1)S(1)}, bf16[1,48,2304]{2,1,0:T(8,128)(2,1)S(1)}, u32[]{:S(2)}, u32[]{:S(2)}) collective-permute-start(bf16[1,48,2304]{2,1,0:T(8,128)(2,1)S(1)} %maximum_bitcast_fusion.1), channel_id=1, source_target_pairs={{0,2},{1,5},{2,0},{3,7},{4,6},{5,1},{6,4},{7,3},{8,10},{9,13},{10,... | collective-permute-start | bytes 663560 | tf_op jit(solution)/shard_map/ppermute | solution.py:803
  19.2 18.4 %collective-permute-start.6 = (bf16[2,48,2304]{2,1,0:T(8,128)(2,1)S(1)}, bf16[2,48,2304]{2,1,0:T(8,128)(2,1)S(1)}, u32[]{:S(2)}, u32[]{:S(2)}) collective-permute-start(bf16[2,48,2304]{2,1,0:T(8,128)(2,1)S(1)} %pad_maximum_fusion.10), channel_id=1, source_target_pairs={{0,16},{1,9},{2,18},{3,11},{4,20},{5,13},{6,22},{7,15},{8,24},{9,1... | collective-permute-start | bytes 1327112 | tf_op jit(solution)/shard_map/ppermute | solution.py:803
  21.6 16.0 %collective-permute-start.5 = (bf16[2,48,1408]{2,1,0:T(8,128)(2,1)S(1)}, bf16[2,48,1408]{2,1,0:T(8,128)(2,1)S(1)}, u32[]{:S(2)}, u32[]{:S(2)}) collective-permute-start(bf16[2,48,1408]{2,1,0:T(8,128)(2,1)S(1)} %pad_maximum_fusion.12), channel_id=1, source_target_pairs={{0,16},{1,9},{2,18},{3,11},{4,20},{5,13},{6,22},{7,15},{8,24},{9,1... | collective-permute-start | bytes 811016 | tf_op jit(solution)/shard_map/ppermute | solution.py:803
  37.8 11.8 %collective-permute-start.7 = (bf16[4,48,1408]{2,1,0:T(8,128)(2,1)S(1)}, bf16[4,48,1408]{2,1,0:T(8,128)(2,1)S(1)}, u32[]{:S(2)}, u32[]{:S(2)}) collective-permute-start(bf16[4,48,1408]{2,1,0:T(8,128)(2,1)S(1)} %pad_maximum_fusion.8), channel_id=1, source_target_pairs={{0,2},{1,5},{2,0},{3,7},{4,6},{5,1},{6,4},{7,3},{8,10},{9,13},{10,... | collective-permute-start | bytes 1622024 | tf_op jit(solution)/shard_map/ppermute | solution.py:803
  41.4 8.2 %collective-permute-start.8 = (bf16[2,48,1408]{2,1,0:T(8,128)(2,1)S(1)}, bf16[2,48,1408]{2,1,0:T(8,128)(2,1)S(1)}, u32[]{:S(2)}, u32[]{:S(2)}) collective-permute-start(bf16[2,48,1408]{2,1,0:T(8,128)(2,1)S(1)} %pad_maximum_fusion.13), channel_id=1, source_target_pairs={{0,8},{1,17},{2,10},{3,19},{4,12},{5,21},{6,14},{7,23},{8,0},{9,25... | collective-permute-start | bytes 811016 | tf_op jit(solution)/shard_map/ppermute | solution.py:803
  41.9 27.3 %collective-permute-start.11 = (bf16[4,48,2304]{2,1,0:T(8,128)(2,1)S(1)}, bf16[4,48,2304]{2,1,0:T(8,128)(2,1)S(1)}, u32[]{:S(2)}, u32[]{:S(2)}) collective-permute-start(bf16[4,48,2304]{2,1,0:T(8,128)(2,1)S(1)} %pad_maximum_fusion.4), channel_id=1, source_target_pairs={{0,2},{1,5},{2,0},{3,7},{4,6},{5,1},{6,4},{7,3},{8,10},{9,13},{10,... | collective-permute-start | bytes 2654216 | tf_op jit(solution)/shard_map/ppermute | solution.py:803
  42.5 26.8 %collective-permute-start.12 = (bf16[2,48,2304]{2,1,0:T(8,128)(2,1)S(1)}, bf16[2,48,2304]{2,1,0:T(8,128)(2,1)S(1)}, u32[]{:S(2)}, u32[]{:S(2)}) collective-permute-start(bf16[2,48,2304]{2,1,0:T(8,128)(2,1)S(1)} %pad_maximum_fusion.11), channel_id=1, source_target_pairs={{0,8},{1,17},{2,10},{3,19},{4,12},{5,21},{6,14},{7,23},{8,0},{9,25... | collective-permute-start | bytes 1327112 | tf_op jit(solution)/shard_map/ppermute | solution.py:803
  49.8 21.9 %collective-permute-start.9 = (bf16[8,48,1408]{2,1,0:T(8,128)(2,1)S(1)}, bf16[8,48,1408]{2,1,0:T(8,128)(2,1)S(1)}, u32[]{:S(2)}, u32[]{:S(2)}) collective-permute-start(bf16[8,48,1408]{2,1,0:T(8,128)(2,1)S(1)} %pad_maximum_fusion.2.refs_0_), channel_id=1, source_target_pairs={{0,4},{1,3},{2,6},{3,1},{4,0},{5,7},{6,2},{7,5},{8,12},{9,11},{10,... | collective-permute-start | bytes 3244040 | tf_op jit(solution)/shard_map/ppermute | solution.py:803
  51.3 20.3 %collective-permute-start.10 = (bf16[4,48,1408]{2,1,0:T(8,128)(2,1)S(1)}, bf16[4,48,1408]{2,1,0:T(8,128)(2,1)S(1)}, u32[]{:S(2)}, u32[]{:S(2)}) collective-permute-start(bf16[4,48,1408]{2,1,0:T(8,128)(2,1)S(1)} %pad_maximum_fusion.9), channel_id=1, source_target_pairs={{0,16},{1,9},{2,18},{3,11},{4,20},{5,13},{6,22},{7,15},{8,24},{9,1... | collective-permute-start | bytes 1622024 | tf_op jit(solution)/shard_map/ppermute | solution.py:803
  72.4 25.4 %collective-permute-start.15 = (bf16[8,48,2304]{2,1,0:T(8,128)(2,1)}, bf16[8,48,2304]{2,1,0:T(8,128)(2,1)}, u32[]{:S(2)}, u32[]{:S(2)}) collective-permute-start(bf16[8,48,2304]{2,1,0:T(8,128)(2,1)} %pad_maximum_fusion.refs_0_), channel_id=1, source_target_pairs={{0,4},{1,3},{2,6},{3,1},{4,0},{5,7},{6,2},{7,5},{8,12},{9,11},{10,... | collective-permute-start | bytes 5308424 | tf_op jit(solution)/shard_map/ppermute | solution.py:803
  74.0 23.7 %collective-permute-start.16 = (bf16[4,48,2304]{2,1,0:T(8,128)(2,1)}, bf16[4,48,2304]{2,1,0:T(8,128)(2,1)}, u32[]{:S(2)}, u32[]{:S(2)}) collective-permute-start(bf16[4,48,2304]{2,1,0:T(8,128)(2,1)} %pad_maximum_fusion.5), channel_id=1, source_target_pairs={{0,16},{1,9},{2,18},{3,11},{4,20},{5,13},{6,22},{7,15},{8,24},{9,1... | collective-permute-start | bytes 2654216 | tf_op jit(solution)/shard_map/ppermute | solution.py:803
  78.9 34.6 %collective-permute-start.23 = (bf16[8,48,2304]{2,1,0:T(8,128)(2,1)}, bf16[8,48,2304]{2,1,0:T(8,128)(2,1)S(1)}, u32[]{:S(2)}, u32[]{:S(2)}) collective-permute-start(bf16[8,48,2304]{2,1,0:T(8,128)(2,1)} %pad_maximum_fusion.refs_0_), channel_id=1, source_target_pairs={{0,1},{1,0},{2,3},{3,2},{4,5},{5,4},{6,7},{7,6},{8,9},{9,8},{10,11... | collective-permute-start | bytes 5308424 | tf_op jit(solution)/shard_map/ppermute | solution.py:803
  97.8 23.8 %collective-permute-start.22 = (bf16[8,48,2304]{2,1,0:T(8,128)(2,1)}, bf16[8,48,2304]{2,1,0:T(8,128)(2,1)S(1)}, u32[]{:S(2)}, u32[]{:S(2)}) collective-permute-start(bf16[8,48,2304]{2,1,0:T(8,128)(2,1)} %collective-permute-done.15.refs_2_), channel_id=1, source_target_pairs={{0,1},{1,0},{2,3},{3,2},{4,5},{5,4},{6,7},{7,6},{8,9},{9,8},{10,11... | collective-permute-start | bytes 5308424 | tf_op jit(solution)/shard_map/ppermute | solution.py:803
  106.3 15.2 %collective-permute-start.21 = (bf16[8,48,1408]{2,1,0:T(8,128)(2,1)S(1)}, bf16[8,48,1408]{2,1,0:T(8,128)(2,1)S(1)}, u32[]{:S(2)}, u32[]{:S(2)}) collective-permute-start(bf16[8,48,1408]{2,1,0:T(8,128)(2,1)S(1)} %pad_maximum_fusion.3.refs_0_), channel_id=1, source_target_pairs={{0,4},{1,3},{2,6},{3,1},{4,0},{5,7},{6,2},{7,5},{8,12},{9,11},{10,... | collective-permute-start | bytes 3244040 | tf_op jit(solution)/shard_map/ppermute | solution.py:803
  121.6 22.5 %collective-permute-start.26 = (bf16[8,48,2304]{2,1,0:T(8,128)(2,1)S(1)}, bf16[8,48,2304]{2,1,0:T(8,128)(2,1)S(1)}, u32[]{:S(2)}, u32[]{:S(2)}) collective-permute-start(bf16[8,48,2304]{2,1,0:T(8,128)(2,1)S(1)} %pad_maximum_fusion.1.refs_0_), channel_id=1, source_target_pairs={{0,4},{1,3},{2,6},{3,1},{4,0},{5,7},{6,2},{7,5},{8,12},{9,11},{10,... | collective-permute-start | bytes 5308424 | tf_op jit(solution)/shard_map/ppermute | solution.py:803
  122.8 35.4 %collective-permute-start.32 = (bf16[8,48,2304]{2,1,0:T(8,128)(2,1)S(1)}, bf16[8,48,2304]{2,1,0:T(8,128)(2,1)S(1)}, u32[]{:S(2)}, u32[]{:S(2)}) collective-permute-start(bf16[8,48,2304]{2,1,0:T(8,128)(2,1)S(1)} %pad_maximum_fusion.1.refs_0_), channel_id=1, source_target_pairs={{0,1},{1,0},{2,3},{3,2},{4,5},{5,4},{6,7},{7,6},{8,9},{9,8},{10,11... | collective-permute-start | bytes 5308424 | tf_op jit(solution)/shard_map/ppermute | solution.py:803
  144.1 14.2 %collective-permute-start.31 = (bf16[8,48,2304]{2,1,0:T(8,128)(2,1)S(1)}, bf16[8,48,2304]{2,1,0:T(8,128)(2,1)S(1)}, u32[]{:S(2)}, u32[]{:S(2)}) collective-permute-start(bf16[8,48,2304]{2,1,0:T(8,128)(2,1)S(1)} %collective-permute-done.26.refs_2_), channel_id=1, source_target_pairs={{0,1},{1,0},{2,3},{3,2},{4,5},{5,4},{6,7},{7,6},{8,9},{9,8},{10,11... | collective-permute-start | bytes 5308424 | tf_op jit(solution)/shard_map/ppermute | solution.py:803
  147.8 7.2 %collective-permute-start.30 = (f32[2,4,384]{2,1,0:T(4,128)S(1)}, f32[2,4,384]{2,1,0:T(4,128)S(1)}, u32[]{:S(2)}, u32[]{:S(2)}) collective-permute-start(f32[2,4,384]{2,1,0:T(4,128)S(1)} %pad_maximum_fusion.15), channel_id=1, source_target_pairs={{0,6},{1,7},{2,4},{3,5},{4,2},{5,3},{6,0},{7,1},{8,14},{9,15},{10,... | collective-permute-start | bytes 36872 | tf_op jit(solution)/shard_map/ppermute | solution.py:803
  179.3 21.6 %collective-permute-start.39 = (bf16[16,48,1536]{2,1,0:T(8,128)(2,1)S(1)}, bf16[16,48,1536]{2,1,0:T(8,128)(2,1)}, u32[]{:S(2)}, u32[]{:S(2)}) collective-permute-start(bf16[16,48,1536]{2,1,0:T(8,128)(2,1)S(1)} %get-tuple-element.293), channel_id=1, source_target_pairs={{0,1},{1,0},{2,3},{3,2},{4,5},{5,4},{6,7},{7,6},{8,9},{9,8},{10,11... | collective-permute-start | bytes 7077896 | tf_op jit(solution)/shard_map/ppermute | solution.py:803
  184.7 16.3 %collective-permute-start.38 = (bf16[8,48,1536]{2,1,0:T(8,128)(2,1)S(1)}, bf16[8,48,1536]{2,1,0:T(8,128)(2,1)S(1)}, u32[]{:S(2)}, u32[]{:S(2)}) collective-permute-start(bf16[8,48,1536]{2,1,0:T(8,128)(2,1)S(1)} %get-tuple-element.286), channel_id=1, source_target_pairs={{0,4},{1,3},{2,6},{3,1},{4,0},{5,7},{6,2},{7,5},{8,12},{9,11},{10,... | collective-permute-start | bytes 3538952 | tf_op jit(solution)/shard_map/ppermute | solution.py:803
  203.7 20.0 %collective-permute-start.40 = (bf16[8,48,1536]{2,1,0:T(8,128)(2,1)S(1)}, bf16[8,48,1536]{2,1,0:T(8,128)(2,1)S(1)}, u32[]{:S(2)}, u32[]{:S(2)}) collective-permute-start(bf16[8,48,1536]{2,1,0:T(8,128)(2,1)S(1)} %get-tuple-element.298), channel_id=1, source_target_pairs={{0,4},{1,3},{2,6},{3,1},{4,0},{5,7},{6,2},{7,5},{8,12},{9,11},{10,... | collective-permute-start | bytes 3538952 | tf_op jit(solution)/shard_map/ppermute | solution.py:803
  204.6 11.2 %collective-permute-start.41 = (bf16[16,48,640]{2,1,0:T(8,128)(2,1)S(1)}, bf16[16,48,640]{2,1,0:T(8,128)(2,1)S(1)}, u32[]{:S(2)}, u32[]{:S(2)}) collective-permute-start(bf16[16,48,640]{2,1,0:T(8,128)(2,1)S(1)} %get-tuple-element.303), channel_id=1, source_target_pairs={{0,1},{1,0},{2,3},{3,2},{4,5},{5,4},{6,7},{7,6},{8,9},{9,8},{10,11... | collective-permute-start | bytes 2949128 | tf_op jit(solution)/shard_map/ppermute | solution.py:803
  213.2 21.9 %collective-permute-start.43 = (bf16[16,48,1536]{2,1,0:T(8,128)(2,1)S(1)}, bf16[16,48,1536]{2,1,0:T(8,128)(2,1)S(1)}, u32[]{:S(2)}, u32[]{:S(2)}) collective-permute-start(bf16[16,48,1536]{2,1,0:T(8,128)(2,1)S(1)} %get-tuple-element.317), channel_id=1, source_target_pairs={{0,1},{1,0},{2,3},{3,2},{4,5},{5,4},{6,7},{7,6},{8,9},{9,8},{10,11... | collective-permute-start | bytes 7077896 | tf_op jit(solution)/shard_map/ppermute | solution.py:803
  213.8 9.9 %collective-permute-start.42 = (bf16[4,48,1536]{2,1,0:T(8,128)(2,1)S(1)}, bf16[4,48,1536]{2,1,0:T(8,128)(2,1)S(1)}, u32[]{:S(2)}, u32[]{:S(2)}) collective-permute-start(bf16[4,48,1536]{2,1,0:T(8,128)(2,1)S(1)} %get-tuple-element.304), channel_id=1, source_target_pairs={{0,2},{1,5},{2,0},{3,7},{4,6},{5,1},{6,4},{7,3},{8,10},{9,13},{10,... | collective-permute-start | bytes 1769480 | tf_op jit(solution)/shard_map/ppermute | solution.py:803
  224.1 11.0 %collective-permute-start.45 = (bf16[2,48,1536]{2,1,0:T(8,128)(2,1)S(1)}, bf16[2,48,1536]{2,1,0:T(8,128)(2,1)S(1)}, u32[]{:S(2)}, u32[]{:S(2)}) collective-permute-start(bf16[2,48,1536]{2,1,0:T(8,128)(2,1)S(1)} %get-tuple-element.318), channel_id=1, source_target_pairs={{0,16},{1,9},{2,18},{3,11},{4,20},{5,13},{6,22},{7,15},{8,24},{9,1... | collective-permute-start | bytes 884744 | tf_op jit(solution)/shard_map/ppermute | solution.py:803
  224.9 10.2 %collective-permute-start.44 = (bf16[8,48,640]{2,1,0:T(8,128)(2,1)S(1)}, bf16[8,48,640]{2,1,0:T(8,128)(2,1)S(1)}, u32[]{:S(2)}, u32[]{:S(2)}) collective-permute-start(bf16[8,48,640]{2,1,0:T(8,128)(2,1)S(1)} %get-tuple-element.310), channel_id=1, source_target_pairs={{0,4},{1,3},{2,6},{3,1},{4,0},{5,7},{6,2},{7,5},{8,12},{9,11},{10,... | collective-permute-start | bytes 1474568 | tf_op jit(solution)/shard_map/ppermute | solution.py:803
  235.1 8.7 %collective-permute-start.49 = (f32[2,2,384]{2,1,0:T(2,128)S(1)}, f32[2,2,384]{2,1,0:T(2,128)S(1)}, u32[]{:S(2)}, u32[]{:S(2)}) collective-permute-start(f32[2,2,384]{2,1,0:T(2,128)S(1)} %pad_maximum_fusion.17), channel_id=1, source_target_pairs={{0,6},{1,7},{2,4},{3,5},{4,2},{5,3},{6,0},{7,1},{8,14},{9,15},{10,... | collective-permute-start | bytes 18440 | tf_op jit(solution)/shard_map/ppermute | solution.py:803
  242.7 22.6 %collective-permute-start.55 = (bf16[16,48,1536]{2,1,0:T(8,128)(2,1)S(1)}, bf16[16,48,1536]{2,1,0:T(8,128)(2,1)S(1)}, u32[]{:S(2)}, u32[]{:S(2)}) collective-permute-start(bf16[16,48,1536]{2,1,0:T(8,128)(2,1)S(1)} %get-tuple-element.351), channel_id=1, source_target_pairs={{0,1},{1,0},{2,3},{3,2},{4,5},{5,4},{6,7},{7,6},{8,9},{9,8},{10,11... | collective-permute-start | bytes 7077896 | tf_op jit(solution)/shard_map/ppermute | solution.py:803
  243.8 21.5 %collective-permute-start.51 = (bf16[8,48,1536]{2,1,0:T(8,128)(2,1)S(1)}, bf16[8,48,1536]{2,1,0:T(8,128)(2,1)S(1)}, u32[]{:S(2)}, u32[]{:S(2)}) collective-permute-start(bf16[8,48,1536]{2,1,0:T(8,128)(2,1)S(1)} %get-tuple-element.333), channel_id=1, source_target_pairs={{0,4},{1,3},{2,6},{3,1},{4,0},{5,7},{6,2},{7,5},{8,12},{9,11},{10,... | collective-permute-start | bytes 3538952 | tf_op jit(solution)/shard_map/ppermute | solution.py:803
  245.0 20.3 %collective-permute-start.52 = (bf16[4,48,1536]{2,1,0:T(8,128)(2,1)S(1)}, bf16[4,48,1536]{2,1,0:T(8,128)(2,1)S(1)}, u32[]{:S(2)}, u32[]{:S(2)}) collective-permute-start(bf16[4,48,1536]{2,1,0:T(8,128)(2,1)S(1)} %get-tuple-element.348), channel_id=1, source_target_pairs={{0,16},{1,9},{2,18},{3,11},{4,20},{5,13},{6,22},{7,15},{8,24},{9,1... | collective-permute-start | bytes 1769480 | tf_op jit(solution)/shard_map/ppermute | solution.py:803
  246.4 17.0 %collective-permute-start.53 = (bf16[4,48,640]{2,1,0:T(8,128)(2,1)S(1)}, bf16[4,48,640]{2,1,0:T(8,128)(2,1)S(1)}, u32[]{:S(2)}, u32[]{:S(2)}) collective-permute-start(bf16[4,48,640]{2,1,0:T(8,128)(2,1)S(1)} %get-tuple-element.349), channel_id=1, source_target_pairs={{0,2},{1,5},{2,0},{3,7},{4,6},{5,1},{6,4},{7,3},{8,10},{9,13},{10,... | collective-permute-start | bytes 737288 | tf_op jit(solution)/shard_map/ppermute | solution.py:803
  248.0 15.0 %collective-permute-start.54 = (bf16[1,48,1536]{2,1,0:T(8,128)(2,1)S(1)}, bf16[1,48,1536]{2,1,0:T(8,128)(2,1)S(1)}, u32[]{:S(2)}, u32[]{:S(2)}) collective-permute-start(bf16[1,48,1536]{2,1,0:T(8,128)(2,1)S(1)} %add_convert_fusion.39), channel_id=1, source_target_pairs={{0,8},{1,17},{2,10},{3,19},{4,12},{5,21},{6,14},{7,23},{8,0},{9,25... | collective-permute-start | bytes 442376 | tf_op jit(solution)/shard_map/ppermute | solution.py:803
  266.6 17.8 %collective-permute-start.58 = (bf16[8,48,1536]{2,1,0:T(8,128)(2,1)S(1)}, bf16[8,48,1536]{2,1,0:T(8,128)(2,1)S(1)}, u32[]{:S(2)}, u32[]{:S(2)}) collective-permute-start(bf16[8,48,1536]{2,1,0:T(8,128)(2,1)S(1)} %get-tuple-element.356), channel_id=1, source_target_pairs={{0,4},{1,3},{2,6},{3,1},{4,0},{5,7},{6,2},{7,5},{8,12},{9,11},{10,... | collective-permute-start | bytes 3538952 | tf_op jit(solution)/shard_map/ppermute | solution.py:803
  267.6 16.8 %collective-permute-start.59 = (bf16[2,48,1536]{2,1,0:T(8,128)(2,1)S(1)}, bf16[2,48,1536]{2,1,0:T(8,128)(2,1)S(1)}, u32[]{:S(2)}, u32[]{:S(2)}) collective-permute-start(bf16[2,48,1536]{2,1,0:T(8,128)(2,1)S(1)} %get-tuple-element.360), channel_id=1, source_target_pairs={{0,8},{1,17},{2,10},{3,19},{4,12},{5,21},{6,14},{7,23},{8,0},{9,25... | collective-permute-start | bytes 884744 | tf_op jit(solution)/shard_map/ppermute | solution.py:803
  268.7 10.0 %collective-permute-start.60 = (bf16[2,48,640]{2,1,0:T(8,128)(2,1)S(1)}, bf16[2,48,640]{2,1,0:T(8,128)(2,1)S(1)}, u32[]{:S(2)}, u32[]{:S(2)}) collective-permute-start(bf16[2,48,640]{2,1,0:T(8,128)(2,1)S(1)} %get-tuple-element.361), channel_id=1, source_target_pairs={{0,16},{1,9},{2,18},{3,11},{4,20},{5,13},{6,22},{7,15},{8,24},{9,1... | collective-permute-start | bytes 368648 | tf_op jit(solution)/shard_map/ppermute | solution.py:803
  271.0 22.5 %collective-permute-start.56 = (bf16[8,48,640]{2,1,0:T(8,128)(2,1)S(1)}, bf16[8,48,640]{2,1,0:T(8,128)(2,1)S(1)}, u32[]{:S(2)}, u32[]{:S(2)}) collective-permute-start(bf16[8,48,640]{2,1,0:T(8,128)(2,1)S(1)} %get-tuple-element.358), channel_id=1, source_target_pairs={{0,4},{1,3},{2,6},{3,1},{4,0},{5,7},{6,2},{7,5},{8,12},{9,11},{10,... | collective-permute-start | bytes 1474568 | tf_op jit(solution)/shard_map/ppermute | solution.py:803
  271.2 19.2 %collective-permute-start.57 = (bf16[4,48,1536]{2,1,0:T(8,128)(2,1)S(1)}, bf16[4,48,1536]{2,1,0:T(8,128)(2,1)S(1)}, u32[]{:S(2)}, u32[]{:S(2)}) collective-permute-start(bf16[4,48,1536]{2,1,0:T(8,128)(2,1)S(1)} %get-tuple-element.359), channel_id=1, source_target_pairs={{0,16},{1,9},{2,18},{3,11},{4,20},{5,13},{6,22},{7,15},{8,24},{9,1... | collective-permute-start | bytes 1769480 | tf_op jit(solution)/shard_map/ppermute | solution.py:803
  284.8 17.8 %collective-permute-start.63 = (bf16[4,48,1536]{2,1,0:T(8,128)(2,1)S(1)}, bf16[4,48,1536]{2,1,0:T(8,128)(2,1)S(1)}, u32[]{:S(2)}, u32[]{:S(2)}) collective-permute-start(bf16[4,48,1536]{2,1,0:T(8,128)(2,1)S(1)} %get-tuple-element.365), channel_id=1, source_target_pairs={{0,2},{1,5},{2,0},{3,7},{4,6},{5,1},{6,4},{7,3},{8,10},{9,13},{10,... | collective-permute-start | bytes 1769480 | tf_op jit(solution)/shard_map/ppermute | solution.py:803
  290.5 13.4 %collective-permute-start.62 = (bf16[2,48,1536]{2,1,0:T(8,128)(2,1)S(1)}, bf16[2,48,1536]{2,1,0:T(8,128)(2,1)S(1)}, u32[]{:S(2)}, u32[]{:S(2)}) collective-permute-start(bf16[2,48,1536]{2,1,0:T(8,128)(2,1)S(1)} %get-tuple-element.367), channel_id=1, source_target_pairs={{0,8},{1,17},{2,10},{3,19},{4,12},{5,21},{6,14},{7,23},{8,0},{9,25... | collective-permute-start | bytes 884744 | tf_op jit(solution)/shard_map/ppermute | solution.py:803
  293.5 7.4 %collective-permute-start.69 = (bf16[1,48,640]{2,1,0:T(8,128)(2,1)S(1)}, bf16[1,48,640]{2,1,0:T(8,128)(2,1)S(1)}, u32[]{:S(2)}, u32[]{:S(2)}) collective-permute-start(bf16[1,48,640]{2,1,0:T(8,128)(2,1)S(1)} %add_convert_fusion.47), channel_id=1, source_target_pairs={{0,8},{1,17},{2,10},{3,19},{4,12},{5,21},{6,14},{7,23},{8,0},{9,25... | collective-permute-start | bytes 184328 | tf_op jit(solution)/shard_map/ppermute | solution.py:803
  293.7 7.3 %collective-permute-start.70 = (bf16[1,48,1536]{2,1,0:T(8,128)(2,1)S(1)}, bf16[1,48,1536]{2,1,0:T(8,128)(2,1)S(1)}, u32[]{:S(2)}, u32[]{:S(2)}) collective-permute-start(bf16[1,48,1536]{2,1,0:T(8,128)(2,1)S(1)} %add_convert_fusion.38), channel_id=1, source_target_pairs={{0,2},{1,5},{2,0},{3,7},{4,6},{5,1},{6,4},{7,3},{8,10},{9,13},{10,... | collective-permute-start | bytes 442376 | tf_op jit(solution)/shard_map/ppermute | solution.py:803
  296.0 9.1 %collective-permute-start.61 = (bf16[4,48,640]{2,1,0:T(8,128)(2,1)S(1)}, bf16[4,48,640]{2,1,0:T(8,128)(2,1)S(1)}, u32[]{:S(2)}, u32[]{:S(2)}) collective-permute-start(bf16[4,48,640]{2,1,0:T(8,128)(2,1)S(1)} %get-tuple-element.369), channel_id=1, source_target_pairs={{0,2},{1,5},{2,0},{3,7},{4,6},{5,1},{6,4},{7,3},{8,10},{9,13},{10,... | collective-permute-start | bytes 737288 | tf_op jit(solution)/shard_map/ppermute | solution.py:803
  301.2 22.6 %collective-permute-start.72 = (f32[24,2944]{1,0:T(8,128)S(1)}, f32[24,2944]{1,0:T(8,128)S(1)}, u32[]{:S(2)}, u32[]{:S(2)}) collective-permute-start(f32[24,2944]{1,0:T(8,128)S(1)} %get-tuple-element.428), channel_id=1, source_target_pairs={{0,1},{1,0},{2,3},{3,2},{4,5},{5,4},{6,7},{7,6},{8,9},{9,8},{10,11... | collective-permute-start | bytes 847880 | tf_op jit(solution)/shard_map/ppermute | solution.py:803
  302.7 10.5 %collective-permute-start.65 = (bf16[2,48,1536]{2,1,0:T(8,128)(2,1)S(1)}, bf16[2,48,1536]{2,1,0:T(8,128)(2,1)S(1)}, u32[]{:S(2)}, u32[]{:S(2)}) collective-permute-start(bf16[2,48,1536]{2,1,0:T(8,128)(2,1)S(1)} %get-tuple-element.371), channel_id=1, source_target_pairs={{0,16},{1,9},{2,18},{3,11},{4,20},{5,13},{6,22},{7,15},{8,24},{9,1... | collective-permute-start | bytes 884744 | tf_op jit(solution)/shard_map/ppermute | solution.py:803
  303.9 12.4 %collective-permute-start.68 = (bf16[1,48,1536]{2,1,0:T(8,128)(2,1)S(1)}, bf16[1,48,1536]{2,1,0:T(8,128)(2,1)S(1)}, u32[]{:S(2)}, u32[]{:S(2)}) collective-permute-start(bf16[1,48,1536]{2,1,0:T(8,128)(2,1)S(1)} %add_convert_fusion.37), channel_id=1, source_target_pairs={{0,2},{1,5},{2,0},{3,7},{4,6},{5,1},{6,4},{7,3},{8,10},{9,13},{10,... | collective-permute-start | bytes 442376 | tf_op jit(solution)/shard_map/ppermute | solution.py:803
  305.2 11.0 %collective-permute-start.64 = (bf16[2,48,640]{2,1,0:T(8,128)(2,1)S(1)}, bf16[2,48,640]{2,1,0:T(8,128)(2,1)S(1)}, u32[]{:S(2)}, u32[]{:S(2)}) collective-permute-start(bf16[2,48,640]{2,1,0:T(8,128)(2,1)S(1)} %get-tuple-element.375), channel_id=1, source_target_pairs={{0,16},{1,9},{2,18},{3,11},{4,20},{5,13},{6,22},{7,15},{8,24},{9,1... | collective-permute-start | bytes 368648 | tf_op jit(solution)/shard_map/ppermute | solution.py:803
  316.4 7.1 %collective-permute-start.67 = (bf16[1,48,1536]{2,1,0:T(8,128)(2,1)S(1)}, bf16[1,48,1536]{2,1,0:T(8,128)(2,1)S(1)}, u32[]{:S(2)}, u32[]{:S(2)}) collective-permute-start(bf16[1,48,1536]{2,1,0:T(8,128)(2,1)S(1)} %add_convert_fusion.36), channel_id=1, source_target_pairs={{0,8},{1,17},{2,10},{3,19},{4,12},{5,21},{6,14},{7,23},{8,0},{9,25... | collective-permute-start | bytes 442376 | tf_op jit(solution)/shard_map/ppermute | solution.py:803
  (39 other events, 202.1 us)

commit v7 on v6

--- a/solution.py
+++ b/solution.py
@@ -407,7 +407,7 @@
     lifted = lifted_ref[...]
     load_wait(up_pairs, sems.at[0])
     load_wait(down_pairs, sems.at[1])
-    step = width // 2
+    step = width
     for k in range(inner // step):
         cols = slice(k * step, (k + 1) * step)
         more = slice(inner + k * step, inner + (k + 1) * step)
@@ -727,7 +727,7 @@
 
 
 def products(left, right_ref, grad_ref, size, source=0, target=0):
-    step = HALVES["out"]
+    step = min(size, 2 * HALVES["out"])
     for k in range(0, size, step):
         right = right_ref[:, source + k : source + k + step]
         grad_ref[:, target + k : target + k + step] = row_product(left, right).astype(BF16)

time: 332 us -> 331 us (level)
  transfers between devices with their start and end apart: 73 -> 73, of which waited for: 29 -> 30; matrix products, arithmetic and copies ran while one was open for 4% -> 4% of each run, Pallas kernels for 17% -> 17%
where the time goes in v7:
time: 331 us; the launch traced here: 327 us
  waiting for transfers between devices  150 us (45%)
  starting transfers between devices  75.9 us (23%)
  Pallas kernels  73.2 us (22%)
  other arithmetic  13.9 us (4%)
  local copies, waits for them, and re-layouts  10.2 us (3%)
  between operations  4.51 us (1%)
    ppermute x73, waiting for transfers between devices, swap(): return lax.ppermute(x, ALL, [(i, i ^ bits[i % 2]) for i in range(count)])  150 us
    ppermute x73, starting transfers between devices, swap(): return lax.ppermute(x, ALL, [(i, i ^ bits[i % 2]) for i in range(count)])  75.9 us
    pallas_call x2, Pallas kernels, back_two(): pl.pallas_call(functools.partial(back_two_kernel, plan, len(weights), rel...  13.3 us
    pallas_call x1, Pallas kernels, turn(): pl.pallas_call(functools.partial(turn_kernel, plan, len(weights), rels),...  11 us
    pallas_call x2, Pallas kernels, front(): pl.pallas_call(functools.partial(front_kernel, plan, len(weights)), out_s...  10.1 us
    pallas_call x1, Pallas kernels, back_ffn(): pl.pallas_call(functools.partial(back_ffn_kernel, plan, len(weights), rel...  8.17 us
    pallas_call x2, Pallas kernels, grad_od(): pl.pallas_call(functools.partial(grad_od_kernel, rels), out_shape=(shape,...  8.14 us
    convert_element_type x24, other arithmetic, joined(): (self.held[part].astype(F32) + self.got[part].astype(F32)).astype(BF16)  7.57 us
  transfers between devices with their start and end apart: 73, of which 30 were waited for; matrix products, arithmetic and copies ran while one was open for 4% of the time, Pallas kernels for 17%

profile of v7, /device:TPU:0, one launch (start us, length us, event | category | flops | bytes accessed | tf_op | source)
XLA Modules:
  0.0 327.4 jit_solution(9265145232203114110)
XLA Ops:
  7.1 3.0 collective-permute-start.1
  12.3 5.2 %collective-permute-done.3 = bf16[1,48,1408]{2,1,0:T(8,128)(2,1)S(1)} collective-permute-done((bf16[1,48,1408]{2,1,0:T(8,128)(2,1)S(1)}, bf16[1,48,1408]{2,1,0:T(8,128)(2,1)S(1)}, u32[]{:S(2)}, u32[]{:S(2)}) %collective-permute-start.3) | collective-permute-done | bytes 135200 | tf_op jit(solution)/shard_map/ppermute | solution.py:803
  19.2 2.4 collective-permute-start.6
  22.2 15.4 %collective-permute-done.5 = bf16[2,48,1408]{2,1,0:T(8,128)(2,1)S(1)} collective-permute-done((bf16[2,48,1408]{2,1,0:T(8,128)(2,1)S(1)}, bf16[2,48,1408]{2,1,0:T(8,128)(2,1)S(1)}, u32[]{:S(2)}, u32[]{:S(2)}) %collective-permute-start.5) | collective-permute-done | bytes 270368 | tf_op jit(solution)/shard_map/ppermute | solution.py:803
  37.8 3.6 %collective-permute-start.7 = (bf16[4,48,1408]{2,1,0:T(8,128)(2,1)S(1)}, bf16[4,48,1408]{2,1,0:T(8,128)(2,1)S(1)}, u32[]{:S(2)}, u32[]{:S(2)}) collective-permute-start(bf16[4,48,1408]{2,1,0:T(8,128)(2,1)S(1)} %pad_maximum_fusion.8), channel_id=1, source_target_pairs={{0,2},{1,5},{2,0},{3,7},{4,6},{5,1},{6,4},{7,3},{8,10},{9,13},{10,... | collective-permute-start | bytes 1622024 | tf_op jit(solution)/shard_map/ppermute | solution.py:803
  43.5 6.0 %collective-permute-done.8 = bf16[2,48,1408]{2,1,0:T(8,128)(2,1)S(1)} collective-permute-done((bf16[2,48,1408]{2,1,0:T(8,128)(2,1)S(1)}, bf16[2,48,1408]{2,1,0:T(8,128)(2,1)S(1)}, u32[]{:S(2)}, u32[]{:S(2)}) %collective-permute-start.8) | collective-permute-done | bytes 270368 | tf_op jit(solution)/shard_map/ppermute | solution.py:803
  51.3 2.7 collective-permute-start.10
  54.0 15.2 %collective-permute-done.12 = bf16[2,48,2304]{2,1,0:T(8,128)(2,1)S(1)} collective-permute-done((bf16[2,48,2304]{2,1,0:T(8,128)(2,1)S(1)}, bf16[2,48,2304]{2,1,0:T(8,128)(2,1)S(1)}, u32[]{:S(2)}, u32[]{:S(2)}) %collective-permute-start.12) | collective-permute-done | bytes 442400 | tf_op jit(solution)/shard_map/ppermute | solution.py:803
  82.0 5.4 %front.2 = (bf16[256,768]{1,0:T(8,128)(2,1)S(1)}, f32[256,768]{1,0:T(8,128)S(1)}, f32[256,768]{1,0:T(8,128)S(1)}, f32[256,384]{1,0:T(8,128)S(1)}, f32[3,256,128]...) custom-call(s32[8]{0:T(128)S(1)} %stack.68.me_ref.info_ref, ...), custom_call_target="tpu_custom_call" | custom-call | flops 1000 | bytes 1000 | tf_op jit(solution)/shard_map/front/pallas_call | solution.py:177
  88.3 9.5 %collective-permute-done.16 = bf16[4,48,2304]{2,1,0:T(8,128)(2,1)} collective-permute-done((bf16[4,48,2304]{2,1,0:T(8,128)(2,1)}, bf16[4,48,2304]{2,1,0:T(8,128)(2,1)}, u32[]{:S(2)}, u32[]{:S(2)}) %collective-permute-start.16) | collective-permute-done | bytes 884768 | tf_op jit(solution)/shard_map/ppermute | solution.py:803
  98.3 2.8 collective-permute-done.17
  102.0 2.6 collective-permute-start.18
  108.8 3.8 %mid.2 = (f32[6,256,128]{2,1,0:T(8,128)S(1)}, f32[2,8,384]{2,1,0:T(8,128)S(1)}, f32[256,768]{1,0:T(8,128)S(1)}, f32[256,128]{1,0:T(8,128)S(1)}, bf16[256,768]{1,...) custom-call(s32[8]{0:T(128)S(1)} %stack.68.me_ref.info_ref, bf16[256,768]{1,0:T(8,128)(2,1)S(1)} %copy-done, ...), custom_call_target="tpu_custom_call" | custom-call | flops 1000 | bytes 1000 | tf_op jit(solution)/shard_map/mid/pallas_call | solution.py:265
  113.5 8.0 %collective-permute-done.21.refs_2_ = bf16[8,48,1408]{2,1,0:T(8,128)(2,1)S(1)} collective-permute-done((bf16[8,48,1408]{2,1,0:T(8,128)(2,1)S(1)}, bf16[8,48,1408]{2,1,0:T(8,128)(2,1)S(1)}, u32[]{:S(2)}, u32[]{:S(2)}) %collective-permute-start.21) | collective-permute-done | bytes 1081376 | tf_op jit(solution)/shard_map/ppermute | solution.py:803
  122.8 5.3 %ffn.1 = (f32[256,3072]{1,0:T(8,128)S(1)}, bf16[256,1536]{1,0:T(8,128)(2,1)S(1)}, f32[256,768]{1,0:T(8,128)S(1)}) custom-call(s32[8]{0:T(128)S(1)} %stack.68.me_ref.info_ref, f32[256,768]{1,0:T(8,128)S(1)} %get-tuple-element.237.after_ref, bf16[256,768]{1,0:T(8,128)(2,1)S(1)} %get-tuple-element.235.lifted_ref.refs_4_, ...), custom_call_target="tpu_custom_call" | custom-call | flops 1000 | bytes 1000 | tf_op jit(solution)/shard_map/ffn/pallas_call | solution.py:311
  128.2 4.7 %front.3 = (bf16[256,768]{1,0:T(8,128)(2,1)S(1)}, f32[256,768]{1,0:T(8,128)S(1)}, f32[256,768]{1,0:T(8,128)S(1)}, f32[256,384]{1,0:T(8,128)S(1)}, f32[3,256,128]...) custom-call(s32[8]{0:T(128)S(1)} %stack.68.me_ref.info_ref, ...), custom_call_target="tpu_custom_call" | custom-call | flops 1000 | bytes 1000 | tf_op jit(solution)/shard_map/front/pallas_call | solution.py:177
  132.9 11.2 %collective-permute-done.26.refs_2_ = bf16[8,48,2304]{2,1,0:T(8,128)(2,1)S(1)} collective-permute-done((bf16[8,48,2304]{2,1,0:T(8,128)(2,1)S(1)}, bf16[8,48,2304]{2,1,0:T(8,128)(2,1)S(1)}, u32[]{:S(2)}, u32[]{:S(2)}) %collective-permute-start.26) | collective-permute-done | bytes 1769504 | tf_op jit(solution)/shard_map/ppermute | solution.py:803
  144.6 3.2 collective-permute-done.27
  147.8 2.2 collective-permute-start.30
  151.3 3.7 %collective-permute-done.28 = f32[2,4,384]{2,1,0:T(4,128)S(1)} collective-permute-done((f32[2,4,384]{2,1,0:T(4,128)S(1)}, f32[2,4,384]{2,1,0:T(4,128)S(1)}, u32[]{:S(2)}, u32[]{:S(2)}) %collective-permute-start.28) | collective-permute-done | bytes 12320 | tf_op jit(solution)/shard_map/ppermute | solution.py:803
  155.0 3.2 mid.3
  158.3 11.0 %turn.1 = (bf16[16,48,1536]{2,1,0:T(8,128)(2,1)S(1)}, bf16[16,48,1536]{2,1,0:T(8,128)(2,1)S(1)}, bf16[256,768]{1,0:T(8,128)(2,1)}, bf16[256,1536]{1,0:T(8,128)(2...) custom-call(s32[8]{0:T(128)S(1)} %stack.68.me_ref.info_ref, ...), custom_call_target="tpu_custom_call" | custom-call | flops 1000 | bytes 1000 | tf_op jit(solution)/shard_map/turn/pallas_call | solution.py:435
  169.4 3.1 back_mid.2
  173.9 4.1 %grad_od.2 = (bf16[16,48,1536]{2,1,0:T(8,128)(2,1)S(1)}, bf16[16,48,1536]{2,1,0:T(8,128)(2,1)S(1)}) custom-call(s32[8]{0:T(128)S(1)} %stack.68.me_ref.info_ref, bf16[256,768]{1,0:T(8,128)(2,1)S(1)} %get-tuple-element.278.gated_ref, bf16[256,768]{1,0:T(8,128)(2,1)S(1)} %get-tuple-element.267.dmid_ref, bf16[256,1536]{1,0:T(8,128)(2,1)S(1)} %get-tuple-element.279.hidden_ref, ...), custom_call_target="tpu_custom_call" | custom-call | flops 1000 | bytes 1000 | tf_op jit(solution)/shard_map/grad_od/pallas_call | solution.py:754
  179.8 2.0 collective-permute-start.35
  184.3 6.2 %back_two.2 = (bf16[16,48,640]{2,1,0:T(8,128)(2,1)S(1)}, bf16[16,48,640]{2,1,0:T(8,128)(2,1)S(1)}, f32[256,768]{1,0:T(8,128)S(1)}, f32[2,768]{1,0:T(2,128)S(1)}) custom-call(s32[8]{0:T(128)S(1)} %stack.68.me_ref.info_ref, f32[256,768]{1,0:T(8,128)S(1)} %get-tuple-element.243.x_ref, f32[8,768]{1,0:T(8,128)S(1)} %get-tuple-element.245.p_ref, ...), custom_call_target="tpu_custom_call" | custom-call | flops 1000 | bytes 1000 | tf_op jit(solution)/shard_map/back_two/pallas_call | solution.py:693
  190.5 9.2 %collective-permute-done.38 = bf16[8,48,1536]{2,1,0:T(8,128)(2,1)S(1)} collective-permute-done((bf16[8,48,1536]{2,1,0:T(8,128)(2,1)S(1)}, bf16[8,48,1536]{2,1,0:T(8,128)(2,1)S(1)}, u32[]{:S(2)}, u32[]{:S(2)}) %collective-permute-start.38) | collective-permute-done | bytes 1179680 | tf_op jit(solution)/shard_map/ppermute | solution.py:803
  199.7 2.4 add_convert_fusion.3
  203.3 8.2 %back_ffn.1 = (bf16[16,48,1536]{2,1,0:T(8,128)(2,1)S(1)}, bf16[16,48,1536]{2,1,0:T(8,128)(2,1)S(1)}, bf16[256,768]{1,0:T(8,128)(2,1)S(1)}, f32[256,768]{1,0:T(8,...) custom-call(s32[8]{0:T(128)S(1)} %stack.68.me_ref.info_ref, f32[256,768]{1,0:T(8,128)S(1)} %get-tuple-element.299.dx_ref, ...), custom_call_target="tpu_custom_call" | custom-call | flops 1000 | bytes 1000 | tf_op jit(solution)/shard_map/back_ffn/pallas_call | solution.py:465
  212.1 2.0 collective-permute-start.42
  214.1 8.3 %collective-permute-done.42 = bf16[4,48,1536]{2,1,0:T(8,128)(2,1)S(1)} collective-permute-done((bf16[4,48,1536]{2,1,0:T(8,128)(2,1)S(1)}, bf16[4,48,1536]{2,1,0:T(8,128)(2,1)S(1)}, u32[]{:S(2)}, u32[]{:S(2)}) %collective-permute-start.42) | collective-permute-done | bytes 589856 | tf_op jit(solution)/shard_map/ppermute | solution.py:803
  225.6 3.7 %back_mid.3 = (bf16[256,768]{1,0:T(8,128)(2,1)S(1)}, f32[6,256,128]{2,1,0:T(8,128)S(1)}, f32[1,768]{1,0:T(1,128)S(1)}, f32[2,8,384]{2,1,0:T(8,128)S(1)}, f32[2,384]{1,0:T(2,128)S(1)}) custom-call(s32[8]{0:T(128)S(1)} %stack.68.me_ref.info_ref, bf16[256,768]{1,0:T(8,128)(2,1)S(1)} %get-tuple-element.311.dmid_ref, f32[8,768]{1,0:T(8,128)S(1)} %get-tuple-element.222.p_ref, ...), custom_call_target="tpu_custom_call" | custom-call | flops 1000 | bytes 1000 | tf_op jit(solution)/shard_map/back_mid/pallas_call | solution.py:541
  229.3 2.9 collective-permute-start.46
  234.0 2.1 collective-permute-start.49
  237.5 4.1 %grad_od.3 = (bf16[16,48,1536]{2,1,0:T(8,128)(2,1)S(1)}, bf16[16,48,1536]{2,1,0:T(8,128)(2,1)S(1)}) custom-call(s32[8]{0:T(128)S(1)} %stack.68.me_ref.info_ref, bf16[256,768]{1,0:T(8,128)(2,1)S(1)} %get-tuple-element.325.gated_ref, bf16[256,768]{1,0:T(8,128)(2,1)S(1)} %get-tuple-element.311.dmid_ref, bf16[256,1536]{1,0:T(8,128)(2,1)S(1)} %copy-done.4, ...), custom_call_target="tpu_custom_call" | custom-call | flops 1000 | bytes 1000 | tf_op jit(solution)/shard_map/grad_od/pallas_call | solution.py:754
  247.9 7.1 %back_two.3 = (bf16[16,48,640]{2,1,0:T(8,128)(2,1)S(1)}, bf16[16,48,640]{2,1,0:T(8,128)(2,1)S(1)}, f32[256,768]{1,0:T(8,128)}, f32[2,768]{1,0:T(2,128)}) custom-call(s32[8]{0:T(128)S(1)} %stack.68.me_ref.info_ref, bf16[256,768]{1,0:T(8,128)(2,1)S(1)} %copy-done, f32[8,768]{1,0:T(8,128)S(1)} %get-tuple-element.222.p_ref, ...), custom_call_target="tpu_custom_call" | custom-call | flops 1000 | bytes 1000 | tf_op jit(solution)/shard_map/back_two/pallas_call | solution.py:693
  255.0 6.1 %collective-permute-done.54 = bf16[1,48,1536]{2,1,0:T(8,128)(2,1)S(1)} collective-permute-done((bf16[1,48,1536]{2,1,0:T(8,128)(2,1)S(1)}, bf16[1,48,1536]{2,1,0:T(8,128)(2,1)S(1)}, u32[]{:S(2)}, u32[]{:S(2)}) %collective-permute-start.54) | collective-permute-done | bytes 147488 | tf_op jit(solution)/shard_map/ppermute | solution.py:803
  267.0 2.7 collective-permute-start.60
  270.4 6.5 %collective-permute-done.60 = bf16[2,48,640]{2,1,0:T(8,128)(2,1)S(1)} collective-permute-done((bf16[2,48,640]{2,1,0:T(8,128)(2,1)S(1)}, bf16[2,48,640]{2,1,0:T(8,128)(2,1)S(1)}, u32[]{:S(2)}, u32[]{:S(2)}) %collective-permute-start.60) | collective-permute-done | bytes 122912 | tf_op jit(solution)/shard_map/ppermute | solution.py:803
  276.9 6.2 %collective-permute-done.59 = bf16[2,48,1536]{2,1,0:T(8,128)(2,1)S(1)} collective-permute-done((bf16[2,48,1536]{2,1,0:T(8,128)(2,1)S(1)}, bf16[2,48,1536]{2,1,0:T(8,128)(2,1)S(1)}, u32[]{:S(2)}, u32[]{:S(2)}) %collective-permute-start.59) | collective-permute-done | bytes 294944 | tf_op jit(solution)/shard_map/ppermute | solution.py:803
  283.5 4.2 %collective-permute-start.63 = (bf16[4,48,1536]{2,1,0:T(8,128)(2,1)S(1)}, bf16[4,48,1536]{2,1,0:T(8,128)(2,1)S(1)}, u32[]{:S(2)}, u32[]{:S(2)}) collective-permute-start(bf16[4,48,1536]{2,1,0:T(8,128)(2,1)S(1)} %get-tuple-element.365), channel_id=1, source_target_pairs={{0,2},{1,5},{2,0},{3,7},{4,6},{5,1},{6,4},{7,3},{8,10},{9,13},{10,... | collective-permute-start | bytes 1769480 | tf_op jit(solution)/shard_map/ppermute | solution.py:803
  289.4 3.3 %collective-permute-start.62 = (bf16[2,48,1536]{2,1,0:T(8,128)(2,1)S(1)}, bf16[2,48,1536]{2,1,0:T(8,128)(2,1)S(1)}, u32[]{:S(2)}, u32[]{:S(2)}) collective-permute-start(bf16[2,48,1536]{2,1,0:T(8,128)(2,1)S(1)} %get-tuple-element.367), channel_id=1, source_target_pairs={{0,8},{1,17},{2,10},{3,19},{4,12},{5,21},{6,14},{7,23},{8,0},{9,25... | collective-permute-start | bytes 884744 | tf_op jit(solution)/shard_map/ppermute | solution.py:803
  295.0 6.2 %collective-permute-done.69 = bf16[1,48,640]{2,1,0:T(8,128)(2,1)S(1)} collective-permute-done((bf16[1,48,640]{2,1,0:T(8,128)(2,1)S(1)}, bf16[1,48,640]{2,1,0:T(8,128)(2,1)S(1)}, u32[]{:S(2)}, u32[]{:S(2)}) %collective-permute-start.69) | collective-permute-done | bytes 61472 | tf_op jit(solution)/shard_map/ppermute | solution.py:803
  303.8 2.0 collective-permute-start.64
  305.8 5.7 %collective-permute-done.65 = bf16[2,48,1536]{2,1,0:T(8,128)(2,1)S(1)} collective-permute-done((bf16[2,48,1536]{2,1,0:T(8,128)(2,1)S(1)}, bf16[2,48,1536]{2,1,0:T(8,128)(2,1)S(1)}, u32[]{:S(2)}, u32[]{:S(2)}) %collective-permute-start.65) | collective-permute-done | bytes 294944 | tf_op jit(solution)/shard_map/ppermute | solution.py:803
  311.6 3.7 %collective-permute-done.64 = bf16[2,48,640]{2,1,0:T(8,128)(2,1)S(1)} collective-permute-done((bf16[2,48,640]{2,1,0:T(8,128)(2,1)S(1)}, bf16[2,48,640]{2,1,0:T(8,128)(2,1)S(1)}, u32[]{:S(2)}, u32[]{:S(2)}) %collective-permute-start.64) | collective-permute-done | bytes 122912 | tf_op jit(solution)/shard_map/ppermute | solution.py:803
  317.5 2.1 collective-permute-done.66
  319.6 2.6 collective-permute-done.67
  (242 shorter events, 75.8 us)
Async XLA Ops:
  7.1 12.0 %collective-permute-start.1 = (bf16[1,48,2304]{2,1,0:T(8,128)(2,1)S(1)}, bf16[1,48,2304]{2,1,0:T(8,128)(2,1)S(1)}, u32[]{:S(2)}, u32[]{:S(2)}) collective-permute-start(bf16[1,48,2304]{2,1,0:T(8,128)(2,1)S(1)} %maximum_bitcast_fusion), channel_id=1, source_target_pairs={{0,8},{1,17},{2,10},{3,19},{4,12},{5,21},{6,14},{7,23},{8,0},{9,25... | collective-permute-start | bytes 663560 | tf_op jit(solution)/shard_map/ppermute | solution.py:803
  10.1 9.0 %collective-permute-start.4 = (bf16[1,48,2304]{2,1,0:T(8,128)(2,1)S(1)}, bf16[1,48,2304]{2,1,0:T(8,128)(2,1)S(1)}, u32[]{:S(2)}, u32[]{:S(2)}) collective-permute-start(bf16[1,48,2304]{2,1,0:T(8,128)(2,1)S(1)} %maximum_bitcast_fusion.1), channel_id=1, source_target_pairs={{0,2},{1,5},{2,0},{3,7},{4,6},{5,1},{6,4},{7,3},{8,10},{9,13},{10,... | collective-permute-start | bytes 663560 | tf_op jit(solution)/shard_map/ppermute | solution.py:803
  12.3 6.8 %collective-permute-start.2 = (bf16[1,48,1408]{2,1,0:T(8,128)(2,1)S(1)}, bf16[1,48,1408]{2,1,0:T(8,128)(2,1)S(1)}, u32[]{:S(2)}, u32[]{:S(2)}) collective-permute-start(bf16[1,48,1408]{2,1,0:T(8,128)(2,1)S(1)} %get-tuple-element.435), channel_id=1, source_target_pairs={{0,8},{1,17},{2,10},{3,19},{4,12},{5,21},{6,14},{7,23},{8,0},{9,25... | collective-permute-start | bytes 405512 | tf_op jit(solution)/shard_map/ppermute | solution.py:803
  19.2 18.4 %collective-permute-start.6 = (bf16[2,48,2304]{2,1,0:T(8,128)(2,1)S(1)}, bf16[2,48,2304]{2,1,0:T(8,128)(2,1)S(1)}, u32[]{:S(2)}, u32[]{:S(2)}) collective-permute-start(bf16[2,48,2304]{2,1,0:T(8,128)(2,1)S(1)} %pad_maximum_fusion.10), channel_id=1, source_target_pairs={{0,16},{1,9},{2,18},{3,11},{4,20},{5,13},{6,22},{7,15},{8,24},{9,1... | collective-permute-start | bytes 1327112 | tf_op jit(solution)/shard_map/ppermute | solution.py:803
  21.6 16.0 %collective-permute-start.5 = (bf16[2,48,1408]{2,1,0:T(8,128)(2,1)S(1)}, bf16[2,48,1408]{2,1,0:T(8,128)(2,1)S(1)}, u32[]{:S(2)}, u32[]{:S(2)}) collective-permute-start(bf16[2,48,1408]{2,1,0:T(8,128)(2,1)S(1)} %pad_maximum_fusion.12), channel_id=1, source_target_pairs={{0,16},{1,9},{2,18},{3,11},{4,20},{5,13},{6,22},{7,15},{8,24},{9,1... | collective-permute-start | bytes 811016 | tf_op jit(solution)/shard_map/ppermute | solution.py:803
  37.8 11.8 %collective-permute-start.7 = (bf16[4,48,1408]{2,1,0:T(8,128)(2,1)S(1)}, bf16[4,48,1408]{2,1,0:T(8,128)(2,1)S(1)}, u32[]{:S(2)}, u32[]{:S(2)}) collective-permute-start(bf16[4,48,1408]{2,1,0:T(8,128)(2,1)S(1)} %pad_maximum_fusion.8), channel_id=1, source_target_pairs={{0,2},{1,5},{2,0},{3,7},{4,6},{5,1},{6,4},{7,3},{8,10},{9,13},{10,... | collective-permute-start | bytes 1622024 | tf_op jit(solution)/shard_map/ppermute | solution.py:803
  41.4 8.2 %collective-permute-start.8 = (bf16[2,48,1408]{2,1,0:T(8,128)(2,1)S(1)}, bf16[2,48,1408]{2,1,0:T(8,128)(2,1)S(1)}, u32[]{:S(2)}, u32[]{:S(2)}) collective-permute-start(bf16[2,48,1408]{2,1,0:T(8,128)(2,1)S(1)} %pad_maximum_fusion.13), channel_id=1, source_target_pairs={{0,8},{1,17},{2,10},{3,19},{4,12},{5,21},{6,14},{7,23},{8,0},{9,25... | collective-permute-start | bytes 811016 | tf_op jit(solution)/shard_map/ppermute | solution.py:803
  41.9 27.3 %collective-permute-start.11 = (bf16[4,48,2304]{2,1,0:T(8,128)(2,1)S(1)}, bf16[4,48,2304]{2,1,0:T(8,128)(2,1)S(1)}, u32[]{:S(2)}, u32[]{:S(2)}) collective-permute-start(bf16[4,48,2304]{2,1,0:T(8,128)(2,1)S(1)} %pad_maximum_fusion.4), channel_id=1, source_target_pairs={{0,2},{1,5},{2,0},{3,7},{4,6},{5,1},{6,4},{7,3},{8,10},{9,13},{10,... | collective-permute-start | bytes 2654216 | tf_op jit(solution)/shard_map/ppermute | solution.py:803
  42.5 26.8 %collective-permute-start.12 = (bf16[2,48,2304]{2,1,0:T(8,128)(2,1)S(1)}, bf16[2,48,2304]{2,1,0:T(8,128)(2,1)S(1)}, u32[]{:S(2)}, u32[]{:S(2)}) collective-permute-start(bf16[2,48,2304]{2,1,0:T(8,128)(2,1)S(1)} %pad_maximum_fusion.11), channel_id=1, source_target_pairs={{0,8},{1,17},{2,10},{3,19},{4,12},{5,21},{6,14},{7,23},{8,0},{9,25... | collective-permute-start | bytes 1327112 | tf_op jit(solution)/shard_map/ppermute | solution.py:803
  49.8 21.9 %collective-permute-start.9 = (bf16[8,48,1408]{2,1,0:T(8,128)(2,1)S(1)}, bf16[8,48,1408]{2,1,0:T(8,128)(2,1)S(1)}, u32[]{:S(2)}, u32[]{:S(2)}) collective-permute-start(bf16[8,48,1408]{2,1,0:T(8,128)(2,1)S(1)} %pad_maximum_fusion.2.refs_0_), channel_id=1, source_target_pairs={{0,4},{1,3},{2,6},{3,1},{4,0},{5,7},{6,2},{7,5},{8,12},{9,11},{10,... | collective-permute-start | bytes 3244040 | tf_op jit(solution)/shard_map/ppermute | solution.py:803
  51.3 20.3 %collective-permute-start.10 = (bf16[4,48,1408]{2,1,0:T(8,128)(2,1)S(1)}, bf16[4,48,1408]{2,1,0:T(8,128)(2,1)S(1)}, u32[]{:S(2)}, u32[]{:S(2)}) collective-permute-start(bf16[4,48,1408]{2,1,0:T(8,128)(2,1)S(1)} %pad_maximum_fusion.9), channel_id=1, source_target_pairs={{0,16},{1,9},{2,18},{3,11},{4,20},{5,13},{6,22},{7,15},{8,24},{9,1... | collective-permute-start | bytes 1622024 | tf_op jit(solution)/shard_map/ppermute | solution.py:803
  72.4 25.4 %collective-permute-start.15 = (bf16[8,48,2304]{2,1,0:T(8,128)(2,1)}, bf16[8,48,2304]{2,1,0:T(8,128)(2,1)}, u32[]{:S(2)}, u32[]{:S(2)}) collective-permute-start(bf16[8,48,2304]{2,1,0:T(8,128)(2,1)} %pad_maximum_fusion.refs_0_), channel_id=1, source_target_pairs={{0,4},{1,3},{2,6},{3,1},{4,0},{5,7},{6,2},{7,5},{8,12},{9,11},{10,... | collective-permute-start | bytes 5308424 | tf_op jit(solution)/shard_map/ppermute | solution.py:803
  74.0 23.7 %collective-permute-start.16 = (bf16[4,48,2304]{2,1,0:T(8,128)(2,1)}, bf16[4,48,2304]{2,1,0:T(8,128)(2,1)}, u32[]{:S(2)}, u32[]{:S(2)}) collective-permute-start(bf16[4,48,2304]{2,1,0:T(8,128)(2,1)} %pad_maximum_fusion.5), channel_id=1, source_target_pairs={{0,16},{1,9},{2,18},{3,11},{4,20},{5,13},{6,22},{7,15},{8,24},{9,1... | collective-permute-start | bytes 2654216 | tf_op jit(solution)/shard_map/ppermute | solution.py:803
  78.9 34.6 %collective-permute-start.23 = (bf16[8,48,2304]{2,1,0:T(8,128)(2,1)}, bf16[8,48,2304]{2,1,0:T(8,128)(2,1)S(1)}, u32[]{:S(2)}, u32[]{:S(2)}) collective-permute-start(bf16[8,48,2304]{2,1,0:T(8,128)(2,1)} %pad_maximum_fusion.refs_0_), channel_id=1, source_target_pairs={{0,1},{1,0},{2,3},{3,2},{4,5},{5,4},{6,7},{7,6},{8,9},{9,8},{10,11... | collective-permute-start | bytes 5308424 | tf_op jit(solution)/shard_map/ppermute | solution.py:803
  97.8 23.8 %collective-permute-start.22 = (bf16[8,48,2304]{2,1,0:T(8,128)(2,1)}, bf16[8,48,2304]{2,1,0:T(8,128)(2,1)S(1)}, u32[]{:S(2)}, u32[]{:S(2)}) collective-permute-start(bf16[8,48,2304]{2,1,0:T(8,128)(2,1)} %collective-permute-done.15.refs_2_), channel_id=1, source_target_pairs={{0,1},{1,0},{2,3},{3,2},{4,5},{5,4},{6,7},{7,6},{8,9},{9,8},{10,11... | collective-permute-start | bytes 5308424 | tf_op jit(solution)/shard_map/ppermute | solution.py:803
  106.3 15.2 %collective-permute-start.21 = (bf16[8,48,1408]{2,1,0:T(8,128)(2,1)S(1)}, bf16[8,48,1408]{2,1,0:T(8,128)(2,1)S(1)}, u32[]{:S(2)}, u32[]{:S(2)}) collective-permute-start(bf16[8,48,1408]{2,1,0:T(8,128)(2,1)S(1)} %pad_maximum_fusion.3.refs_0_), channel_id=1, source_target_pairs={{0,4},{1,3},{2,6},{3,1},{4,0},{5,7},{6,2},{7,5},{8,12},{9,11},{10,... | collective-permute-start | bytes 3244040 | tf_op jit(solution)/shard_map/ppermute | solution.py:803
  121.6 22.5 %collective-permute-start.26 = (bf16[8,48,2304]{2,1,0:T(8,128)(2,1)S(1)}, bf16[8,48,2304]{2,1,0:T(8,128)(2,1)S(1)}, u32[]{:S(2)}, u32[]{:S(2)}) collective-permute-start(bf16[8,48,2304]{2,1,0:T(8,128)(2,1)S(1)} %pad_maximum_fusion.1.refs_0_), channel_id=1, source_target_pairs={{0,4},{1,3},{2,6},{3,1},{4,0},{5,7},{6,2},{7,5},{8,12},{9,11},{10,... | collective-permute-start | bytes 5308424 | tf_op jit(solution)/shard_map/ppermute | solution.py:803
  122.8 35.4 %collective-permute-start.32 = (bf16[8,48,2304]{2,1,0:T(8,128)(2,1)S(1)}, bf16[8,48,2304]{2,1,0:T(8,128)(2,1)S(1)}, u32[]{:S(2)}, u32[]{:S(2)}) collective-permute-start(bf16[8,48,2304]{2,1,0:T(8,128)(2,1)S(1)} %pad_maximum_fusion.1.refs_0_), channel_id=1, source_target_pairs={{0,1},{1,0},{2,3},{3,2},{4,5},{5,4},{6,7},{7,6},{8,9},{9,8},{10,11... | collective-permute-start | bytes 5308424 | tf_op jit(solution)/shard_map/ppermute | solution.py:803
  144.1 14.2 %collective-permute-start.31 = (bf16[8,48,2304]{2,1,0:T(8,128)(2,1)S(1)}, bf16[8,48,2304]{2,1,0:T(8,128)(2,1)S(1)}, u32[]{:S(2)}, u32[]{:S(2)}) collective-permute-start(bf16[8,48,2304]{2,1,0:T(8,128)(2,1)S(1)} %collective-permute-done.26.refs_2_), channel_id=1, source_target_pairs={{0,1},{1,0},{2,3},{3,2},{4,5},{5,4},{6,7},{7,6},{8,9},{9,8},{10,11... | collective-permute-start | bytes 5308424 | tf_op jit(solution)/shard_map/ppermute | solution.py:803
  147.8 7.2 %collective-permute-start.30 = (f32[2,4,384]{2,1,0:T(4,128)S(1)}, f32[2,4,384]{2,1,0:T(4,128)S(1)}, u32[]{:S(2)}, u32[]{:S(2)}) collective-permute-start(f32[2,4,384]{2,1,0:T(4,128)S(1)} %pad_maximum_fusion.15), channel_id=1, source_target_pairs={{0,6},{1,7},{2,4},{3,5},{4,2},{5,3},{6,0},{7,1},{8,14},{9,15},{10,... | collective-permute-start | bytes 36872 | tf_op jit(solution)/shard_map/ppermute | solution.py:803
  178.0 21.7 %collective-permute-start.39 = (bf16[16,48,1536]{2,1,0:T(8,128)(2,1)S(1)}, bf16[16,48,1536]{2,1,0:T(8,128)(2,1)}, u32[]{:S(2)}, u32[]{:S(2)}) collective-permute-start(bf16[16,48,1536]{2,1,0:T(8,128)(2,1)S(1)} %get-tuple-element.293), channel_id=1, source_target_pairs={{0,1},{1,0},{2,3},{3,2},{4,5},{5,4},{6,7},{7,6},{8,9},{9,8},{10,11... | collective-permute-start | bytes 7077896 | tf_op jit(solution)/shard_map/ppermute | solution.py:803
  183.4 16.3 %collective-permute-start.38 = (bf16[8,48,1536]{2,1,0:T(8,128)(2,1)S(1)}, bf16[8,48,1536]{2,1,0:T(8,128)(2,1)S(1)}, u32[]{:S(2)}, u32[]{:S(2)}) collective-permute-start(bf16[8,48,1536]{2,1,0:T(8,128)(2,1)S(1)} %get-tuple-element.286), channel_id=1, source_target_pairs={{0,4},{1,3},{2,6},{3,1},{4,0},{5,7},{6,2},{7,5},{8,12},{9,11},{10,... | collective-permute-start | bytes 3538952 | tf_op jit(solution)/shard_map/ppermute | solution.py:803
  202.5 20.2 %collective-permute-start.40 = (bf16[8,48,1536]{2,1,0:T(8,128)(2,1)S(1)}, bf16[8,48,1536]{2,1,0:T(8,128)(2,1)S(1)}, u32[]{:S(2)}, u32[]{:S(2)}) collective-permute-start(bf16[8,48,1536]{2,1,0:T(8,128)(2,1)S(1)} %get-tuple-element.298), channel_id=1, source_target_pairs={{0,4},{1,3},{2,6},{3,1},{4,0},{5,7},{6,2},{7,5},{8,12},{9,11},{10,... | collective-permute-start | bytes 3538952 | tf_op jit(solution)/shard_map/ppermute | solution.py:803
  203.3 10.8 %collective-permute-start.41 = (bf16[16,48,640]{2,1,0:T(8,128)(2,1)S(1)}, bf16[16,48,640]{2,1,0:T(8,128)(2,1)S(1)}, u32[]{:S(2)}, u32[]{:S(2)}) collective-permute-start(bf16[16,48,640]{2,1,0:T(8,128)(2,1)S(1)} %get-tuple-element.303), channel_id=1, source_target_pairs={{0,1},{1,0},{2,3},{3,2},{4,5},{5,4},{6,7},{7,6},{8,9},{9,8},{10,11... | collective-permute-start | bytes 2949128 | tf_op jit(solution)/shard_map/ppermute | solution.py:803
  211.5 22.4 %collective-permute-start.43 = (bf16[16,48,1536]{2,1,0:T(8,128)(2,1)S(1)}, bf16[16,48,1536]{2,1,0:T(8,128)(2,1)S(1)}, u32[]{:S(2)}, u32[]{:S(2)}) collective-permute-start(bf16[16,48,1536]{2,1,0:T(8,128)(2,1)S(1)} %get-tuple-element.317), channel_id=1, source_target_pairs={{0,1},{1,0},{2,3},{3,2},{4,5},{5,4},{6,7},{7,6},{8,9},{9,8},{10,11... | collective-permute-start | bytes 7077896 | tf_op jit(solution)/shard_map/ppermute | solution.py:803
  212.1 10.3 %collective-permute-start.42 = (bf16[4,48,1536]{2,1,0:T(8,128)(2,1)S(1)}, bf16[4,48,1536]{2,1,0:T(8,128)(2,1)S(1)}, u32[]{:S(2)}, u32[]{:S(2)}) collective-permute-start(bf16[4,48,1536]{2,1,0:T(8,128)(2,1)S(1)} %get-tuple-element.304), channel_id=1, source_target_pairs={{0,2},{1,5},{2,0},{3,7},{4,6},{5,1},{6,4},{7,3},{8,10},{9,13},{10,... | collective-permute-start | bytes 1769480 | tf_op jit(solution)/shard_map/ppermute | solution.py:803
  223.1 10.8 %collective-permute-start.45 = (bf16[2,48,1536]{2,1,0:T(8,128)(2,1)S(1)}, bf16[2,48,1536]{2,1,0:T(8,128)(2,1)S(1)}, u32[]{:S(2)}, u32[]{:S(2)}) collective-permute-start(bf16[2,48,1536]{2,1,0:T(8,128)(2,1)S(1)} %get-tuple-element.318), channel_id=1, source_target_pairs={{0,16},{1,9},{2,18},{3,11},{4,20},{5,13},{6,22},{7,15},{8,24},{9,1... | collective-permute-start | bytes 884744 | tf_op jit(solution)/shard_map/ppermute | solution.py:803
  224.1 9.8 %collective-permute-start.44 = (bf16[8,48,640]{2,1,0:T(8,128)(2,1)S(1)}, bf16[8,48,640]{2,1,0:T(8,128)(2,1)S(1)}, u32[]{:S(2)}, u32[]{:S(2)}) collective-permute-start(bf16[8,48,640]{2,1,0:T(8,128)(2,1)S(1)} %get-tuple-element.310), channel_id=1, source_target_pairs={{0,4},{1,3},{2,6},{3,1},{4,0},{5,7},{6,2},{7,5},{8,12},{9,11},{10,... | collective-permute-start | bytes 1474568 | tf_op jit(solution)/shard_map/ppermute | solution.py:803
  234.0 8.7 %collective-permute-start.49 = (f32[2,2,384]{2,1,0:T(2,128)S(1)}, f32[2,2,384]{2,1,0:T(2,128)S(1)}, u32[]{:S(2)}, u32[]{:S(2)}) collective-permute-start(f32[2,2,384]{2,1,0:T(2,128)S(1)} %pad_maximum_fusion.17), channel_id=1, source_target_pairs={{0,6},{1,7},{2,4},{3,5},{4,2},{5,3},{6,0},{7,1},{8,14},{9,15},{10,... | collective-permute-start | bytes 18440 | tf_op jit(solution)/shard_map/ppermute | solution.py:803
  241.6 22.0 %collective-permute-start.55 = (bf16[16,48,1536]{2,1,0:T(8,128)(2,1)S(1)}, bf16[16,48,1536]{2,1,0:T(8,128)(2,1)S(1)}, u32[]{:S(2)}, u32[]{:S(2)}) collective-permute-start(bf16[16,48,1536]{2,1,0:T(8,128)(2,1)S(1)} %get-tuple-element.351), channel_id=1, source_target_pairs={{0,1},{1,0},{2,3},{3,2},{4,5},{5,4},{6,7},{7,6},{8,9},{9,8},{10,11... | collective-permute-start | bytes 7077896 | tf_op jit(solution)/shard_map/ppermute | solution.py:803
  242.7 21.0 %collective-permute-start.51 = (bf16[8,48,1536]{2,1,0:T(8,128)(2,1)S(1)}, bf16[8,48,1536]{2,1,0:T(8,128)(2,1)S(1)}, u32[]{:S(2)}, u32[]{:S(2)}) collective-permute-start(bf16[8,48,1536]{2,1,0:T(8,128)(2,1)S(1)} %get-tuple-element.333), channel_id=1, source_target_pairs={{0,4},{1,3},{2,6},{3,1},{4,0},{5,7},{6,2},{7,5},{8,12},{9,11},{10,... | collective-permute-start | bytes 3538952 | tf_op jit(solution)/shard_map/ppermute | solution.py:803
  243.4 20.3 %collective-permute-start.52 = (bf16[4,48,1536]{2,1,0:T(8,128)(2,1)S(1)}, bf16[4,48,1536]{2,1,0:T(8,128)(2,1)S(1)}, u32[]{:S(2)}, u32[]{:S(2)}) collective-permute-start(bf16[4,48,1536]{2,1,0:T(8,128)(2,1)S(1)} %get-tuple-element.348), channel_id=1, source_target_pairs={{0,16},{1,9},{2,18},{3,11},{4,20},{5,13},{6,22},{7,15},{8,24},{9,1... | collective-permute-start | bytes 1769480 | tf_op jit(solution)/shard_map/ppermute | solution.py:803
  245.2 17.0 %collective-permute-start.53 = (bf16[4,48,640]{2,1,0:T(8,128)(2,1)S(1)}, bf16[4,48,640]{2,1,0:T(8,128)(2,1)S(1)}, u32[]{:S(2)}, u32[]{:S(2)}) collective-permute-start(bf16[4,48,640]{2,1,0:T(8,128)(2,1)S(1)} %get-tuple-element.349), channel_id=1, source_target_pairs={{0,2},{1,5},{2,0},{3,7},{4,6},{5,1},{6,4},{7,3},{8,10},{9,13},{10,... | collective-permute-start | bytes 737288 | tf_op jit(solution)/shard_map/ppermute | solution.py:803
  246.6 14.6 %collective-permute-start.54 = (bf16[1,48,1536]{2,1,0:T(8,128)(2,1)S(1)}, bf16[1,48,1536]{2,1,0:T(8,128)(2,1)S(1)}, u32[]{:S(2)}, u32[]{:S(2)}) collective-permute-start(bf16[1,48,1536]{2,1,0:T(8,128)(2,1)S(1)} %add_convert_fusion.39), channel_id=1, source_target_pairs={{0,8},{1,17},{2,10},{3,19},{4,12},{5,21},{6,14},{7,23},{8,0},{9,25... | collective-permute-start | bytes 442376 | tf_op jit(solution)/shard_map/ppermute | solution.py:803
  265.0 18.2 %collective-permute-start.58 = (bf16[8,48,1536]{2,1,0:T(8,128)(2,1)S(1)}, bf16[8,48,1536]{2,1,0:T(8,128)(2,1)S(1)}, u32[]{:S(2)}, u32[]{:S(2)}) collective-permute-start(bf16[8,48,1536]{2,1,0:T(8,128)(2,1)S(1)} %get-tuple-element.356), channel_id=1, source_target_pairs={{0,4},{1,3},{2,6},{3,1},{4,0},{5,7},{6,2},{7,5},{8,12},{9,11},{10,... | collective-permute-start | bytes 3538952 | tf_op jit(solution)/shard_map/ppermute | solution.py:803
  266.5 16.7 %collective-permute-start.59 = (bf16[2,48,1536]{2,1,0:T(8,128)(2,1)S(1)}, bf16[2,48,1536]{2,1,0:T(8,128)(2,1)S(1)}, u32[]{:S(2)}, u32[]{:S(2)}) collective-permute-start(bf16[2,48,1536]{2,1,0:T(8,128)(2,1)S(1)} %get-tuple-element.360), channel_id=1, source_target_pairs={{0,8},{1,17},{2,10},{3,19},{4,12},{5,21},{6,14},{7,23},{8,0},{9,25... | collective-permute-start | bytes 884744 | tf_op jit(solution)/shard_map/ppermute | solution.py:803
  267.0 10.0 %collective-permute-start.60 = (bf16[2,48,640]{2,1,0:T(8,128)(2,1)S(1)}, bf16[2,48,640]{2,1,0:T(8,128)(2,1)S(1)}, u32[]{:S(2)}, u32[]{:S(2)}) collective-permute-start(bf16[2,48,640]{2,1,0:T(8,128)(2,1)S(1)} %get-tuple-element.361), channel_id=1, source_target_pairs={{0,16},{1,9},{2,18},{3,11},{4,20},{5,13},{6,22},{7,15},{8,24},{9,1... | collective-permute-start | bytes 368648 | tf_op jit(solution)/shard_map/ppermute | solution.py:803
  269.9 22.8 %collective-permute-start.56 = (bf16[8,48,640]{2,1,0:T(8,128)(2,1)S(1)}, bf16[8,48,640]{2,1,0:T(8,128)(2,1)S(1)}, u32[]{:S(2)}, u32[]{:S(2)}) collective-permute-start(bf16[8,48,640]{2,1,0:T(8,128)(2,1)S(1)} %get-tuple-element.358), channel_id=1, source_target_pairs={{0,4},{1,3},{2,6},{3,1},{4,0},{5,7},{6,2},{7,5},{8,12},{9,11},{10,... | collective-permute-start | bytes 1474568 | tf_op jit(solution)/shard_map/ppermute | solution.py:803
  270.1 19.2 %collective-permute-start.57 = (bf16[4,48,1536]{2,1,0:T(8,128)(2,1)S(1)}, bf16[4,48,1536]{2,1,0:T(8,128)(2,1)S(1)}, u32[]{:S(2)}, u32[]{:S(2)}) collective-permute-start(bf16[4,48,1536]{2,1,0:T(8,128)(2,1)S(1)} %get-tuple-element.359), channel_id=1, source_target_pairs={{0,16},{1,9},{2,18},{3,11},{4,20},{5,13},{6,22},{7,15},{8,24},{9,1... | collective-permute-start | bytes 1769480 | tf_op jit(solution)/shard_map/ppermute | solution.py:803
  283.5 18.1 %collective-permute-start.63 = (bf16[4,48,1536]{2,1,0:T(8,128)(2,1)S(1)}, bf16[4,48,1536]{2,1,0:T(8,128)(2,1)S(1)}, u32[]{:S(2)}, u32[]{:S(2)}) collective-permute-start(bf16[4,48,1536]{2,1,0:T(8,128)(2,1)S(1)} %get-tuple-element.365), channel_id=1, source_target_pairs={{0,2},{1,5},{2,0},{3,7},{4,6},{5,1},{6,4},{7,3},{8,10},{9,13},{10,... | collective-permute-start | bytes 1769480 | tf_op jit(solution)/shard_map/ppermute | solution.py:803
  289.4 14.1 %collective-permute-start.62 = (bf16[2,48,1536]{2,1,0:T(8,128)(2,1)S(1)}, bf16[2,48,1536]{2,1,0:T(8,128)(2,1)S(1)}, u32[]{:S(2)}, u32[]{:S(2)}) collective-permute-start(bf16[2,48,1536]{2,1,0:T(8,128)(2,1)S(1)} %get-tuple-element.367), channel_id=1, source_target_pairs={{0,8},{1,17},{2,10},{3,19},{4,12},{5,21},{6,14},{7,23},{8,0},{9,25... | collective-permute-start | bytes 884744 | tf_op jit(solution)/shard_map/ppermute | solution.py:803
  292.7 8.5 %collective-permute-start.69 = (bf16[1,48,640]{2,1,0:T(8,128)(2,1)S(1)}, bf16[1,48,640]{2,1,0:T(8,128)(2,1)S(1)}, u32[]{:S(2)}, u32[]{:S(2)}) collective-permute-start(bf16[1,48,640]{2,1,0:T(8,128)(2,1)S(1)} %add_convert_fusion.47), channel_id=1, source_target_pairs={{0,8},{1,17},{2,10},{3,19},{4,12},{5,21},{6,14},{7,23},{8,0},{9,25... | collective-permute-start | bytes 184328 | tf_op jit(solution)/shard_map/ppermute | solution.py:803
  292.9 8.3 %collective-permute-start.70 = (bf16[1,48,1536]{2,1,0:T(8,128)(2,1)S(1)}, bf16[1,48,1536]{2,1,0:T(8,128)(2,1)S(1)}, u32[]{:S(2)}, u32[]{:S(2)}) collective-permute-start(bf16[1,48,1536]{2,1,0:T(8,128)(2,1)S(1)} %add_convert_fusion.38), channel_id=1, source_target_pairs={{0,2},{1,5},{2,0},{3,7},{4,6},{5,1},{6,4},{7,3},{8,10},{9,13},{10,... | collective-permute-start | bytes 442376 | tf_op jit(solution)/shard_map/ppermute | solution.py:803
  293.6 10.2 %collective-permute-start.61 = (bf16[4,48,640]{2,1,0:T(8,128)(2,1)S(1)}, bf16[4,48,640]{2,1,0:T(8,128)(2,1)S(1)}, u32[]{:S(2)}, u32[]{:S(2)}) collective-permute-start(bf16[4,48,640]{2,1,0:T(8,128)(2,1)S(1)} %get-tuple-element.369), channel_id=1, source_target_pairs={{0,2},{1,5},{2,0},{3,7},{4,6},{5,1},{6,4},{7,3},{8,10},{9,13},{10,... | collective-permute-start | bytes 737288 | tf_op jit(solution)/shard_map/ppermute | solution.py:803
  301.5 21.0 %collective-permute-start.72 = (f32[24,2944]{1,0:T(8,128)S(1)}, f32[24,2944]{1,0:T(8,128)S(1)}, u32[]{:S(2)}, u32[]{:S(2)}) collective-permute-start(f32[24,2944]{1,0:T(8,128)S(1)} %get-tuple-element.428), channel_id=1, source_target_pairs={{0,1},{1,0},{2,3},{3,2},{4,5},{5,4},{6,7},{7,6},{8,9},{9,8},{10,11... | collective-permute-start | bytes 847880 | tf_op jit(solution)/shard_map/ppermute | solution.py:803
  301.7 9.8 %collective-permute-start.65 = (bf16[2,48,1536]{2,1,0:T(8,128)(2,1)S(1)}, bf16[2,48,1536]{2,1,0:T(8,128)(2,1)S(1)}, u32[]{:S(2)}, u32[]{:S(2)}) collective-permute-start(bf16[2,48,1536]{2,1,0:T(8,128)(2,1)S(1)} %get-tuple-element.371), channel_id=1, source_target_pairs={{0,16},{1,9},{2,18},{3,11},{4,20},{5,13},{6,22},{7,15},{8,24},{9,1... | collective-permute-start | bytes 884744 | tf_op jit(solution)/shard_map/ppermute | solution.py:803
  303.5 12.2 %collective-permute-start.68 = (bf16[1,48,1536]{2,1,0:T(8,128)(2,1)S(1)}, bf16[1,48,1536]{2,1,0:T(8,128)(2,1)S(1)}, u32[]{:S(2)}, u32[]{:S(2)}) collective-permute-start(bf16[1,48,1536]{2,1,0:T(8,128)(2,1)S(1)} %add_convert_fusion.37), channel_id=1, source_target_pairs={{0,2},{1,5},{2,0},{3,7},{4,6},{5,1},{6,4},{7,3},{8,10},{9,13},{10,... | collective-permute-start | bytes 442376 | tf_op jit(solution)/shard_map/ppermute | solution.py:803
  303.8 11.5 %collective-permute-start.64 = (bf16[2,48,640]{2,1,0:T(8,128)(2,1)S(1)}, bf16[2,48,640]{2,1,0:T(8,128)(2,1)S(1)}, u32[]{:S(2)}, u32[]{:S(2)}) collective-permute-start(bf16[2,48,640]{2,1,0:T(8,128)(2,1)S(1)} %get-tuple-element.375), channel_id=1, source_target_pairs={{0,16},{1,9},{2,18},{3,11},{4,20},{5,13},{6,22},{7,15},{8,24},{9,1... | collective-permute-start | bytes 368648 | tf_op jit(solution)/shard_map/ppermute | solution.py:803
  (39 other events, 203.2 us)
